TPU v7x, 32 devices: a whole 2x2x4 slice. The times are simulated.
32 devices in a mesh: dp: 16 (over z, y, x), tensor: 2 (over core).
Axes of the slice: x: 2, y: 2, z: 4, core: 2. Of those that a mesh axis runs over, the one named last changes fastest.
Arguments:
- tokens: bfloat16 [16384, 1024], P(('dp', 'tensor')), may hold values from -6 to 6
- w_query: bfloat16 [1024, 1024], P('dp', 'tensor'), may hold values from -0.1875 to 0.1875
- w_key: bfloat16 [1024, 1024], P('dp', 'tensor'), may hold values from -0.1875 to 0.1875
- w_value: bfloat16 [1024, 1024], P('dp', 'tensor'), may hold values from -0.1875 to 0.1875
- w_gate: bfloat16 [1024, 1024], P('dp', 'tensor'), may hold values from -0.1875 to 0.1875
- w_out: bfloat16 [1024, 1024], P('tensor', 'dp'), may hold values from -0.1875 to 0.1875
- w_first: bfloat16 [1024, 2816], P('dp', 'tensor'), may hold values from -0.1875 to 0.1875
- w_second: bfloat16 [1024, 2816], P('dp', 'tensor'), may hold values from -0.1875 to 0.1875
- w_down: bfloat16 [2816, 1024], P('tensor', 'dp'), may hold values from -0.109375 to 0.109375
- decay_rates: float32 [8], P('tensor'), may hold values from 0.00048828125 to 0.05
- cotangent: bfloat16 [16384, 1024], P(('dp', 'tensor')), may hold values from -6 to 6
Outputs:
- layer_out: bfloat16 [16384, 1024], P(('dp', 'tensor'))
- tokens_grad: float32 [16384, 1024], P(('dp', 'tensor'))
- grad_query: float32 [1024, 1024], P('dp', 'tensor')
- grad_key: float32 [1024, 1024], P('dp', 'tensor')
- grad_value: float32 [1024, 1024], P('dp', 'tensor')
- grad_gate: float32 [1024, 1024], P('dp', 'tensor')
- grad_out: float32 [1024, 1024], P('tensor', 'dp')
- grad_first: float32 [1024, 2816], P('dp', 'tensor')
- grad_second: float32 [1024, 2816], P('dp', 'tensor')
- grad_down: float32 [2816, 1024], P('tensor', 'dp')
All inputs are finite; a program needn't handle non-finite values.
Results may differ from a plain program's by a relative error of at most 0.014.
Values may be sent and summed in bfloat16 or wider, within the bound.
No kernel may reach another device: no remote copies, remote signals or barrier semaphores. Data moves between devices by JAX's collectives and lax.ppermute only.
A program may use at most 192 MiB of HBM per device.

v0:
```python
import jax
import jax.numpy as jnp
from jax import lax
from jax.sharding import PartitionSpec as P

eps = 1e-06
wide = jnp.float32
narrow = jnp.bfloat16


def inverse_rms(values):
    return lax.rsqrt(jnp.mean(values * values, axis=-1, keepdims=True) + eps)


def times_transposed(left, right):
    return lax.dot_general(left, right, (((1,), (1,)), ((), ())), preferred_element_type=wide)


def transposed_times(left, right):
    return lax.dot_general(left, right, (((0,), (0,)), ((), ())), preferred_element_type=wide)


def norm_back(grad, normed, scale):
    return scale * (grad - normed * jnp.mean(grad * normed, axis=-1, keepdims=True))


def silu_slope(values):
    sigma = jax.nn.sigmoid(values)
    return sigma * (1.0 + values * (1.0 - sigma))


def fetch_attn(w_query, w_key, w_value, w_gate, w_out):
    return (
        lax.all_gather(w_query, "dp", axis=0, tiled=True),
        lax.all_gather(w_key, "dp", axis=0, tiled=True),
        lax.all_gather(w_value, "dp", axis=0, tiled=True),
        lax.all_gather(w_gate, "dp", axis=0, tiled=True),
        lax.all_gather(w_out, "dp", axis=1, tiled=True),
    )


def fetch_ffn(w_first, w_second, w_down):
    return (
        lax.all_gather(w_first, "dp", axis=0, tiled=True),
        lax.all_gather(w_second, "dp", axis=0, tiled=True),
        lax.all_gather(w_down, "dp", axis=1, tiled=True),
    )


def decay_tables(rates, size):
    position = jnp.arange(size).astype(wide)
    distance = position[:, None] - position[None, :]
    causal = distance >= 0
    safe = jnp.where(causal, distance, 0.0)
    inner = jnp.where(causal[None], jnp.exp(-rates[:, None, None] * safe[None]), 0.0)
    ahead = jnp.exp(-rates[None, :] * position[:, None])
    outof = jnp.exp(-rates[None, :] * (size - position[:, None]))
    whole = jnp.exp(-rates * size)
    return (inner, ahead, outof, whole)


def attend(query, keys, values, rates, block):
    length, width = query.shape
    heads = rates.shape[0]
    head_size = width // heads
    blocks = length // block
    inner, ahead, outof, whole = decay_tables(rates, block)

    def split(array):
        return array.reshape(blocks, block, heads, head_size)

    def advance(state, pieces):
        q_blk, k_blk, v_blk = pieces
        scores = jnp.einsum("ihd,jhd->hij", q_blk, k_blk, preferred_element_type=wide) * inner
        weights = scores.astype(narrow)
        local = jnp.einsum("hij,jhd->ihd", weights, v_blk, preferred_element_type=wide)
        carried = (
            jnp.einsum("ihd,hde->ihe", q_blk, state.astype(narrow), preferred_element_type=wide)
            * ahead[:, :, None]
        )
        k_weighted = (k_blk.astype(wide) * outof[:, :, None]).astype(narrow)
        state = state * whole[:, None, None] + jnp.einsum(
            "jhd,jhe->hde", k_weighted, v_blk, preferred_element_type=wide
        )
        return (state, local + carried)

    start_state = jnp.zeros((heads, head_size, head_size), wide)
    _, result = lax.scan(advance, start_state, (split(query), split(keys), split(values)))
    return result.reshape(length, width)


def attend_back(query, keys, values, grad_out, rates, block):
    length, width = query.shape
    heads = rates.shape[0]
    head_size = width // heads
    blocks = length // block
    inner, ahead, outof, whole = decay_tables(rates, block)

    def split(array):
        return array.reshape(blocks, block, heads, head_size)

    def forward_step(state, pieces):
        k_blk, v_blk, g_blk = pieces
        grad_scores = (
            jnp.einsum("ihe,jhe->hij", g_blk, v_blk, preferred_element_type=wide) * inner
        ).astype(narrow)
        local = jnp.einsum("hij,jhd->ihd", grad_scores, k_blk, preferred_element_type=wide)
        g_ahead = (g_blk.astype(wide) * ahead[:, :, None]).astype(narrow)
        carried = jnp.einsum(
            "ihe,hde->ihd", g_ahead, state.astype(narrow), preferred_element_type=wide
        )
        k_weighted = (k_blk.astype(wide) * outof[:, :, None]).astype(narrow)
        state = state * whole[:, None, None] + jnp.einsum(
            "jhd,jhe->hde", k_weighted, v_blk, preferred_element_type=wide
        )
        return (state, local + carried)

    def reverse_step(state, pieces):
        q_blk, k_blk, v_blk, g_blk = pieces
        weights = (
            jnp.einsum("ihd,jhd->hij", q_blk, k_blk, preferred_element_type=wide) * inner
        ).astype(narrow)
        grad_scores = (
            jnp.einsum("ihe,jhe->hij", g_blk, v_blk, preferred_element_type=wide) * inner
        ).astype(narrow)
        state_low = state.astype(narrow)
        k_weighted = (k_blk.astype(wide) * outof[:, :, None]).astype(narrow)
        grad_v = jnp.einsum("hij,ihe->jhe", weights, g_blk, preferred_element_type=wide)
        grad_v = grad_v + jnp.einsum(
            "jhd,hde->jhe", k_weighted, state_low, preferred_element_type=wide
        )
        grad_k = jnp.einsum("hij,ihd->jhd", grad_scores, q_blk, preferred_element_type=wide)
        grad_k = (
            grad_k
            + jnp.einsum("jhe,hde->jhd", v_blk, state_low, preferred_element_type=wide)
            * outof[:, :, None]
        )
        g_ahead = (g_blk.astype(wide) * ahead[:, :, None]).astype(narrow)
        state = state * whole[:, None, None] + jnp.einsum(
            "ihd,ihe->hde", q_blk, g_ahead, preferred_element_type=wide
        )
        return (state, (grad_k, grad_v))

    start_state = jnp.zeros((heads, head_size, head_size), wide)
    grad_blocks = split(grad_out)
    _, grad_q = lax.scan(forward_step, start_state, (split(keys), split(values), grad_blocks))
    _, (grad_k, grad_v) = lax.scan(
        reverse_step,
        start_state,
        (split(query), split(keys), split(values), grad_blocks),
        reverse=True,
    )
    return (
        grad_q.reshape(length, width),
        grad_k.reshape(length, width),
        grad_v.reshape(length, width),
    )


def shards(
    tokens,
    w_query,
    w_key,
    w_value,
    w_gate,
    w_out,
    w_first,
    w_second,
    w_down,
    decay_rates,
    cotangent,
):
    inputs = tokens.astype(wide)
    scale_in = inverse_rms(inputs)
    normed_in = inputs * scale_in
    gathered_in = lax.all_gather(normed_in.astype(narrow), "tensor", axis=0, tiled=True)
    length = gathered_in.shape[0]
    width = gathered_in.shape[1]
    block = min(512, length // 2)
    full_q, full_k, full_v, full_u, full_o = fetch_attn(w_query, w_key, w_value, w_gate, w_out)
    proj_q = jnp.dot(gathered_in, full_q, preferred_element_type=wide)
    proj_k = jnp.dot(gathered_in, full_k, preferred_element_type=wide)
    proj_v = jnp.dot(gathered_in, full_v, preferred_element_type=wide)
    proj_u = jnp.dot(gathered_in, full_u, preferred_element_type=wide)
    query = jax.nn.silu(proj_q).astype(narrow)
    keys = jax.nn.silu(proj_k).astype(narrow)
    values = proj_v.astype(narrow)
    attended = attend(query, keys, values, decay_rates, block)
    total_sq = lax.psum(jnp.sum(attended * attended, axis=1), "tensor")
    scale_out = lax.rsqrt(total_sq / width + eps)[:, None]
    normed_out = attended * scale_out
    gated = (normed_out * proj_u).astype(narrow)
    branch_attn = lax.psum_scatter(
        jnp.dot(gated, full_o, preferred_element_type=wide),
        "tensor",
        scatter_dimension=0,
        tiled=True,
    )
    middle = inputs + branch_attn
    scale_mid = inverse_rms(middle)
    normed_mid = middle * scale_mid
    gathered_mid = lax.all_gather(normed_mid.astype(narrow), "tensor", axis=0, tiled=True)
    full_first, full_second, full_down = fetch_ffn(w_first, w_second, w_down)
    first = jnp.dot(gathered_mid, full_first, preferred_element_type=wide)
    second = jnp.dot(gathered_mid, full_second, preferred_element_type=wide)
    squashed = (first * second).astype(narrow)
    branch_ffn = lax.psum_scatter(
        jnp.dot(squashed, full_down, preferred_element_type=wide),
        "tensor",
        scatter_dimension=0,
        tiled=True,
    )
    layer_out = (middle + branch_ffn).astype(narrow)
    back_first, back_second, back_down = fetch_ffn(w_first, w_second, w_down)
    grad_rows = lax.all_gather(cotangent, "tensor", axis=0, tiled=True)
    grad_squashed = times_transposed(grad_rows, back_down)
    grad_down = transposed_times(squashed, grad_rows)
    grad_a = (grad_squashed * second).astype(narrow)
    grad_b = (grad_squashed * first).astype(narrow)
    grad_first = transposed_times(gathered_mid, grad_a)
    grad_second = transposed_times(gathered_mid, grad_b)
    grad_mid_norm = lax.psum_scatter(
        times_transposed(grad_a, back_first) + times_transposed(grad_b, back_second),
        "tensor",
        scatter_dimension=0,
        tiled=True,
    )
    ffn_sums = (
        lax.psum_scatter(grad_first, "dp", scatter_dimension=0, tiled=True),
        lax.psum_scatter(grad_second, "dp", scatter_dimension=0, tiled=True),
        lax.psum_scatter(grad_down, "dp", scatter_dimension=1, tiled=True),
    )
    grad_middle = cotangent.astype(wide) + norm_back(grad_mid_norm, normed_mid, scale_mid)
    back_q, back_k, back_v, back_u, back_o = fetch_attn(w_query, w_key, w_value, w_gate, w_out)
    grad_branch = lax.all_gather(grad_middle.astype(narrow), "tensor", axis=0, tiled=True)
    grad_gated = times_transposed(grad_branch, back_o)
    grad_wout = transposed_times(gated, grad_branch)
    grad_normed = grad_gated * proj_u
    grad_unit = (grad_gated * normed_out).astype(narrow)
    cross = lax.psum(jnp.sum(grad_normed * normed_out, axis=1), "tensor")
    grad_attended = (scale_out * (grad_normed - normed_out * (cross / width)[:, None])).astype(
        narrow
    )
    grad_query, grad_keys, grad_values = attend_back(
        query, keys, values, grad_attended, decay_rates, block
    )
    grad_proj_q = (grad_query * silu_slope(proj_q)).astype(narrow)
    grad_proj_k = (grad_keys * silu_slope(proj_k)).astype(narrow)
    grad_proj_v = grad_values.astype(narrow)
    grad_wq = transposed_times(gathered_in, grad_proj_q)
    grad_wk = transposed_times(gathered_in, grad_proj_k)
    grad_wv = transposed_times(gathered_in, grad_proj_v)
    grad_wu = transposed_times(gathered_in, grad_unit)
    total = times_transposed(grad_proj_q, back_q)
    total = total + times_transposed(grad_proj_k, back_k)
    total = total + times_transposed(grad_proj_v, back_v)
    grad_in_norm = lax.psum_scatter(
        total + times_transposed(grad_unit, back_u), "tensor", scatter_dimension=0, tiled=True
    )
    attn_sums = (
        lax.psum_scatter(grad_wq, "dp", scatter_dimension=0, tiled=True),
        lax.psum_scatter(grad_wk, "dp", scatter_dimension=0, tiled=True),
        lax.psum_scatter(grad_wv, "dp", scatter_dimension=0, tiled=True),
        lax.psum_scatter(grad_wu, "dp", scatter_dimension=0, tiled=True),
        lax.psum_scatter(grad_wout, "dp", scatter_dimension=1, tiled=True),
    )
    tokens_grad = grad_middle + norm_back(grad_in_norm, normed_in, scale_in)
    return (
        layer_out,
        tokens_grad,
        attn_sums[0],
        attn_sums[1],
        attn_sums[2],
        attn_sums[3],
        attn_sums[4],
        ffn_sums[0],
        ffn_sums[1],
        ffn_sums[2],
    )


def solution(mesh):
    return jax.shard_map(
        shards,
        mesh=mesh,
        in_specs=(
            P(("dp", "tensor"), None),
            P("dp", "tensor"),
            P("dp", "tensor"),
            P("dp", "tensor"),
            P("dp", "tensor"),
            P("tensor", "dp"),
            P("dp", "tensor"),
            P("dp", "tensor"),
            P("tensor", "dp"),
            P("tensor"),
            P(("dp", "tensor"), None),
        ),
        out_specs=(
            P(("dp", "tensor"), None),
            P(("dp", "tensor"), None),
            P("dp", "tensor"),
            P("dp", "tensor"),
            P("dp", "tensor"),
            P("dp", "tensor"),
            P("tensor", "dp"),
            P("dp", "tensor"),
            P("dp", "tensor"),
            P("tensor", "dp"),
        ),
        check_vma=False,
    )
```

profile of v0, /device:TPU:0, one launch (start us, length us, event | category | flops | bytes accessed | tf_op | source)
XLA Modules:
  0.0 1525.6 jit_solution(10304688180796724625)
XLA Ops:
  15.9 52.6 %all-gather.15.cloned.1.call-done = bf16[1024,512]{1,0:T(8,128)(2,1)} async-done(((bf16[64,512]{1,0:T(8,128)(2,1)}), bf16[1024,512]{1,0:T(8,128)(2,1)}) %all-gather.15.cloned.1.call-update) | async-done | bytes 1048592 | tf_op jit(solution)/shard_map/all_gather | solution.py:35
  68.6 11.6 all-gather.13.cloned.1.call-done
  80.1 4.7 multiply_convert_fusion.17
  85.8 53.4 %all-gather.19.cloned.1.call-done = bf16[1024,512]{1,0:T(8,128)(2,1)} async-done(((bf16[64,512]{1,0:T(8,128)(2,1)}), bf16[1024,512]{1,0:T(8,128)(2,1)}) %all-gather.19.cloned.1.call-update) | async-done | bytes 1048592 | tf_op jit(solution)/shard_map/all_gather | solution.py:34
  139.2 4.6 multiply_convert_fusion.16
  145.0 50.8 %all-gather.17.cloned.1.call-done = bf16[1024,512]{1,0:T(8,128)(2,1)} async-done(((bf16[64,512]{1,0:T(8,128)(2,1)}), bf16[1024,512]{1,0:T(8,128)(2,1)}) %all-gather.17.cloned.1.call-update) | async-done | bytes 1048592 | tf_op jit(solution)/shard_map/all_gather | solution.py:36
  201.4 16.3 %while.54 = (s32[]{:T(128)}, f32[4,128,128]{2,1,0:T(8,128)S(1)}, f32[2,512,4,128]{1,3,2,0:T(8,128)}, f32[4]{0:T(128)S(1)}, bf16[2,512,4,128]{1,3,2,0:T(8,128)(2,...) while((s32[]{:T(128)}, f32[4,128,128]{2,1,0:T(8,128)S(1)}, ...), condition=%wide.region_2.3_spmd.clone.clone.clone.clone, body=%wide.region_1.2_spmd.clone.clone.clone.sunk.clone | while | flops 676859904 | bytes 9477780 | solution.py:88
  202.6 4.0 fusion.252
  210.7 4.0 fusion.252
  226.1 26.2 %all-gather.21.cloned.1.call-done = bf16[1024,512]{1,0:T(8,128)(2,1)} async-done(((bf16[64,512]{1,0:T(8,128)(2,1)}), bf16[1024,512]{1,0:T(8,128)(2,1)}) %all-gather.21.cloned.1.call-update) | async-done | bytes 1048592 | tf_op jit(solution)/shard_map/all_gather | solution.py:37
  252.4 5.2 multiply_convert_fusion.15
  257.6 51.4 %all-gather.23.cloned.1.call-done = bf16[512,1024]{0,1:T(8,128)(2,1)} async-done(((bf16[512,64]{0,1:T(8,128)(2,1)}), bf16[512,1024]{0,1:T(8,128)(2,1)}) %all-gather.23.cloned.1.call-update) | async-done | bytes 1048592 | tf_op jit(solution)/shard_map/all_gather | solution.py:38
  309.0 4.5 fusion.143
  314.3 10.2 reduce-scatter.13.cloned.1.call-done
  330.0 64.6 %all-gather.27.cloned.1.call-done = bf16[1024,1408]{1,0:T(8,128)(2,1)} async-done(((bf16[64,1408]{1,0:T(8,128)(2,1)}), bf16[1024,1408]{1,0:T(8,128)(2,1)}) %all-gather.27.cloned.1.call-update) | async-done | bytes 2883600 | tf_op jit(solution)/shard_map/all_gather | solution.py:44
  394.6 11.4 all-gather.25.cloned.1.call-done
  406.0 8.3 fusion.144
  414.3 61.5 %all-gather.29.cloned.1.call-done = bf16[1024,1408]{1,0:T(8,128)(2,1)} async-done(((bf16[64,1408]{1,0:T(8,128)(2,1)}), bf16[1024,1408]{1,0:T(8,128)(2,1)}) %all-gather.29.cloned.1.call-update) | async-done | bytes 2883600 | tf_op jit(solution)/shard_map/all_gather | solution.py:45
  475.8 8.3 fusion.145
  486.6 69.8 %all-gather.31.cloned.1.call-done = bf16[1408,1024]{0,1:T(8,128)(2,1)} async-done(((bf16[1408,64]{0,1:T(8,128)(2,1)}), bf16[1408,1024]{0,1:T(8,128)(2,1)}) %all-gather.31.cloned.1.call-update) | async-done | bytes 2883600 | tf_op jit(solution)/shard_map/all_gather | solution.py:46
  556.4 11.0 multiply_convert_fusion.10
  571.4 5.0 convolution_add_fusion.3
  576.5 10.8 reduce-scatter.17.cloned.1.call-done
  593.9 10.7 all-gather.35.cloned.1.call-done
  604.7 6.0 multiply_reduce_fusion
  623.4 17.4 %while.55 = (s32[]{:T(128)}, f32[4,128,128]{2,1,0:T(8,128)}, f32[2,512,4,128]{3,2,1,0:T(4,128)}, f32[4]{0:T(128)S(1)}, bf16[2,512,4,128]{1,3,2,0:T(8,128)(2,1)S(...) while((s32[]{:T(128)}, f32[4,128,128]{2,1,0:T(8,128)}, ...), condition=%wide.region_13.14_spmd.clone.clone.clone.clone, body=%wide.region_12.13_spmd.clone.clone.clone.sunk.clone | while | flops 677384192 | bytes 21013192 | solution.py:146
  642.5 33.2 %while.56 = (s32[]{:T(128)}, f32[4,128,128]{2,1,0:T(8,128)S(1)}, f32[2,512,4,128]{3,2,1,0:T(4,128)}, bf16[2,512,4,128]{1,3,2,0:T(8,128)(2,1)}, f32[4]{0:T(128)S(...) while((s32[]{:T(128)}, f32[4,128,128]{2,1,0:T(8,128)S(1)}, ...), condition=%wide.region_15.16_spmd.clone.clone.clone.clone, body=%wide.region_14.15_spmd.clone.clone.clone.sunk.clone | while | flops 1286148096 | bytes 39372132 | solution.py:147
  644.4 4.3 fusion.268
  652.2 4.1 fusion.270
  661.0 4.3 fusion.268
  668.8 4.1 fusion.270
  690.8 8.2 fusion.146
  700.6 7.7 fusion.154
  708.4 7.1 fusion.155
  717.7 7.5 fusion.156
  726.8 3.9 fusion.153
  732.3 3.9 fusion.150
  736.3 3.8 fusion.151
  740.2 3.8 fusion.135
  750.1 5.0 fusion.131
  755.1 94.6 %reduce-scatter.31.cloned.1.call-done = f32[64,1408]{1,0:T(8,128)} async-done(((f32[1024,1408]{1,0:T(8,128)}), f32[64,1408]{1,0:T(8,128)}) %reduce-scatter.31.cloned.1.call-update) | async-done | bytes 360464 | tf_op jit(solution)/shard_map/reduce_scatter | solution.py:229
  849.7 129.1 %reduce-scatter.33.cloned.1.call-done = f32[64,1408]{1,0:T(8,128)} async-done(((f32[1024,1408]{1,0:T(8,128)}), f32[64,1408]{1,0:T(8,128)}) %reduce-scatter.33.cloned.1.call-update) | async-done | bytes 360464 | tf_op jit(solution)/shard_map/reduce_scatter | solution.py:230
  978.8 129.9 %reduce-scatter.35.cloned.1.call-done = f32[1408,64]{0,1:T(8,128)} async-done(((f32[1408,1024]{0,1:T(8,128)}), f32[1408,64]{0,1:T(8,128)}) %reduce-scatter.35.cloned.1.call-update) | async-done | bytes 360464 | tf_op jit(solution)/shard_map/reduce_scatter | solution.py:231
  1108.8 86.0 %reduce-scatter.29.cloned.1.call-done = f32[512,64]{0,1:T(8,128)} async-done(((f32[512,1024]{0,1:T(8,128)}), f32[512,64]{0,1:T(8,128)}) %reduce-scatter.29.cloned.1.call-update) | async-done | bytes 131088 | tf_op jit(solution)/shard_map/reduce_scatter | solution.py:265
  1194.7 80.8 %reduce-scatter.21.cloned.1.call-done = f32[64,512]{1,0:T(8,128)} async-done(((f32[1024,512]{1,0:T(8,128)}), f32[64,512]{1,0:T(8,128)}) %reduce-scatter.21.cloned.1.call-update) | async-done | bytes 131088 | tf_op jit(solution)/shard_map/reduce_scatter | solution.py:261
  1275.5 80.9 %reduce-scatter.23.cloned.1.call-done = f32[64,512]{1,0:T(8,128)} async-done(((f32[1024,512]{1,0:T(8,128)}), f32[64,512]{1,0:T(8,128)}) %reduce-scatter.23.cloned.1.call-update) | async-done | bytes 131088 | tf_op jit(solution)/shard_map/reduce_scatter | solution.py:262
  1356.4 80.9 %reduce-scatter.25.cloned.1.call-done = f32[64,512]{1,0:T(8,128)} async-done(((f32[1024,512]{1,0:T(8,128)}), f32[64,512]{1,0:T(8,128)}) %reduce-scatter.25.cloned.1.call-update) | async-done | bytes 131088 | tf_op jit(solution)/shard_map/reduce_scatter | solution.py:263
  1437.4 80.9 %reduce-scatter.27.cloned.1.call-done = f32[64,512]{1,0:T(8,128)} async-done(((f32[1024,512]{1,0:T(8,128)}), f32[64,512]{1,0:T(8,128)}) %reduce-scatter.27.cloned.1.call-update) | async-done | bytes 131088 | tf_op jit(solution)/shard_map/reduce_scatter | solution.py:264
  (235 shorter events, 128.3 us)
Async XLA Ops:
  7.2 61.4 %all-gather.15.cloned.1.call-start = ((), (), s32[]{:S(2)}) async-start(), calls=%async_computation.13 | async-start | bytes 1114112 | tf_op jit(solution)/shard_map/all_gather | solution.py:35
  7.9 72.2 %all-gather.13.cloned.1.call-start = ((), (), s32[]{:S(2)}) async-start(), calls=%async_computation.12 | async-start | bytes 3145728 | tf_op jit(solution)/shard_map/all_gather | solution.py:176
  9.5 6.2 copy-start.32
  9.5 6.4 copy-start.40
  12.0 127.3 %all-gather.19.cloned.1.call-start = ((), (), s32[]{:S(2)}) async-start(), calls=%async_computation.15 | async-start | bytes 1114112 | tf_op jit(solution)/shard_map/all_gather | solution.py:34
  12.7 183.1 %all-gather.17.cloned.1.call-start = ((), (), s32[]{:S(2)}) async-start(), calls=%async_computation.14 | async-start | bytes 1114112 | tf_op jit(solution)/shard_map/all_gather | solution.py:36
  13.3 239.1 %all-gather.21.cloned.1.call-start = ((), (), s32[]{:S(2)}) async-start(), calls=%async_computation.16 | async-start | bytes 1114112 | tf_op jit(solution)/shard_map/all_gather | solution.py:37
  13.9 295.1 %all-gather.23.cloned.1.call-start = ((), (), s32[]{:S(2)}) async-start(), calls=%async_computation.17 | async-start | bytes 1114112 | tf_op jit(solution)/shard_map/all_gather | solution.py:38
  14.4 310.1 %reduce-scatter.13.cloned.1.call-start = ((), (), s32[]{:S(2)}) async-start(), calls=%async_computation.18 | async-start | bytes 6291456 | tf_op jit(solution)/shard_map/reduce_scatter | solution.py:193
  217.6 3.3 copy-start.30
  257.6 55.9 %copy-start.29 = (bf16[1024,512]{0,1:T(8,128)(2,1)}, bf16[1024,512]{0,1:T(8,128)(2,1)S(1)}, u32[]{:S(2)}) copy-start(bf16[1024,512]{0,1:T(8,128)(2,1)S(1)} %get-tuple-element.892) | copy-start | bytes 3145732
  313.5 11.1 copy-start.4
  313.5 81.1 %all-gather.27.cloned.1.call-start = ((), (), s32[]{:S(2)}) async-start(), calls=%async_computation.20 | async-start | bytes 3063808 | tf_op jit(solution)/shard_map/all_gather | solution.py:44
  314.3 91.7 %all-gather.25.cloned.1.call-start = ((), (), s32[]{:S(2)}) async-start(), calls=%async_computation.19 | async-start | bytes 3145728 | tf_op jit(solution)/shard_map/all_gather | solution.py:202
  328.0 147.7 %all-gather.29.cloned.1.call-start = ((), (), s32[]{:S(2)}) async-start(), calls=%async_computation.21 | async-start | bytes 3063808 | tf_op jit(solution)/shard_map/all_gather | solution.py:45
  328.6 158.0 %all-gather.33.cloned.1.call-start = ((), (), s32[]{:S(2)}) async-start(), calls=%async_computation.24 | async-start | bytes 3145728 | tf_op jit(solution)/shard_map/all_gather | solution.py:215
  329.4 227.0 %all-gather.31.cloned.1.call-start = ((), (), s32[]{:S(2)}) async-start(), calls=%async_computation.22 | async-start | bytes 3063808 | tf_op jit(solution)/shard_map/all_gather | solution.py:46
  329.9 257.3 %reduce-scatter.17.cloned.1.call-start = ((), (), s32[]{:S(2)}) async-start(), calls=%async_computation.25 | async-start | bytes 6291456 | tf_op jit(solution)/shard_map/reduce_scatter | solution.py:222
  556.4 11.0 copy-start.34
  567.5 3.5 copy-start.20
  567.5 3.5 copy-start.19
  567.5 3.9 copy-start.35
  576.4 28.3 %all-gather.35.cloned.1.call-start = ((), (), s32[]{:S(2)}) async-start(), calls=%async_computation.26 | async-start | bytes 3145728 | tf_op jit(solution)/shard_map/all_gather | solution.py:235
  587.3 2.9 copy-start.9
  587.3 3.5 copy-start.11
  587.3 3.7 copy-start.13
  592.6 12.0 copy-start.25
  592.6 154.2 %reduce-scatter.19.cloned.1.call-start = ((), (), s32[]{:S(2)}) async-start(), calls=%async_computation.27 | async-start | bytes 6291456 | tf_op jit(solution)/shard_map/reduce_scatter | solution.py:257
  623.4 3.5 copy-start
  631.7 3.5 copy-start
  642.5 6.3 copy-start.2
  644.4 4.3 copy-start.6
  656.2 2.8 copy-start.3
  659.1 6.4 copy-start.2
  661.0 4.3 copy-start.6
  672.9 2.8 copy-start.3
  675.7 2.7 copy-start.16
  678.5 2.8 copy-start.22
  690.7 59.3 %reduce-scatter.15.cloned.1.call-start = ((), (), s32[]{:S(2)}) async-start(), calls=%async_computation.23 | async-start | bytes 6291456 | tf_op jit(solution)/shard_map/reduce_scatter | solution.py:207
  699.0 150.7 %reduce-scatter.31.cloned.1.call-start = ((), (), s32[]{:S(2)}) async-start(), calls=%async_computation.33 | async-start | bytes 6127616 | tf_op jit(solution)/shard_map/reduce_scatter | solution.py:229
  708.4 270.5 %reduce-scatter.33.cloned.1.call-start = ((), (), s32[]{:S(2)}) async-start(), calls=%async_computation.34 | async-start | bytes 6127616 | tf_op jit(solution)/shard_map/reduce_scatter | solution.py:230
  715.6 393.2 %reduce-scatter.35.cloned.1.call-start = ((), (), s32[]{:S(2)}) async-start(), calls=%async_computation.35 | async-start | bytes 6127616 | tf_op jit(solution)/shard_map/reduce_scatter | solution.py:231
  725.2 469.5 %reduce-scatter.29.cloned.1.call-start = ((), (), s32[]{:S(2)}) async-start(), calls=%async_computation.32 | async-start | bytes 2228224 | tf_op jit(solution)/shard_map/reduce_scatter | solution.py:265
  730.7 544.8 %reduce-scatter.21.cloned.1.call-start = ((), (), s32[]{:S(2)}) async-start(), calls=%async_computation.28 | async-start | bytes 2228224 | tf_op jit(solution)/shard_map/reduce_scatter | solution.py:261
  736.2 620.2 %reduce-scatter.23.cloned.1.call-start = ((), (), s32[]{:S(2)}) async-start(), calls=%async_computation.29 | async-start | bytes 2228224 | tf_op jit(solution)/shard_map/reduce_scatter | solution.py:262
  740.1 697.3 %reduce-scatter.25.cloned.1.call-start = ((), (), s32[]{:S(2)}) async-start(), calls=%async_computation.30 | async-start | bytes 2228224 | tf_op jit(solution)/shard_map/reduce_scatter | solution.py:263
  744.0 774.3 %reduce-scatter.27.cloned.1.call-start = ((), (), s32[]{:S(2)}) async-start(), calls=%async_computation.31 | async-start | bytes 2228224 | tf_op jit(solution)/shard_map/reduce_scatter | solution.py:264
  746.8 3.3 copy-start.10
  (25 other events, 40.6 us)
Sparse Core Ops, SparseCore 0:
  10.7 57.7 all-gather.14
  70.7 9.3 all-gather.12
  82.9 56.2 all-gather.18
  141.8 53.9 all-gather.16
  198.4 53.9 all-gather.20
  255.0 53.9 all-gather.22
  313.6 10.8 reduce-scatter.12
  327.3 67.2 all-gather.26
  396.7 9.2 all-gather.24
  408.6 67.1 all-gather.28
  477.3 9.2 all-gather.32
  489.2 67.1 all-gather.30
  576.5 10.6 reduce-scatter.16
  592.8 11.8 all-gather.34
  690.8 13.2 reduce-scatter.18
  706.2 13.3 reduce-scatter.14
  722.3 127.3 reduce-scatter.30
  852.4 126.3 reduce-scatter.32
  981.7 126.9 reduce-scatter.34
  1111.5 83.2 reduce-scatter.28
  1197.6 77.8 reduce-scatter.20
  1278.4 78.0 reduce-scatter.22
  1359.3 78.0 reduce-scatter.24
  1440.1 78.1 reduce-scatter.26
where the time goes:
time: 1530 us
  waiting for transfers between devices  1260 us (82%)
  matrix products  173 us (11%)
  local copies, waits for them, and re-layouts  45.6 us (3%)
  other arithmetic  28.9 us (2%)
    reduce_scatter x1, waiting for transfers between devices, shards(): lax.psum_scatter(grad_down, 'dp', scatter_dimension=1, tiled=True)  130 us
    reduce_scatter x1, waiting for transfers between devices, shards(): lax.psum_scatter(grad_second, 'dp', scatter_dimension=0, tiled=True)  129 us
    reduce_scatter x1, waiting for transfers between devices, shards(): lax.psum_scatter(grad_first, 'dp', scatter_dimension=0, tiled=True)  94.6 us
    reduce_scatter x1, waiting for transfers between devices, shards(): lax.psum_scatter(grad_wout, 'dp', scatter_dimension=1, tiled=True)  86 us
    reduce_scatter x1, waiting for transfers between devices, shards(): lax.psum_scatter(grad_wv, 'dp', scatter_dimension=0, tiled=True)  80.9 us
    reduce_scatter x1, waiting for transfers between devices, shards(): lax.psum_scatter(grad_wk, 'dp', scatter_dimension=0, tiled=True)  80.9 us
    reduce_scatter x1, waiting for transfers between devices, shards(): lax.psum_scatter(grad_wu, 'dp', scatter_dimension=0, tiled=True)  80.9 us
    reduce_scatter x1, waiting for transfers between devices, shards(): lax.psum_scatter(grad_wq, 'dp', scatter_dimension=0, tiled=True)  80.8 us
  transfers between devices with their start and end apart: 24, of which 22 were waited for; matrix products, arithmetic and copies ran while one was open for 8% of the time, Pallas kernels for 0%

commit v1 on v0

v1 whole, which is shorter than its diff:
```python
import functools

import jax
import jax.numpy as jnp
import numpy as np
from jax import lax
from jax.experimental import pallas as pl
from jax.experimental.pallas import tpu as pltpu
from jax.sharding import PartitionSpec as P

eps = 1e-06
wide = jnp.float32
narrow = jnp.bfloat16
window = 5


def dot(left, right, dims):
    return lax.dot_general(left, right, (dims, ((), ())), preferred_element_type=wide)


def nn(left, right):
    return dot(left, right, ((1,), (0,)))


def nt(left, right):
    return dot(left, right, ((1,), (1,)))


def tn(left, right):
    return dot(left, right, ((0,), (0,)))


def inverse_rms(values):
    return lax.rsqrt(jnp.mean(values * values, axis=-1, keepdims=True) + eps)


def norm_back(grad, normed, scale):
    return scale * (grad - normed * jnp.mean(grad * normed, axis=-1, keepdims=True))


def silu_slope(values):
    sigma = jax.nn.sigmoid(values)
    return sigma * (1.0 + values * (1.0 - sigma))


class Exchange:

    def __init__(self, size):
        self.size = size
        self.sent = []

    def __call__(self, array, bit):
        if len(self.sent) >= window:
            array = lax.optimization_barrier((array, self.sent[-window]))[0]
        pairs = [(i, i ^ bit) for i in range(self.size)]
        result = lax.ppermute(array, "dp", pairs)
        self.sent.append(result)
        return result


def inner_bits(size):
    bits = []
    bit = size // 2
    while bit >= 4:
        bits.append(bit)
        bit //= 2
    return bits


def block_offsets(size):
    order = [0]
    for bit in inner_bits(size) + [1, 2]:
        order = order + [entry ^ bit for entry in order]
    return np.array(order, np.int32)


def gather_all(send, shards):
    bits = inner_bits(send.size)
    depth = len(bits)
    count = len(shards)
    held = list(shards)
    pieces = [None] * count
    for step in range(count + depth + 1):
        c = step - depth - 1
        if 0 <= c < count:
            first, side, up = pieces[c]
            if c % 2 == 0:
                pieces[c] = (first, side, up, send(side, 2))
            else:
                pieces[c] = (first, side, up, send(up, 1))
        c = step - depth
        if 0 <= c < count:
            pieces[c] = (held[c], send(held[c], 1), send(held[c], 2))
        for level in range(depth - 1, -1, -1):
            c = step - level
            if 0 <= c < count:
                held[c] = jnp.concatenate([held[c], send(held[c], bits[level])], axis=0)
    return pieces


def scatter(send, grads, turn):
    first, side, up, far = (piece.astype(wide) for piece in grads)
    low = lambda value: value.astype(narrow)
    if turn:
        from_up = send(low(up), 2)
        side = side + send(low(far), 2).astype(wide)
        from_side = send(low(side), 1)
    else:
        from_side = send(low(side), 1)
        up = up + send(low(far), 1).astype(wide)
        from_up = send(low(up), 2)
    total = first + from_side.astype(wide) + from_up.astype(wide)
    for bit in reversed(inner_bits(send.size)):
        half = total.shape[0] // 2
        total = total[:half] + send(low(total[half:]), bit).astype(wide)
    return total


def tables(rate, size):
    row = lax.broadcasted_iota(jnp.int32, (size, 1), 0).astype(wide)
    col = lax.broadcasted_iota(jnp.int32, (1, size), 1).astype(wide)
    ahead = jnp.exp(-rate * row)
    inner = jnp.where(col <= row, ahead * jnp.exp(rate * col), 0.0)
    outof = jnp.exp(-rate * (size - row))
    return inner, ahead, outof


def attend_kernel(turn_ref, rate_ref, q_ref, k_ref, v_ref, o_ref):
    size = q_ref.shape[0] // 2
    inner, ahead, outof = tables(rate_ref[pl.program_id(0)], size)
    turn = turn_ref[0]
    early = pl.ds(pl.multiple_of(turn * size, size), size)
    late = pl.ds(pl.multiple_of((1 - turn) * size, size), size)

    def local(rows):
        weights = (nt(q_ref[rows, :], k_ref[rows, :]) * inner).astype(narrow)
        return nn(weights, v_ref[rows, :])

    weighted = (k_ref[early, :].astype(wide) * outof).astype(narrow)
    state = tn(weighted, v_ref[early, :]).astype(narrow)
    o_ref[early, :] = local(early)
    o_ref[late, :] = local(late) + nn(q_ref[late, :], state) * ahead


def attend_back_kernel(
    turn_ref, rate_ref, q_ref, k_ref, v_ref, g_ref, pq_ref, pk_ref, dq_ref, dk_ref, dv_ref
):
    size = q_ref.shape[0] // 2
    inner, ahead, outof = tables(rate_ref[pl.program_id(0)], size)
    turn = turn_ref[0]
    early = pl.ds(pl.multiple_of(turn * size, size), size)
    late = pl.ds(pl.multiple_of((1 - turn) * size, size), size)

    def local(rows):
        q, k, v, g = (ref[rows, :] for ref in (q_ref, k_ref, v_ref, g_ref))
        weights = (nt(q, k) * inner).astype(narrow)
        grad_scores = (nt(g, v) * inner).astype(narrow)
        return nn(grad_scores, k), tn(grad_scores, q), tn(weights, g)

    def store(rows, dq, dk, dv):
        dq_ref[rows, :] = (dq * silu_slope(pq_ref[rows, :])).astype(narrow)
        dk_ref[rows, :] = (dk * silu_slope(pk_ref[rows, :])).astype(narrow)
        dv_ref[rows, :] = dv.astype(narrow)

    weighted = (k_ref[early, :].astype(wide) * outof).astype(narrow)
    state = tn(weighted, v_ref[early, :]).astype(narrow)
    g_ahead = (g_ref[late, :].astype(wide) * ahead).astype(narrow)
    grad_state = tn(q_ref[late, :], g_ahead).astype(narrow)
    dq, dk, dv = local(late)
    store(late, dq + nt(g_ahead, state), dk, dv)
    dq, dk, dv = local(early)
    store(
        early,
        dq,
        dk + nt(v_ref[early, :], grad_state) * outof,
        dv + nn(weighted, grad_state),
    )


def per_head(kernel, turn, rates, arrays, out_types):
    heads = rates.shape[0]
    length, columns = arrays[0].shape
    spec = pl.BlockSpec((length, columns // heads), lambda h: (0, h))
    scalar = pl.BlockSpec(memory_space=pltpu.SMEM)
    return pl.pallas_call(
        kernel,
        grid=(heads,),
        in_specs=[scalar, scalar] + [spec] * len(arrays),
        out_specs=[spec] * len(out_types),
        out_shape=[jax.ShapeDtypeStruct((length, columns), t) for t in out_types],
    )(turn, rates, *arrays)


def ffn_kernel(*refs, chained):
    n_ref, g_ref, nt_ref, gt_ref, w0, w1, w2, w3 = refs[:8]
    if chained:
        y_in, d_in, y_ref, d_ref, o_ref, s_ref, da_ref, db_ref = refs[8:]
    else:
        y_ref, d_ref, o_ref, s_ref, da_ref, db_ref = refs[8:]
    step = pl.program_id(0)
    tile = y_ref.shape[0]
    n = s_ref.shape[1]
    quarter = w0.shape[0]
    pieces = (w0, w1, w2, w3)
    tiles = n_ref.shape[0] // tile

    @pl.when(step < tiles)
    def _():
        rows = pl.ds(pl.multiple_of(step * tile, tile), tile)
        ab = jnp.zeros((tile, 2 * n), wide)
        ds = jnp.zeros((tile, n), wide)
        for i, ref in enumerate(pieces):
            cols = slice(i * quarter, (i + 1) * quarter)
            ab += nn(n_ref[rows, cols], ref[:, : 2 * n])
            ds += nn(g_ref[rows, cols], ref[:, 2 * n :])
        a = ab[:, :n]
        b = ab[:, n:]
        s = (a * b).astype(narrow)
        da = (ds * b).astype(narrow)
        db = (ds * a).astype(narrow)
        s_ref[rows, :] = s
        da_ref[rows, :] = da
        db_ref[rows, :] = db
        for i, ref in enumerate(pieces):
            cols = slice(i * quarter, (i + 1) * quarter)
            y = nt(s, ref[:, 2 * n :])
            d = nt(da, ref[:, :n]) + nt(db, ref[:, n : 2 * n])
            if chained:
                y = y + y_in[:, cols]
                d = d + d_in[:, cols]
            y_ref[:, cols] = y
            d_ref[:, cols] = d

    @pl.when(step >= tiles)
    def _():
        o_ref[:, :n] = nn(nt_ref[...], da_ref[...]).astype(o_ref.dtype)
        o_ref[:, n : 2 * n] = nn(nt_ref[...], db_ref[...]).astype(o_ref.dtype)
        o_ref[:, 2 * n :] = nn(gt_ref[...], s_ref[...]).astype(o_ref.dtype)


def ffn_chunk(normed, grad, normed_t, grad_t, pieces, sums):
    length, width = normed.shape
    quarter, n3 = pieces[0].shape
    n = n3 // 3
    tile = 256
    tiles = length // tile
    whole = lambda shape: pl.BlockSpec(shape, lambda i: (0, 0))
    rows = pl.BlockSpec((tile, width), lambda i: (jnp.minimum(i, tiles - 1), 0))
    part = pl.BlockSpec((quarter, length), lambda i: (jnp.maximum(i - tiles, 0), 0))
    out_part = pl.BlockSpec((quarter, n3), lambda i: (jnp.maximum(i - tiles, 0), 0))
    chained = sums is not None
    return pl.pallas_call(
        functools.partial(ffn_kernel, chained=chained),
        grid=(tiles + 4,),
        in_specs=[whole((length, width))] * 2
        + [part] * 2
        + [whole((quarter, n3))] * 4
        + ([rows] * 2 if chained else []),
        out_specs=[rows, rows, out_part],
        out_shape=[
            jax.ShapeDtypeStruct((length, width), wide),
            jax.ShapeDtypeStruct((length, width), wide),
            jax.ShapeDtypeStruct((width, n3), narrow),
        ],
        scratch_shapes=[pltpu.VMEM((length, n), narrow)] * 3,
    )(normed, grad, normed_t, grad_t, *pieces, *(sums if chained else ()))


def quarters(array):
    q = array.shape[0] // 4
    return [array[i * q : (i + 1) * q] for i in range(4)]


def ffn_cuts(total):
    cuts = []
    left = total
    while left > 0:
        take = min(512, left)
        cuts.append((total - left, take))
        left -= take
    return cuts


def shards(
    size,
    tokens,
    w_query,
    w_key,
    w_value,
    w_gate,
    w_out,
    w_first,
    w_second,
    w_down,
    decay_rates,
    cotangent,
):
    send = Exchange(size)
    swap = lambda value: lax.ppermute(value, "tensor", [(0, 1), (1, 0)])
    me = lax.axis_index("dp")
    turn = lax.axis_index("tensor").astype(jnp.int32).reshape(1)
    rows, width = tokens.shape
    span = width // size
    offsets = jnp.asarray(np.repeat(block_offsets(size), span))
    place = jnp.bitwise_xor(offsets, me) * span + jnp.arange(width) % span
    shuffle = (jnp.arange(width)[:, None] == place[None, :]).astype(narrow)

    cuts = ffn_cuts(w_first.shape[1])
    down_t = w_down.T
    ffn_shards = [
        jnp.concatenate([w[:, at : at + n] for w in (w_first, w_second, down_t)], axis=1)
        for at, n in cuts
    ]
    gathered = gather_all(send, [w_query, w_key, w_value, w_gate, w_out.T] + ffn_shards)
    full_q, full_k, full_v, full_u, full_o = (
        jnp.concatenate(pieces, axis=0) for pieces in gathered[:5]
    )

    inputs = nn(tokens, shuffle)
    scale_in = inverse_rms(inputs)
    normed_in = inputs * scale_in
    own_in = normed_in.astype(narrow)
    both_in = jnp.concatenate([own_in, swap(own_in)], axis=0)
    own_cot = nn(cotangent, shuffle).astype(narrow)
    both_cot = jnp.concatenate([own_cot, swap(own_cot)], axis=0)
    cot_t = both_cot.T
    in_t = both_in.T

    proj_q = nn(both_in, full_q)
    proj_k = nn(both_in, full_k)
    proj_v = nn(both_in, full_v)
    proj_u = nn(both_in, full_u)
    query = jax.nn.silu(proj_q).astype(narrow)
    keys = jax.nn.silu(proj_k).astype(narrow)
    values = proj_v.astype(narrow)
    attended = per_head(attend_kernel, turn, decay_rates, (query, keys, values), (wide,))[0]

    def both_sum(part):
        other = swap(part)
        return part + jnp.concatenate([other[rows:], other[:rows]], axis=0)

    total_sq = both_sum(jnp.sum(attended * attended, axis=1))
    scale_out = lax.rsqrt(total_sq / width + eps)[:, None]
    normed_out = attended * scale_out
    gated = (normed_out * proj_u).astype(narrow)
    branch = nt(gated, full_o)
    middle = inputs + branch[:rows] + swap(branch[rows:])
    scale_mid = inverse_rms(middle)
    normed_mid = middle * scale_mid
    own_mid = normed_mid.astype(narrow)
    both_mid = jnp.concatenate([own_mid, swap(own_mid)], axis=0)
    mid_t = both_mid.T

    sums = None
    ffn_grads = []
    for c in range(len(cuts)):
        y_sum, d_sum, grads = ffn_chunk(
            both_mid, both_cot, mid_t, cot_t, gathered[5 + c], sums
        )
        sums = (y_sum, d_sum)
        ffn_grads.append(scatter(send, quarters(grads), c % 2 == 0))

    grad_mid_norm = d_sum[:rows] + swap(d_sum[rows:])
    grad_middle = own_cot.astype(wide) + norm_back(grad_mid_norm, normed_mid, scale_mid)
    own_e = grad_middle.astype(narrow)
    both_e = jnp.concatenate([own_e, swap(own_e)], axis=0)
    grad_gated = nn(both_e, full_o)
    grad_wout = tn(both_e, gated)
    attn_grads = [scatter(send, quarters(grad_wout), True)]
    grad_normed = grad_gated * proj_u
    grad_unit = (grad_gated * normed_out).astype(narrow)
    attn_grads.append(scatter(send, quarters(nn(in_t, grad_unit)), False))
    cross = both_sum(jnp.sum(grad_normed * normed_out, axis=1))
    grad_attended = (scale_out * (grad_normed - normed_out * (cross / width)[:, None])).astype(
        narrow
    )
    grad_q, grad_k, grad_v = per_head(
        attend_back_kernel,
        turn,
        decay_rates,
        (query, keys, values, grad_attended, proj_q, proj_k),
        (narrow, narrow, narrow),
    )
    attn_grads.append(scatter(send, quarters(nn(in_t, grad_q)), True))
    attn_grads.append(scatter(send, quarters(nn(in_t, grad_k)), False))
    attn_grads.append(scatter(send, quarters(nn(in_t, grad_v)), True))

    total = nt(grad_q, full_q) + nt(grad_k, full_k) + nt(grad_v, full_v) + nt(grad_unit, full_u)
    grad_in_norm = total[:rows] + swap(total[rows:])
    tokens_grad = grad_middle + norm_back(grad_in_norm, normed_in, scale_in)
    layer_out = (middle + y_sum[:rows] + swap(y_sum[rows:])).astype(narrow)
    layer_out = nt(layer_out, shuffle).astype(narrow)
    parts = []
    rest = tokens_grad
    for _ in range(3):
        part = lax.reduce_precision(rest, 8, 7)
        parts.append(part.astype(narrow))
        rest = rest - part
    tokens_grad = nt(parts[0], shuffle) + (nt(parts[1], shuffle) + nt(parts[2], shuffle))
    thirds = [
        jnp.concatenate([grad[:, i * n : (i + 1) * n] for grad, (_, n) in zip(ffn_grads, cuts)], axis=1)
        for i in range(3)
    ]
    return (
        layer_out,
        tokens_grad,
        attn_grads[2],
        attn_grads[3],
        attn_grads[4],
        attn_grads[1],
        attn_grads[0].T,
        thirds[0],
        thirds[1],
        thirds[2].T,
    )


def solution(mesh):
    return jax.shard_map(
        functools.partial(shards, mesh.shape["dp"]),
        mesh=mesh,
        in_specs=(
            P(("dp", "tensor"), None),
            P("dp", "tensor"),
            P("dp", "tensor"),
            P("dp", "tensor"),
            P("dp", "tensor"),
            P("tensor", "dp"),
            P("dp", "tensor"),
            P("dp", "tensor"),
            P("tensor", "dp"),
            P("tensor"),
            P(("dp", "tensor"), None),
        ),
        out_specs=(
            P(("dp", "tensor"), None),
            P(("dp", "tensor"), None),
            P("dp", "tensor"),
            P("dp", "tensor"),
            P("dp", "tensor"),
            P("dp", "tensor"),
            P("tensor", "dp"),
            P("dp", "tensor"),
            P("dp", "tensor"),
            P("tensor", "dp"),
        ),
        check_vma=False,
    )
```

time: 1530 us -> 525 us (0.34)
  waiting for transfers between devices: 1260 us -> 193 us
  matrix products: 173 us -> 56.5 us
  starting transfers between devices: 1.14 us -> 87.2 us
  Pallas kernels: 0 us -> 82.7 us
    reduce_scatter x12 -> x0, waiting for transfers between devices: 784 us -> none  [the longest x1 130 us: shards(): lax.psum_scatter(grad_down, 'dp', scatter_dimension=1, tiled=True)]
    all_gather x12 -> x0, waiting for transfers between devices: 467 us -> none  [the longest x1 69.8 us: fetch_ffn(): lax.all_gather(w_down, 'dp', axis=1, tiled=True)]
    ppermute x0 -> x90, waiting for transfers between devices: none -> 193 us  [the longest x80 193 us: __call__(): result = lax.ppermute(array, 'dp', pairs)]
    dot_general x46 -> x21, matrix products: 173 us -> 56.5 us  [dot(): lax.dot_general(left, right, (dims, ((), ())), preferred_element_type=wide)]
    ppermute x0 -> x90, starting transfers between devices: none -> 87.2 us  [the longest x80 86.1 us: __call__(): result = lax.ppermute(array, 'dp', pairs)]
    pallas_call x0 -> x5, Pallas kernels: none -> 82.7 us  [the longest x3 66.1 us: ffn_chunk(): pl.pallas_call(functools.partial(ffn_kernel, chained=chained), grid=(tile...]
    slice x0 -> x38, local copies, waits for them, and re-layouts: none -> 16.4 us  [the longest x8 8.18 us: quarters(): return [array[i * q:(i + 1) * q] for i in range(4)]]
  transfers between devices with their start and end apart: 24 -> 90, of which waited for: 22 -> 42; matrix products, arithmetic and copies ran while one was open for 8% -> 27% of each run, Pallas kernels for 0% -> 16%
where the time goes in v1:
time: 525 us; the launch traced here: 517 us
  waiting for transfers between devices  193 us (37%)
  starting transfers between devices  87.2 us (17%)
  Pallas kernels  82.7 us (16%)
  matrix products  56.5 us (11%)
  local copies, waits for them, and re-layouts  52.2 us (10%)
  other arithmetic  42.7 us (8%)
    ppermute x80, waiting for transfers between devices, __call__(): result = lax.ppermute(array, 'dp', pairs)  193 us
    ppermute x80, starting transfers between devices, __call__(): result = lax.ppermute(array, 'dp', pairs)  86.1 us
    pallas_call x3, Pallas kernels, ffn_chunk(): pl.pallas_call(functools.partial(ffn_kernel, chained=chained), grid=(tile...  66.1 us
    dot_general x21, matrix products, dot(): lax.dot_general(left, right, (dims, ((), ())), preferred_element_type=wide)  56.5 us
    pallas_call x2, Pallas kernels, per_head(): pl.pallas_call(kernel, grid=(heads,), in_specs=[scalar, scalar] + [spec]...  16.7 us
    unnamed x138, local copies, waits for them, and re-layouts  14.8 us
    pallas_call x2, local copies, waits for them, and re-layouts, ffn_chunk(): pl.pallas_call(functools.partial(ffn_kernel, chained=chained), grid=(tile...  10.7 us
  transfers between devices with their start and end apart: 90, of which 42 were waited for; matrix products, arithmetic and copies ran while one was open for 27% of the time, Pallas kernels for 16%

profile of v1, /device:TPU:0, one launch (start us, length us, event | category | flops | bytes accessed | tf_op | source)
XLA Modules:
  0.0 517.1 jit_solution(12475559756861373189)
XLA Ops:
  0.7 4.1 collective-permute-start.5
  16.6 4.5 collective-permute-done.2
  31.9 3.2 collective-permute-start.17
  37.3 3.0 collective-permute-start.22
  48.0 4.3 collective-permute-done.23
  59.4 4.8 collective-permute-done.10
  67.9 5.1 multiply_convert_fusion.3
  73.0 4.7 multiply_convert_fusion.4
  80.6 4.2 convolution_convert_fusion.v_ref
  84.8 6.3 %shard_map.195 = f32[1024,512]{1,0:T(8,128)} custom-call(s32[1]{0:T(128)} %bitcast.1.turn_ref, f32[4]{0:T(128)} %rate_ref.3, bf16[1024,512]{1,0:T(8,128)(2,1)} %get-tuple-element.256.q_ref, bf16[1024,512]{1,0:T(8,128)(2,1)} %get-tuple-element.258.k_ref, bf16[1024,512]{1,0:T(8,128)(2,1)} %convolution_convert_fusion.v_ref), custom_call_target="tpu_custom_call" | custom-call | tf_op jit(solution)/shard_map/pallas_call | solution.py:185
  98.5 4.5 multiply_convert_fusion.2
  107.7 3.4 collective-permute-start.30
  111.1 9.5 %collective-permute-done.30 = bf16[64,1536]{1,0:T(8,128)(2,1)S(1)} collective-permute-done((bf16[64,1536]{1,0:T(8,128)(2,1)S(1)}, bf16[64,1536]{1,0:T(8,128)(2,1)S(1)}, u32[]{:S(2)}, u32[]{:S(2)}) %collective-permute-start.30) | collective-permute-done | bytes 196640 | tf_op jit(solution)/shard_map/ppermute | solution.py:56
  124.7 6.7 %collective-permute-done.31 = bf16[64,1536]{1,0:T(8,128)(2,1)S(1)} collective-permute-done((bf16[64,1536]{1,0:T(8,128)(2,1)S(1)}, bf16[64,1536]{1,0:T(8,128)(2,1)S(1)}, u32[]{:S(2)}, u32[]{:S(2)}) %collective-permute-start.31) | collective-permute-done | bytes 196640 | tf_op jit(solution)/shard_map/ppermute | solution.py:56
  131.4 4.5 collective-permute-done.33
  140.8 4.7 collective-permute-done.34
  145.6 8.8 %collective-permute-done.39.refs_5_ = bf16[256,1536]{1,0:T(8,128)(2,1)S(1)} collective-permute-done((bf16[256,1536]{1,0:T(8,128)(2,1)S(1)}, bf16[256,1536]{1,0:T(8,128)(2,1)S(1)}, u32[]{:S(2)}, u32[]{:S(2)}) %collective-permute-start.39) | collective-permute-done | bytes 786464 | tf_op jit(solution)/shard_map/ppermute | solution.py:56
  159.1 4.8 collective-permute-done.32
  164.6 10.3 %collective-permute-done.40.refs_5_ = bf16[256,1536]{1,0:T(8,128)(2,1)} collective-permute-done((bf16[256,1536]{1,0:T(8,128)(2,1)S(1)}, bf16[256,1536]{1,0:T(8,128)(2,1)}, u32[]{:S(2)}, u32[]{:S(2)}) %collective-permute-start.40) | collective-permute-done | bytes 786464 | tf_op jit(solution)/shard_map/ppermute | solution.py:56
  179.1 3.9 copy.31.refs_1_
  185.3 4.1 fusion.55
  189.4 3.9 copy.30.refs_0_
  193.3 17.9 %shard_map.196 = (f32[1024,1024]{1,0:T(8,128)}, f32[1024,1024]{1,0:T(8,128)}, bf16[1024,1536]{1,0:T(8,128)(2,1)}) custom-call(bf16[1024,1024]{1,0:T(8,128)(2,1)} %copy.30.refs_0_, bf16[1024,1024]{1,0:T(8,128)(2,1)} %copy.31.refs_1_, bf16[1024,1024]{1,0:T(8,128)(2,1)} %get-tuple-element.199.refs_2_, bf16[1024,1024]{1,0:T(8,128)(2,1)} %get-tuple-element.197.refs_3_, ...), custom_call_target="tpu_custom_call" | custom-call | tf_op jit(solution)/shard_map/pallas_call | solution.py:252
  219.7 24.1 %collective-permute-done.41.refs_6_ = bf16[256,1152]{1,0:T(8,128)(2,1)} collective-permute-done((bf16[256,1152]{1,0:T(8,128)(2,1)}, bf16[256,1152]{1,0:T(8,128)(2,1)}, u32[]{:S(2)}, u32[]{:S(2)}) %collective-permute-start.41) | collective-permute-done | bytes 589856 | tf_op jit(solution)/shard_map/ppermute | solution.py:56
  245.5 30.5 %shard_map.197 = (f32[1024,1024]{1,0:T(8,128)}, f32[1024,1024]{1,0:T(8,128)}, bf16[1024,1536]{1,0:T(8,128)(2,1)}) custom-call(bf16[1024,1024]{1,0:T(8,128)(2,1)} %copy.30.refs_0_, bf16[1024,1024]{1,0:T(8,128)(2,1)} %copy.31.refs_1_, bf16[1024,1024]{1,0:T(8,128)(2,1)} %get-tuple-element.199.refs_2_, bf16[1024,1024]{1,0:T(8,128)(2,1)} %get-tuple-element.197.refs_3_, ...), custom_call_target="tpu_custom_call" | custom-call | tf_op jit(solution)/shard_map/pallas_call | solution.py:252
  282.9 17.6 %shard_map.198 = (f32[1024,1024]{1,0:T(8,128)}, f32[1024,1024]{1,0:T(8,128)}, bf16[1024,1152]{1,0:T(8,128)(2,1)}) custom-call(bf16[1024,1024]{1,0:T(8,128)(2,1)} %copy.30.refs_0_, bf16[1024,1024]{1,0:T(8,128)(2,1)} %copy.31.refs_1_, bf16[1024,1024]{1,0:T(8,128)(2,1)} %get-tuple-element.199.refs_2_, bf16[1024,1024]{1,0:T(8,128)(2,1)} %get-tuple-element.197.refs_3_, ...), custom_call_target="tpu_custom_call" | custom-call | tf_op jit(solution)/shard_map/pallas_call | solution.py:252
  300.6 5.4 %copy.34 = f32[1024,1024]{0,1:T(8,128)} copy(f32[1024,1024]{1,0:T(8,128)} %get-tuple-element.137) | data formatting | bytes 8388608 | tf_op jit(solution)/shard_map/pallas_call | solution.py:252
  306.0 3.3 slice.410
  310.5 5.3 %copy.32 = f32[1024,1024]{0,1:T(8,128)} copy(f32[1024,1024]{1,0:T(8,128)} %get-tuple-element.136) | data formatting | bytes 8388608 | tf_op jit(solution)/shard_map/pallas_call | solution.py:252
  322.3 7.7 %collective-permute-done.51 = bf16[256,1536]{1,0:T(8,128)(2,1)} collective-permute-done((bf16[256,1536]{1,0:T(8,128)(2,1)}, bf16[256,1536]{1,0:T(8,128)(2,1)}, u32[]{:S(2)}, u32[]{:S(2)}) %collective-permute-start.51) | collective-permute-done | bytes 786464 | tf_op jit(solution)/shard_map/ppermute | solution.py:56
  331.8 14.4 %collective-permute-done.63 = bf16[256,1536]{1,0:T(8,128)(2,1)S(1)} collective-permute-done((bf16[256,1536]{1,0:T(8,128)(2,1)S(1)}, bf16[256,1536]{1,0:T(8,128)(2,1)S(1)}, u32[]{:S(2)}, u32[]{:S(2)}) %collective-permute-start.63) | collective-permute-done | bytes 786464 | tf_op jit(solution)/shard_map/ppermute | solution.py:56
  351.6 4.1 fusion.63
  358.2 5.9 %collective-permute-done.52 = bf16[256,1152]{1,0:T(8,128)(2,1)S(1)} collective-permute-done((bf16[256,1152]{1,0:T(8,128)(2,1)S(1)}, bf16[256,1152]{1,0:T(8,128)(2,1)S(1)}, u32[]{:S(2)}, u32[]{:S(2)}) %collective-permute-start.52) | collective-permute-done | bytes 589856 | tf_op jit(solution)/shard_map/ppermute | solution.py:56
  366.0 6.9 %collective-permute-done.69 = bf16[128,1536]{1,0:T(8,128)(2,1)S(1)} collective-permute-done((bf16[128,1536]{1,0:T(8,128)(2,1)S(1)}, bf16[128,1536]{1,0:T(8,128)(2,1)S(1)}, u32[]{:S(2)}, u32[]{:S(2)}) %collective-permute-start.69) | collective-permute-done | bytes 393248 | tf_op jit(solution)/shard_map/ppermute | solution.py:56
  389.6 4.5 fusion.82
  396.3 10.4 %shard_map.199 = (bf16[1024,512]{1,0:T(8,128)(2,1)}, bf16[1024,512]{1,0:T(8,128)(2,1)}, bf16[1024,512]{1,0:T(8,128)(2,1)}) custom-call(s32[1]{0:T(128)} %bitcast.1.turn_ref, f32[4]{0:T(128)} %rate_ref.3, bf16[1024,512]{1,0:T(8,128)(2,1)} %get-tuple-element.256.q_ref, bf16[1024,512]{1,0:T(8,128)(2,1)} %get-tuple-element.258.k_ref, ...), custom_call_target="tpu_custom_call" | custom-call | tf_op jit(solution)/shard_map/pallas_call | solution.py:185
  406.7 2.9 fusion.87
  409.7 2.9 fusion.81
  414.0 2.9 fusion.84
  421.4 2.9 fusion.85
  426.9 8.4 %collective-permute-done.76 = bf16[64,1152]{1,0:T(8,128)(2,1)S(1)} collective-permute-done((bf16[64,1152]{1,0:T(8,128)(2,1)S(1)}, bf16[64,1152]{1,0:T(8,128)(2,1)S(1)}, u32[]{:S(2)}, u32[]{:S(2)}) %collective-permute-start.76) | collective-permute-done | bytes 147488 | tf_op jit(solution)/shard_map/ppermute | solution.py:56
  440.4 5.4 %collective-permute-done.59 = bf16[256,512]{1,0:T(8,128)(2,1)S(1)} collective-permute-done((bf16[256,512]{1,0:T(8,128)(2,1)S(1)}, bf16[256,512]{1,0:T(8,128)(2,1)S(1)}, u32[]{:S(2)}, u32[]{:S(2)}) %collective-permute-start.59) | collective-permute-done | bytes 262176 | tf_op jit(solution)/shard_map/ppermute | solution.py:56
  447.0 4.5 collective-permute-done.54
  456.5 4.3 collective-permute-done.60
  461.0 5.4 %collective-permute-done.55 = bf16[256,512]{1,0:T(8,128)(2,1)S(1)} collective-permute-done((bf16[256,512]{1,0:T(8,128)(2,1)S(1)}, bf16[256,512]{1,0:T(8,128)(2,1)S(1)}, u32[]{:S(2)}, u32[]{:S(2)}) %collective-permute-start.55) | collective-permute-done | bytes 262176 | tf_op jit(solution)/shard_map/ppermute | solution.py:56
  469.9 5.2 %collective-permute-done.61 = bf16[256,512]{1,0:T(8,128)(2,1)S(1)} collective-permute-done((bf16[256,512]{1,0:T(8,128)(2,1)S(1)}, bf16[256,512]{1,0:T(8,128)(2,1)S(1)}, u32[]{:S(2)}, u32[]{:S(2)}) %collective-permute-start.61) | collective-permute-done | bytes 262176 | tf_op jit(solution)/shard_map/ppermute | solution.py:56
  491.6 3.6 collective-permute-done.86
  498.9 3.1 collective-permute-done.88
  (412 shorter events, 191.9 us)
Async XLA Ops:
  8.2 59.7 %collective-permute-start = (bf16[512,1024]{0,1:T(8,128)(2,1)}, bf16[512,1024]{0,1:T(8,128)(2,1)}, u32[]{:S(2)}, u32[]{:S(2)}) collective-permute-start(bf16[512,1024]{0,1:T(8,128)(2,1)} %fusion.21), channel_id=1, source_target_pairs={{0,1},{1,0},{2,3},{3,2},{4,5},{5,4},{6,7},{7,6},{8,9},{9,8},{10,11... | collective-permute-start | bytes 3145736 | tf_op jit(solution)/shard_map/ppermute | solution.py:299
  12.3 15.4 %collective-permute-start.7 = (bf16[128,512]{1,0:T(8,128)(2,1)S(1)}, bf16[128,512]{1,0:T(8,128)(2,1)S(1)}, u32[]{:S(2)}, u32[]{:S(2)}) collective-permute-start(bf16[128,512]{1,0:T(8,128)(2,1)S(1)} %pad_maximum_fusion.19), channel_id=1, source_target_pairs={{0,8},{2,10},{4,12},{6,14},{8,0},{10,2},{12,4},{14,6},{16,24},{18,... | collective-permute-start | bytes 393224 | tf_op jit(solution)/shard_map/ppermute | solution.py:56
  21.9 21.3 %collective-permute-start.3 = (bf16[256,512]{1,0:T(8,128)(2,1)}, bf16[256,512]{1,0:T(8,128)(2,1)S(1)}, u32[]{:S(2)}, u32[]{:S(2)}) collective-permute-start(bf16[256,512]{1,0:T(8,128)(2,1)} %get-tuple-element.231), channel_id=1, source_target_pairs={{0,2},{2,0},{4,6},{6,4},{8,10},{10,8},{12,14},{14,12},{16,18},{18,... | collective-permute-start | bytes 786440 | tf_op jit(solution)/shard_map/ppermute | solution.py:56
  23.5 20.2 %collective-permute-start.4 = (bf16[256,512]{1,0:T(8,128)(2,1)}, bf16[256,512]{1,0:T(8,128)(2,1)S(1)}, u32[]{:S(2)}, u32[]{:S(2)}) collective-permute-start(bf16[256,512]{1,0:T(8,128)(2,1)} %get-tuple-element.231), channel_id=1, source_target_pairs={{0,4},{2,6},{4,0},{6,2},{8,12},{10,14},{12,8},{14,10},{16,20},{18,... | collective-permute-start | bytes 786440 | tf_op jit(solution)/shard_map/ppermute | solution.py:56
  64.2 13.5 %collective-permute-start.15 = (bf16[256,512]{1,0:T(8,128)(2,1)S(1)}, bf16[256,512]{1,0:T(8,128)(2,1)S(1)}, u32[]{:S(2)}, u32[]{:S(2)}) collective-permute-start(bf16[256,512]{1,0:T(8,128)(2,1)S(1)} %collective-permute-done.13), channel_id=1, source_target_pairs={{0,4},{2,6},{4,0},{6,2},{8,12},{10,14},{12,8},{14,10},{16,20},{18,... | collective-permute-start | bytes 786440 | tf_op jit(solution)/shard_map/ppermute | solution.py:56
  66.5 11.2 %collective-permute-start.20 = (bf16[256,512]{1,0:T(8,128)(2,1)S(1)}, bf16[256,512]{1,0:T(8,128)(2,1)}, u32[]{:S(2)}, u32[]{:S(2)}) collective-permute-start(bf16[256,512]{1,0:T(8,128)(2,1)S(1)} %get-tuple-element.110), channel_id=1, source_target_pairs={{0,4},{2,6},{4,0},{6,2},{8,12},{10,14},{12,8},{14,10},{16,20},{18,... | collective-permute-start | bytes 786440 | tf_op jit(solution)/shard_map/ppermute | solution.py:56
  67.0 12.0 %collective-permute-start.19 = (bf16[256,512]{1,0:T(8,128)(2,1)S(1)}, bf16[256,512]{1,0:T(8,128)(2,1)S(1)}, u32[]{:S(2)}, u32[]{:S(2)}) collective-permute-start(bf16[256,512]{1,0:T(8,128)(2,1)S(1)} %get-tuple-element.110), channel_id=1, source_target_pairs={{0,2},{2,0},{4,6},{6,4},{8,10},{10,8},{12,14},{14,12},{16,18},{18,... | collective-permute-start | bytes 786440 | tf_op jit(solution)/shard_map/ppermute | solution.py:56
  77.7 17.9 %collective-permute-start.21 = (bf16[256,512]{1,0:T(8,128)(2,1)}, bf16[256,512]{1,0:T(8,128)(2,1)}, u32[]{:S(2)}, u32[]{:S(2)}) collective-permute-start(bf16[256,512]{1,0:T(8,128)(2,1)} %collective-permute-done.20), channel_id=1, source_target_pairs={{0,2},{2,0},{4,6},{6,4},{8,10},{10,8},{12,14},{14,12},{16,18},{18,... | collective-permute-start | bytes 786440 | tf_op jit(solution)/shard_map/ppermute | solution.py:56
  79.0 16.6 %collective-permute-start.24 = (bf16[256,512]{1,0:T(8,128)(2,1)S(1)}, bf16[256,512]{1,0:T(8,128)(2,1)}, u32[]{:S(2)}, u32[]{:S(2)}) collective-permute-start(bf16[256,512]{1,0:T(8,128)(2,1)S(1)} %pad_maximum_fusion.14), channel_id=1, source_target_pairs={{0,2},{2,0},{4,6},{6,4},{8,10},{10,8},{12,14},{14,12},{16,18},{18,... | collective-permute-start | bytes 786440 | tf_op jit(solution)/shard_map/ppermute | solution.py:56
  79.8 24.4 %collective-permute-start.25 = (bf16[256,512]{1,0:T(8,128)(2,1)S(1)}, bf16[256,512]{1,0:T(8,128)(2,1)}, u32[]{:S(2)}, u32[]{:S(2)}) collective-permute-start(bf16[256,512]{1,0:T(8,128)(2,1)S(1)} %pad_maximum_fusion.14), channel_id=1, source_target_pairs={{0,4},{2,6},{4,0},{6,2},{8,12},{10,14},{12,8},{14,10},{16,20},{18,... | collective-permute-start | bytes 786440 | tf_op jit(solution)/shard_map/ppermute | solution.py:56
  106.8 31.6 %collective-permute-start.27 = (f32[512,1024]{0,1:T(8,128)S(1)}, f32[512,1024]{0,1:T(8,128)S(1)}, u32[]{:S(2)}, u32[]{:S(2)}) collective-permute-start(f32[512,1024]{0,1:T(8,128)S(1)} %slice.403), channel_id=1, source_target_pairs={{0,1},{1,0},{2,3},{3,2},{4,5},{5,4},{6,7},{7,6},{8,9},{9,8},{10,11... | collective-permute-start | bytes 6291464 | tf_op jit(solution)/shard_map/ppermute | solution.py:299
  107.7 12.9 %collective-permute-start.30 = (bf16[64,1536]{1,0:T(8,128)(2,1)S(1)}, bf16[64,1536]{1,0:T(8,128)(2,1)S(1)}, u32[]{:S(2)}, u32[]{:S(2)}) collective-permute-start(bf16[64,1536]{1,0:T(8,128)(2,1)S(1)} %pad_maximum_fusion.16), channel_id=1, source_target_pairs={{0,16},{2,18},{4,20},{6,22},{8,24},{10,26},{12,28},{14,30},{16,0},... | collective-permute-start | bytes 589832 | tf_op jit(solution)/shard_map/ppermute | solution.py:56
  120.6 15.3 %collective-permute-start.33 = (bf16[128,1536]{1,0:T(8,128)(2,1)S(1)}, bf16[128,1536]{1,0:T(8,128)(2,1)S(1)}, u32[]{:S(2)}, u32[]{:S(2)}) collective-permute-start(bf16[128,1536]{1,0:T(8,128)(2,1)S(1)} %pad_maximum_fusion.10), channel_id=1, source_target_pairs={{0,8},{2,10},{4,12},{6,14},{8,0},{10,2},{12,4},{14,6},{16,24},{18,... | collective-permute-start | bytes 1179656 | tf_op jit(solution)/shard_map/ppermute | solution.py:56
  124.7 51.7 %collective-permute-start.29 = (bf16[512,1024]{0,1:T(8,128)(2,1)S(1)}, bf16[512,1024]{0,1:T(8,128)(2,1)S(1)}, u32[]{:S(2)}, u32[]{:S(2)}) collective-permute-start(bf16[512,1024]{0,1:T(8,128)(2,1)S(1)} %fusion.26), channel_id=1, source_target_pairs={{0,1},{1,0},{2,3},{3,2},{4,5},{5,4},{6,7},{7,6},{8,9},{9,8},{10,11... | collective-permute-start | bytes 3145736 | tf_op jit(solution)/shard_map/ppermute | solution.py:299
  136.0 22.8 %collective-permute-start.36 = (bf16[256,1536]{1,0:T(8,128)(2,1)S(1)}, bf16[256,1536]{1,0:T(8,128)(2,1)}, u32[]{:S(2)}, u32[]{:S(2)}) collective-permute-start(bf16[256,1536]{1,0:T(8,128)(2,1)S(1)} %pad_maximum_fusion.6.refs_4_), channel_id=1, source_target_pairs={{0,4},{2,6},{4,0},{6,2},{8,12},{10,14},{12,8},{14,10},{16,20},{18,... | collective-permute-start | bytes 2359304 | tf_op jit(solution)/shard_map/ppermute | solution.py:56
  136.3 18.1 %collective-permute-start.39 = (bf16[256,1536]{1,0:T(8,128)(2,1)S(1)}, bf16[256,1536]{1,0:T(8,128)(2,1)S(1)}, u32[]{:S(2)}, u32[]{:S(2)}) collective-permute-start(bf16[256,1536]{1,0:T(8,128)(2,1)S(1)} %pad_maximum_fusion.6.refs_4_), channel_id=1, source_target_pairs={{0,2},{2,0},{4,6},{6,4},{8,10},{10,8},{12,14},{14,12},{16,18},{18,... | collective-permute-start | bytes 2359304 | tf_op jit(solution)/shard_map/ppermute | solution.py:56
  140.8 44.5 %collective-permute-start.28 = (bf16[512,1024]{0,1:T(8,128)(2,1)}, bf16[512,1024]{0,1:T(8,128)(2,1)}, u32[]{:S(2)}, u32[]{:S(2)}) collective-permute-start(bf16[512,1024]{0,1:T(8,128)(2,1)} %multiply_convert_fusion.5), channel_id=1, source_target_pairs={{0,1},{1,0},{2,3},{3,2},{4,5},{5,4},{6,7},{7,6},{8,9},{9,8},{10,11... | collective-permute-start | bytes 3145736 | tf_op jit(solution)/shard_map/ppermute | solution.py:299
  154.4 20.5 %collective-permute-start.40 = (bf16[256,1536]{1,0:T(8,128)(2,1)S(1)}, bf16[256,1536]{1,0:T(8,128)(2,1)}, u32[]{:S(2)}, u32[]{:S(2)}) collective-permute-start(bf16[256,1536]{1,0:T(8,128)(2,1)S(1)} %pad_maximum_fusion.7.refs_4_), channel_id=1, source_target_pairs={{0,2},{2,0},{4,6},{6,4},{8,10},{10,8},{12,14},{14,12},{16,18},{18,... | collective-permute-start | bytes 2359304 | tf_op jit(solution)/shard_map/ppermute | solution.py:56
  158.8 34.5 %collective-permute-start.37 = (bf16[256,1536]{1,0:T(8,128)(2,1)}, bf16[256,1536]{1,0:T(8,128)(2,1)}, u32[]{:S(2)}, u32[]{:S(2)}) collective-permute-start(bf16[256,1536]{1,0:T(8,128)(2,1)} %collective-permute-done.36.refs_6_), channel_id=1, source_target_pairs={{0,2},{2,0},{4,6},{6,4},{8,10},{10,8},{12,14},{14,12},{16,18},{18,... | collective-permute-start | bytes 2359304 | tf_op jit(solution)/shard_map/ppermute | solution.py:56
  174.9 39.0 %collective-permute-start.44 = (bf16[256,1536]{1,0:T(8,128)(2,1)}, bf16[256,1536]{1,0:T(8,128)(2,1)}, u32[]{:S(2)}, u32[]{:S(2)}) collective-permute-start(bf16[256,1536]{1,0:T(8,128)(2,1)} %collective-permute-done.40.refs_5_), channel_id=1, source_target_pairs={{0,4},{2,6},{4,0},{6,2},{8,12},{10,14},{12,8},{14,10},{16,20},{18,... | collective-permute-start | bytes 2359304 | tf_op jit(solution)/shard_map/ppermute | solution.py:56
  183.0 32.4 %collective-permute-start.35 = (bf16[128,1152]{1,0:T(8,128)(2,1)}, bf16[128,1152]{1,0:T(8,128)(2,1)}, u32[]{:S(2)}, u32[]{:S(2)}) collective-permute-start(bf16[128,1152]{1,0:T(8,128)(2,1)} %pad_maximum_fusion.13), channel_id=1, source_target_pairs={{0,8},{2,10},{4,12},{6,14},{8,0},{10,2},{12,4},{14,6},{16,24},{18,... | collective-permute-start | bytes 884744 | tf_op jit(solution)/shard_map/ppermute | solution.py:56
  184.8 34.8 %collective-permute-start.42 = (bf16[256,1536]{1,0:T(8,128)(2,1)}, bf16[256,1536]{1,0:T(8,128)(2,1)}, u32[]{:S(2)}, u32[]{:S(2)}) collective-permute-start(bf16[256,1536]{1,0:T(8,128)(2,1)} %copy-done.11), channel_id=1, source_target_pairs={{0,4},{2,6},{4,0},{6,2},{8,12},{10,14},{12,8},{14,10},{16,20},{18,... | collective-permute-start | bytes 2359304 | tf_op jit(solution)/shard_map/ppermute | solution.py:56
  213.9 62.1 %collective-permute-start.50 = (bf16[256,1536]{1,0:T(8,128)(2,1)}, bf16[256,1536]{1,0:T(8,128)(2,1)}, u32[]{:S(2)}, u32[]{:S(2)}) collective-permute-start(bf16[256,1536]{1,0:T(8,128)(2,1)} %get-tuple-element.144), channel_id=1, source_target_pairs={{0,4},{2,6},{4,0},{6,2},{8,12},{10,14},{12,8},{14,10},{16,20},{18,... | collective-permute-start | bytes 2359304 | tf_op jit(solution)/shard_map/ppermute | solution.py:56
  217.3 26.5 %collective-permute-start.41 = (bf16[256,1152]{1,0:T(8,128)(2,1)}, bf16[256,1152]{1,0:T(8,128)(2,1)}, u32[]{:S(2)}, u32[]{:S(2)}) collective-permute-start(bf16[256,1152]{1,0:T(8,128)(2,1)} %pad_maximum_fusion.8.refs_4_), channel_id=1, source_target_pairs={{0,4},{2,6},{4,0},{6,2},{8,12},{10,14},{12,8},{14,10},{16,20},{18,... | collective-permute-start | bytes 1769480 | tf_op jit(solution)/shard_map/ppermute | solution.py:56
  217.8 60.6 %collective-permute-start.38 = (bf16[256,1152]{1,0:T(8,128)(2,1)}, bf16[256,1152]{1,0:T(8,128)(2,1)}, u32[]{:S(2)}, u32[]{:S(2)}) collective-permute-start(bf16[256,1152]{1,0:T(8,128)(2,1)} %pad_maximum_fusion.8.refs_4_), channel_id=1, source_target_pairs={{0,2},{2,0},{4,6},{6,4},{8,10},{10,8},{12,14},{14,12},{16,18},{18,... | collective-permute-start | bytes 1769480 | tf_op jit(solution)/shard_map/ppermute | solution.py:56
  243.8 39.2 %collective-permute-start.43 = (bf16[256,1152]{1,0:T(8,128)(2,1)}, bf16[256,1152]{1,0:T(8,128)(2,1)}, u32[]{:S(2)}, u32[]{:S(2)}) collective-permute-start(bf16[256,1152]{1,0:T(8,128)(2,1)} %collective-permute-done.41.refs_6_), channel_id=1, source_target_pairs={{0,2},{2,0},{4,6},{6,4},{8,10},{10,8},{12,14},{14,12},{16,18},{18,... | collective-permute-start | bytes 1769480 | tf_op jit(solution)/shard_map/ppermute | solution.py:56
  245.1 73.0 %collective-permute-start.62 = (bf16[256,1536]{1,0:T(8,128)(2,1)}, bf16[256,1536]{1,0:T(8,128)(2,1)}, u32[]{:S(2)}, u32[]{:S(2)}) collective-permute-start(bf16[256,1536]{1,0:T(8,128)(2,1)} %get-tuple-element.156), channel_id=1, source_target_pairs={{0,4},{2,6},{4,0},{6,2},{8,12},{10,14},{12,8},{14,10},{16,20},{18,... | collective-permute-start | bytes 2359304 | tf_op jit(solution)/shard_map/ppermute | solution.py:56
  278.4 41.5 %collective-permute-start.56 = (bf16[256,1536]{1,0:T(8,128)(2,1)}, bf16[256,1536]{1,0:T(8,128)(2,1)}, u32[]{:S(2)}, u32[]{:S(2)}) collective-permute-start(bf16[256,1536]{1,0:T(8,128)(2,1)} %add_convert_fusion), channel_id=1, source_target_pairs={{0,2},{2,0},{4,6},{6,4},{8,10},{10,8},{12,14},{14,12},{16,18},{18,... | collective-permute-start | bytes 2359304 | tf_op jit(solution)/shard_map/ppermute | solution.py:56
  309.2 39.2 %collective-permute-start.46 = (f32[512,1024]{0,1:T(8,128)}, f32[512,1024]{0,1:T(8,128)}, u32[]{:S(2)}, u32[]{:S(2)}) collective-permute-start(f32[512,1024]{0,1:T(8,128)} %slice.410), channel_id=1, source_target_pairs={{0,1},{1,0},{2,3},{3,2},{4,5},{5,4},{6,7},{7,6},{8,9},{9,8},{10,11... | collective-permute-start | bytes 6291464 | tf_op jit(solution)/shard_map/ppermute | solution.py:299
  309.2 20.7 %collective-permute-start.51 = (bf16[256,1536]{1,0:T(8,128)(2,1)}, bf16[256,1536]{1,0:T(8,128)(2,1)}, u32[]{:S(2)}, u32[]{:S(2)}) collective-permute-start(bf16[256,1536]{1,0:T(8,128)(2,1)} %get-tuple-element.145), channel_id=1, source_target_pairs={{0,2},{2,0},{4,6},{6,4},{8,10},{10,8},{12,14},{14,12},{16,18},{18,... | collective-permute-start | bytes 2359304 | tf_op jit(solution)/shard_map/ppermute | solution.py:56
  317.7 37.9 %collective-permute-start.45 = (f32[512,1024]{0,1:T(8,128)S(1)}, f32[512,1024]{0,1:T(8,128)S(1)}, u32[]{:S(2)}, u32[]{:S(2)}) collective-permute-start(f32[512,1024]{0,1:T(8,128)S(1)} %slice.408), channel_id=1, source_target_pairs={{0,1},{1,0},{2,3},{3,2},{4,5},{5,4},{6,7},{7,6},{8,9},{9,8},{10,11... | collective-permute-start | bytes 6291464 | tf_op jit(solution)/shard_map/ppermute | solution.py:299
  318.2 28.1 %collective-permute-start.63 = (bf16[256,1536]{1,0:T(8,128)(2,1)S(1)}, bf16[256,1536]{1,0:T(8,128)(2,1)S(1)}, u32[]{:S(2)}, u32[]{:S(2)}) collective-permute-start(bf16[256,1536]{1,0:T(8,128)(2,1)S(1)} %copy-done.34), channel_id=1, source_target_pairs={{0,2},{2,0},{4,6},{6,4},{8,10},{10,8},{12,14},{14,12},{16,18},{18,... | collective-permute-start | bytes 2359304 | tf_op jit(solution)/shard_map/ppermute | solution.py:56
  322.1 24.7 %collective-permute-start.68 = (bf16[128,1536]{1,0:T(8,128)(2,1)S(1)}, bf16[128,1536]{1,0:T(8,128)(2,1)S(1)}, u32[]{:S(2)}, u32[]{:S(2)}) collective-permute-start(bf16[128,1536]{1,0:T(8,128)(2,1)S(1)} %slice.563), channel_id=1, source_target_pairs={{0,8},{2,10},{4,12},{6,14},{8,0},{10,2},{12,4},{14,6},{16,24},{18,... | collective-permute-start | bytes 1179656 | tf_op jit(solution)/shard_map/ppermute | solution.py:56
  331.3 33.0 %collective-permute-start.57 = (bf16[256,1536]{1,0:T(8,128)(2,1)S(1)}, bf16[256,1536]{1,0:T(8,128)(2,1)S(1)}, u32[]{:S(2)}, u32[]{:S(2)}) collective-permute-start(bf16[256,1536]{1,0:T(8,128)(2,1)S(1)} %add_convert_fusion.1), channel_id=1, source_target_pairs={{0,4},{2,6},{4,0},{6,2},{8,12},{10,14},{12,8},{14,10},{16,20},{18,... | collective-permute-start | bytes 2359304 | tf_op jit(solution)/shard_map/ppermute | solution.py:56
  346.2 17.9 %collective-permute-start.52 = (bf16[256,1152]{1,0:T(8,128)(2,1)S(1)}, bf16[256,1152]{1,0:T(8,128)(2,1)S(1)}, u32[]{:S(2)}, u32[]{:S(2)}) collective-permute-start(bf16[256,1152]{1,0:T(8,128)(2,1)S(1)} %copy-done.36), channel_id=1, source_target_pairs={{0,4},{2,6},{4,0},{6,2},{8,12},{10,14},{12,8},{14,10},{16,20},{18,... | collective-permute-start | bytes 1769480 | tf_op jit(solution)/shard_map/ppermute | solution.py:56
  346.8 28.5 %collective-permute-start.64 = (bf16[256,1152]{1,0:T(8,128)(2,1)S(1)}, bf16[256,1152]{1,0:T(8,128)(2,1)S(1)}, u32[]{:S(2)}, u32[]{:S(2)}) collective-permute-start(bf16[256,1152]{1,0:T(8,128)(2,1)S(1)} %copy-done.35), channel_id=1, source_target_pairs={{0,4},{2,6},{4,0},{6,2},{8,12},{10,14},{12,8},{14,10},{16,20},{18,... | collective-permute-start | bytes 1769480 | tf_op jit(solution)/shard_map/ppermute | solution.py:56
  348.4 16.4 %collective-permute-start.74 = (bf16[64,1536]{1,0:T(8,128)(2,1)S(1)}, bf16[64,1536]{1,0:T(8,128)(2,1)S(1)}, u32[]{:S(2)}, u32[]{:S(2)}) collective-permute-start(bf16[64,1536]{1,0:T(8,128)(2,1)S(1)} %slice.566), channel_id=1, source_target_pairs={{0,16},{2,18},{4,20},{6,22},{8,24},{10,26},{12,28},{14,30},{16,0},... | collective-permute-start | bytes 589832 | tf_op jit(solution)/shard_map/ppermute | solution.py:56
  355.6 26.9 %collective-permute-start.47 = (bf16[512,1024]{0,1:T(8,128)(2,1)S(1)}, bf16[512,1024]{0,1:T(8,128)(2,1)S(1)}, u32[]{:S(2)}, u32[]{:S(2)}) collective-permute-start(bf16[512,1024]{0,1:T(8,128)(2,1)S(1)} %get-tuple-element.186), channel_id=1, source_target_pairs={{0,1},{1,0},{2,3},{3,2},{4,5},{5,4},{6,7},{7,6},{8,9},{9,8},{10,11... | collective-permute-start | bytes 3145736 | tf_op jit(solution)/shard_map/ppermute | solution.py:299
  364.9 12.3 %collective-permute-start.58 = (bf16[256,1152]{1,0:T(8,128)(2,1)S(1)}, bf16[256,1152]{1,0:T(8,128)(2,1)S(1)}, u32[]{:S(2)}, u32[]{:S(2)}) collective-permute-start(bf16[256,1152]{1,0:T(8,128)(2,1)S(1)} %add_convert_fusion.2), channel_id=1, source_target_pairs={{0,2},{2,0},{4,6},{6,4},{8,10},{10,8},{12,14},{14,12},{16,18},{18,... | collective-permute-start | bytes 1769480 | tf_op jit(solution)/shard_map/ppermute | solution.py:56
  378.2 46.1 %collective-permute-start.70 = (bf16[128,1152]{1,0:T(8,128)(2,1)}, bf16[128,1152]{1,0:T(8,128)(2,1)}, u32[]{:S(2)}, u32[]{:S(2)}) collective-permute-start(bf16[128,1152]{1,0:T(8,128)(2,1)} %slice.565), channel_id=1, source_target_pairs={{0,8},{2,10},{4,12},{6,14},{8,0},{10,2},{12,4},{14,6},{16,24},{18,... | collective-permute-start | bytes 884744 | tf_op jit(solution)/shard_map/ppermute | solution.py:56
  385.9 49.5 %collective-permute-start.53 = (bf16[256,512]{1,0:T(8,128)(2,1)}, bf16[256,512]{1,0:T(8,128)(2,1)}, u32[]{:S(2)}, u32[]{:S(2)}) collective-permute-start(bf16[256,512]{1,0:T(8,128)(2,1)} %get-tuple-element.147), channel_id=1, source_target_pairs={{0,4},{2,6},{4,0},{6,2},{8,12},{10,14},{12,8},{14,10},{16,20},{18,... | collective-permute-start | bytes 786440 | tf_op jit(solution)/shard_map/ppermute | solution.py:56
  386.3 53.9 %collective-permute-start.65 = (bf16[256,512]{1,0:T(8,128)(2,1)}, bf16[256,512]{1,0:T(8,128)(2,1)}, u32[]{:S(2)}, u32[]{:S(2)}) collective-permute-start(bf16[256,512]{1,0:T(8,128)(2,1)} %get-tuple-element.159), channel_id=1, source_target_pairs={{0,4},{2,6},{4,0},{6,2},{8,12},{10,14},{12,8},{14,10},{16,20},{18,... | collective-permute-start | bytes 786440 | tf_op jit(solution)/shard_map/ppermute | solution.py:56
  421.1 86.9 %collective-permute-start.49 = (f32[512,1024]{0,1:T(8,128)S(1)}, f32[512,1024]{0,1:T(8,128)S(1)}, u32[]{:S(2)}, u32[]{:S(2)}) collective-permute-start(f32[512,1024]{0,1:T(8,128)S(1)} %slice.412), channel_id=1, source_target_pairs={{0,1},{1,0},{2,3},{3,2},{4,5},{5,4},{6,7},{7,6},{8,9},{9,8},{10,11... | collective-permute-start | bytes 6291464 | tf_op jit(solution)/shard_map/ppermute | solution.py:299
  438.4 13.1 %collective-permute-start.54 = (bf16[256,512]{1,0:T(8,128)(2,1)S(1)}, bf16[256,512]{1,0:T(8,128)(2,1)S(1)}, u32[]{:S(2)}, u32[]{:S(2)}) collective-permute-start(bf16[256,512]{1,0:T(8,128)(2,1)S(1)} %copy-done.50), channel_id=1, source_target_pairs={{0,2},{2,0},{4,6},{6,4},{8,10},{10,8},{12,14},{14,12},{16,18},{18,... | collective-permute-start | bytes 786440 | tf_op jit(solution)/shard_map/ppermute | solution.py:56
  440.3 15.9 %collective-permute-start.66 = (bf16[256,512]{1,0:T(8,128)(2,1)S(1)}, bf16[256,512]{1,0:T(8,128)(2,1)S(1)}, u32[]{:S(2)}, u32[]{:S(2)}) collective-permute-start(bf16[256,512]{1,0:T(8,128)(2,1)S(1)} %copy-done.49), channel_id=1, source_target_pairs={{0,2},{2,0},{4,6},{6,4},{8,10},{10,8},{12,14},{14,12},{16,18},{18,... | collective-permute-start | bytes 786440 | tf_op jit(solution)/shard_map/ppermute | solution.py:56
  452.6 13.8 %collective-permute-start.55 = (bf16[256,512]{1,0:T(8,128)(2,1)S(1)}, bf16[256,512]{1,0:T(8,128)(2,1)S(1)}, u32[]{:S(2)}, u32[]{:S(2)}) collective-permute-start(bf16[256,512]{1,0:T(8,128)(2,1)S(1)} %get-tuple-element.149), channel_id=1, source_target_pairs={{0,4},{2,6},{4,0},{6,2},{8,12},{10,14},{12,8},{14,10},{16,20},{18,... | collective-permute-start | bytes 786440 | tf_op jit(solution)/shard_map/ppermute | solution.py:56
  456.2 13.2 %collective-permute-start.67 = (bf16[256,512]{1,0:T(8,128)(2,1)S(1)}, bf16[256,512]{1,0:T(8,128)(2,1)S(1)}, u32[]{:S(2)}, u32[]{:S(2)}) collective-permute-start(bf16[256,512]{1,0:T(8,128)(2,1)S(1)} %get-tuple-element.161), channel_id=1, source_target_pairs={{0,4},{2,6},{4,0},{6,2},{8,12},{10,14},{12,8},{14,10},{16,20},{18,... | collective-permute-start | bytes 786440 | tf_op jit(solution)/shard_map/ppermute | solution.py:56
  469.3 12.4 %collective-permute-start.80 = (bf16[256,512]{1,0:T(8,128)(2,1)S(1)}, bf16[256,512]{1,0:T(8,128)(2,1)S(1)}, u32[]{:S(2)}, u32[]{:S(2)}) collective-permute-start(bf16[256,512]{1,0:T(8,128)(2,1)S(1)} %get-tuple-element.174), channel_id=1, source_target_pairs={{0,2},{2,0},{4,6},{6,4},{8,10},{10,8},{12,14},{14,12},{16,18},{18,... | collective-permute-start | bytes 786440 | tf_op jit(solution)/shard_map/ppermute | solution.py:56
  (99 other events, 834.3 us)

commit v2 on v1

v2 whole, which is shorter than its diff:
```python
import functools

import jax
import jax.numpy as jnp
import numpy as np
from jax import lax
from jax.experimental import pallas as pl
from jax.experimental.pallas import tpu as pltpu
from jax.sharding import PartitionSpec as P

eps = 1e-06
wide = jnp.float32
narrow = jnp.bfloat16
in_flight = 6
per_link = 2
tile_width = 512


def dot(left, right, dims):
    return lax.dot_general(left, right, (dims, ((), ())), preferred_element_type=wide)


def nn(left, right):
    return dot(left, right, ((1,), (0,)))


def nt(left, right):
    return dot(left, right, ((1,), (1,)))


def tn(left, right):
    return dot(left, right, ((0,), (0,)))


def inverse_rms(values):
    return lax.rsqrt(jnp.mean(values * values, axis=-1, keepdims=True) + eps)


def norm_back(grad, normed, scale):
    return scale * (grad - normed * jnp.mean(grad * normed, axis=-1, keepdims=True))


def silu_slope(values):
    sigma = jax.nn.sigmoid(values)
    return sigma * (1.0 + values * (1.0 - sigma))


class Exchange:

    def __init__(self, size):
        self.size = size
        self.sent = []
        self.links = {1: [], 2: [], 4: []}

    def __call__(self, array, bit):
        link = self.links[min(bit, 4)]
        ahead = [q[-n] for q, n in ((self.sent, in_flight), (link, per_link)) if len(q) >= n]
        if ahead:
            array = lax.optimization_barrier((array, *ahead))[0]
        pairs = [(i, i ^ bit) for i in range(self.size)]
        result = lax.ppermute(array, "dp", pairs)
        self.sent.append(result)
        link.append(result)
        return result


def inner_bits(size):
    bits = []
    bit = size // 2
    while bit >= 4:
        bits.append(bit)
        bit //= 2
    return bits


def block_offsets(size):
    order = [0]
    for bit in inner_bits(size) + [1, 2]:
        order = order + [entry ^ bit for entry in order]
    return np.array(order, np.int32)


class Gather:

    def __init__(self, send, shard, turn):
        self.send = send
        self.held = shard
        self.turn = turn

    def inner(self, bit):
        self.held = jnp.concatenate([self.held, self.send(self.held, bit)], axis=0)

    def sides(self):
        self.side = self.send(self.held, 1)
        self.up = self.send(self.held, 2)

    def far(self):
        far = self.send(self.side, 2) if self.turn else self.send(self.up, 1)
        self.pieces = [self.held, self.side, self.up, far]


def low(value):
    return value.astype(narrow)


class Scatter:

    def __init__(self, send, pieces, turn):
        self.send = send
        self.first, self.side, self.up, self.away = pieces
        self.turn = turn

    def far(self):
        if self.turn:
            self.far_got = self.send(self.away, 2)
        else:
            self.far_got = self.send(self.away, 1)

    def near(self):
        if self.turn:
            self.near_got = self.send(self.up, 2)
        else:
            self.near_got = self.send(self.side, 1)

    def sides(self):
        rest = self.side if self.turn else self.up
        rest = low(rest.astype(wide) + self.far_got.astype(wide))
        got = self.send(rest, 1 if self.turn else 2)
        self.total = self.first.astype(wide) + self.near_got.astype(wide) + got.astype(wide)

    def inner(self, bit):
        half = self.total.shape[0] // 2
        got = self.send(low(self.total[half:]), bit)
        self.total = self.total[:half] + got.astype(wide)

    def rest(self):
        for bit in reversed(inner_bits(self.send.size)):
            self.inner(bit)


def tables(rate, size):
    row = lax.broadcasted_iota(jnp.int32, (size, 1), 0).astype(wide)
    col = lax.broadcasted_iota(jnp.int32, (1, size), 1).astype(wide)
    ahead = jnp.exp(-rate * row)
    inner = jnp.where(col <= row, ahead * jnp.exp(rate * col), 0.0)
    outof = jnp.exp(-rate * (size - row))
    return inner, ahead, outof


def attend_kernel(turn_ref, rate_ref, q_ref, k_ref, v_ref, o_ref):
    size = q_ref.shape[0] // 2
    inner, ahead, outof = tables(rate_ref[pl.program_id(0)], size)
    turn = turn_ref[0]
    early = pl.ds(pl.multiple_of(turn * size, size), size)
    late = pl.ds(pl.multiple_of((1 - turn) * size, size), size)

    def local(rows):
        weights = (nt(q_ref[rows, :], k_ref[rows, :]) * inner).astype(narrow)
        return nn(weights, v_ref[rows, :])

    weighted = (k_ref[early, :].astype(wide) * outof).astype(narrow)
    state = tn(weighted, v_ref[early, :]).astype(narrow)
    o_ref[early, :] = local(early)
    o_ref[late, :] = local(late) + nn(q_ref[late, :], state) * ahead


def per_head(kernel, turn, rates, arrays, out_types):
    heads = rates.shape[0]
    length, columns = arrays[0].shape
    spec = pl.BlockSpec((length, columns // heads), lambda h: (0, h))
    scalar = pl.BlockSpec(memory_space=pltpu.SMEM)
    return pl.pallas_call(
        kernel,
        grid=(heads,),
        in_specs=[scalar, scalar] + [spec] * len(arrays),
        out_specs=[spec] * len(out_types),
        out_shape=[jax.ShapeDtypeStruct((length, columns), t) for t in out_types],
    )(turn, rates, *arrays)


def rows_of(refs):
    half = refs[0].shape[0]
    return [(ref, slice(i * half, (i + 1) * half)) for i, ref in enumerate(refs)]


def project_kernel(own_ref, other_ref, w0, w1, w2, w3, *outs, form):
    weight = jnp.concatenate([ref[...] for ref in (w0, w1, w2, w3)], axis=0)
    for ref, rows in rows_of((own_ref, other_ref)):
        value = nn(ref[...], weight)
        if form == "silu":
            outs[0][rows, :] = value
            outs[1][rows, :] = jax.nn.silu(value).astype(narrow)
        else:
            outs[0][rows, :] = value.astype(outs[0].dtype)


def project(pair, pieces, form):
    rows = pair[0].shape[0]
    length, width = 2 * rows, pieces[0].shape[1]
    types = {"silu": (wide, narrow), "wide": (wide,), "narrow": (narrow,)}[form]
    return pl.pallas_call(
        functools.partial(project_kernel, form=form),
        out_shape=[jax.ShapeDtypeStruct((length, width), t) for t in types],
    )(*pair, *pieces)


def branch_kernel(o_ref, scale_ref, u_ref, w0, w1, w2, w3, gated_ref, own_ref, other_ref):
    rows = own_ref.shape[0]
    quarter = w0.shape[0]
    for half, out in ((slice(0, rows), own_ref), (slice(rows, 2 * rows), other_ref)):
        gated = (o_ref[half, :] * scale_ref[half, :] * u_ref[half, :]).astype(narrow)
        gated_ref[half, :] = gated
        for i, ref in enumerate((w0, w1, w2, w3)):
            out[:, i * quarter : (i + 1) * quarter] = nt(gated, ref[...]).astype(out.dtype)


def branch(attended, scale, proj_u, pieces):
    length, heads = attended.shape
    rows, width = length // 2, 4 * pieces[0].shape[0]
    return pl.pallas_call(
        branch_kernel,
        out_shape=[
            jax.ShapeDtypeStruct((length, heads), narrow),
            jax.ShapeDtypeStruct((rows, width), wide),
            jax.ShapeDtypeStruct((rows, width), narrow),
        ],
    )(attended, scale, proj_u, *pieces)


def unbranch_kernel(
    own_ref, other_ref, o_ref, scale_ref, u_ref, w0, w1, w2, w3, grad_ref, unit_ref, cross_ref
):
    weight = jnp.concatenate([ref[...] for ref in (w0, w1, w2, w3)], axis=0)
    for ref, rows in rows_of((own_ref, other_ref)):
        value = nn(ref[...], weight)
        normed = o_ref[rows, :] * scale_ref[rows, :]
        unit_ref[rows, :] = (value * normed).astype(narrow)
        value = value * u_ref[rows, :]
        grad_ref[rows, :] = value
        cross_ref[rows, :] = jnp.sum(value * normed, axis=1, keepdims=True)


def unbranch(pair, attended, scale, proj_u, pieces):
    length, heads = attended.shape
    return pl.pallas_call(
        unbranch_kernel,
        out_shape=[
            jax.ShapeDtypeStruct((length, heads), wide),
            jax.ShapeDtypeStruct((length, heads), narrow),
            jax.ShapeDtypeStruct((length, 1), wide),
        ],
    )(*pair, attended, scale, proj_u, *pieces)


def attend_back_kernel(
    turn_ref,
    rate_ref,
    scale_ref,
    cross_ref,
    q_ref,
    k_ref,
    v_ref,
    pq_ref,
    pk_ref,
    gn_ref,
    o_ref,
    dq_ref,
    dk_ref,
    dv_ref,
    g_ref,
):
    size = q_ref.shape[0] // 2
    inner, ahead, outof = tables(rate_ref[pl.program_id(0)], size)
    turn = turn_ref[0]
    early = pl.ds(pl.multiple_of(turn * size, size), size)
    late = pl.ds(pl.multiple_of((1 - turn) * size, size), size)
    scale = scale_ref[...]
    normed = o_ref[...] * scale
    g_ref[...] = (scale * (gn_ref[...] - normed * cross_ref[...])).astype(narrow)

    def local(rows):
        q, k, v, g = (ref[rows, :] for ref in (q_ref, k_ref, v_ref, g_ref))
        weights = (nt(q, k) * inner).astype(narrow)
        grad_scores = (nt(g, v) * inner).astype(narrow)
        return nn(grad_scores, k), tn(grad_scores, q), tn(weights, g)

    def store(rows, dq, dk, dv):
        dq_ref[rows, :] = (dq * silu_slope(pq_ref[rows, :])).astype(narrow)
        dk_ref[rows, :] = (dk * silu_slope(pk_ref[rows, :])).astype(narrow)
        dv_ref[rows, :] = dv.astype(narrow)

    weighted = (k_ref[early, :].astype(wide) * outof).astype(narrow)
    state = tn(weighted, v_ref[early, :]).astype(narrow)
    g_ahead = (g_ref[late, :].astype(wide) * ahead).astype(narrow)
    grad_state = tn(q_ref[late, :], g_ahead).astype(narrow)
    dq, dk, dv = local(late)
    store(late, dq + nt(g_ahead, state), dk, dv)
    dq, dk, dv = local(early)
    store(
        early,
        dq,
        dk + nt(v_ref[early, :], grad_state) * outof,
        dv + nn(weighted, grad_state),
    )


def attend_back(turn, rates, scale, cross, arrays):
    heads = rates.shape[0]
    length, columns = arrays[0].shape
    spec = pl.BlockSpec((length, columns // heads), lambda h: (0, h))
    column = pl.BlockSpec((length, 1), lambda h: (0, 0))
    scalar = pl.BlockSpec(memory_space=pltpu.SMEM)
    return pl.pallas_call(
        attend_back_kernel,
        grid=(heads,),
        in_specs=[scalar, scalar, column, column] + [spec] * len(arrays),
        out_specs=[spec] * 3,
        out_shape=[jax.ShapeDtypeStruct((length, columns), narrow)] * 3,
        scratch_shapes=[pltpu.VMEM((length, columns // heads), narrow)],
    )(turn, rates, scale, cross, *arrays)


def weight_grad_kernel(own_ref, other_ref, *refs):
    count = len(refs) // 2
    for z_ref, out in zip(refs[:count], refs[count:]):
        total = 0.0
        for ref, rows in rows_of((own_ref, other_ref)):
            total += tn(ref[...], z_ref[rows, :])
        out[0] = total.astype(narrow)


def weight_grads(pair, arrays):
    rows, width = pair[0].shape
    quarter = width // 4
    columns = arrays[0].shape[1]
    part = pl.BlockSpec((rows, quarter), lambda i: (0, i))
    whole = pl.BlockSpec((2 * rows, columns), lambda i: (0, 0))
    outs = pl.pallas_call(
        weight_grad_kernel,
        grid=(4,),
        in_specs=[part] * 2 + [whole] * len(arrays),
        out_specs=[pl.BlockSpec((1, quarter, columns), lambda i: (i, 0, 0))] * len(arrays),
        out_shape=[jax.ShapeDtypeStruct((4, quarter, columns), narrow)] * len(arrays),
    )(*pair, *arrays)
    return [[out[i] for i in range(4)] for out in outs]


def ffn_kernel(*refs, count, chained, last):
    n_refs, g_refs = refs[0:2], refs[2:4]
    refs = refs[4:]
    piece_refs = [refs[4 * i : 4 * i + 4] for i in range(count)]
    refs = refs[4 * count :]
    if chained:
        befores, refs = refs[:4], refs[4:]
    sums, refs = refs[:4], refs[4:]
    grad_refs = [refs[4 * i : 4 * i + 4] for i in range(count)]
    w_ref, s_ref, d_ref = refs[4 * count : 4 * count + 3]
    accs = refs[4 * count + 3 :]
    rows = n_refs[0].shape[0]
    quarter = w_ref.shape[0] // 4
    n = s_ref.shape[1]

    for c in range(count):
        for i, ref in enumerate(piece_refs[c]):
            w_ref[i * quarter : (i + 1) * quarter, :] = ref[...]
        for h in range(2):
            half = slice(h * rows, (h + 1) * rows)
            ab = nn(n_refs[h][...], w_ref[:, : 2 * n])
            ds = nn(g_refs[h][...], w_ref[:, 2 * n :])
            a = ab[:, :n]
            b = ab[:, n:]
            s_ref[half, :] = (a * b).astype(narrow)
            d_ref[half, :n] = (ds * b).astype(narrow)
            d_ref[half, n:] = (ds * a).astype(narrow)
            y = nt(s_ref[half, :], w_ref[:, 2 * n :])
            d = nt(d_ref[half, :], w_ref[:, : 2 * n])
            for value, k in ((y, h), (d, 2 + h)):
                if c > 0:
                    value = value + accs[k][...]
                elif chained:
                    value = value + befores[k][...]
                if c == count - 1:
                    sums[k][...] = value.astype(sums[k].dtype)
                else:
                    accs[k][...] = value
        for i in range(4):
            cols = slice(i * quarter, (i + 1) * quarter)
            out = grad_refs[c][i]
            out[:, : 2 * n] = sum(
                tn(n_refs[h][:, cols], d_ref[h * rows : (h + 1) * rows, :]) for h in range(2)
            ).astype(narrow)
            out[:, 2 * n :] = sum(
                tn(g_refs[h][:, cols], s_ref[h * rows : (h + 1) * rows, :]) for h in range(2)
            ).astype(narrow)


def ffn(normed, grad, tiles, sums, last):
    rows, width = normed[0].shape
    count = len(tiles)
    quarter, n3 = tiles[0][0].shape
    n = n3 // 3
    flat = [piece for pieces in tiles for piece in pieces]
    other = narrow if last else wide
    types = [wide, other, wide, other]
    outs = pl.pallas_call(
        functools.partial(ffn_kernel, count=count, chained=sums is not None, last=last),
        out_shape=[jax.ShapeDtypeStruct((rows, width), t) for t in types]
        + [jax.ShapeDtypeStruct((quarter, n3), narrow)] * (4 * count),
        scratch_shapes=[
            pltpu.VMEM((width, n3), narrow),
            pltpu.VMEM((2 * rows, n), narrow),
            pltpu.VMEM((2 * rows, 2 * n), narrow),
        ]
        + [pltpu.VMEM((rows, width), wide)] * (4 if count > 1 else 0),
    )(*normed, *grad, *flat, *(sums or ()))
    return outs[:4], [outs[4 + 4 * i : 8 + 4 * i] for i in range(count)]


def ffn_cuts(total):
    cuts = []
    left = total
    while left > 0:
        take = min(tile_width, left)
        cuts.append((total - left, take))
        left -= take
    return cuts


def shards(
    size,
    tokens,
    w_query,
    w_key,
    w_value,
    w_gate,
    w_out,
    w_first,
    w_second,
    w_down,
    decay_rates,
    cotangent,
):
    send = Exchange(size)
    swap = lambda value: lax.ppermute(value, "tensor", [(0, 1), (1, 0)])
    me = lax.axis_index("dp")
    turn = lax.axis_index("tensor").astype(jnp.int32).reshape(1)
    rows, width = tokens.shape
    span = width // size
    offsets = jnp.asarray(np.repeat(block_offsets(size), span))
    place = jnp.bitwise_xor(offsets, me) * span + jnp.arange(width) % span
    shuffle = (jnp.arange(width)[:, None] == place[None, :]).astype(narrow)

    cuts = ffn_cuts(w_first.shape[1])
    down_t = w_down.T
    att = [
        Gather(send, w, i % 2 == 0)
        for i, w in enumerate((w_query, w_key, w_value, w_gate, w_out.T))
    ]
    mlp = [
        Gather(
            send,
            jnp.concatenate([w[:, at : at + n] for w in (w_first, w_second, down_t)], axis=1),
            i % 2 == 0,
        )
        for i, (at, n) in enumerate(cuts)
    ]
    bits = inner_bits(size)
    for step in range(len(att) + len(bits) + 1):
        c = step - len(bits) - 1
        if 0 <= c < len(att):
            att[c].far()
        c = step - len(bits)
        if 0 <= c < len(att):
            att[c].sides()
        for level in range(len(bits) - 1, -1, -1):
            c = step - level
            if 0 <= c < len(att):
                att[c].inner(bits[level])
            elif len(att) <= c < len(att) + len(mlp):
                mlp[c - len(att)].inner(bits[level])
    step = len(att) + len(bits) + 1
    for level in range(len(bits)):
        for c in range(max(0, step - level - len(att)), len(mlp)):
            mlp[c].inner(bits[level])
    for c in range(len(mlp) + 1):
        if c < len(mlp):
            mlp[c].sides()
        if c > 0:
            mlp[c - 1].far()
    full_q, full_k, full_v, full_u, full_o = (gather.pieces for gather in att)

    inputs = nn(tokens, shuffle)
    scale_in = inverse_rms(inputs)
    normed_in = inputs * scale_in
    own_in = low(normed_in)
    pair_in = (own_in, swap(own_in))
    own_cot = low(nn(cotangent, shuffle))
    pair_cot = (own_cot, swap(own_cot))

    proj_q, query = project(pair_in, full_q, "silu")
    proj_k, keys = project(pair_in, full_k, "silu")
    values = project(pair_in, full_v, "narrow")[0]
    proj_u = project(pair_in, full_u, "wide")[0]
    attended = per_head(attend_kernel, turn, decay_rates, (query, keys, values), (wide,))[0]

    def both_sum(part):
        other = swap(part)
        return part + jnp.concatenate([other[rows:], other[:rows]], axis=0)

    total_sq = both_sum(jnp.sum(attended * attended, axis=1))
    scale_out = lax.rsqrt(total_sq / width + eps)[:, None]
    gated, branch_own, branch_other = branch(attended, scale_out, proj_u, full_o)
    middle = inputs + branch_own + swap(branch_other).astype(wide)
    scale_mid = inverse_rms(middle)
    normed_mid = middle * scale_mid
    own_mid = low(normed_mid)
    pair_mid = (own_mid, swap(own_mid))

    tiles = [gather.pieces for gather in mlp]
    sums, grads = ffn(pair_mid, pair_cot, tiles[:-1], None, False)
    outs = [Scatter(send, grad, i % 2 == 0) for i, grad in enumerate(grads)]
    for stage in (Scatter.far, Scatter.near, Scatter.sides):
        for out in outs:
            stage(out)
    (y_own, y_other, d_own, d_other), grads = ffn(pair_mid, pair_cot, tiles[-1:], sums, True)
    outs.append(Scatter(send, grads[0], len(outs) % 2 == 0))
    for stage in (Scatter.far, Scatter.near, Scatter.sides):
        stage(outs[-1])
    for out in outs:
        out.rest()

    grad_mid_norm = d_own + swap(d_other).astype(wide)
    grad_middle = own_cot.astype(wide) + norm_back(grad_mid_norm, normed_mid, scale_mid)
    own_e = low(grad_middle)
    pair_e = (own_e, swap(own_e))
    grad_normed, grad_unit, cross = unbranch(pair_e, attended, scale_out, proj_u, full_o)
    cross = both_sum(cross[:, 0]) / width
    late = [
        Scatter(send, weight_grads(pair_e, (gated,))[0], True),
        Scatter(send, weight_grads(pair_in, (grad_unit,))[0], False),
    ]
    for stage in (Scatter.far, Scatter.near, Scatter.sides):
        for out in late:
            stage(out)
    grad_q, grad_k, grad_v = attend_back(
        turn,
        decay_rates,
        scale_out,
        cross[:, None],
        (query, keys, values, proj_q, proj_k, grad_normed, attended),
    )
    last = [
        Scatter(send, grad, i % 2 == 0)
        for i, grad in enumerate(weight_grads(pair_in, (grad_q, grad_k, grad_v)))
    ]
    for stage in (Scatter.far, Scatter.near, Scatter.sides):
        for out in last:
            stage(out)
    for out in late + last:
        out.rest()

    join = lambda pieces: jnp.concatenate(pieces, axis=0)
    total = nt(grad_q, join(full_q)) + nt(grad_k, join(full_k))
    total = total + (nt(grad_v, join(full_v)) + nt(grad_unit, join(full_u)))
    grad_in_norm = total[:rows] + swap(low(total[rows:])).astype(wide)
    tokens_grad = grad_middle + norm_back(grad_in_norm, normed_in, scale_in)
    layer_out = low(middle + y_own + swap(y_other).astype(wide))
    layer_out = low(nt(layer_out, shuffle))
    parts = []
    rest = tokens_grad
    for _ in range(3):
        part = lax.reduce_precision(rest, 8, 7)
        parts.append(low(part))
        rest = rest - part
    tokens_grad = nt(parts[0], shuffle) + (nt(parts[1], shuffle) + nt(parts[2], shuffle))
    thirds = [
        jnp.concatenate(
            [out.total[:, i * n : (i + 1) * n] for out, (_, n) in zip(outs, cuts)], axis=1
        )
        for i in range(3)
    ]
    return (
        layer_out,
        tokens_grad,
        last[0].total,
        last[1].total,
        last[2].total,
        late[1].total,
        late[0].total.T,
        thirds[0],
        thirds[1],
        thirds[2].T,
    )


def solution(mesh):
    return jax.shard_map(
        functools.partial(shards, mesh.shape["dp"]),
        mesh=mesh,
        in_specs=(
            P(("dp", "tensor"), None),
            P("dp", "tensor"),
            P("dp", "tensor"),
            P("dp", "tensor"),
            P("dp", "tensor"),
            P("tensor", "dp"),
            P("dp", "tensor"),
            P("dp", "tensor"),
            P("tensor", "dp"),
            P("tensor"),
            P(("dp", "tensor"), None),
        ),
        out_specs=(
            P(("dp", "tensor"), None),
            P(("dp", "tensor"), None),
            P("dp", "tensor"),
            P("dp", "tensor"),
            P("dp", "tensor"),
            P("dp", "tensor"),
            P("tensor", "dp"),
            P("dp", "tensor"),
            P("dp", "tensor"),
            P("tensor", "dp"),
        ),
        check_vma=False,
    )
```

time: 525 us -> 443 us (0.84)
  waiting for transfers between devices: 193 us -> 135 us
  matrix products: 56.5 us -> 25.1 us
  Pallas kernels: 82.7 us -> 105 us
  local copies, waits for them, and re-layouts: 52.2 us -> 34.5 us
  starting transfers between devices: 87.2 us -> 95.8 us
    ppermute x80, waiting for transfers between devices: 193 us -> 135 us  [__call__(): result = lax.ppermute(array, 'dp', pairs)]
    pallas_call x3 -> x12, Pallas kernels: 66.1 us -> 98.9 us  [the longest x2 39.9 us: ffn(): pl.pallas_call(functools.partial(ffn_kernel, count=count, chained=sums is...]
    dot_general x21 -> x10, matrix products: 56.5 us -> 25.1 us  [dot(): lax.dot_general(left, right, (dims, ((), ())), preferred_element_type=wide)]
    slice x31 -> x20, local copies, waits for them, and re-layouts: 16.3 us -> 2.95 us  [the longest x1 1.8 us: shards(): grad_in_norm = total[:rows] + swap(low(total[rows:])).astype(wide)]
    pallas_call x2 -> x0, local copies, waits for them, and re-layouts: 10.7 us -> none  [ffn_chunk(): pl.pallas_call(functools.partial(ffn_kernel, chained=chained), grid=(tile...]
    pallas_call x2 -> x1, Pallas kernels: 16.7 us -> 6.14 us  [per_head(): pl.pallas_call(kernel, grid=(heads,), in_specs=[scalar, scalar] + [spec]...]
    ppermute x80, starting transfers between devices: 86.1 us -> 94.5 us  [__call__(): result = lax.ppermute(array, 'dp', pairs)]
    unnamed x138 -> x240, local copies, waits for them, and re-layouts: 14.8 us -> 22.8 us
  transfers between devices with their start and end apart: 90 -> 90, of which waited for: 42 -> 37; matrix products, arithmetic and copies ran while one was open for 27% -> 20% of each run, Pallas kernels for 16% -> 24%
where the time goes in v2:
time: 443 us; the launch traced here: 436 us
  waiting for transfers between devices  135 us (30%)
  Pallas kernels  105 us (24%)
  starting transfers between devices  95.8 us (22%)
  other arithmetic  38.2 us (9%)
  local copies, waits for them, and re-layouts  34.5 us (8%)
  matrix products  25.1 us (6%)
    ppermute x80, waiting for transfers between devices, __call__(): result = lax.ppermute(array, 'dp', pairs)  135 us
    ppermute x80, starting transfers between devices, __call__(): result = lax.ppermute(array, 'dp', pairs)  94.5 us
    pallas_call x2, Pallas kernels, ffn(): pl.pallas_call(functools.partial(ffn_kernel, count=count, chained=sums is...  39.9 us
    dot_general x10, matrix products, dot(): lax.dot_general(left, right, (dims, ((), ())), preferred_element_type=wide)  25.1 us
    unnamed x240, local copies, waits for them, and re-layouts  22.8 us
    pallas_call x4, Pallas kernels, project(): pl.pallas_call(functools.partial(project_kernel, form=form), out_shape=[j...  18.1 us
    pallas_call x3, Pallas kernels, weight_grads(): pl.pallas_call(weight_grad_kernel, grid=(4,), in_specs=[part] * 2 + [whol...  17.1 us
    pallas_call x1, Pallas kernels, attend_back(): pl.pallas_call(attend_back_kernel, grid=(heads,), in_specs=[scalar, scala...  12.3 us
  transfers between devices with their start and end apart: 90, of which 37 were waited for; matrix products, arithmetic and copies ran while one was open for 20% of the time, Pallas kernels for 24%

profile of v2, /device:TPU:0, one launch (start us, length us, event | category | flops | bytes accessed | tf_op | source)
XLA Modules:
  0.0 436.3 jit_solution(13516415161793953011)
XLA Ops:
  0.7 4.1 collective-permute-start.1
  15.5 2.8 collective-permute-done.6
  25.4 3.0 collective-permute-done.7
  28.5 2.1 collective-permute-start.15
  38.6 5.3 %collective-permute-done.9.w2 = bf16[256,512]{1,0:T(8,128)(2,1)S(1)} collective-permute-done((bf16[256,512]{1,0:T(8,128)(2,1)S(1)}, bf16[256,512]{1,0:T(8,128)(2,1)S(1)}, u32[]{:S(2)}, u32[]{:S(2)}) %collective-permute-start.9) | collective-permute-done | bytes 262176 | tf_op jit(solution)/shard_map/ppermute | solution.py:61
  60.3 4.8 %shard_map.196 = (f32[1024,512]{1,0:T(8,128)}, bf16[1024,512]{1,0:T(8,128)(2,1)}) custom-call(bf16[512,1024]{1,0:T(8,128)(2,1)} %copy-done.2, bf16[512,1024]{1,0:T(8,128)(2,1)} %copy-done.3, bf16[256,512]{1,0:T(8,128)(2,1)} %copy-done.88, bf16[256,512]{1,0:T(8,128)(2,1)} %copy-done.40, bf16[256,512]{1,0:T(8,128)(2,1)} %copy-done.46, bf16[256,512]{1,0:T(8,128)(2,1)} %copy-done.48), custom_call_target="tpu_custom_call" | custom-call | tf_op jit(solution)/shard_map/pallas_call | solution.py:201
  65.1 4.8 %shard_map.195 = (f32[1024,512]{1,0:T(8,128)}, bf16[1024,512]{1,0:T(8,128)(2,1)}) custom-call(bf16[512,1024]{1,0:T(8,128)(2,1)} %copy-done.2, bf16[512,1024]{1,0:T(8,128)(2,1)} %copy-done.3, bf16[256,512]{1,0:T(8,128)(2,1)} %copy-done.89, bf16[256,512]{1,0:T(8,128)(2,1)} %copy-done.38, bf16[256,512]{1,0:T(8,128)(2,1)} %copy-done.36, bf16[256,512]{1,0:T(8,128)(2,1)} %copy-done.44), custom_call_target="tpu_custom_call" | custom-call | tf_op jit(solution)/shard_map/pallas_call | solution.py:201
  72.2 4.1 shard_map.197.v_ref
  76.3 6.1 %shard_map.198.o_ref = f32[1024,512]{1,0:T(8,128)} custom-call(s32[1]{0:T(128)} %bitcast.1.turn_ref, f32[4]{0:T(128)} %rate_ref.3, bf16[1024,512]{1,0:T(8,128)(2,1)} %get-tuple-element.123.q_ref, bf16[1024,512]{1,0:T(8,128)(2,1)} %get-tuple-element.130.k_ref, bf16[1024,512]{1,0:T(8,128)(2,1)} %shard_map.197.v_ref), custom_call_target="tpu_custom_call" | custom-call | tf_op jit(solution)/shard_map/pallas_call | solution.py:172
  90.5 4.1 collective-permute-done.24.w1
  97.4 2.4 collective-permute-done.22.w3
  100.5 4.4 %shard_map.199.u_ref = f32[1024,512]{1,0:T(8,128)} custom-call(bf16[512,1024]{1,0:T(8,128)(2,1)} %copy-done.2, bf16[512,1024]{1,0:T(8,128)(2,1)} %copy-done.3, bf16[256,512]{1,0:T(8,128)(2,1)} %get-tuple-element.138.w0, bf16[256,512]{1,0:T(8,128)(2,1)} %collective-permute-done.19.w1, bf16[256,512]{1,0:T(8,128)(2,1)} %copy-done.52, bf16[256,512]{1,0:T(8,128)(2,1)} %copy-done.54), custom_call_target="tpu_custom_call" | custom-call | tf_op jit(solution)/shard_map/pallas_call | solution.py:201
  110.3 5.2 %shard_map.200 = (bf16[1024,512]{1,0:T(8,128)(2,1)}, f32[512,1024]{1,0:T(8,128)}, bf16[512,1024]{1,0:T(8,128)(2,1)}) custom-call(f32[1024,512]{1,0:T(8,128)} %shard_map.198.o_ref, f32[1024,1]{1,0:T(8,128)} %rsqrt.27.scale_ref, f32[1024,512]{1,0:T(8,128)} %shard_map.199.u_ref, bf16[256,512]{1,0:T(8,128)(2,1)} %copy-done.26, bf16[256,512]{1,0:T(8,128)(2,1)} %copy-done.30, ...), custom_call_target="tpu_custom_call" | custom-call | tf_op jit(solution)/shard_map/pallas_call | solution.py:220
  117.3 2.7 fusion.19.refs_2_
  122.0 3.6 collective-permute-done.35
  131.3 14.7 %collective-permute-done.38.refs_10_ = bf16[256,1536]{1,0:T(8,128)(2,1)S(1)} collective-permute-done((bf16[256,1536]{1,0:T(8,128)(2,1)S(1)}, bf16[256,1536]{1,0:T(8,128)(2,1)S(1)}, u32[]{:S(2)}, u32[]{:S(2)}) %collective-permute-start.38) | collective-permute-done | bytes 786464 | tf_op jit(solution)/shard_map/ppermute | solution.py:61
  149.3 11.4 %collective-permute-done.37.refs_5_ = bf16[256,1152]{1,0:T(8,128)(2,1)} collective-permute-done((bf16[256,1152]{1,0:T(8,128)(2,1)}, bf16[256,1152]{1,0:T(8,128)(2,1)}, u32[]{:S(2)}, u32[]{:S(2)}) %collective-permute-start.37) | collective-permute-done | bytes 589856 | tf_op jit(solution)/shard_map/ppermute | solution.py:61
  165.4 10.5 %collective-permute-done.44.refs_11_ = bf16[256,1536]{1,0:T(8,128)(2,1)S(1)} collective-permute-done((bf16[256,1536]{1,0:T(8,128)(2,1)S(1)}, bf16[256,1536]{1,0:T(8,128)(2,1)S(1)}, u32[]{:S(2)}, u32[]{:S(2)}) %collective-permute-start.44) | collective-permute-done | bytes 786464 | tf_op jit(solution)/shard_map/ppermute | solution.py:61
  176.8 24.9 %shard_map.201 = (f32[512,1024]{1,0:T(8,128)}, f32[512,1024]{1,0:T(8,128)}, f32[512,1024]{1,0:T(8,128)}, f32[512,1024]{1,0:T(8,128)}, bf16[256,1536]{1,0:T(8,128...) custom-call(bf16[512,1024]{1,0:T(8,128)(2,1)} %copy-done.11, ...), custom_call_target="tpu_custom_call" | custom-call | tf_op jit(solution)/shard_map/pallas_call | solution.py:405
  211.1 15.0 %shard_map.202 = (f32[512,1024]{1,0:T(8,128)}, bf16[512,1024]{1,0:T(8,128)(2,1)}, f32[512,1024]{1,0:T(8,128)}, bf16[512,1024]{1,0:T(8,128)(2,1)}, bf16[256,1152]...) custom-call(bf16[512,1024]{1,0:T(8,128)(2,1)} %copy-done.11, ...), custom_call_target="tpu_custom_call" | custom-call | tf_op jit(solution)/shard_map/pallas_call | solution.py:405
  226.6 10.5 %collective-permute-done.52 = bf16[256,1536]{1,0:T(8,128)(2,1)} collective-permute-done((bf16[256,1536]{1,0:T(8,128)(2,1)}, bf16[256,1536]{1,0:T(8,128)(2,1)}, u32[]{:S(2)}, u32[]{:S(2)}) %collective-permute-start.52) | collective-permute-done | bytes 786464 | tf_op jit(solution)/shard_map/ppermute | solution.py:61
  244.9 2.1 fusion.38
  247.0 2.4 fusion.18
  249.4 4.2 collective-permute-done.58
  255.9 5.8 %collective-permute-done.55 = bf16[256,1536]{1,0:T(8,128)(2,1)S(1)} collective-permute-done((bf16[256,1536]{1,0:T(8,128)(2,1)S(1)}, bf16[256,1536]{1,0:T(8,128)(2,1)S(1)}, u32[]{:S(2)}, u32[]{:S(2)}) %collective-permute-start.55) | collective-permute-done | bytes 786464 | tf_op jit(solution)/shard_map/ppermute | solution.py:61
  263.2 4.2 collective-permute-done.53
  272.1 4.0 collective-permute-done.56
  281.1 6.4 %shard_map.203 = (f32[1024,512]{1,0:T(8,128)}, bf16[1024,512]{1,0:T(8,128)(2,1)}, f32[1024,1]{1,0:T(8,128)}) custom-call(bf16[512,1024]{1,0:T(8,128)(2,1)} %copy-done.12, bf16[512,1024]{1,0:T(8,128)(2,1)} %copy-done.19, f32[1024,512]{1,0:T(8,128)} %shard_map.198.o_ref, f32[1024,1]{1,0:T(8,128)} %rsqrt.27.scale_ref, f32[1024,512]{1,0:T(8,128)} %shard_map.199.u_ref, ...), custom_call_target="tpu_custom_call" | custom-call | tf_op jit(solution)/shard_map/pallas_call | solution.py:245
  288.9 5.0 %shard_map.207 = bf16[4,256,512]{2,1,0:T(8,128)(2,1)} custom-call(bf16[512,1024]{1,0:T(8,128)(2,1)} %copy-done.12, bf16[512,1024]{1,0:T(8,128)(2,1)} %copy-done.19, bf16[1024,512]{1,0:T(8,128)(2,1)} %get-tuple-element.202.refs_0_), custom_call_target="tpu_custom_call" | custom-call | tf_op jit(solution)/shard_map/pallas_call | solution.py:338
  295.8 4.5 %fusion.50 = f32[1024,1024]{1,0:T(8,128)} fusion(bf16[1024,512]{1,0:T(8,128)(2,1)S(1)} %copy-done.66, bf16[1024,512]{1,0:T(8,128)(2,1)} %copy-done.108), kind=kOutput, calls=%fused_computation.194 | convolution fusion | flops 1073741824 | bytes 6291456 | tf_op jit(solution)/shard_map/dot_general | solution.py:20
  300.3 4.9 %shard_map.206 = bf16[4,256,512]{2,1,0:T(8,128)(2,1)} custom-call(bf16[512,1024]{1,0:T(8,128)(2,1)} %copy-done.2, bf16[512,1024]{1,0:T(8,128)(2,1)} %copy-done.3, bf16[1024,512]{1,0:T(8,128)(2,1)} %get-tuple-element.177.refs_0_), custom_call_target="tpu_custom_call" | custom-call | tf_op jit(solution)/shard_map/pallas_call | solution.py:338
  309.1 12.3 %shard_map.204 = (bf16[1024,512]{1,0:T(8,128)(2,1)}, bf16[1024,512]{1,0:T(8,128)(2,1)}, bf16[1024,512]{1,0:T(8,128)(2,1)}) custom-call(s32[1]{0:T(128)} %bitcast.1.turn_ref, f32[4]{0:T(128)} %rate_ref.3, f32[1024,1]{1,0:T(8,128)} %rsqrt.27.scale_ref, f32[1024,1]{1,0:T(8,128)} %add_multiply_fusion.cross_ref, bf16[1024,512]{1,0:T(8,128)(2,1)} %get-tuple-element.123.q_ref, ...), custom_call_target="tpu_custom_call" | custom-call | tf_op jit(solution)/shard_map/pallas_call | solution.py:313
  321.5 2.6 fusion.49
  326.6 4.6 %add_add_fusion = f32[1024,1024]{1,0:T(8,128)} fusion(f32[1024,1024]{1,0:T(8,128)S(1)} %copy-done.22, f32[1024,1024]{1,0:T(8,128)S(1)} %fusion.48, f32[1024,1024]{1,0:T(8,128)S(1)} %fusion.49, bf16[1024,512]{1,0:T(8,128)(2,1)S(1)} %copy-done.18, bf16[1024,512]{1,0:T(8,128)(2,1)} %constant_dynamic-update-slice_fusion.24), kind=kOutput, calls=%fused_computation | convolution fusion | flops 1076887552 | bytes 18874368 | tf_op jit(solution)/shard_map/dot_general | solution.py:20
  331.3 7.2 %shard_map.205 = (bf16[4,256,512]{2,1,0:T(8,128)(2,1)}, bf16[4,256,512]{2,1,0:T(8,128)(2,1)}, bf16[4,256,512]{2,1,0:T(8,128)(2,1)}) custom-call(bf16[512,1024]{1,0:T(8,128)(2,1)} %copy-done.2, bf16[512,1024]{1,0:T(8,128)(2,1)} %copy-done.3, bf16[1024,512]{1,0:T(8,128)(2,1)} %get-tuple-element.174.refs_0_, bf16[1024,512]{1,0:T(8,128)(2,1)} %get-tuple-element.175.refs_1_, ...), custom_call_target="tpu_custom_call" | custom-call | tf_op jit(solution)/shard_map/pallas_call | solution.py:338
  352.3 6.8 %collective-permute-done.60 = bf16[64,1536]{1,0:T(8,128)(2,1)S(1)} collective-permute-done((bf16[64,1536]{1,0:T(8,128)(2,1)S(1)}, bf16[64,1536]{1,0:T(8,128)(2,1)S(1)}, u32[]{:S(2)}, u32[]{:S(2)}) %collective-permute-start.60) | collective-permute-done | bytes 196640 | tf_op jit(solution)/shard_map/ppermute | solution.py:61
  364.1 6.0 %collective-permute-done.73 = bf16[64,1152]{1,0:T(8,128)(2,1)S(1)} collective-permute-done((bf16[64,1152]{1,0:T(8,128)(2,1)S(1)}, bf16[64,1152]{1,0:T(8,128)(2,1)S(1)}, u32[]{:S(2)}, u32[]{:S(2)}) %collective-permute-start.73) | collective-permute-done | bytes 147488 | tf_op jit(solution)/shard_map/ppermute | solution.py:61
  376.9 2.6 collective-permute-done.74
  390.1 2.7 add_add_fusion.1
  392.9 2.2 collective-permute-start.83
  398.9 2.8 collective-permute-done.76
  402.4 5.5 %collective-permute-done.79 = bf16[128,512]{1,0:T(8,128)(2,1)S(1)} collective-permute-done((bf16[128,512]{1,0:T(8,128)(2,1)S(1)}, bf16[128,512]{1,0:T(8,128)(2,1)S(1)}, u32[]{:S(2)}, u32[]{:S(2)}) %collective-permute-start.79) | collective-permute-done | bytes 131104 | tf_op jit(solution)/shard_map/ppermute | solution.py:61
  408.0 3.4 collective-permute-start.84
  411.4 3.0 collective-permute-done.80
  414.4 2.2 collective-permute-start.85
  424.2 2.2 collective-permute-start.87
  427.7 2.4 collective-permute-done.87
  432.3 3.1 collective-permute-done.89
  (501 shorter events, 172.1 us)
Async XLA Ops:
  7.2 51.6 %collective-permute-start = (bf16[512,1024]{1,0:T(8,128)(2,1)S(1)}, bf16[512,1024]{1,0:T(8,128)(2,1)S(1)}, u32[]{:S(2)}, u32[]{:S(2)}) collective-permute-start(bf16[512,1024]{1,0:T(8,128)(2,1)S(1)} %fusion.16.own_ref), channel_id=1, source_target_pairs={{0,1},{1,0},{2,3},{3,2},{4,5},{5,4},{6,7},{7,6},{8,9},{9,8},{10,11... | collective-permute-start | bytes 3145736 | tf_op jit(solution)/shard_map/ppermute | solution.py:444
  31.2 13.1 %collective-permute-start.8 = (bf16[256,512]{1,0:T(8,128)(2,1)S(1)}, bf16[256,512]{1,0:T(8,128)(2,1)S(1)}, u32[]{:S(2)}, u32[]{:S(2)}) collective-permute-start(bf16[256,512]{1,0:T(8,128)(2,1)S(1)} %get-tuple-element.127.w0), channel_id=1, source_target_pairs={{0,2},{2,0},{4,6},{6,4},{8,10},{10,8},{12,14},{14,12},{16,18},{18,... | collective-permute-start | bytes 786440 | tf_op jit(solution)/shard_map/ppermute | solution.py:61
  50.0 19.8 %collective-permute-start.26 = (bf16[64,1536]{1,0:T(8,128)(2,1)}, bf16[64,1536]{1,0:T(8,128)(2,1)}, u32[]{:S(2)}, u32[]{:S(2)}) collective-permute-start(bf16[64,1536]{1,0:T(8,128)(2,1)} %pad_maximum_fusion.9), channel_id=1, source_target_pairs={{0,16},{2,18},{4,20},{6,22},{8,24},{10,26},{12,28},{14,30},{16,0},... | collective-permute-start | bytes 589832 | tf_op jit(solution)/shard_map/ppermute | solution.py:61
  52.5 19.7 %collective-permute-start.16 = (bf16[256,512]{1,0:T(8,128)(2,1)S(1)}, bf16[256,512]{1,0:T(8,128)(2,1)}, u32[]{:S(2)}, u32[]{:S(2)}) collective-permute-start(bf16[256,512]{1,0:T(8,128)(2,1)S(1)} %collective-permute-done.13.w1), channel_id=1, source_target_pairs={{0,4},{2,6},{4,0},{6,2},{8,12},{10,14},{12,8},{14,10},{16,20},{18,... | collective-permute-start | bytes 786440 | tf_op jit(solution)/shard_map/ppermute | solution.py:61
  56.7 14.1 %collective-permute-start.23 = (bf16[128,512]{1,0:T(8,128)(2,1)}, bf16[128,512]{1,0:T(8,128)(2,1)}, u32[]{:S(2)}, u32[]{:S(2)}) collective-permute-start(bf16[128,512]{1,0:T(8,128)(2,1)} %pad_maximum_fusion.16), channel_id=1, source_target_pairs={{0,8},{2,10},{4,12},{6,14},{8,0},{10,2},{12,4},{14,6},{16,24},{18,... | collective-permute-start | bytes 393224 | tf_op jit(solution)/shard_map/ppermute | solution.py:61
  58.2 27.2 %collective-permute-start.19 = (bf16[256,512]{1,0:T(8,128)(2,1)}, bf16[256,512]{1,0:T(8,128)(2,1)}, u32[]{:S(2)}, u32[]{:S(2)}) collective-permute-start(bf16[256,512]{1,0:T(8,128)(2,1)} %get-tuple-element.138.w0), channel_id=1, source_target_pairs={{0,2},{2,0},{4,6},{6,4},{8,10},{10,8},{12,14},{14,12},{16,18},{18,... | collective-permute-start | bytes 786440 | tf_op jit(solution)/shard_map/ppermute | solution.py:61
  58.9 28.2 %collective-permute-start.20 = (bf16[256,512]{1,0:T(8,128)(2,1)}, bf16[256,512]{1,0:T(8,128)(2,1)S(1)}, u32[]{:S(2)}, u32[]{:S(2)}) collective-permute-start(bf16[256,512]{1,0:T(8,128)(2,1)} %get-tuple-element.138.w0), channel_id=1, source_target_pairs={{0,4},{2,6},{4,0},{6,2},{8,12},{10,14},{12,8},{14,10},{16,20},{18,... | collective-permute-start | bytes 786440 | tf_op jit(solution)/shard_map/ppermute | solution.py:61
  70.8 24.8 %collective-permute-start.31 = (bf16[64,1536]{1,0:T(8,128)(2,1)}, bf16[64,1536]{1,0:T(8,128)(2,1)S(1)}, u32[]{:S(2)}, u32[]{:S(2)}) collective-permute-start(bf16[64,1536]{1,0:T(8,128)(2,1)} %pad_maximum_fusion.10), channel_id=1, source_target_pairs={{0,16},{2,18},{4,20},{6,22},{8,24},{10,26},{12,28},{14,30},{16,0},... | collective-permute-start | bytes 589832 | tf_op jit(solution)/shard_map/ppermute | solution.py:61
  86.1 21.7 %collective-permute-start.25 = (bf16[256,512]{1,0:T(8,128)(2,1)S(1)}, bf16[256,512]{1,0:T(8,128)(2,1)S(1)}, u32[]{:S(2)}, u32[]{:S(2)}) collective-permute-start(bf16[256,512]{1,0:T(8,128)(2,1)S(1)} %pad_maximum_fusion.8.w0), channel_id=1, source_target_pairs={{0,4},{2,6},{4,0},{6,2},{8,12},{10,14},{12,8},{14,10},{16,20},{18,... | collective-permute-start | bytes 786440 | tf_op jit(solution)/shard_map/ppermute | solution.py:61
  88.5 16.4 %collective-permute-start.33 = (bf16[128,1536]{1,0:T(8,128)(2,1)S(1)}, bf16[128,1536]{1,0:T(8,128)(2,1)}, u32[]{:S(2)}, u32[]{:S(2)}) collective-permute-start(bf16[128,1536]{1,0:T(8,128)(2,1)S(1)} %pad_maximum_fusion.4), channel_id=1, source_target_pairs={{0,8},{2,10},{4,12},{6,14},{8,0},{10,2},{12,4},{14,6},{16,24},{18,... | collective-permute-start | bytes 1179656 | tf_op jit(solution)/shard_map/ppermute | solution.py:61
  94.6 14.9 %collective-permute-start.27 = (bf16[256,512]{1,0:T(8,128)(2,1)S(1)}, bf16[256,512]{1,0:T(8,128)(2,1)S(1)}, u32[]{:S(2)}, u32[]{:S(2)}) collective-permute-start(bf16[256,512]{1,0:T(8,128)(2,1)S(1)} %collective-permute-done.24.w1), channel_id=1, source_target_pairs={{0,4},{2,6},{4,0},{6,2},{8,12},{10,14},{12,8},{14,10},{16,20},{18,... | collective-permute-start | bytes 786440 | tf_op jit(solution)/shard_map/ppermute | solution.py:61
  95.7 19.7 %collective-permute-start.32 = (bf16[64,1152]{1,0:T(8,128)(2,1)S(1)}, bf16[64,1152]{1,0:T(8,128)(2,1)S(1)}, u32[]{:S(2)}, u32[]{:S(2)}) collective-permute-start(bf16[64,1152]{1,0:T(8,128)(2,1)S(1)} %copy-done.102), channel_id=1, source_target_pairs={{0,16},{2,18},{4,20},{6,22},{8,24},{10,26},{12,28},{14,30},{16,0},... | collective-permute-start | bytes 442376 | tf_op jit(solution)/shard_map/ppermute | solution.py:61
  107.9 19.7 %collective-permute-start.36 = (bf16[256,1536]{1,0:T(8,128)(2,1)}, bf16[256,1536]{1,0:T(8,128)(2,1)}, u32[]{:S(2)}, u32[]{:S(2)}) collective-permute-start(bf16[256,1536]{1,0:T(8,128)(2,1)} %pad_maximum_fusion.refs_4_), channel_id=1, source_target_pairs={{0,2},{2,0},{4,6},{6,4},{8,10},{10,8},{12,14},{14,12},{16,18},{18,... | collective-permute-start | bytes 2359304 | tf_op jit(solution)/shard_map/ppermute | solution.py:61
  108.6 20.3 %collective-permute-start.41 = (bf16[256,1536]{1,0:T(8,128)(2,1)}, bf16[256,1536]{1,0:T(8,128)(2,1)}, u32[]{:S(2)}, u32[]{:S(2)}) collective-permute-start(bf16[256,1536]{1,0:T(8,128)(2,1)} %pad_maximum_fusion.refs_4_), channel_id=1, source_target_pairs={{0,4},{2,6},{4,0},{6,2},{8,12},{10,14},{12,8},{14,10},{16,20},{18,... | collective-permute-start | bytes 2359304 | tf_op jit(solution)/shard_map/ppermute | solution.py:61
  115.5 14.1 %collective-permute-start.28 = (bf16[512,1024]{1,0:T(8,128)(2,1)}, bf16[512,1024]{1,0:T(8,128)(2,1)S(1)}, u32[]{:S(2)}, u32[]{:S(2)}) collective-permute-start(bf16[512,1024]{1,0:T(8,128)(2,1)} %get-tuple-element.147), channel_id=1, source_target_pairs={{0,1},{1,0},{2,3},{3,2},{4,5},{5,4},{6,7},{7,6},{8,9},{9,8},{10,11... | collective-permute-start | bytes 3145736 | tf_op jit(solution)/shard_map/ppermute | solution.py:444
  120.1 45.3 %collective-permute-start.30 = (bf16[512,1024]{1,0:T(8,128)(2,1)S(1)}, bf16[512,1024]{1,0:T(8,128)(2,1)S(1)}, u32[]{:S(2)}, u32[]{:S(2)}) collective-permute-start(bf16[512,1024]{1,0:T(8,128)(2,1)S(1)} %fusion.19.refs_2_), channel_id=1, source_target_pairs={{0,1},{1,0},{2,3},{3,2},{4,5},{5,4},{6,7},{7,6},{8,9},{9,8},{10,11... | collective-permute-start | bytes 3145736 | tf_op jit(solution)/shard_map/ppermute | solution.py:444
  125.6 20.4 %collective-permute-start.38 = (bf16[256,1536]{1,0:T(8,128)(2,1)S(1)}, bf16[256,1536]{1,0:T(8,128)(2,1)S(1)}, u32[]{:S(2)}, u32[]{:S(2)}) collective-permute-start(bf16[256,1536]{1,0:T(8,128)(2,1)S(1)} %pad_maximum_fusion.1.refs_8_), channel_id=1, source_target_pairs={{0,4},{2,6},{4,0},{6,2},{8,12},{10,14},{12,8},{14,10},{16,20},{18,... | collective-permute-start | bytes 2359304 | tf_op jit(solution)/shard_map/ppermute | solution.py:61
  127.5 20.4 %collective-permute-start.40 = (bf16[256,1536]{1,0:T(8,128)(2,1)S(1)}, bf16[256,1536]{1,0:T(8,128)(2,1)S(1)}, u32[]{:S(2)}, u32[]{:S(2)}) collective-permute-start(bf16[256,1536]{1,0:T(8,128)(2,1)S(1)} %pad_maximum_fusion.1.refs_8_), channel_id=1, source_target_pairs={{0,2},{2,0},{4,6},{6,4},{8,10},{10,8},{12,14},{14,12},{16,18},{18,... | collective-permute-start | bytes 2359304 | tf_op jit(solution)/shard_map/ppermute | solution.py:61
  128.9 31.8 %collective-permute-start.37 = (bf16[256,1152]{1,0:T(8,128)(2,1)}, bf16[256,1152]{1,0:T(8,128)(2,1)}, u32[]{:S(2)}, u32[]{:S(2)}) collective-permute-start(bf16[256,1152]{1,0:T(8,128)(2,1)} %pad_maximum_fusion.2.refs_4_), channel_id=1, source_target_pairs={{0,2},{2,0},{4,6},{6,4},{8,10},{10,8},{12,14},{14,12},{16,18},{18,... | collective-permute-start | bytes 1769480 | tf_op jit(solution)/shard_map/ppermute | solution.py:61
  129.5 33.1 %collective-permute-start.42 = (bf16[256,1536]{1,0:T(8,128)(2,1)}, bf16[256,1536]{1,0:T(8,128)(2,1)S(1)}, u32[]{:S(2)}, u32[]{:S(2)}) collective-permute-start(bf16[256,1536]{1,0:T(8,128)(2,1)} %collective-permute-done.36.refs_5_), channel_id=1, source_target_pairs={{0,4},{2,6},{4,0},{6,2},{8,12},{10,14},{12,8},{14,10},{16,20},{18,... | collective-permute-start | bytes 2359304 | tf_op jit(solution)/shard_map/ppermute | solution.py:61
  146.0 30.9 %collective-permute-start.29 = (bf16[512,1024]{1,0:T(8,128)(2,1)S(1)}, bf16[512,1024]{1,0:T(8,128)(2,1)}, u32[]{:S(2)}, u32[]{:S(2)}) collective-permute-start(bf16[512,1024]{1,0:T(8,128)(2,1)S(1)} %multiply_convert_fusion.refs_0_), channel_id=1, source_target_pairs={{0,1},{1,0},{2,3},{3,2},{4,5},{5,4},{6,7},{7,6},{8,9},{9,8},{10,11... | collective-permute-start | bytes 3145736 | tf_op jit(solution)/shard_map/ppermute | solution.py:444
  147.9 28.0 %collective-permute-start.44 = (bf16[256,1536]{1,0:T(8,128)(2,1)S(1)}, bf16[256,1536]{1,0:T(8,128)(2,1)S(1)}, u32[]{:S(2)}, u32[]{:S(2)}) collective-permute-start(bf16[256,1536]{1,0:T(8,128)(2,1)S(1)} %collective-permute-done.38.refs_10_), channel_id=1, source_target_pairs={{0,2},{2,0},{4,6},{6,4},{8,10},{10,8},{12,14},{14,12},{16,18},{18,... | collective-permute-start | bytes 2359304 | tf_op jit(solution)/shard_map/ppermute | solution.py:61
  160.7 41.1 %collective-permute-start.39 = (bf16[256,1152]{1,0:T(8,128)(2,1)}, bf16[256,1152]{1,0:T(8,128)(2,1)}, u32[]{:S(2)}, u32[]{:S(2)}) collective-permute-start(bf16[256,1152]{1,0:T(8,128)(2,1)} %pad_maximum_fusion.2.refs_4_), channel_id=1, source_target_pairs={{0,4},{2,6},{4,0},{6,2},{8,12},{10,14},{12,8},{14,10},{16,20},{18,... | collective-permute-start | bytes 1769480 | tf_op jit(solution)/shard_map/ppermute | solution.py:61
  162.6 39.1 %collective-permute-start.43 = (bf16[256,1152]{1,0:T(8,128)(2,1)}, bf16[256,1152]{1,0:T(8,128)(2,1)}, u32[]{:S(2)}, u32[]{:S(2)}) collective-permute-start(bf16[256,1152]{1,0:T(8,128)(2,1)} %collective-permute-done.37.refs_5_), channel_id=1, source_target_pairs={{0,4},{2,6},{4,0},{6,2},{8,12},{10,14},{12,8},{14,10},{16,20},{18,... | collective-permute-start | bytes 1769480 | tf_op jit(solution)/shard_map/ppermute | solution.py:61
  201.7 24.3 %collective-permute-start.54 = (bf16[256,1536]{1,0:T(8,128)(2,1)}, bf16[256,1536]{1,0:T(8,128)(2,1)}, u32[]{:S(2)}, u32[]{:S(2)}) collective-permute-start(bf16[256,1536]{1,0:T(8,128)(2,1)} %get-tuple-element.190), channel_id=1, source_target_pairs={{0,4},{2,6},{4,0},{6,2},{8,12},{10,14},{12,8},{14,10},{16,20},{18,... | collective-permute-start | bytes 2359304 | tf_op jit(solution)/shard_map/ppermute | solution.py:61
  202.8 34.4 %collective-permute-start.52 = (bf16[256,1536]{1,0:T(8,128)(2,1)}, bf16[256,1536]{1,0:T(8,128)(2,1)}, u32[]{:S(2)}, u32[]{:S(2)}) collective-permute-start(bf16[256,1536]{1,0:T(8,128)(2,1)} %get-tuple-element.186), channel_id=1, source_target_pairs={{0,4},{2,6},{4,0},{6,2},{8,12},{10,14},{12,8},{14,10},{16,20},{18,... | collective-permute-start | bytes 2359304 | tf_op jit(solution)/shard_map/ppermute | solution.py:61
  207.7 32.1 %collective-permute-start.51 = (bf16[256,1536]{1,0:T(8,128)(2,1)}, bf16[256,1536]{1,0:T(8,128)(2,1)}, u32[]{:S(2)}, u32[]{:S(2)}) collective-permute-start(bf16[256,1536]{1,0:T(8,128)(2,1)} %get-tuple-element.184), channel_id=1, source_target_pairs={{0,2},{2,0},{4,6},{6,4},{8,10},{10,8},{12,14},{14,12},{16,18},{18,... | collective-permute-start | bytes 2359304 | tf_op jit(solution)/shard_map/ppermute | solution.py:61
  210.1 44.4 %collective-permute-start.50 = (bf16[256,1536]{1,0:T(8,128)(2,1)}, bf16[256,1536]{1,0:T(8,128)(2,1)}, u32[]{:S(2)}, u32[]{:S(2)}) collective-permute-start(bf16[256,1536]{1,0:T(8,128)(2,1)} %get-tuple-element.181), channel_id=1, source_target_pairs={{0,2},{2,0},{4,6},{6,4},{8,10},{10,8},{12,14},{14,12},{16,18},{18,... | collective-permute-start | bytes 2359304 | tf_op jit(solution)/shard_map/ppermute | solution.py:61
  226.1 20.9 %collective-permute-start.45 = (bf16[512,1024]{1,0:T(8,128)(2,1)}, bf16[512,1024]{1,0:T(8,128)(2,1)S(1)}, u32[]{:S(2)}, u32[]{:S(2)}) collective-permute-start(bf16[512,1024]{1,0:T(8,128)(2,1)} %get-tuple-element.167), channel_id=1, source_target_pairs={{0,1},{1,0},{2,3},{3,2},{4,5},{5,4},{6,7},{7,6},{8,9},{9,8},{10,11... | collective-permute-start | bytes 3145736 | tf_op jit(solution)/shard_map/ppermute | solution.py:444
  226.1 16.6 %collective-permute-start.46 = (bf16[512,1024]{1,0:T(8,128)(2,1)}, bf16[512,1024]{1,0:T(8,128)(2,1)S(1)}, u32[]{:S(2)}, u32[]{:S(2)}) collective-permute-start(bf16[512,1024]{1,0:T(8,128)(2,1)} %get-tuple-element.169), channel_id=1, source_target_pairs={{0,1},{1,0},{2,3},{3,2},{4,5},{5,4},{6,7},{7,6},{8,9},{9,8},{10,11... | collective-permute-start | bytes 3145736 | tf_op jit(solution)/shard_map/ppermute | solution.py:444
  237.1 16.4 %collective-permute-start.58 = (bf16[256,1152]{1,0:T(8,128)(2,1)}, bf16[256,1152]{1,0:T(8,128)(2,1)S(1)}, u32[]{:S(2)}, u32[]{:S(2)}) collective-permute-start(bf16[256,1152]{1,0:T(8,128)(2,1)} %get-tuple-element.196), channel_id=1, source_target_pairs={{0,4},{2,6},{4,0},{6,2},{8,12},{10,14},{12,8},{14,10},{16,20},{18,... | collective-permute-start | bytes 1769480 | tf_op jit(solution)/shard_map/ppermute | solution.py:61
  241.2 20.5 %collective-permute-start.55 = (bf16[256,1536]{1,0:T(8,128)(2,1)S(1)}, bf16[256,1536]{1,0:T(8,128)(2,1)S(1)}, u32[]{:S(2)}, u32[]{:S(2)}) collective-permute-start(bf16[256,1536]{1,0:T(8,128)(2,1)S(1)} %add_convert_fusion.1), channel_id=1, source_target_pairs={{0,2},{2,0},{4,6},{6,4},{8,10},{10,8},{12,14},{14,12},{16,18},{18,... | collective-permute-start | bytes 2359304 | tf_op jit(solution)/shard_map/ppermute | solution.py:61
  242.6 24.7 %collective-permute-start.53 = (bf16[256,1536]{1,0:T(8,128)(2,1)S(1)}, bf16[256,1536]{1,0:T(8,128)(2,1)S(1)}, u32[]{:S(2)}, u32[]{:S(2)}) collective-permute-start(bf16[256,1536]{1,0:T(8,128)(2,1)S(1)} %add_convert_fusion.2), channel_id=1, source_target_pairs={{0,4},{2,6},{4,0},{6,2},{8,12},{10,14},{12,8},{14,10},{16,20},{18,... | collective-permute-start | bytes 2359304 | tf_op jit(solution)/shard_map/ppermute | solution.py:61
  247.0 33.2 %collective-permute-start.47 = (bf16[512,1024]{1,0:T(8,128)(2,1)S(1)}, bf16[512,1024]{1,0:T(8,128)(2,1)S(1)}, u32[]{:S(2)}, u32[]{:S(2)}) collective-permute-start(bf16[512,1024]{1,0:T(8,128)(2,1)S(1)} %get-tuple-element.234.own_ref), channel_id=1, source_target_pairs={{0,1},{1,0},{2,3},{3,2},{4,5},{5,4},{6,7},{7,6},{8,9},{9,8},{10,11... | collective-permute-start | bytes 3145736 | tf_op jit(solution)/shard_map/ppermute | solution.py:444
  254.5 87.1 %collective-permute-start.61 = (bf16[256,1152]{1,0:T(8,128)(2,1)}, bf16[256,1152]{1,0:T(8,128)(2,1)}, u32[]{:S(2)}, u32[]{:S(2)}) collective-permute-start(bf16[256,1152]{1,0:T(8,128)(2,1)} %add_convert_fusion.3), channel_id=1, source_target_pairs={{0,2},{2,0},{4,6},{6,4},{8,10},{10,8},{12,14},{14,12},{16,18},{18,... | collective-permute-start | bytes 1769480 | tf_op jit(solution)/shard_map/ppermute | solution.py:61
  267.4 74.5 %collective-permute-start.64 = (bf16[256,1152]{1,0:T(8,128)(2,1)}, bf16[256,1152]{1,0:T(8,128)(2,1)}, u32[]{:S(2)}, u32[]{:S(2)}) collective-permute-start(bf16[256,1152]{1,0:T(8,128)(2,1)} %get-tuple-element.205), channel_id=1, source_target_pairs={{0,4},{2,6},{4,0},{6,2},{8,12},{10,14},{12,8},{14,10},{16,20},{18,... | collective-permute-start | bytes 1769480 | tf_op jit(solution)/shard_map/ppermute | solution.py:61
  277.0 66.7 %collective-permute-start.59 = (bf16[64,1536]{1,0:T(8,128)(2,1)}, bf16[64,1536]{1,0:T(8,128)(2,1)}, u32[]{:S(2)}, u32[]{:S(2)}) collective-permute-start(bf16[64,1536]{1,0:T(8,128)(2,1)} %slice.447), channel_id=1, source_target_pairs={{0,16},{2,18},{4,20},{6,22},{8,24},{10,26},{12,28},{14,30},{16,0},... | collective-permute-start | bytes 589832 | tf_op jit(solution)/shard_map/ppermute | solution.py:61
  278.8 66.9 %collective-permute-start.57 = (bf16[128,1536]{1,0:T(8,128)(2,1)S(1)}, bf16[128,1536]{1,0:T(8,128)(2,1)}, u32[]{:S(2)}, u32[]{:S(2)}) collective-permute-start(bf16[128,1536]{1,0:T(8,128)(2,1)S(1)} %slice.445), channel_id=1, source_target_pairs={{0,8},{2,10},{4,12},{6,14},{8,0},{10,2},{12,4},{14,6},{16,24},{18,... | collective-permute-start | bytes 1179656 | tf_op jit(solution)/shard_map/ppermute | solution.py:61
  288.8 18.2 %collective-permute-start.48 = (f32[1024]{0:T(1024)S(1)}, f32[1024]{0:T(1024)S(1)}, u32[]{:S(2)}, u32[]{:S(2)}) collective-permute-start(f32[1024]{0:T(1024)S(1)} %reduce), channel_id=1, source_target_pairs={{0,1},{1,0},{2,3},{3,2},{4,5},{5,4},{6,7},{7,6},{8,9},{9,8},{10,11... | collective-permute-start | bytes 12296 | tf_op jit(solution)/shard_map/ppermute | solution.py:444
  307.0 42.2 %collective-permute-start.63 = (bf16[256,512]{1,0:T(8,128)(2,1)}, bf16[256,512]{1,0:T(8,128)(2,1)}, u32[]{:S(2)}, u32[]{:S(2)}) collective-permute-start(bf16[256,512]{1,0:T(8,128)(2,1)} %get-tuple-element.203), channel_id=1, source_target_pairs={{0,4},{2,6},{4,0},{6,2},{8,12},{10,14},{12,8},{14,10},{16,20},{18,... | collective-permute-start | bytes 786440 | tf_op jit(solution)/shard_map/ppermute | solution.py:61
  341.7 43.4 %collective-permute-start.49 = (bf16[512,1024]{1,0:T(8,128)(2,1)S(1)}, bf16[512,1024]{1,0:T(8,128)(2,1)S(1)}, u32[]{:S(2)}, u32[]{:S(2)}) collective-permute-start(bf16[512,1024]{1,0:T(8,128)(2,1)S(1)} %slice.443), channel_id=1, source_target_pairs={{0,1},{1,0},{2,3},{3,2},{4,5},{5,4},{6,7},{7,6},{8,9},{9,8},{10,11... | collective-permute-start | bytes 3145736 | tf_op jit(solution)/shard_map/ppermute | solution.py:444
  348.5 12.7 %collective-permute-start.72 = (bf16[128,1152]{1,0:T(8,128)(2,1)S(1)}, bf16[128,1152]{1,0:T(8,128)(2,1)S(1)}, u32[]{:S(2)}, u32[]{:S(2)}) collective-permute-start(bf16[128,1152]{1,0:T(8,128)(2,1)S(1)} %slice.446), channel_id=1, source_target_pairs={{0,8},{2,10},{4,12},{6,14},{8,0},{10,2},{12,4},{14,6},{16,24},{18,... | collective-permute-start | bytes 884744 | tf_op jit(solution)/shard_map/ppermute | solution.py:61
  349.2 12.7 %collective-permute-start.65 = (bf16[256,512]{1,0:T(8,128)(2,1)S(1)}, bf16[256,512]{1,0:T(8,128)(2,1)S(1)}, u32[]{:S(2)}, u32[]{:S(2)}) collective-permute-start(bf16[256,512]{1,0:T(8,128)(2,1)S(1)} %copy-done.97), channel_id=1, source_target_pairs={{0,4},{2,6},{4,0},{6,2},{8,12},{10,14},{12,8},{14,10},{16,20},{18,... | collective-permute-start | bytes 786440 | tf_op jit(solution)/shard_map/ppermute | solution.py:61
  359.1 14.5 %collective-permute-start.62 = (bf16[256,512]{1,0:T(8,128)(2,1)S(1)}, bf16[256,512]{1,0:T(8,128)(2,1)S(1)}, u32[]{:S(2)}, u32[]{:S(2)}) collective-permute-start(bf16[256,512]{1,0:T(8,128)(2,1)S(1)} %copy-done.96), channel_id=1, source_target_pairs={{0,2},{2,0},{4,6},{6,4},{8,10},{10,8},{12,14},{14,12},{16,18},{18,... | collective-permute-start | bytes 786440 | tf_op jit(solution)/shard_map/ppermute | solution.py:61
  375.6 17.3 %collective-permute-start.81 = (bf16[256,512]{1,0:T(8,128)(2,1)S(1)}, bf16[256,512]{1,0:T(8,128)(2,1)S(1)}, u32[]{:S(2)}, u32[]{:S(2)}) collective-permute-start(bf16[256,512]{1,0:T(8,128)(2,1)S(1)} %get-tuple-element.225), channel_id=1, source_target_pairs={{0,2},{2,0},{4,6},{6,4},{8,10},{10,8},{12,14},{14,12},{16,18},{18,... | collective-permute-start | bytes 786440 | tf_op jit(solution)/shard_map/ppermute | solution.py:61
  379.5 15.5 %collective-permute-start.75 = (bf16[256,512]{1,0:T(8,128)(2,1)S(1)}, bf16[256,512]{1,0:T(8,128)(2,1)S(1)}, u32[]{:S(2)}, u32[]{:S(2)}) collective-permute-start(bf16[256,512]{1,0:T(8,128)(2,1)S(1)} %get-tuple-element.219), channel_id=1, source_target_pairs={{0,4},{2,6},{4,0},{6,2},{8,12},{10,14},{12,8},{14,10},{16,20},{18,... | collective-permute-start | bytes 786440 | tf_op jit(solution)/shard_map/ppermute | solution.py:61
  382.8 14.1 %collective-permute-start.70 = (bf16[256,512]{1,0:T(8,128)(2,1)S(1)}, bf16[256,512]{1,0:T(8,128)(2,1)S(1)}, u32[]{:S(2)}, u32[]{:S(2)}) collective-permute-start(bf16[256,512]{1,0:T(8,128)(2,1)S(1)} %fusion.29), channel_id=1, source_target_pairs={{0,2},{2,0},{4,6},{6,4},{8,10},{10,8},{12,14},{14,12},{16,18},{18,... | collective-permute-start | bytes 786440 | tf_op jit(solution)/shard_map/ppermute | solution.py:61
  385.0 13.7 %collective-permute-start.71 = (bf16[256,512]{1,0:T(8,128)(2,1)S(1)}, bf16[256,512]{1,0:T(8,128)(2,1)S(1)}, u32[]{:S(2)}, u32[]{:S(2)}) collective-permute-start(bf16[256,512]{1,0:T(8,128)(2,1)S(1)} %fusion.28), channel_id=1, source_target_pairs={{0,4},{2,6},{4,0},{6,2},{8,12},{10,14},{12,8},{14,10},{16,20},{18,... | collective-permute-start | bytes 786440 | tf_op jit(solution)/shard_map/ppermute | solution.py:61
  (152 other events, 1594.3 us)

commit v3 on v2

v3 whole, which is shorter than its diff:
```python
import functools

import jax
import jax.numpy as jnp
import numpy as np
from jax import lax
from jax.experimental import pallas as pl
from jax.experimental.pallas import tpu as pltpu
from jax.sharding import PartitionSpec as P

eps = 1e-06
wide = jnp.float32
narrow = jnp.bfloat16
in_flight = 6
per_link = 2
tile_width = 512


def dot(left, right, dims):
    return lax.dot_general(left, right, (dims, ((), ())), preferred_element_type=wide)


def nn(left, right):
    return dot(left, right, ((1,), (0,)))


def nt(left, right):
    return dot(left, right, ((1,), (1,)))


def tn(left, right):
    return dot(left, right, ((0,), (0,)))


def inverse_rms(values):
    return lax.rsqrt(jnp.mean(values * values, axis=-1, keepdims=True) + eps)


def norm_back(grad, normed, scale):
    return scale * (grad - normed * jnp.mean(grad * normed, axis=-1, keepdims=True))


class Exchange:

    def __init__(self, size):
        self.size = size
        self.sent = []
        self.links = {1: [], 2: [], 4: []}

    def __call__(self, array, bit):
        link = self.links[min(bit, 4)]
        ahead = [q[-n] for q, n in ((self.sent, in_flight), (link, per_link)) if len(q) >= n]
        if ahead:
            array = lax.optimization_barrier((array, *ahead))[0]
        pairs = [(i, i ^ bit) for i in range(self.size)]
        result = lax.ppermute(array, "dp", pairs)
        self.sent.append(result)
        link.append(result)
        return result


def inner_bits(size):
    bits = []
    bit = size // 2
    while bit >= 4:
        bits.append(bit)
        bit //= 2
    return bits


def block_offsets(size):
    order = [0]
    for bit in inner_bits(size) + [1, 2]:
        order = order + [entry ^ bit for entry in order]
    return np.array(order, np.int32)


class Gather:

    def __init__(self, send, shard, turn):
        self.send = send
        self.held = shard
        self.turn = turn

    def inner(self, bit):
        self.held = jnp.concatenate([self.held, self.send(self.held, bit)], axis=0)

    def sides(self):
        self.side = self.send(self.held, 1)
        self.up = self.send(self.held, 2)

    def far(self):
        far = self.send(self.side, 2) if self.turn else self.send(self.up, 1)
        self.pieces = [self.held, self.side, self.up, far]


def low(value):
    return value.astype(narrow)


class Scatter:

    def __init__(self, send, pieces, turn):
        self.send = send
        self.first, self.side, self.up, self.away = pieces
        self.turn = turn

    def far(self):
        if self.turn:
            self.far_got = self.send(self.away, 2)
        else:
            self.far_got = self.send(self.away, 1)

    def near(self):
        if self.turn:
            self.near_got = self.send(self.up, 2)
        else:
            self.near_got = self.send(self.side, 1)

    def sides(self):
        rest = self.side if self.turn else self.up
        rest = low(rest.astype(wide) + self.far_got.astype(wide))
        got = self.send(rest, 1 if self.turn else 2)
        self.total = self.first.astype(wide) + self.near_got.astype(wide) + got.astype(wide)

    def inner(self, bit):
        half = self.total.shape[0] // 2
        got = self.send(low(self.total[half:]), bit)
        self.total = self.total[:half] + got.astype(wide)

    def rest(self):
        for bit in reversed(inner_bits(self.send.size)):
            self.inner(bit)


def tables(rate, size):
    row = lax.broadcasted_iota(jnp.int32, (size, 1), 0).astype(wide)
    col = lax.broadcasted_iota(jnp.int32, (1, size), 1).astype(wide)
    ahead = jnp.exp(-rate * row)
    inner = jnp.where(col <= row, ahead * jnp.exp(rate * col), 0.0)
    outof = jnp.exp(-rate * (size - row))
    return inner, ahead, outof


def cost(flops, *arrays):
    size = sum(a.size * jnp.dtype(a.dtype).itemsize for a in arrays)
    return pl.CostEstimate(flops=int(flops), transcendentals=0, bytes_accessed=int(size))


def rows_of(refs):
    half = refs[0].shape[0]
    return [(ref, slice(i * half, (i + 1) * half)) for i, ref in enumerate(refs)]


def join(refs):
    return jnp.concatenate([ref[...] for ref in refs], axis=0)


def row_sums(values):
    ones = jnp.ones((8, values.shape[1]), wide)
    return lax.dot_general(
        ones,
        values,
        (((1,), (1,)), ((), ())),
        precision=lax.Precision.HIGHEST,
        preferred_element_type=wide,
    )


def column(own, other):
    half = own.shape[1] // 2
    total = own + jnp.concatenate([other[:, half:], other[:, :half]], axis=1)
    return jnp.transpose(total)[:, :1]


def spans(turn_ref, size):
    turn = turn_ref[0]
    early = pl.ds(pl.multiple_of(turn * size, size), size)
    late = pl.ds(pl.multiple_of((1 - turn) * size, size), size)
    return early, late


def front_kernel(turn_ref, rate_ref, own_ref, other_ref, *refs, heads):
    wq, wk, wv = refs[0:4], refs[4:8], refs[8:12]
    q_ref, k_ref, v_ref, sq_ref, sk_ref, o_ref, sum_ref = refs[12:]
    pair = rows_of((own_ref, other_ref))
    for pieces, out, slope in ((wq, q_ref, sq_ref), (wk, k_ref, sk_ref)):
        weight = join(pieces)
        for ref, rows in pair:
            value = nn(ref[...], weight)
            sigma = jax.nn.sigmoid(value)
            out[rows, :] = low(value * sigma)
            slope[rows, :] = low(sigma * (1.0 + value * (1.0 - sigma)))
    weight = join(wv)
    for ref, rows in pair:
        v_ref[rows, :] = low(nn(ref[...], weight))
    size = own_ref.shape[0]
    early, late = spans(turn_ref, size)
    wide_head = q_ref.shape[1] // heads
    sums = 0.0
    for j in range(heads):
        cols = slice(j * wide_head, (j + 1) * wide_head)
        inner, ahead, outof = tables(rate_ref[pl.program_id(0) * heads + j], size)

        def local(rows):
            weights = low(nt(q_ref[rows, cols], k_ref[rows, cols]) * inner)
            return nn(weights, v_ref[rows, cols])

        weighted = low(k_ref[early, cols].astype(wide) * outof)
        state = low(tn(weighted, v_ref[early, cols]))
        o_ref[early, cols] = local(early)
        o_ref[late, cols] = local(late) + nn(q_ref[late, cols], state) * ahead
    values = o_ref[...]
    sums = row_sums(values * values)

    @pl.when(pl.program_id(0) == 0)
    def _():
        sum_ref[...] = sums

    @pl.when(pl.program_id(0) > 0)
    def _():
        sum_ref[...] += sums


def front(turn, rates, pair, pieces):
    rows, width = pair[0].shape
    quarter, columns = pieces[0][0].shape
    steps = 2
    block = columns // steps
    scalar = pl.BlockSpec(memory_space=pltpu.SMEM)
    whole = lambda shape: pl.BlockSpec(shape, lambda i: (0, 0))
    piece = pl.BlockSpec((quarter, block), lambda i: (0, i))
    out = pl.BlockSpec((2 * rows, block), lambda i: (0, i))
    types = [narrow] * 5 + [wide]
    return pl.pallas_call(
        functools.partial(front_kernel, heads=rates.shape[0] // steps),
        cost_estimate=cost(18 * rows * width * columns, *pair, *pair, *pair, *pair, *pair),
        grid=(steps,),
        in_specs=[scalar, scalar] + [whole((rows, width))] * 2 + [piece] * 12,
        out_specs=[out] * 6 + [whole((8, 2 * rows))],
        out_shape=[jax.ShapeDtypeStruct((2 * rows, columns), t) for t in types]
        + [jax.ShapeDtypeStruct((8, 2 * rows), wide)],
    )(turn, rates, *pair, *(p for ps in pieces for p in ps))


def gate_kernel(own_ref, other_ref, w0, w1, w2, w3, u_ref):
    weight = join((w0, w1, w2, w3))
    for ref, rows in rows_of((own_ref, other_ref)):
        u_ref[rows, :] = nn(ref[...], weight).astype(u_ref.dtype)


def gate(pair, pieces):
    rows = pair[0].shape[0]
    return pl.pallas_call(
        gate_kernel,
        cost_estimate=cost(4 * rows * pieces[0].size * 4, *pair, *pair),
        out_shape=jax.ShapeDtypeStruct((2 * rows, pieces[0].shape[1]), wide),
    )(*pair, *pieces)


def branch_kernel(
    sum_ref, got_ref, o_ref, u_ref, w0, w1, w2, w3, gated_ref, scale_ref, own_ref, other_ref
):
    rows = own_ref.shape[0]
    quarter = w0.shape[0]
    scale = lax.rsqrt(column(sum_ref[...], got_ref[...]) / (4 * quarter) + eps)
    scale_ref[...] = scale
    gated_ref[...] = low(o_ref[...] * scale * u_ref[...])
    for i, ref in enumerate((w0, w1, w2, w3)):
        cols = slice(i * quarter, (i + 1) * quarter)
        value = nt(gated_ref[...], ref[...])
        own_ref[:, cols] = value[:rows]
        other_ref[:, cols] = low(value[rows:])


def branch(sums, got, attended, proj_u, pieces):
    length, heads = attended.shape
    rows, width = length // 2, 4 * pieces[0].shape[0]
    return pl.pallas_call(
        branch_kernel,
        cost_estimate=cost(2 * length * heads * width, attended, attended, attended, proj_u),
        out_shape=[
            jax.ShapeDtypeStruct((length, heads), narrow),
            jax.ShapeDtypeStruct((length, 1), wide),
            jax.ShapeDtypeStruct((rows, width), wide),
            jax.ShapeDtypeStruct((rows, width), narrow),
        ],
    )(sums, got, attended, proj_u, *pieces)


def unbranch_kernel(
    own_ref, other_ref, o_ref, scale_ref, u_ref, w0, w1, w2, w3, grad_ref, unit_ref, cross_ref
):
    weight = join((w0, w1, w2, w3))
    for ref, rows in rows_of((own_ref, other_ref)):
        value = nn(ref[...], weight)
        normed = o_ref[rows, :] * scale_ref[rows, :]
        unit_ref[rows, :] = low(value * normed)
        value = value * u_ref[rows, :]
        grad_ref[rows, :] = value
        cross_ref[:, rows] = row_sums(value * normed)


def unbranch(pair, attended, scale, proj_u, pieces):
    length, heads = attended.shape
    width = pair[0].shape[1]
    return pl.pallas_call(
        unbranch_kernel,
        cost_estimate=cost(2 * length * heads * width, attended, attended, attended, proj_u),
        out_shape=[
            jax.ShapeDtypeStruct((length, heads), wide),
            jax.ShapeDtypeStruct((length, heads), narrow),
            jax.ShapeDtypeStruct((8, length), wide),
        ],
    )(*pair, attended, scale, proj_u, *pieces)


def attend_back_kernel(
    turn_ref,
    rate_ref,
    scale_ref,
    cross_ref,
    got_ref,
    q_ref,
    k_ref,
    v_ref,
    sq_ref,
    sk_ref,
    gn_ref,
    o_ref,
    dq_ref,
    dk_ref,
    dv_ref,
    g_ref,
    c_ref,
    *,
    width,
):
    size = q_ref.shape[0] // 2
    inner, ahead, outof = tables(rate_ref[pl.program_id(0)], size)
    early, late = spans(turn_ref, size)

    @pl.when(pl.program_id(0) == 0)
    def _():
        c_ref[...] = column(cross_ref[...], got_ref[...]) / width

    scale = scale_ref[...]
    normed = o_ref[...] * scale
    g_ref[...] = low(scale * (gn_ref[...] - normed * c_ref[...]))

    def local(rows):
        q, k, v, g = (ref[rows, :] for ref in (q_ref, k_ref, v_ref, g_ref))
        weights = low(nt(q, k) * inner)
        grad_scores = low(nt(g, v) * inner)
        return nn(grad_scores, k), tn(grad_scores, q), tn(weights, g)

    def store(rows, dq, dk, dv):
        dq_ref[rows, :] = low(dq * sq_ref[rows, :].astype(wide))
        dk_ref[rows, :] = low(dk * sk_ref[rows, :].astype(wide))
        dv_ref[rows, :] = low(dv)

    weighted = low(k_ref[early, :].astype(wide) * outof)
    state = low(tn(weighted, v_ref[early, :]))
    g_ahead = low(g_ref[late, :].astype(wide) * ahead)
    grad_state = low(tn(q_ref[late, :], g_ahead))
    dq, dk, dv = local(late)
    store(late, dq + nt(g_ahead, state), dk, dv)
    dq, dk, dv = local(early)
    store(
        early,
        dq,
        dk + nt(v_ref[early, :], grad_state) * outof,
        dv + nn(weighted, grad_state),
    )


def attend_back(turn, rates, scale, cross, got, arrays, width):
    heads = rates.shape[0]
    length, columns = arrays[0].shape
    spec = pl.BlockSpec((length, columns // heads), lambda h: (0, h))
    col = pl.BlockSpec((length, 1), lambda h: (0, 0))
    row = pl.BlockSpec((8, length), lambda h: (0, 0))
    scalar = pl.BlockSpec(memory_space=pltpu.SMEM)
    return pl.pallas_call(
        functools.partial(attend_back_kernel, width=width),
        cost_estimate=cost(12 * length * length * columns, *arrays, *arrays, *arrays),
        grid=(heads,),
        in_specs=[scalar, scalar, col, row, row] + [spec] * len(arrays),
        out_specs=[spec] * 3,
        out_shape=[jax.ShapeDtypeStruct((length, columns), narrow)] * 3,
        scratch_shapes=[
            pltpu.VMEM((length, columns // heads), narrow),
            pltpu.VMEM((length, 1), wide),
        ],
    )(turn, rates, scale, cross, got, *arrays)


def weight_grad_kernel(own_ref, other_ref, *refs):
    count = len(refs) // 5
    pair = rows_of((own_ref, other_ref))
    quarter = refs[count].shape[0]
    for j in range(count):
        for i in range(4):
            cols = slice(i * quarter, (i + 1) * quarter)
            total = sum(tn(ref[:, cols], refs[j][rows, :]) for ref, rows in pair)
            refs[count + 4 * j + i][...] = low(total)


def weight_grads(pair, arrays):
    rows, width = pair[0].shape
    columns = arrays[0].shape[1]
    outs = pl.pallas_call(
        weight_grad_kernel,
        cost_estimate=cost(4 * rows * width * columns * len(arrays), *pair, *arrays, *arrays),
        out_shape=[jax.ShapeDtypeStruct((width // 4, columns), narrow)] * (4 * len(arrays)),
    )(*pair, *arrays)
    return [outs[4 * j : 4 * j + 4] for j in range(len(arrays))]


def input_grad_kernel(*refs):
    grads, pieces, (own_ref, other_ref) = refs[:4], refs[4:20], refs[20:]
    quarter = pieces[0].shape[0]
    rows = own_ref.shape[0]
    for i in range(4):
        cols = slice(i * quarter, (i + 1) * quarter)
        value = sum(nt(grads[j][...], pieces[4 * j + i][...]) for j in range(4))
        own_ref[:, cols] = value[:rows]
        other_ref[:, cols] = low(value[rows:])


def input_grad(grads, pieces):
    length, columns = grads[0].shape
    rows, width = length // 2, 4 * pieces[0][0].shape[0]
    return pl.pallas_call(
        input_grad_kernel,
        cost_estimate=cost(8 * length * columns * width, *grads, *grads, *grads),
        out_shape=[
            jax.ShapeDtypeStruct((rows, width), wide),
            jax.ShapeDtypeStruct((rows, width), narrow),
        ],
    )(*grads, *(p for ps in pieces for p in ps))


def ffn_kernel(*refs, count):
    n_in, g_in = refs[0:2], refs[2:4]
    w_in = [refs[4 + 4 * c : 8 + 4 * c] for c in range(count)]
    refs = refs[4 + 4 * count :]
    sums_out = refs[0:4]
    o_out = [refs[4 + 4 * c : 8 + 4 * c] for c in range(count)]
    n_ref, g_ref, w_ref, s_ref, d_ref, acc_ref, low_ref, o_ref, in_sem, out_sem = refs[
        4 + 4 * count :
    ]
    rows = n_ref.shape[1]
    quarter = w_ref.shape[1] // 4
    n = s_ref.shape[2]
    part = lambda i: slice(i * quarter, (i + 1) * quarter)

    ready = [pltpu.make_async_copy(n_in[h], n_ref.at[h], in_sem.at[h]) for h in range(2)]
    ready += [pltpu.make_async_copy(g_in[h], g_ref.at[h], in_sem.at[2 + h]) for h in range(2)]
    load = [
        [
            pltpu.make_async_copy(
                w_in[c][i], w_ref.at[c, part(i), :], in_sem.at[4 + 4 * c + i]
            )
            for i in range(4)
        ]
        for c in range(count)
    ]
    for copy in load[0] + ready:
        copy.start()
    for copies in load[1:]:
        for copy in copies:
            copy.start()
    for copy in load[0] + ready:
        copy.wait()
    stores = []
    for c in range(count):
        if c > 0:
            for copy in load[c]:
                copy.wait()

        def half(h, carry, c=c):
            ab = nn(n_ref[h], w_ref[c, :, : 2 * n])
            ds = nn(g_ref[h], w_ref[c, :, 2 * n :])
            a = ab[:, :n]
            b = ab[:, n:]
            s_ref[h] = low(a * b)
            d_ref[h, :, :n] = low(ds * b)
            d_ref[h, :, n:] = low(ds * a)
            return carry

        lax.fori_loop(0, 2, half, 0)
        y = nt(s_ref[...].reshape(2 * rows, n), w_ref[c, :, 2 * n :]).reshape(2, rows, -1)
        d = nt(d_ref[...].reshape(2 * rows, 2 * n), w_ref[c, :, : 2 * n]).reshape(2, rows, -1)
        if c == 0:
            acc_ref[0] = y
            acc_ref[1] = d
        else:
            acc_ref[0] += y
            acc_ref[1] += d
        if c == count - 1:
            for k in range(2):
                low_ref[k] = low(acc_ref[k, 1])
                for at, source in ((2 * k, acc_ref.at[k, 0]), (2 * k + 1, low_ref.at[k])):
                    copy = pltpu.make_async_copy(source, sums_out[at], out_sem.at[at])
                    copy.start()
                    stores.append(copy)
        for i in (3, 2, 1, 0):
            o_ref[c, part(i), : 2 * n] = low(
                sum(tn(n_ref[h, :, part(i)], d_ref[h]) for h in range(2))
            )
            o_ref[c, part(i), 2 * n :] = low(
                sum(tn(g_ref[h, :, part(i)], s_ref[h]) for h in range(2))
            )
            copy = pltpu.make_async_copy(
                o_ref.at[c, part(i), :], o_out[c][i], out_sem.at[4 + 4 * c + i]
            )
            copy.start()
            stores.append(copy)
    for copy in stores:
        copy.wait()


def ffn(normed, grad, tiles):
    rows, width = normed[0].shape
    count = len(tiles)
    quarter, n3 = tiles[0][0].shape
    n = n3 // 3
    flat = [piece for pieces in tiles for piece in pieces]
    hbm = pl.BlockSpec(memory_space=pl.ANY)
    outs = pl.pallas_call(
        functools.partial(ffn_kernel, count=count),
        cost_estimate=cost(12 * rows * width * n3 * count, *flat, *flat, *normed, *grad),
        in_specs=[hbm] * (4 + 4 * count),
        out_specs=[hbm] * (4 + 4 * count),
        out_shape=[
            jax.ShapeDtypeStruct((rows, width), t) for t in (wide, narrow, wide, narrow)
        ]
        + [jax.ShapeDtypeStruct((quarter, n3), narrow)] * (4 * count),
        scratch_shapes=[
            pltpu.VMEM((2, rows, width), narrow),
            pltpu.VMEM((2, rows, width), narrow),
            pltpu.VMEM((count, width, n3), narrow),
            pltpu.VMEM((2, rows, n), narrow),
            pltpu.VMEM((2, rows, 2 * n), narrow),
            pltpu.VMEM((2, 2, rows, width), wide),
            pltpu.VMEM((2, rows, width), narrow),
            pltpu.VMEM((count, width, n3), narrow),
            pltpu.SemaphoreType.DMA((4 + 4 * count,)),
            pltpu.SemaphoreType.DMA((4 + 4 * count,)),
        ],
    )(*normed, *grad, *flat)
    return outs[:4], [outs[4 + 4 * i : 8 + 4 * i] for i in range(count)]


def ffn_cuts(total):
    cuts = []
    left = total
    while left > 0:
        take = min(tile_width, left)
        cuts.append((total - left, take))
        left -= take
    return cuts


def shards(
    size,
    tokens,
    w_query,
    w_key,
    w_value,
    w_gate,
    w_out,
    w_first,
    w_second,
    w_down,
    decay_rates,
    cotangent,
):
    send = Exchange(size)
    swap = lambda value: lax.ppermute(value, "tensor", [(0, 1), (1, 0)])
    me = lax.axis_index("dp")
    turn = lax.axis_index("tensor").astype(jnp.int32).reshape(1)
    rows, width = tokens.shape
    span = width // size
    offsets = jnp.asarray(np.repeat(block_offsets(size), span))
    place = jnp.bitwise_xor(offsets, me) * span + jnp.arange(width) % span
    shuffle = (jnp.arange(width)[:, None] == place[None, :]).astype(narrow)

    cuts = ffn_cuts(w_first.shape[1])
    down_t = w_down.T
    att = [
        Gather(send, w, i % 2 == 0)
        for i, w in enumerate((w_query, w_key, w_value, w_gate, w_out.T))
    ]
    mlp = [
        Gather(
            send,
            jnp.concatenate([w[:, at : at + n] for w in (w_first, w_second, down_t)], axis=1),
            i % 2 == 0,
        )
        for i, (at, n) in enumerate(cuts)
    ]
    bits = inner_bits(size)
    for step in range(len(att) + len(bits) + 1):
        c = step - len(bits) - 1
        if 0 <= c < len(att):
            att[c].far()
        c = step - len(bits)
        if 0 <= c < len(att):
            att[c].sides()
        for level in range(len(bits) - 1, -1, -1):
            c = step - level
            if 0 <= c < len(att):
                att[c].inner(bits[level])
            elif len(att) <= c < len(att) + len(mlp):
                mlp[c - len(att)].inner(bits[level])
    step = len(att) + len(bits) + 1
    for level in range(len(bits)):
        for c in range(max(0, step - level - len(att)), len(mlp)):
            mlp[c].inner(bits[level])
    for c in range(len(mlp) + 1):
        if c < len(mlp):
            mlp[c].sides()
        if c > 0:
            mlp[c - 1].far()
    full_q, full_k, full_v, full_u, full_o = (gather.pieces for gather in att)

    inputs = low(nn(tokens, shuffle)).astype(wide)
    scale_in = inverse_rms(inputs)
    normed_in = inputs * scale_in
    own_in = low(normed_in)
    pair_in = (own_in, swap(own_in))
    own_cot = low(nn(cotangent, shuffle))
    pair_cot = (own_cot, swap(own_cot))

    query, keys, values, slope_q, slope_k, attended, sums = front(
        turn, decay_rates, pair_in, (full_q, full_k, full_v)
    )
    proj_u = gate(pair_in, full_u)
    gated, scale_out, branch_own, branch_other = branch(
        sums, swap(sums), attended, proj_u, full_o
    )
    middle = inputs + branch_own + swap(branch_other).astype(wide)
    scale_mid = inverse_rms(middle)
    normed_mid = middle * scale_mid
    own_mid = low(normed_mid)
    pair_mid = (own_mid, swap(own_mid))

    tiles = [gather.pieces for gather in mlp]
    sums_a, grads = ffn(pair_mid, pair_cot, tiles[:-1])
    outs = [Scatter(send, grad, i % 2 == 0) for i, grad in enumerate(grads)]
    for stage in (Scatter.far, Scatter.near, Scatter.sides):
        for out in outs:
            stage(out)
    sums_b, grads = ffn(pair_mid, pair_cot, tiles[-1:])
    outs.append(Scatter(send, grads[0], len(outs) % 2 == 0))
    for stage in (Scatter.far, Scatter.near, Scatter.sides):
        stage(outs[-1])
    for out in outs:
        out.rest()

    y_sum, grad_mid_norm = (
        (sums_a[i] + sums_b[i])
        + (swap(sums_a[i + 1]).astype(wide) + swap(sums_b[i + 1]).astype(wide))
        for i in (0, 2)
    )
    grad_middle = own_cot.astype(wide) + norm_back(grad_mid_norm, normed_mid, scale_mid)
    own_e = low(grad_middle)
    pair_e = (own_e, swap(own_e))
    grad_normed, grad_unit, cross = unbranch(pair_e, attended, scale_out, proj_u, full_o)
    late = [
        Scatter(send, weight_grads(pair_e, (gated,))[0], True),
        Scatter(send, weight_grads(pair_in, (grad_unit,))[0], False),
    ]
    for stage in (Scatter.far, Scatter.near, Scatter.sides):
        for out in late:
            stage(out)
    grad_q, grad_k, grad_v = attend_back(
        turn,
        decay_rates,
        scale_out,
        cross,
        swap(cross),
        (query, keys, values, slope_q, slope_k, grad_normed, attended),
        width,
    )
    last = [
        Scatter(send, grad, i % 2 == 0)
        for i, grad in enumerate(weight_grads(pair_in, (grad_q, grad_k, grad_v)))
    ]
    for stage in (Scatter.far, Scatter.near, Scatter.sides):
        for out in last:
            stage(out)
    for out in late + last:
        out.rest()

    total_own, total_other = input_grad(
        (grad_q, grad_k, grad_v, grad_unit), (full_q, full_k, full_v, full_u)
    )
    grad_in_norm = total_own + swap(total_other).astype(wide)
    tokens_grad = grad_middle + norm_back(grad_in_norm, normed_in, scale_in)
    layer_out = low(middle + y_sum)
    layer_out = low(nt(layer_out, shuffle))
    parts = []
    rest = tokens_grad
    for _ in range(3):
        part = lax.reduce_precision(rest, 8, 7)
        parts.append(low(part))
        rest = rest - part
    tokens_grad = nt(parts[0], shuffle) + (nt(parts[1], shuffle) + nt(parts[2], shuffle))
    thirds = [
        jnp.concatenate(
            [out.total[:, i * n : (i + 1) * n] for out, (_, n) in zip(outs, cuts)], axis=1
        )
        for i in range(3)
    ]
    return (
        layer_out,
        tokens_grad,
        last[0].total,
        last[1].total,
        last[2].total,
        late[1].total,
        late[0].total.T,
        thirds[0],
        thirds[1],
        thirds[2].T,
    )


def solution(mesh):
    return jax.shard_map(
        functools.partial(shards, mesh.shape["dp"]),
        mesh=mesh,
        in_specs=(
            P(("dp", "tensor"), None),
            P("dp", "tensor"),
            P("dp", "tensor"),
            P("dp", "tensor"),
            P("dp", "tensor"),
            P("tensor", "dp"),
            P("dp", "tensor"),
            P("dp", "tensor"),
            P("tensor", "dp"),
            P("tensor"),
            P(("dp", "tensor"), None),
        ),
        out_specs=(
            P(("dp", "tensor"), None),
            P(("dp", "tensor"), None),
            P("dp", "tensor"),
            P("dp", "tensor"),
            P("dp", "tensor"),
            P("dp", "tensor"),
            P("tensor", "dp"),
            P("dp", "tensor"),
            P("dp", "tensor"),
            P("tensor", "dp"),
        ),
        check_vma=False,
    )
```

time: 443 us -> 436 us (0.984)
  waiting for transfers between devices: 135 us -> 171 us
  local copies, waits for them, and re-layouts: 34.5 us -> 15.4 us
  matrix products: 25.1 us -> 12.2 us
  starting transfers between devices: 95.8 us -> 89.5 us
    ppermute x80, waiting for transfers between devices: 135 us -> 170 us  [__call__(): result = lax.ppermute(array, 'dp', pairs)]
    dot_general x10 -> x6, matrix products: 25.1 us -> 12.2 us  [dot(): lax.dot_general(left, right, (dims, ((), ())), preferred_element_type=wide)]
    unnamed x240 -> x192, local copies, waits for them, and re-layouts: 22.8 us -> 10.7 us
    ppermute x80, starting transfers between devices: 94.5 us -> 88 us  [__call__(): result = lax.ppermute(array, 'dp', pairs)]
    squeeze x5 -> x0, local copies, waits for them, and re-layouts: 4.99 us -> none  [weight_grads(): return [[out[i] for i in range(4)] for out in outs]]
    pallas_call x13 -> x11, Pallas kernels: 105 us -> 106 us  [the longest x2 38.2 us: ffn(): pl.pallas_call(functools.partial(ffn_kernel, count=count), cost_estimate=...]
  transfers between devices with their start and end apart: 90 -> 92, of which waited for: 37 -> 36; matrix products, arithmetic and copies ran while one was open for 20% -> 13% of each run, Pallas kernels for 24% -> 25%
where the time goes in v3:
time: 436 us; the launch traced here: 430 us
  waiting for transfers between devices  171 us (39%)
  Pallas kernels  106 us (24%)
  starting transfers between devices  89.5 us (21%)
  other arithmetic  34.4 us (8%)
  local copies, waits for them, and re-layouts  15.4 us (4%)
  matrix products  12.2 us (3%)
    ppermute x80, waiting for transfers between devices, __call__(): result = lax.ppermute(array, 'dp', pairs)  170 us
    ppermute x80, starting transfers between devices, __call__(): result = lax.ppermute(array, 'dp', pairs)  88 us
    pallas_call x2, Pallas kernels, ffn(): pl.pallas_call(functools.partial(ffn_kernel, count=count), cost_estimate=...  38.2 us
    pallas_call x3, Pallas kernels, weight_grads(): pl.pallas_call(weight_grad_kernel, cost_estimate=cost(4 * rows * width *...  14.4 us
    pallas_call x1, Pallas kernels, front(): pl.pallas_call(functools.partial(front_kernel, heads=rates.shape[0] // st...  13.6 us
    pallas_call x1, Pallas kernels, attend_back(): pl.pallas_call(functools.partial(attend_back_kernel, width=width), cost_e...  12.8 us
    dot_general x6, matrix products, dot(): lax.dot_general(left, right, (dims, ((), ())), preferred_element_type=wide)  12.2 us
    unnamed x192, local copies, waits for them, and re-layouts  10.7 us
  transfers between devices with their start and end apart: 92, of which 36 were waited for; matrix products, arithmetic and copies ran while one was open for 13% of the time, Pallas kernels for 25%

profile of v3, /device:TPU:0, one launch (start us, length us, event | category | flops | bytes accessed | tf_op | source)
XLA Modules:
  0.0 430.3 jit_solution(3215225591266814565)
XLA Ops:
  0.7 4.1 collective-permute-start.1
  11.7 2.3 fusion.26.refs_2_
  16.9 3.6 collective-permute-done.6
  26.2 3.4 collective-permute-done.7
  29.5 2.8 collective-permute-start.15
  36.1 3.4 collective-permute-done.12
  42.1 2.8 collective-permute-done.5.refs_3_.refs_7_
  48.4 3.2 collective-permute-done.14.refs_10_.refs_14_
  52.8 2.3 collective-permute-done.11.refs_7_.refs_11_
  55.1 2.2 collective-permute-start.16
  60.3 3.3 collective-permute-done.19.w1.refs_17_
  67.3 2.6 collective-permute-done.26
  77.4 13.6 %shard_map.195 = (bf16[1024,512]{1,0:T(8,128)(2,1)}, bf16[1024,512]{1,0:T(8,128)(2,1)}, bf16[1024,512]{1,0:T(8,128)(2,1)}, bf16[1024,512]{1,0:T(8,128)(2,1)}, bf...) custom-call(s32[1]{0:T(128)} %bitcast.1.turn_ref, f32[4]{0:T(128)} %rate_ref.3, ...), custom_call_target="tpu_custom_call" | custom-call | flops 4831838208 | bytes 10485760 | tf_op jit(solution)/shard_map/pallas_call | solution.py:235
  91.1 4.4 %shard_map.196.u_ref = f32[1024,512]{1,0:T(8,128)} custom-call(bf16[512,1024]{1,0:T(8,128)(2,1)} %copy-done.7, bf16[512,1024]{1,0:T(8,128)(2,1)} %copy-done.12, bf16[256,512]{1,0:T(8,128)(2,1)} %constant_dynamic-update-slice_fusion.9.w0.refs_16_, bf16[256,512]{1,0:T(8,128)(2,1)} %copy-done.38, bf16[256,512]{1,0:T(8,128)(2,1)} %collective-permute-done.20.w2.refs_18_, ...), custom_call_target="tpu_custom_call" | custom-call | flops 1073741824 | bytes 4194304 | tf_op jit(solution)/shard_map/pallas_call | solution.py:254
  96.3 5.8 %shard_map.197 = (bf16[1024,512]{1,0:T(8,128)(2,1)}, f32[1024,1]{1,0:T(8,128)}, f32[512,1024]{1,0:T(8,128)}, bf16[512,1024]{1,0:T(8,128)(2,1)}) custom-call(f32[8,1024]{1,0:T(8,128)} %get-tuple-element.157.sum_ref, f32[8,1024]{1,0:T(8,128)} %copy-done.57, f32[1024,512]{1,0:T(8,128)} %get-tuple-element.158.o_ref, f32[1024,512]{1,0:T(8,128)} %shard_map.196.u_ref, ...), custom_call_target="tpu_custom_call" | custom-call | flops 1073741824 | bytes 8388608 | tf_op jit(solution)/shard_map/pallas_call | solution.py:279
  109.3 4.5 %collective-permute-done.35 = bf16[64,1152]{1,0:T(8,128)(2,1)S(1)} collective-permute-done((bf16[64,1152]{1,0:T(8,128)(2,1)S(1)}, bf16[64,1152]{1,0:T(8,128)(2,1)S(1)}, u32[]{:S(2)}, u32[]{:S(2)}) %collective-permute-start.35) | collective-permute-done | bytes 147488 | tf_op jit(solution)/shard_map/ppermute | solution.py:56
  113.7 5.1 %collective-permute-done.37 = bf16[128,1536]{1,0:T(8,128)(2,1)S(1)} collective-permute-done((bf16[128,1536]{1,0:T(8,128)(2,1)S(1)}, bf16[128,1536]{1,0:T(8,128)(2,1)S(1)}, u32[]{:S(2)}, u32[]{:S(2)}) %collective-permute-start.37) | collective-permute-done | bytes 393248 | tf_op jit(solution)/shard_map/ppermute | solution.py:56
  122.4 4.4 %collective-permute-done.34.refs_6_ = bf16[256,1536]{1,0:T(8,128)(2,1)S(1)} collective-permute-done((bf16[256,1536]{1,0:T(8,128)(2,1)S(1)}, bf16[256,1536]{1,0:T(8,128)(2,1)S(1)}, u32[]{:S(2)}, u32[]{:S(2)}) %collective-permute-start.34) | collective-permute-done | bytes 786464 | tf_op jit(solution)/shard_map/ppermute | solution.py:56
  127.7 15.3 %collective-permute-done.38.refs_9_ = bf16[256,1536]{1,0:T(8,128)(2,1)S(1)} collective-permute-done((bf16[256,1536]{1,0:T(8,128)(2,1)S(1)}, bf16[256,1536]{1,0:T(8,128)(2,1)S(1)}, u32[]{:S(2)}, u32[]{:S(2)}) %collective-permute-start.38) | collective-permute-done | bytes 786464 | tf_op jit(solution)/shard_map/ppermute | solution.py:56
  147.0 27.5 %collective-permute-done.42.refs_5_ = bf16[256,1152]{1,0:T(8,128)(2,1)} collective-permute-done((bf16[256,1152]{1,0:T(8,128)(2,1)}, bf16[256,1152]{1,0:T(8,128)(2,1)}, u32[]{:S(2)}, u32[]{:S(2)}) %collective-permute-start.42) | collective-permute-done | bytes 589856 | tf_op jit(solution)/shard_map/ppermute | solution.py:56
  178.4 25.3 %shard_map.198 = (f32[512,1024]{1,0:T(8,128)}, bf16[512,1024]{1,0:T(8,128)(2,1)}, f32[512,1024]{1,0:T(8,128)}, bf16[512,1024]{1,0:T(8,128)(2,1)}, bf16[256,1536]...) custom-call(bf16[512,1024]{1,0:T(8,128)(2,1)} %copy-done.24, ...), custom_call_target="tpu_custom_call" | custom-call | flops 19327352832 | bytes 16777216 | tf_op jit(solution)/shard_map/pallas_call | solution.py:531
  207.9 12.9 %shard_map.199 = (f32[512,1024]{1,0:T(8,128)}, bf16[512,1024]{1,0:T(8,128)(2,1)}, f32[512,1024]{1,0:T(8,128)}, bf16[512,1024]{1,0:T(8,128)(2,1)}, bf16[256,1152]...) custom-call(bf16[512,1024]{1,0:T(8,128)(2,1)} %copy-done.24, ...), custom_call_target="tpu_custom_call" | custom-call | flops 7247757312 | bytes 8912896 | tf_op jit(solution)/shard_map/pallas_call | solution.py:531
  220.8 3.8 collective-permute-done.54
  226.3 11.8 %collective-permute-done.53 = bf16[256,1536]{1,0:T(8,128)(2,1)} collective-permute-done((bf16[256,1536]{1,0:T(8,128)(2,1)}, bf16[256,1536]{1,0:T(8,128)(2,1)}, u32[]{:S(2)}, u32[]{:S(2)}) %collective-permute-start.53) | collective-permute-done | bytes 786464 | tf_op jit(solution)/shard_map/ppermute | solution.py:56
  244.6 3.6 fusion.33
  249.3 2.6 fusion.25
  252.0 21.4 %collective-permute-done.60 = bf16[256,1152]{1,0:T(8,128)(2,1)S(1)} collective-permute-done((bf16[256,1152]{1,0:T(8,128)(2,1)S(1)}, bf16[256,1152]{1,0:T(8,128)(2,1)S(1)}, u32[]{:S(2)}, u32[]{:S(2)}) %collective-permute-start.60) | collective-permute-done | bytes 589856 | tf_op jit(solution)/shard_map/ppermute | solution.py:56
  280.4 6.0 %collective-permute-done.58 = bf16[128,1536]{1,0:T(8,128)(2,1)S(1)} collective-permute-done((bf16[128,1536]{1,0:T(8,128)(2,1)S(1)}, bf16[128,1536]{1,0:T(8,128)(2,1)S(1)}, u32[]{:S(2)}, u32[]{:S(2)}) %collective-permute-start.58) | collective-permute-done | bytes 393248 | tf_op jit(solution)/shard_map/ppermute | solution.py:56
  290.6 7.3 %shard_map.200 = (f32[1024,512]{1,0:T(8,128)}, bf16[1024,512]{1,0:T(8,128)(2,1)}, f32[8,1024]{1,0:T(8,128)}) custom-call(bf16[512,1024]{1,0:T(8,128)(2,1)} %copy-done.6, bf16[512,1024]{1,0:T(8,128)(2,1)} %copy-done.15, f32[1024,512]{1,0:T(8,128)} %get-tuple-element.158.o_ref, f32[1024,1]{1,0:T(8,128)} %get-tuple-element.193.scale_ref, ...), custom_call_target="tpu_custom_call" | custom-call | flops 1073741824 | bytes 8388608 | tf_op jit(solution)/shard_map/pallas_call | solution.py:307
  297.9 3.8 shard_map.205
  301.8 3.9 shard_map.204
  306.7 12.8 %shard_map.201 = (bf16[1024,512]{1,0:T(8,128)(2,1)}, bf16[1024,512]{1,0:T(8,128)(2,1)}, bf16[1024,512]{1,0:T(8,128)(2,1)}) custom-call(s32[1]{0:T(128)} %bitcast.1.turn_ref, f32[4]{0:T(128)} %rate_ref.3, f32[1024,1]{1,0:T(8,128)} %get-tuple-element.193.scale_ref, f32[8,1024]{1,0:T(8,128)} %get-tuple-element.194.cross_ref, f32[8,1024]{1,0:T(8,128)} %copy-done.89, ...), custom_call_target="tpu_custom_call" | custom-call | flops 6442450944 | bytes 28311552 | tf_op jit(solution)/shard_map/pallas_call | solution.py:384
  319.5 6.7 %shard_map.203 = (bf16[256,512]{1,0:T(8,128)(2,1)}, bf16[256,512]{1,0:T(8,128)(2,1)}, bf16[256,512]{1,0:T(8,128)(2,1)}, bf16[256,512]{1,0:T(8,128)(2,1)}, bf16[2...) custom-call(bf16[512,1024]{1,0:T(8,128)(2,1)} %copy-done.7, ...), custom_call_target="tpu_custom_call" | custom-call | flops 3221225472 | bytes 8388608 | tf_op jit(solution)/shard_map/pallas_call | solution.py:412
  326.2 9.5 %shard_map.202 = (f32[512,1024]{1,0:T(8,128)}, bf16[512,1024]{1,0:T(8,128)(2,1)}) custom-call(bf16[1024,512]{1,0:T(8,128)(2,1)} %get-tuple-element.201.refs_0_, bf16[1024,512]{1,0:T(8,128)(2,1)} %get-tuple-element.202.refs_1_, bf16[1024,512]{1,0:T(8,128)(2,1)} %get-tuple-element.203.refs_2_, bf16[1024,512]{1,0:T(8,128)(2,1)} %get-tuple-element.204.refs_3_.refs_0_, ...), custom_call_target="tpu_custom_call" | custom-call | flops 4294967296 | bytes 12582912 | tf_op jit(solution)/shard_map/pallas_call | solution.py:434
  346.9 6.3 %collective-permute-done.62 = bf16[64,1536]{1,0:T(8,128)(2,1)S(1)} collective-permute-done((bf16[64,1536]{1,0:T(8,128)(2,1)S(1)}, bf16[64,1536]{1,0:T(8,128)(2,1)S(1)}, u32[]{:S(2)}, u32[]{:S(2)}) %collective-permute-start.62) | collective-permute-done | bytes 196640 | tf_op jit(solution)/shard_map/ppermute | solution.py:56
  358.5 5.6 %collective-permute-done.75 = bf16[64,1152]{1,0:T(8,128)(2,1)S(1)} collective-permute-done((bf16[64,1152]{1,0:T(8,128)(2,1)S(1)}, bf16[64,1152]{1,0:T(8,128)(2,1)S(1)}, u32[]{:S(2)}, u32[]{:S(2)}) %collective-permute-start.75) | collective-permute-done | bytes 147488 | tf_op jit(solution)/shard_map/ppermute | solution.py:56
  371.0 2.5 collective-permute-done.76
  374.4 2.2 collective-permute-done.71
  384.9 3.0 add_add_fusion
  388.0 2.6 collective-permute-start.85
  394.0 2.9 collective-permute-done.78
  398.2 5.2 %collective-permute-done.81 = bf16[128,512]{1,0:T(8,128)(2,1)S(1)} collective-permute-done((bf16[128,512]{1,0:T(8,128)(2,1)S(1)}, bf16[128,512]{1,0:T(8,128)(2,1)S(1)}, u32[]{:S(2)}, u32[]{:S(2)}) %collective-permute-start.81) | collective-permute-done | bytes 131104 | tf_op jit(solution)/shard_map/ppermute | solution.py:56
  403.4 2.4 collective-permute-start.86
  405.8 4.7 %collective-permute-done.82 = bf16[128,512]{1,0:T(8,128)(2,1)S(1)} collective-permute-done((bf16[128,512]{1,0:T(8,128)(2,1)S(1)}, bf16[128,512]{1,0:T(8,128)(2,1)S(1)}, u32[]{:S(2)}, u32[]{:S(2)}) %collective-permute-start.82) | collective-permute-done | bytes 131104 | tf_op jit(solution)/shard_map/ppermute | solution.py:56
  413.5 4.0 collective-permute-done.87
  418.5 2.2 collective-permute-start.89
  420.7 3.2 collective-permute-done.90
  426.5 2.7 collective-permute-done.91
  (435 shorter events, 130.2 us)
Async XLA Ops:
  0.7 14.2 %collective-permute-start.1 = (bf16[64,512]{1,0:T(8,128)(2,1)}, bf16[64,512]{1,0:T(8,128)(2,1)S(1)}, u32[]{:S(2)}, u32[]{:S(2)}) collective-permute-start(bf16[64,512]{1,0:T(8,128)(2,1)} %param.13), channel_id=1, source_target_pairs={{0,16},{2,18},{4,20},{6,22},{8,24},{10,26},{12,28},{14,30},{16,0},... | collective-permute-start | bytes 196616 | tf_op jit(solution)/shard_map/ppermute | solution.py:56
  47.7 27.7 %collective-permute-start = (bf16[512,1024]{1,0:T(8,128)(2,1)S(1)}, bf16[512,1024]{1,0:T(8,128)(2,1)S(1)}, u32[]{:S(2)}, u32[]{:S(2)}) collective-permute-start(bf16[512,1024]{1,0:T(8,128)(2,1)S(1)} %fusion.10.own_ref), channel_id=1, source_target_pairs={{0,1},{1,0},{2,3},{3,2},{4,5},{5,4},{6,7},{7,6},{8,9},{9,8},{10,11... | collective-permute-start | bytes 3145736 | tf_op jit(solution)/shard_map/ppermute | solution.py:581
  59.8 12.1 %collective-permute-start.20 = (bf16[256,512]{1,0:T(8,128)(2,1)}, bf16[256,512]{1,0:T(8,128)(2,1)}, u32[]{:S(2)}, u32[]{:S(2)}) collective-permute-start(bf16[256,512]{1,0:T(8,128)(2,1)} %constant_dynamic-update-slice_fusion.9.w0.refs_16_), channel_id=1, source_target_pairs={{0,4},{2,6},{4,0},{6,2},{8,12},{10,14},{12,8},{14,10},{16,20},{18,... | collective-permute-start | bytes 786440 | tf_op jit(solution)/shard_map/ppermute | solution.py:56
  71.6 31.0 %collective-permute-start.33 = (bf16[64,1536]{1,0:T(8,128)(2,1)}, bf16[64,1536]{1,0:T(8,128)(2,1)}, u32[]{:S(2)}, u32[]{:S(2)}) collective-permute-start(bf16[64,1536]{1,0:T(8,128)(2,1)} %pad_maximum_fusion.10), channel_id=1, source_target_pairs={{0,16},{2,18},{4,20},{6,22},{8,24},{10,26},{12,28},{14,30},{16,0},... | collective-permute-start | bytes 589832 | tf_op jit(solution)/shard_map/ppermute | solution.py:56
  72.0 33.0 %collective-permute-start.31 = (bf16[128,1536]{1,0:T(8,128)(2,1)}, bf16[128,1536]{1,0:T(8,128)(2,1)}, u32[]{:S(2)}, u32[]{:S(2)}) collective-permute-start(bf16[128,1536]{1,0:T(8,128)(2,1)} %pad_maximum_fusion.3), channel_id=1, source_target_pairs={{0,8},{2,10},{4,12},{6,14},{8,0},{10,2},{12,4},{14,6},{16,24},{18,... | collective-permute-start | bytes 1179656 | tf_op jit(solution)/shard_map/ppermute | solution.py:56
  72.0 23.6 %collective-permute-start.25 = (bf16[256,512]{1,0:T(8,128)(2,1)S(1)}, bf16[256,512]{1,0:T(8,128)(2,1)}, u32[]{:S(2)}, u32[]{:S(2)}) collective-permute-start(bf16[256,512]{1,0:T(8,128)(2,1)S(1)} %pad_maximum_fusion.8.w0), channel_id=1, source_target_pairs={{0,4},{2,6},{4,0},{6,2},{8,12},{10,14},{12,8},{14,10},{16,20},{18,... | collective-permute-start | bytes 786440 | tf_op jit(solution)/shard_map/ppermute | solution.py:56
  73.5 17.5 %collective-permute-start.22 = (bf16[256,512]{1,0:T(8,128)(2,1)}, bf16[256,512]{1,0:T(8,128)(2,1)}, u32[]{:S(2)}, u32[]{:S(2)}) collective-permute-start(bf16[256,512]{1,0:T(8,128)(2,1)} %collective-permute-done.20.w2.refs_18_), channel_id=1, source_target_pairs={{0,2},{2,0},{4,6},{6,4},{8,10},{10,8},{12,14},{14,12},{16,18},{18,... | collective-permute-start | bytes 786440 | tf_op jit(solution)/shard_map/ppermute | solution.py:56
  75.4 20.2 %collective-permute-start.27 = (bf16[256,512]{1,0:T(8,128)(2,1)}, bf16[256,512]{1,0:T(8,128)(2,1)S(1)}, u32[]{:S(2)}, u32[]{:S(2)}) collective-permute-start(bf16[256,512]{1,0:T(8,128)(2,1)} %collective-permute-done.24.w1), channel_id=1, source_target_pairs={{0,4},{2,6},{4,0},{6,2},{8,12},{10,14},{12,8},{14,10},{16,20},{18,... | collective-permute-start | bytes 786440 | tf_op jit(solution)/shard_map/ppermute | solution.py:56
  102.1 19.0 %collective-permute-start.28 = (bf16[512,1024]{1,0:T(8,128)(2,1)}, bf16[512,1024]{1,0:T(8,128)(2,1)S(1)}, u32[]{:S(2)}, u32[]{:S(2)}) collective-permute-start(bf16[512,1024]{1,0:T(8,128)(2,1)} %get-tuple-element.170), channel_id=1, source_target_pairs={{0,1},{1,0},{2,3},{3,2},{4,5},{5,4},{6,7},{7,6},{8,9},{9,8},{10,11... | collective-permute-start | bytes 3145736 | tf_op jit(solution)/shard_map/ppermute | solution.py:581
  105.0 13.9 %collective-permute-start.37 = (bf16[128,1536]{1,0:T(8,128)(2,1)S(1)}, bf16[128,1536]{1,0:T(8,128)(2,1)S(1)}, u32[]{:S(2)}, u32[]{:S(2)}) collective-permute-start(bf16[128,1536]{1,0:T(8,128)(2,1)S(1)} %pad_maximum_fusion.4), channel_id=1, source_target_pairs={{0,8},{2,10},{4,12},{6,14},{8,0},{10,2},{12,4},{14,6},{16,24},{18,... | collective-permute-start | bytes 1179656 | tf_op jit(solution)/shard_map/ppermute | solution.py:56
  106.3 20.5 %collective-permute-start.34 = (bf16[256,1536]{1,0:T(8,128)(2,1)S(1)}, bf16[256,1536]{1,0:T(8,128)(2,1)S(1)}, u32[]{:S(2)}, u32[]{:S(2)}) collective-permute-start(bf16[256,1536]{1,0:T(8,128)(2,1)S(1)} %pad_maximum_fusion.refs_4_), channel_id=1, source_target_pairs={{0,4},{2,6},{4,0},{6,2},{8,12},{10,14},{12,8},{14,10},{16,20},{18,... | collective-permute-start | bytes 2359304 | tf_op jit(solution)/shard_map/ppermute | solution.py:56
  107.2 20.4 %collective-permute-start.32 = (bf16[256,1536]{1,0:T(8,128)(2,1)S(1)}, bf16[256,1536]{1,0:T(8,128)(2,1)S(1)}, u32[]{:S(2)}, u32[]{:S(2)}) collective-permute-start(bf16[256,1536]{1,0:T(8,128)(2,1)S(1)} %pad_maximum_fusion.refs_4_), channel_id=1, source_target_pairs={{0,2},{2,0},{4,6},{6,4},{8,10},{10,8},{12,14},{14,12},{16,18},{18,... | collective-permute-start | bytes 2359304 | tf_op jit(solution)/shard_map/ppermute | solution.py:56
  119.9 23.1 %collective-permute-start.38 = (bf16[256,1536]{1,0:T(8,128)(2,1)S(1)}, bf16[256,1536]{1,0:T(8,128)(2,1)S(1)}, u32[]{:S(2)}, u32[]{:S(2)}) collective-permute-start(bf16[256,1536]{1,0:T(8,128)(2,1)S(1)} %pad_maximum_fusion.1.refs_8_), channel_id=1, source_target_pairs={{0,2},{2,0},{4,6},{6,4},{8,10},{10,8},{12,14},{14,12},{16,18},{18,... | collective-permute-start | bytes 2359304 | tf_op jit(solution)/shard_map/ppermute | solution.py:56
  120.1 24.0 %collective-permute-start.39 = (bf16[256,1536]{1,0:T(8,128)(2,1)S(1)}, bf16[256,1536]{1,0:T(8,128)(2,1)S(1)}, u32[]{:S(2)}, u32[]{:S(2)}) collective-permute-start(bf16[256,1536]{1,0:T(8,128)(2,1)S(1)} %pad_maximum_fusion.1.refs_8_), channel_id=1, source_target_pairs={{0,4},{2,6},{4,0},{6,2},{8,12},{10,14},{12,8},{14,10},{16,20},{18,... | collective-permute-start | bytes 2359304 | tf_op jit(solution)/shard_map/ppermute | solution.py:56
  121.1 24.7 %collective-permute-start.41 = (bf16[128,1152]{1,0:T(8,128)(2,1)S(1)}, bf16[128,1152]{1,0:T(8,128)(2,1)S(1)}, u32[]{:S(2)}, u32[]{:S(2)}) collective-permute-start(bf16[128,1152]{1,0:T(8,128)(2,1)S(1)} %pad_maximum_fusion.7), channel_id=1, source_target_pairs={{0,8},{2,10},{4,12},{6,14},{8,0},{10,2},{12,4},{14,6},{16,24},{18,... | collective-permute-start | bytes 884744 | tf_op jit(solution)/shard_map/ppermute | solution.py:56
  126.8 49.8 %collective-permute-start.30 = (bf16[512,1024]{1,0:T(8,128)(2,1)S(1)}, bf16[512,1024]{1,0:T(8,128)(2,1)S(1)}, u32[]{:S(2)}, u32[]{:S(2)}) collective-permute-start(bf16[512,1024]{1,0:T(8,128)(2,1)S(1)} %copy-done.13), channel_id=1, source_target_pairs={{0,1},{1,0},{2,3},{3,2},{4,5},{5,4},{6,7},{7,6},{8,9},{9,8},{10,11... | collective-permute-start | bytes 3145736 | tf_op jit(solution)/shard_map/ppermute | solution.py:581
  127.7 50.8 %collective-permute-start.29 = (bf16[512,1024]{1,0:T(8,128)(2,1)S(1)}, bf16[512,1024]{1,0:T(8,128)(2,1)}, u32[]{:S(2)}, u32[]{:S(2)}) collective-permute-start(bf16[512,1024]{1,0:T(8,128)(2,1)S(1)} %multiply_convert_fusion.refs_0_), channel_id=1, source_target_pairs={{0,1},{1,0},{2,3},{3,2},{4,5},{5,4},{6,7},{7,6},{8,9},{9,8},{10,11... | collective-permute-start | bytes 3145736 | tf_op jit(solution)/shard_map/ppermute | solution.py:581
  143.0 32.5 %collective-permute-start.36 = (bf16[256,1536]{1,0:T(8,128)(2,1)S(1)}, bf16[256,1536]{1,0:T(8,128)(2,1)S(1)}, u32[]{:S(2)}, u32[]{:S(2)}) collective-permute-start(bf16[256,1536]{1,0:T(8,128)(2,1)S(1)} %collective-permute-done.32.refs_5_), channel_id=1, source_target_pairs={{0,4},{2,6},{4,0},{6,2},{8,12},{10,14},{12,8},{14,10},{16,20},{18,... | collective-permute-start | bytes 2359304 | tf_op jit(solution)/shard_map/ppermute | solution.py:56
  144.1 32.5 %collective-permute-start.40 = (bf16[256,1536]{1,0:T(8,128)(2,1)S(1)}, bf16[256,1536]{1,0:T(8,128)(2,1)S(1)}, u32[]{:S(2)}, u32[]{:S(2)}) collective-permute-start(bf16[256,1536]{1,0:T(8,128)(2,1)S(1)} %collective-permute-done.39.refs_10_), channel_id=1, source_target_pairs={{0,2},{2,0},{4,6},{6,4},{8,10},{10,8},{12,14},{14,12},{16,18},{18,... | collective-permute-start | bytes 2359304 | tf_op jit(solution)/shard_map/ppermute | solution.py:56
  146.7 27.8 %collective-permute-start.42 = (bf16[256,1152]{1,0:T(8,128)(2,1)}, bf16[256,1152]{1,0:T(8,128)(2,1)}, u32[]{:S(2)}, u32[]{:S(2)}) collective-permute-start(bf16[256,1152]{1,0:T(8,128)(2,1)} %pad_maximum_fusion.2.refs_4_), channel_id=1, source_target_pairs={{0,2},{2,0},{4,6},{6,4},{8,10},{10,8},{12,14},{14,12},{16,18},{18,... | collective-permute-start | bytes 1769480 | tf_op jit(solution)/shard_map/ppermute | solution.py:56
  174.5 29.2 %collective-permute-start.43 = (bf16[256,1152]{1,0:T(8,128)(2,1)}, bf16[256,1152]{1,0:T(8,128)(2,1)}, u32[]{:S(2)}, u32[]{:S(2)}) collective-permute-start(bf16[256,1152]{1,0:T(8,128)(2,1)} %pad_maximum_fusion.2.refs_4_), channel_id=1, source_target_pairs={{0,4},{2,6},{4,0},{6,2},{8,12},{10,14},{12,8},{14,10},{16,20},{18,... | collective-permute-start | bytes 1769480 | tf_op jit(solution)/shard_map/ppermute | solution.py:56
  175.6 30.8 %collective-permute-start.44 = (bf16[256,1152]{1,0:T(8,128)(2,1)}, bf16[256,1152]{1,0:T(8,128)(2,1)}, u32[]{:S(2)}, u32[]{:S(2)}) collective-permute-start(bf16[256,1152]{1,0:T(8,128)(2,1)} %collective-permute-done.42.refs_5_), channel_id=1, source_target_pairs={{0,4},{2,6},{4,0},{6,2},{8,12},{10,14},{12,8},{14,10},{16,20},{18,... | collective-permute-start | bytes 1769480 | tf_op jit(solution)/shard_map/ppermute | solution.py:56
  203.8 20.8 %collective-permute-start.54 = (bf16[256,1536]{1,0:T(8,128)(2,1)}, bf16[256,1536]{1,0:T(8,128)(2,1)}, u32[]{:S(2)}, u32[]{:S(2)}) collective-permute-start(bf16[256,1536]{1,0:T(8,128)(2,1)} %get-tuple-element.217), channel_id=1, source_target_pairs={{0,4},{2,6},{4,0},{6,2},{8,12},{10,14},{12,8},{14,10},{16,20},{18,... | collective-permute-start | bytes 2359304 | tf_op jit(solution)/shard_map/ppermute | solution.py:56
  204.9 69.5 %collective-permute-start.52 = (bf16[256,1536]{1,0:T(8,128)(2,1)}, bf16[256,1536]{1,0:T(8,128)(2,1)}, u32[]{:S(2)}, u32[]{:S(2)}) collective-permute-start(bf16[256,1536]{1,0:T(8,128)(2,1)} %get-tuple-element.212), channel_id=1, source_target_pairs={{0,2},{2,0},{4,6},{6,4},{8,10},{10,8},{12,14},{14,12},{16,18},{18,... | collective-permute-start | bytes 2359304 | tf_op jit(solution)/shard_map/ppermute | solution.py:56
  206.3 33.3 %collective-permute-start.56 = (bf16[256,1536]{1,0:T(8,128)(2,1)}, bf16[256,1536]{1,0:T(8,128)(2,1)}, u32[]{:S(2)}, u32[]{:S(2)}) collective-permute-start(bf16[256,1536]{1,0:T(8,128)(2,1)} %get-tuple-element.221), channel_id=1, source_target_pairs={{0,4},{2,6},{4,0},{6,2},{8,12},{10,14},{12,8},{14,10},{16,20},{18,... | collective-permute-start | bytes 2359304 | tf_op jit(solution)/shard_map/ppermute | solution.py:56
  207.4 30.7 %collective-permute-start.53 = (bf16[256,1536]{1,0:T(8,128)(2,1)}, bf16[256,1536]{1,0:T(8,128)(2,1)}, u32[]{:S(2)}, u32[]{:S(2)}) collective-permute-start(bf16[256,1536]{1,0:T(8,128)(2,1)} %get-tuple-element.215), channel_id=1, source_target_pairs={{0,2},{2,0},{4,6},{6,4},{8,10},{10,8},{12,14},{14,12},{16,18},{18,... | collective-permute-start | bytes 2359304 | tf_op jit(solution)/shard_map/ppermute | solution.py:56
  207.9 32.4 %collective-permute-start.47 = (bf16[512,1024]{1,0:T(8,128)(2,1)}, bf16[512,1024]{1,0:T(8,128)(2,1)}, u32[]{:S(2)}, u32[]{:S(2)}) collective-permute-start(bf16[512,1024]{1,0:T(8,128)(2,1)} %get-tuple-element.191), channel_id=1, source_target_pairs={{0,1},{1,0},{2,3},{3,2},{4,5},{5,4},{6,7},{7,6},{8,9},{9,8},{10,11... | collective-permute-start | bytes 3145736 | tf_op jit(solution)/shard_map/ppermute | solution.py:581
  224.6 16.9 %collective-permute-start.48 = (bf16[512,1024]{1,0:T(8,128)(2,1)}, bf16[512,1024]{1,0:T(8,128)(2,1)S(1)}, u32[]{:S(2)}, u32[]{:S(2)}) collective-permute-start(bf16[512,1024]{1,0:T(8,128)(2,1)} %get-tuple-element.192), channel_id=1, source_target_pairs={{0,1},{1,0},{2,3},{3,2},{4,5},{5,4},{6,7},{7,6},{8,9},{9,8},{10,11... | collective-permute-start | bytes 3145736 | tf_op jit(solution)/shard_map/ppermute | solution.py:581
  240.3 34.9 %collective-permute-start.57 = (bf16[256,1536]{1,0:T(8,128)(2,1)S(1)}, bf16[256,1536]{1,0:T(8,128)(2,1)S(1)}, u32[]{:S(2)}, u32[]{:S(2)}) collective-permute-start(bf16[256,1536]{1,0:T(8,128)(2,1)S(1)} %add_convert_fusion.1), channel_id=1, source_target_pairs={{0,2},{2,0},{4,6},{6,4},{8,10},{10,8},{12,14},{14,12},{16,18},{18,... | collective-permute-start | bytes 2359304 | tf_op jit(solution)/shard_map/ppermute | solution.py:56
  241.5 36.5 %collective-permute-start.55 = (bf16[256,1536]{1,0:T(8,128)(2,1)S(1)}, bf16[256,1536]{1,0:T(8,128)(2,1)S(1)}, u32[]{:S(2)}, u32[]{:S(2)}) collective-permute-start(bf16[256,1536]{1,0:T(8,128)(2,1)S(1)} %add_convert_fusion.2), channel_id=1, source_target_pairs={{0,4},{2,6},{4,0},{6,2},{8,12},{10,14},{12,8},{14,10},{16,20},{18,... | collective-permute-start | bytes 2359304 | tf_op jit(solution)/shard_map/ppermute | solution.py:56
  248.3 25.1 %collective-permute-start.60 = (bf16[256,1152]{1,0:T(8,128)(2,1)S(1)}, bf16[256,1152]{1,0:T(8,128)(2,1)S(1)}, u32[]{:S(2)}, u32[]{:S(2)}) collective-permute-start(bf16[256,1152]{1,0:T(8,128)(2,1)S(1)} %copy-done.71), channel_id=1, source_target_pairs={{0,4},{2,6},{4,0},{6,2},{8,12},{10,14},{12,8},{14,10},{16,20},{18,... | collective-permute-start | bytes 1769480 | tf_op jit(solution)/shard_map/ppermute | solution.py:56
  249.3 40.2 %collective-permute-start.49 = (bf16[512,1024]{1,0:T(8,128)(2,1)S(1)}, bf16[512,1024]{1,0:T(8,128)(2,1)S(1)}, u32[]{:S(2)}, u32[]{:S(2)}) collective-permute-start(bf16[512,1024]{1,0:T(8,128)(2,1)S(1)} %get-tuple-element.280.own_ref), channel_id=1, source_target_pairs={{0,1},{1,0},{2,3},{3,2},{4,5},{5,4},{6,7},{7,6},{8,9},{9,8},{10,11... | collective-permute-start | bytes 3145736 | tf_op jit(solution)/shard_map/ppermute | solution.py:581
  274.3 61.3 %collective-permute-start.63 = (bf16[256,1152]{1,0:T(8,128)(2,1)}, bf16[256,1152]{1,0:T(8,128)(2,1)}, u32[]{:S(2)}, u32[]{:S(2)}) collective-permute-start(bf16[256,1152]{1,0:T(8,128)(2,1)} %add_convert_fusion.3), channel_id=1, source_target_pairs={{0,2},{2,0},{4,6},{6,4},{8,10},{10,8},{12,14},{14,12},{16,18},{18,... | collective-permute-start | bytes 1769480 | tf_op jit(solution)/shard_map/ppermute | solution.py:56
  279.4 56.6 %collective-permute-start.66 = (bf16[256,1152]{1,0:T(8,128)(2,1)}, bf16[256,1152]{1,0:T(8,128)(2,1)}, u32[]{:S(2)}, u32[]{:S(2)}) collective-permute-start(bf16[256,1152]{1,0:T(8,128)(2,1)} %get-tuple-element.239), channel_id=1, source_target_pairs={{0,4},{2,6},{4,0},{6,2},{8,12},{10,14},{12,8},{14,10},{16,20},{18,... | collective-permute-start | bytes 1769480 | tf_op jit(solution)/shard_map/ppermute | solution.py:56
  286.6 51.1 %collective-permute-start.61 = (bf16[64,1536]{1,0:T(8,128)(2,1)S(1)}, bf16[64,1536]{1,0:T(8,128)(2,1)S(1)}, u32[]{:S(2)}, u32[]{:S(2)}) collective-permute-start(bf16[64,1536]{1,0:T(8,128)(2,1)S(1)} %slice.297), channel_id=1, source_target_pairs={{0,16},{2,18},{4,20},{6,22},{8,24},{10,26},{12,28},{14,30},{16,0},... | collective-permute-start | bytes 589832 | tf_op jit(solution)/shard_map/ppermute | solution.py:56
  288.0 52.0 %collective-permute-start.59 = (bf16[128,1536]{1,0:T(8,128)(2,1)S(1)}, bf16[128,1536]{1,0:T(8,128)(2,1)}, u32[]{:S(2)}, u32[]{:S(2)}) collective-permute-start(bf16[128,1536]{1,0:T(8,128)(2,1)S(1)} %slice.295), channel_id=1, source_target_pairs={{0,8},{2,10},{4,12},{6,14},{8,0},{10,2},{12,4},{14,6},{16,24},{18,... | collective-permute-start | bytes 1179656 | tf_op jit(solution)/shard_map/ppermute | solution.py:56
  305.6 38.3 %collective-permute-start.65 = (bf16[256,512]{1,0:T(8,128)(2,1)}, bf16[256,512]{1,0:T(8,128)(2,1)}, u32[]{:S(2)}, u32[]{:S(2)}) collective-permute-start(bf16[256,512]{1,0:T(8,128)(2,1)} %get-tuple-element.236), channel_id=1, source_target_pairs={{0,4},{2,6},{4,0},{6,2},{8,12},{10,14},{12,8},{14,10},{16,20},{18,... | collective-permute-start | bytes 786440 | tf_op jit(solution)/shard_map/ppermute | solution.py:56
  335.7 43.4 %collective-permute-start.51 = (bf16[512,1024]{1,0:T(8,128)(2,1)}, bf16[512,1024]{1,0:T(8,128)(2,1)S(1)}, u32[]{:S(2)}, u32[]{:S(2)}) collective-permute-start(bf16[512,1024]{1,0:T(8,128)(2,1)} %get-tuple-element.206), channel_id=1, source_target_pairs={{0,1},{1,0},{2,3},{3,2},{4,5},{5,4},{6,7},{7,6},{8,9},{9,8},{10,11... | collective-permute-start | bytes 3145736 | tf_op jit(solution)/shard_map/ppermute | solution.py:581
  341.2 12.0 %collective-permute-start.62 = (bf16[64,1536]{1,0:T(8,128)(2,1)S(1)}, bf16[64,1536]{1,0:T(8,128)(2,1)S(1)}, u32[]{:S(2)}, u32[]{:S(2)}) collective-permute-start(bf16[64,1536]{1,0:T(8,128)(2,1)S(1)} %slice.298), channel_id=1, source_target_pairs={{0,16},{2,18},{4,20},{6,22},{8,24},{10,26},{12,28},{14,30},{16,0},... | collective-permute-start | bytes 589832 | tf_op jit(solution)/shard_map/ppermute | solution.py:56
  342.4 12.8 %collective-permute-start.74 = (bf16[128,1152]{1,0:T(8,128)(2,1)S(1)}, bf16[128,1152]{1,0:T(8,128)(2,1)S(1)}, u32[]{:S(2)}, u32[]{:S(2)}) collective-permute-start(bf16[128,1152]{1,0:T(8,128)(2,1)S(1)} %slice.296), channel_id=1, source_target_pairs={{0,8},{2,10},{4,12},{6,14},{8,0},{10,2},{12,4},{14,6},{16,24},{18,... | collective-permute-start | bytes 884744 | tf_op jit(solution)/shard_map/ppermute | solution.py:56
  343.9 12.2 %collective-permute-start.67 = (bf16[256,512]{1,0:T(8,128)(2,1)S(1)}, bf16[256,512]{1,0:T(8,128)(2,1)S(1)}, u32[]{:S(2)}, u32[]{:S(2)}) collective-permute-start(bf16[256,512]{1,0:T(8,128)(2,1)S(1)} %copy-done.87), channel_id=1, source_target_pairs={{0,4},{2,6},{4,0},{6,2},{8,12},{10,14},{12,8},{14,10},{16,20},{18,... | collective-permute-start | bytes 786440 | tf_op jit(solution)/shard_map/ppermute | solution.py:56
  353.2 14.1 %collective-permute-start.64 = (bf16[256,512]{1,0:T(8,128)(2,1)S(1)}, bf16[256,512]{1,0:T(8,128)(2,1)S(1)}, u32[]{:S(2)}, u32[]{:S(2)}) collective-permute-start(bf16[256,512]{1,0:T(8,128)(2,1)S(1)} %copy-done.85), channel_id=1, source_target_pairs={{0,2},{2,0},{4,6},{6,4},{8,10},{10,8},{12,14},{14,12},{16,18},{18,... | collective-permute-start | bytes 786440 | tf_op jit(solution)/shard_map/ppermute | solution.py:56
  356.1 13.0 %collective-permute-start.68 = (bf16[256,512]{1,0:T(8,128)(2,1)S(1)}, bf16[256,512]{1,0:T(8,128)(2,1)S(1)}, u32[]{:S(2)}, u32[]{:S(2)}) collective-permute-start(bf16[256,512]{1,0:T(8,128)(2,1)S(1)} %copy-done.86), channel_id=1, source_target_pairs={{0,4},{2,6},{4,0},{6,2},{8,12},{10,14},{12,8},{14,10},{16,20},{18,... | collective-permute-start | bytes 786440 | tf_op jit(solution)/shard_map/ppermute | solution.py:56
  357.2 12.9 %collective-permute-start.79 = (bf16[256,512]{1,0:T(8,128)(2,1)S(1)}, bf16[256,512]{1,0:T(8,128)(2,1)S(1)}, u32[]{:S(2)}, u32[]{:S(2)}) collective-permute-start(bf16[256,512]{1,0:T(8,128)(2,1)S(1)} %add_convert_fusion.6), channel_id=1, source_target_pairs={{0,2},{2,0},{4,6},{6,4},{8,10},{10,8},{12,14},{14,12},{16,18},{18,... | collective-permute-start | bytes 786440 | tf_op jit(solution)/shard_map/ppermute | solution.py:56
  370.3 17.7 %collective-permute-start.83 = (bf16[256,512]{1,0:T(8,128)(2,1)S(1)}, bf16[256,512]{1,0:T(8,128)(2,1)S(1)}, u32[]{:S(2)}, u32[]{:S(2)}) collective-permute-start(bf16[256,512]{1,0:T(8,128)(2,1)S(1)} %copy-done.82), channel_id=1, source_target_pairs={{0,2},{2,0},{4,6},{6,4},{8,10},{10,8},{12,14},{14,12},{16,18},{18,... | collective-permute-start | bytes 786440 | tf_op jit(solution)/shard_map/ppermute | solution.py:56
  373.4 17.1 %collective-permute-start.77 = (bf16[256,512]{1,0:T(8,128)(2,1)S(1)}, bf16[256,512]{1,0:T(8,128)(2,1)S(1)}, u32[]{:S(2)}, u32[]{:S(2)}) collective-permute-start(bf16[256,512]{1,0:T(8,128)(2,1)S(1)} %copy-done.81), channel_id=1, source_target_pairs={{0,4},{2,6},{4,0},{6,2},{8,12},{10,14},{12,8},{14,10},{16,20},{18,... | collective-permute-start | bytes 786440 | tf_op jit(solution)/shard_map/ppermute | solution.py:56
  376.6 16.4 %collective-permute-start.72 = (bf16[256,512]{1,0:T(8,128)(2,1)S(1)}, bf16[256,512]{1,0:T(8,128)(2,1)S(1)}, u32[]{:S(2)}, u32[]{:S(2)}) collective-permute-start(bf16[256,512]{1,0:T(8,128)(2,1)S(1)} %add_convert_fusion.9), channel_id=1, source_target_pairs={{0,2},{2,0},{4,6},{6,4},{8,10},{10,8},{12,14},{14,12},{16,18},{18,... | collective-permute-start | bytes 786440 | tf_op jit(solution)/shard_map/ppermute | solution.py:56
  379.1 14.8 %collective-permute-start.73 = (bf16[256,512]{1,0:T(8,128)(2,1)S(1)}, bf16[256,512]{1,0:T(8,128)(2,1)S(1)}, u32[]{:S(2)}, u32[]{:S(2)}) collective-permute-start(bf16[256,512]{1,0:T(8,128)(2,1)S(1)} %add_convert_fusion.8), channel_id=1, source_target_pairs={{0,4},{2,6},{4,0},{6,2},{8,12},{10,14},{12,8},{14,10},{16,20},{18,... | collective-permute-start | bytes 786440 | tf_op jit(solution)/shard_map/ppermute | solution.py:56
  (136 other events, 1581.7 us)

commit v4 on v3

v4 whole, which is shorter than its diff:
```python
import functools

import jax
import jax.numpy as jnp
import numpy as np
from jax import lax
from jax.experimental import pallas as pl
from jax.experimental.pallas import tpu as pltpu
from jax.sharding import PartitionSpec as P

eps = 1e-06
wide = jnp.float32
narrow = jnp.bfloat16
tile_width = 512


def dot(left, right, dims):
    return lax.dot_general(left, right, (dims, ((), ())), preferred_element_type=wide)


def nn(left, right):
    return dot(left, right, ((1,), (0,)))


def nt(left, right):
    return dot(left, right, ((1,), (1,)))


def tn(left, right):
    return dot(left, right, ((0,), (0,)))


def inverse_rms(values):
    return lax.rsqrt(jnp.mean(values * values, axis=-1, keepdims=True) + eps)


def norm_back(grad, normed, scale):
    return scale * (grad - normed * jnp.mean(grad * normed, axis=-1, keepdims=True))


class Exchange:

    def __init__(self, size):
        self.size = size
        self.before = {}

    def __call__(self, array, bit):
        if bit >= 4 and bit in self.before:
            (array,) = held_back((array,), self.before[bit])
        pairs = [(i, i ^ bit) for i in range(self.size)]
        result = lax.ppermute(array, "dp", pairs)
        self.before[bit] = result
        return result


def held_back(values, *waits):
    values = tuple(values)
    if not waits:
        return values
    return lax.optimization_barrier((*values, *waits))[: len(values)]


def inner_bits(size):
    bits = []
    bit = size // 2
    while bit >= 4:
        bits.append(bit)
        bit //= 2
    return bits


def block_offsets(size):
    order = [0]
    for bit in inner_bits(size) + [1, 2]:
        order = order + [entry ^ bit for entry in order]
    return np.array(order, np.int32)


class Gather:

    def __init__(self, send, shard):
        self.send = send
        self.parts = (shard,)

    def join(self, after):
        if after:
            self.parts = held_back(self.parts, *after)
        self.held = jnp.concatenate(self.parts, axis=0)

    def inner(self, level, *after):
        self.join(after)
        bit = inner_bits(self.send.size)[level]
        self.got = (self.send(self.held, bit),)
        self.parts = (self.held, *self.got)

    def rest(self, *after):
        for level in range(1, len(inner_bits(self.send.size))):
            self.inner(level, *after)

    def sides(self, *after):
        self.join(after)
        self.got = (self.send(self.held, 1), self.send(self.held, 2))

    def far(self, *after):
        half = self.held.shape[0] // 2
        side, up = held_back(self.got, *after)
        self.last = (self.send(side[:half], 2), self.send(up[half:], 1))
        self.pieces = [self.held, *self.got, *self.last]


def low(value):
    return value.astype(narrow)


def merge_kernel(up_ref, side_ref, to_up_ref, to_side_ref, up_out, side_out):
    up_out[...] = low(up_ref[...].astype(wide) + to_up_ref[...].astype(wide))
    side_out[...] = low(side_ref[...].astype(wide) + to_side_ref[...].astype(wide))


def merge(up, side, to_up, to_side):
    half = to_up.shape
    block = lambda i: pl.BlockSpec(half, lambda _: (i, 0))
    return pl.pallas_call(
        merge_kernel,
        grid=(1,),
        in_specs=[block(0), block(1), block(0), block(0)],
        out_specs=[block(0), block(1)],
        out_shape=[jax.ShapeDtypeStruct(a.shape, a.dtype) for a in (up, side)],
        input_output_aliases={0: 0, 1: 1},
        cost_estimate=cost(up.size, up, up, up),
    )(up, side, to_up, to_side)


class Scatter:

    def __init__(self, send, pieces):
        self.send = send
        self.first, self.side, self.up, *self.away = pieces
        self.moves = ["far", "sides", *reversed(inner_bits(send.size)), "end"]
        self.rest = None

    def move(self, *after):
        name = self.moves.pop(0)
        if name == "far":
            away = held_back(self.away, *after)
            self.got = tuple(self.send(a, b) for a, b in zip(away, (1, 2)))
            return
        if name == "sides":
            self.got = held_back(self.got, *after)
            self.sent = merge(self.up, self.side, *self.got)
            self.got = (self.send(self.sent[1], 1), self.send(self.sent[0], 2))
        elif name == "end":
            self.add(after)
        else:
            self.add(after)
            self.got = (self.send(self.split(), name),)

    def add(self, after):
        got = held_back(self.got, *after)
        rest = self.first.astype(wide) if self.rest is None else self.rest
        self.total = rest + sum(g.astype(wide) for g in got)

    def split(self):
        half = self.total.shape[0] // 2
        self.rest = self.total[:half]
        return low(self.total[half:])


def move_along(scatters, *after):
    name = scatters[0].moves[0]
    assert all(out.moves[0] == name for out in scatters)
    parts = []
    for out in scatters:
        out.moves.pop(0)
        out.add(after)
        parts.append(out.split())
    got = scatters[0].send(jnp.concatenate(parts, axis=1), name)
    at = 0
    for out, part in zip(scatters, parts):
        out.got = (got[:, at : at + part.shape[1]],)
        at += part.shape[1]


def tables(rate, size):
    row = lax.broadcasted_iota(jnp.int32, (size, 1), 0).astype(wide)
    col = lax.broadcasted_iota(jnp.int32, (1, size), 1).astype(wide)
    ahead = jnp.exp(-rate * row)
    inner = jnp.where(col <= row, ahead * jnp.exp(rate * col), 0.0)
    outof = jnp.exp(-rate * (size - row))
    return inner, ahead, outof


def cost(flops, *arrays):
    size = sum(a.size * jnp.dtype(a.dtype).itemsize for a in arrays)
    return pl.CostEstimate(flops=int(flops), transcendentals=0, bytes_accessed=int(size))


def rows_of(refs):
    half = refs[0].shape[0]
    return [(ref, slice(i * half, (i + 1) * half)) for i, ref in enumerate(refs)]


def join(refs):
    return jnp.concatenate([ref[...] for ref in refs], axis=0)


def row_sums(values):
    ones = jnp.ones((8, values.shape[1]), wide)
    return lax.dot_general(
        ones,
        values,
        (((1,), (1,)), ((), ())),
        precision=lax.Precision.HIGHEST,
        preferred_element_type=wide,
    )


def column(own, other):
    half = own.shape[1] // 2
    total = own + jnp.concatenate([other[:, half:], other[:, :half]], axis=1)
    return jnp.transpose(total)[:, :1]


def spans(turn_ref, size):
    turn = turn_ref[0]
    early = pl.ds(pl.multiple_of(turn * size, size), size)
    late = pl.ds(pl.multiple_of((1 - turn) * size, size), size)
    return early, late


def cumulative(refs):
    at = 0
    result = []
    for ref in refs:
        result.append((ref, slice(at, at + ref.shape[0])))
        at += ref.shape[0]
    return result


def whole(array):
    return pl.BlockSpec(array.shape, lambda i: (0, 0))


def columns_of(pieces, j, width):
    return [pl.BlockSpec((p.shape[0], width), lambda i: (0, j)) for p in pieces]


def front_kernel(turn_ref, rate_ref, own_ref, other_ref, *refs, heads):
    wq, wk, wv = refs[0:5], refs[5:10], refs[10:15]
    q_ref, k_ref, v_ref, sq_ref, sk_ref, o_ref, sum_ref = refs[15:]
    pair = rows_of((own_ref, other_ref))
    for pieces, out, slope in ((wq, q_ref, sq_ref), (wk, k_ref, sk_ref)):
        weight = join(pieces)
        for ref, rows in pair:
            value = nn(ref[...], weight)
            sigma = jax.nn.sigmoid(value)
            out[rows, :] = low(value * sigma)
            slope[rows, :] = low(sigma * (1.0 + value * (1.0 - sigma)))
    weight = join(wv)
    for ref, rows in pair:
        v_ref[rows, :] = low(nn(ref[...], weight))
    size = own_ref.shape[0]
    early, late = spans(turn_ref, size)
    wide_head = q_ref.shape[1] // heads
    sums = 0.0
    for j in range(heads):
        cols = slice(j * wide_head, (j + 1) * wide_head)
        inner, ahead, outof = tables(rate_ref[pl.program_id(0) * heads + j], size)

        def local(rows):
            weights = low(nt(q_ref[rows, cols], k_ref[rows, cols]) * inner)
            return nn(weights, v_ref[rows, cols])

        weighted = low(k_ref[early, cols].astype(wide) * outof)
        state = low(tn(weighted, v_ref[early, cols]))
        o_ref[early, cols] = local(early)
        o_ref[late, cols] = local(late) + nn(q_ref[late, cols], state) * ahead
    values = o_ref[...]
    sums = row_sums(values * values)

    @pl.when(pl.program_id(0) == 0)
    def _():
        sum_ref[...] = sums

    @pl.when(pl.program_id(0) > 0)
    def _():
        sum_ref[...] += sums


def front(turn, rates, pair, pieces):
    rows, width = pair[0].shape
    columns = pieces[0].shape[1] // 3
    steps = 2
    block = columns // steps
    scalar = pl.BlockSpec(memory_space=pltpu.SMEM)
    piece = lambda p, j: pl.BlockSpec((p.shape[0], block), lambda i: (0, i + steps * j))
    out = pl.BlockSpec((2 * rows, block), lambda i: (0, i))
    sums = jax.ShapeDtypeStruct((8, 2 * rows), wide)
    types = [narrow] * 5 + [wide]
    return pl.pallas_call(
        functools.partial(front_kernel, heads=rates.shape[0] // steps),
        cost_estimate=cost(18 * rows * width * columns, *pair, *pair, *pair, *pair, *pair),
        grid=(steps,),
        in_specs=[scalar, scalar]
        + [whole(p) for p in pair]
        + [piece(p, j) for j in range(3) for p in pieces],
        out_specs=[out] * 6 + [whole(sums)],
        out_shape=[jax.ShapeDtypeStruct((2 * rows, columns), t) for t in types] + [sums],
    )(turn, rates, *pair, *pieces, *pieces, *pieces)


def gate_kernel(own_ref, other_ref, *refs):
    weight = join(refs[:-1])
    for ref, rows in rows_of((own_ref, other_ref)):
        refs[-1][rows, :] = nn(ref[...], weight).astype(refs[-1].dtype)


def gate(pair, pieces):
    rows, width = pair[0].shape
    columns = pieces[0].shape[1] // 2
    out = jax.ShapeDtypeStruct((2 * rows, columns), wide)
    return pl.pallas_call(
        gate_kernel,
        cost_estimate=cost(4 * rows * width * columns, *pair, *pair),
        grid=(1,),
        in_specs=[whole(p) for p in pair] + columns_of(pieces, 0, columns),
        out_specs=whole(out),
        out_shape=out,
    )(*pair, *pieces)


def branch_kernel(sum_ref, got_ref, o_ref, u_ref, *refs):
    pieces, (gated_ref, scale_ref, own_ref, other_ref) = refs[:5], refs[5:]
    rows, width = own_ref.shape
    scale = lax.rsqrt(column(sum_ref[...], got_ref[...]) / width + eps)
    scale_ref[...] = scale
    gated_ref[...] = low(o_ref[...] * scale * u_ref[...])
    for ref, cols in cumulative(pieces):
        value = nt(gated_ref[...], ref[...])
        own_ref[:, cols] = value[:rows]
        other_ref[:, cols] = low(value[rows:])


def branch(sums, got, attended, proj_u, pieces):
    length, columns = attended.shape
    rows, width = length // 2, sum(p.shape[0] for p in pieces)
    ins = (sums, got, attended, proj_u)
    outs = [
        jax.ShapeDtypeStruct((length, columns), narrow),
        jax.ShapeDtypeStruct((length, 1), wide),
        jax.ShapeDtypeStruct((rows, width), wide),
        jax.ShapeDtypeStruct((rows, width), narrow),
    ]
    return pl.pallas_call(
        branch_kernel,
        cost_estimate=cost(2 * length * columns * width, attended, attended, attended, proj_u),
        grid=(1,),
        in_specs=[whole(a) for a in ins] + columns_of(pieces, 1, columns),
        out_specs=[whole(a) for a in outs],
        out_shape=outs,
    )(*ins, *pieces)


def unbranch_kernel(own_ref, other_ref, o_ref, scale_ref, u_ref, *refs):
    pieces, (grad_ref, unit_ref, cross_ref) = refs[:5], refs[5:]
    weight = join(pieces)
    for ref, rows in rows_of((own_ref, other_ref)):
        value = nn(ref[...], weight)
        normed = o_ref[rows, :] * scale_ref[rows, :]
        unit_ref[rows, :] = low(value * normed)
        value = value * u_ref[rows, :]
        grad_ref[rows, :] = value
        cross_ref[:, rows] = row_sums(value * normed)


def unbranch(pair, attended, scale, proj_u, pieces):
    length, columns = attended.shape
    width = pair[0].shape[1]
    ins = (*pair, attended, scale, proj_u)
    outs = [
        jax.ShapeDtypeStruct((length, columns), wide),
        jax.ShapeDtypeStruct((length, columns), narrow),
        jax.ShapeDtypeStruct((8, length), wide),
    ]
    return pl.pallas_call(
        unbranch_kernel,
        cost_estimate=cost(2 * length * columns * width, attended, attended, attended, proj_u),
        grid=(1,),
        in_specs=[whole(a) for a in ins] + columns_of(pieces, 1, columns),
        out_specs=[whole(a) for a in outs],
        out_shape=outs,
    )(*ins, *pieces)


def attend_back_kernel(
    turn_ref,
    rate_ref,
    scale_ref,
    cross_ref,
    got_ref,
    q_ref,
    k_ref,
    v_ref,
    sq_ref,
    sk_ref,
    gn_ref,
    o_ref,
    dq_ref,
    dk_ref,
    dv_ref,
    g_ref,
    c_ref,
    *,
    width,
):
    size = q_ref.shape[0] // 2
    inner, ahead, outof = tables(rate_ref[pl.program_id(0)], size)
    early, late = spans(turn_ref, size)

    @pl.when(pl.program_id(0) == 0)
    def _():
        c_ref[...] = column(cross_ref[...], got_ref[...]) / width

    scale = scale_ref[...]
    normed = o_ref[...] * scale
    g_ref[...] = low(scale * (gn_ref[...] - normed * c_ref[...]))

    def local(rows):
        q, k, v, g = (ref[rows, :] for ref in (q_ref, k_ref, v_ref, g_ref))
        weights = low(nt(q, k) * inner)
        grad_scores = low(nt(g, v) * inner)
        return nn(grad_scores, k), tn(grad_scores, q), tn(weights, g)

    def store(rows, dq, dk, dv):
        dq_ref[rows, :] = low(dq * sq_ref[rows, :].astype(wide))
        dk_ref[rows, :] = low(dk * sk_ref[rows, :].astype(wide))
        dv_ref[rows, :] = low(dv)

    weighted = low(k_ref[early, :].astype(wide) * outof)
    state = low(tn(weighted, v_ref[early, :]))
    g_ahead = low(g_ref[late, :].astype(wide) * ahead)
    grad_state = low(tn(q_ref[late, :], g_ahead))
    dq, dk, dv = local(late)
    store(late, dq + nt(g_ahead, state), dk, dv)
    dq, dk, dv = local(early)
    store(
        early,
        dq,
        dk + nt(v_ref[early, :], grad_state) * outof,
        dv + nn(weighted, grad_state),
    )


def attend_back(turn, rates, scale, cross, got, arrays, width):
    heads = rates.shape[0]
    length, columns = arrays[0].shape
    spec = pl.BlockSpec((length, columns // heads), lambda h: (0, h))
    col = pl.BlockSpec((length, 1), lambda h: (0, 0))
    row = pl.BlockSpec((8, length), lambda h: (0, 0))
    scalar = pl.BlockSpec(memory_space=pltpu.SMEM)
    return pl.pallas_call(
        functools.partial(attend_back_kernel, width=width),
        cost_estimate=cost(12 * length * length * columns, *arrays, *arrays, *arrays),
        grid=(heads,),
        in_specs=[scalar, scalar, col, row, row] + [spec] * len(arrays),
        out_specs=[spec] * 3,
        out_shape=[jax.ShapeDtypeStruct((length, columns), narrow)] * 3,
        scratch_shapes=[
            pltpu.VMEM((length, columns // heads), narrow),
            pltpu.VMEM((length, 1), wide),
        ],
    )(turn, rates, scale, cross, got, *arrays)


def weight_grad_kernel(*refs, count, each):
    pairs, refs = [refs[2 * j : 2 * j + 2] for j in range(each)], refs[2 * each :]
    arrays, outs = refs[:count], refs[count:]
    columns = arrays[0].shape[1]
    for out, cols in cumulative(outs):
        for j, array in enumerate(arrays):
            pair = rows_of(pairs[j % each])
            total = sum(tn(ref[:, cols], array[rows, :]) for ref, rows in pair)
            out[:, j * columns : (j + 1) * columns] = low(total)


def piece_rows(width):
    return [width // 4] * 3 + [width // 8] * 2


def weight_grads(pairs, arrays):
    rows, width = pairs[0][0].shape
    columns = arrays[0].shape[1]
    count = len(arrays)
    return pl.pallas_call(
        functools.partial(weight_grad_kernel, count=count, each=len(pairs)),
        cost_estimate=cost(4 * rows * width * columns * count, *pairs[0], *arrays, *arrays),
        out_shape=[
            jax.ShapeDtypeStruct((r, count * columns), narrow) for r in piece_rows(width)
        ],
    )(*(a for pair in pairs for a in pair), *arrays)


def input_grad_kernel(*refs):
    grads, refs, (own_ref, other_ref) = refs[:4], refs[4:24], refs[24:]
    pieces = [cumulative(refs[5 * j : 5 * j + 5]) for j in range(4)]
    rows = own_ref.shape[0]
    for i in range(5):
        cols = pieces[0][i][1]
        value = sum(nt(grads[j][...], pieces[j][i][0][...]) for j in range(4))
        own_ref[:, cols] = value[:rows]
        other_ref[:, cols] = low(value[rows:])


def input_grad(grads, first, second):
    length, columns = grads[0].shape
    rows, width = length // 2, sum(p.shape[0] for p in first)
    outs = [
        jax.ShapeDtypeStruct((rows, width), wide),
        jax.ShapeDtypeStruct((rows, width), narrow),
    ]
    return pl.pallas_call(
        input_grad_kernel,
        cost_estimate=cost(8 * length * columns * width, *grads, *grads, *grads),
        grid=(1,),
        in_specs=[whole(g) for g in grads]
        + [spec for j in range(3) for spec in columns_of(first, j, columns)]
        + columns_of(second, 0, columns),
        out_specs=[whole(a) for a in outs],
        out_shape=outs,
    )(*grads, *first, *first, *first, *second)


def ffn_kernel(*refs, chained, last):
    n_in, g_in, w_in = refs[0:2], refs[2:4], refs[4:9]
    refs = refs[9:]
    if chained:
        before, refs = refs[:4], refs[4:]
    sums_out, o_out = refs[0:4], refs[4:9]
    n_ref, g_ref, w_ref, s_ref, d_ref, acc_ref, low_ref, o_ref, in_sem, out_sem = refs[9:]
    rows = n_ref.shape[1]
    n = s_ref.shape[2]
    pieces = cumulative(w_in)

    load = [
        pltpu.make_async_copy(ref, w_ref.at[part, :], in_sem.at[4 + i])
        for i, (ref, part) in enumerate(pieces)
    ]
    load += [pltpu.make_async_copy(n_in[h], n_ref.at[h], in_sem.at[h]) for h in range(2)]
    load += [pltpu.make_async_copy(g_in[h], g_ref.at[h], in_sem.at[2 + h]) for h in range(2)]
    for copy in load:
        copy.start()
    accs = [acc_ref.at[k // 2, k % 2] for k in range(4)]
    fill = []
    if chained:
        fill = [pltpu.make_async_copy(before[k], accs[k], in_sem.at[9 + k]) for k in range(4)]
    for copy in fill:
        copy.start()
    for copy in load:
        copy.wait()

    def half(h, carry):
        ab = nn(n_ref[h], w_ref[:, : 2 * n])
        ds = nn(g_ref[h], w_ref[:, 2 * n :])
        a = ab[:, :n]
        b = ab[:, n:]
        s_ref[h] = low(a * b)
        d_ref[h, :, :n] = low(ds * b)
        d_ref[h, :, n:] = low(ds * a)
        return carry

    lax.fori_loop(0, 2, half, 0)
    for copy in fill:
        copy.wait()
    y = nt(s_ref[...].reshape(2 * rows, n), w_ref[:, 2 * n :]).reshape(2, rows, -1)
    d = nt(d_ref[...].reshape(2 * rows, 2 * n), w_ref[:, : 2 * n]).reshape(2, rows, -1)
    for k, value in enumerate((y, d)):
        if chained:
            acc_ref[k] += value
        else:
            acc_ref[k] = value
    stores = []
    for k in range(4):
        source = accs[k]
        if last and k % 2 == 1:
            low_ref[k // 2] = low(acc_ref[k // 2, 1])
            source = low_ref.at[k // 2]
        stores.append(pltpu.make_async_copy(source, sums_out[k], out_sem.at[k]))
        stores[-1].start()
    for i, (_, part) in reversed(list(enumerate(pieces))):
        o_ref[part, : 2 * n] = low(sum(tn(n_ref[h, :, part], d_ref[h]) for h in range(2)))
        o_ref[part, 2 * n :] = low(sum(tn(g_ref[h, :, part], s_ref[h]) for h in range(2)))
        stores.append(pltpu.make_async_copy(o_ref.at[part, :], o_out[i], out_sem.at[4 + i]))
        stores[-1].start()
    for copy in stores:
        copy.wait()


def ffn(normed, grad, pieces, sums, last):
    rows, width = normed[0].shape
    n3 = pieces[0].shape[1]
    n = n3 // 3
    hbm = pl.BlockSpec(memory_space=pl.ANY)
    ins = (*normed, *grad, *pieces, *(sums or ()))
    other = narrow if last else wide
    outs = pl.pallas_call(
        functools.partial(ffn_kernel, chained=sums is not None, last=last),
        cost_estimate=cost(12 * rows * width * n3, *ins, *ins),
        in_specs=[hbm] * len(ins),
        out_specs=[hbm] * 9,
        out_shape=[jax.ShapeDtypeStruct((rows, width), t) for t in (wide, other, wide, other)]
        + [jax.ShapeDtypeStruct((r, n3), narrow) for r in piece_rows(width)],
        scratch_shapes=[
            pltpu.VMEM((2, rows, width), narrow),
            pltpu.VMEM((2, rows, width), narrow),
            pltpu.VMEM((width, n3), narrow),
            pltpu.VMEM((2, rows, n), narrow),
            pltpu.VMEM((2, rows, 2 * n), narrow),
            pltpu.VMEM((2, 2, rows, width), wide),
            pltpu.VMEM((2, rows, width), narrow),
            pltpu.VMEM((width, n3), narrow),
            pltpu.SemaphoreType.DMA((13,)),
            pltpu.SemaphoreType.DMA((9,)),
        ],
    )(*ins)
    return outs[:4], outs[4:]


def ffn_cuts(total):
    cuts = []
    left = total
    while left > 0:
        take = min(tile_width, left)
        cuts.append((total - left, take))
        left -= take
    return cuts


def shards(
    size,
    tokens,
    w_query,
    w_key,
    w_value,
    w_gate,
    w_out,
    w_first,
    w_second,
    w_down,
    decay_rates,
    cotangent,
):
    send = Exchange(size)
    swap = lambda value: lax.ppermute(value, "tensor", [(0, 1), (1, 0)])
    me = lax.axis_index("dp")
    turn = lax.axis_index("tensor").astype(jnp.int32).reshape(1)
    rows, width = tokens.shape
    span = width // size
    offsets = jnp.asarray(np.repeat(block_offsets(size), span))
    place = jnp.bitwise_xor(offsets, me) * span + jnp.arange(width) % span
    shuffle = (jnp.arange(width)[:, None] == place[None, :]).astype(narrow)

    cuts = ffn_cuts(w_first.shape[1])
    down_t = w_down.T
    beside = lambda *arrays: jnp.concatenate(arrays, axis=1)
    first = Gather(send, beside(w_query, w_key, w_value))
    second = Gather(send, beside(w_gate, w_out.T))
    mlp = [
        Gather(send, beside(*(w[:, at : at + n] for w in (w_first, w_second, down_t))))
        for at, n in cuts
    ]
    first.inner(0)
    first.rest()
    second.inner(0, *first.parts[1:])
    first.sides()
    second.rest()
    first.far()
    second.sides(*first.got)
    mlp[0].inner(0, *first.got)

    inputs = low(nn(tokens, shuffle)).astype(wide)
    scale_in = inverse_rms(inputs)
    normed_in = inputs * scale_in
    own_in = low(normed_in)
    pair_in = (own_in, swap(own_in))
    own_cot = low(nn(cotangent, shuffle))
    pair_cot = (own_cot, swap(own_cot))

    pair_in = held_back(pair_in, pair_cot[1])
    query, keys, values, slope_q, slope_k, attended, sums = front(
        turn, decay_rates, pair_in, first.pieces
    )
    attended, sums = held_back((attended, sums), *second.got)
    second.far(attended)
    mlp[0].rest(attended)
    pair_gate = held_back(pair_in, attended)
    mlp[0].sides(*second.last)
    mlp[1].inner(0, attended)
    mlp[1].rest(*second.last)
    mlp[2].inner(0, *second.last)
    proj_u = gate(pair_gate, second.pieces)
    (attended_late,) = held_back((attended,), proj_u)
    gated, scale_out, branch_own, branch_other = branch(
        sums, swap(sums), attended_late, proj_u, second.pieces
    )
    branch_own, branch_other, gated = held_back(
        (branch_own, branch_other, gated), *mlp[0].got, *mlp[1].got, *mlp[2].got
    )
    mlp[0].far(gated)
    mlp[2].rest(gated)
    middle = inputs + branch_own + swap(branch_other).astype(wide)
    scale_mid = inverse_rms(middle)
    normed_mid = middle * scale_mid
    own_mid = low(normed_mid)
    mlp[1].sides(*mlp[0].last)
    mlp[2].sides(*mlp[0].last)
    pair_mid = (own_mid, swap(own_mid))

    pair_mid = held_back(pair_mid, *mlp[2].parts)
    sums, grads = ffn(pair_mid, pair_cot, mlp[0].pieces, None, False)
    outs = [Scatter(send, grads)]
    mlp[1].far(grads[0])
    mlp[2].far(grads[0])
    outs[0].move(grads[0])
    sums, grads = ffn(pair_mid, pair_cot, mlp[1].pieces, sums, False)
    grads = held_back(grads, *mlp[2].last, *outs[0].got)
    outs.append(Scatter(send, grads))
    outs[1].move(grads[0])
    outs[0].move(grads[0])
    pair_mid = held_back(pair_mid, *outs[0].sent)
    sums, grads = ffn(pair_mid, pair_cot, mlp[2].pieces, sums, True)
    outs.append(Scatter(send, grads))
    y_own, y_other, d_own, d_other = held_back(sums, *outs[1].got)
    outs[2].move(d_other)

    grad_mid_norm = d_own + swap(d_other).astype(wide)
    grad_middle = own_cot.astype(wide) + norm_back(grad_mid_norm, normed_mid, scale_mid)
    own_e = low(grad_middle)
    pair_e = (own_e, swap(own_e))
    outs[1].move(own_e)
    pair_e_late = held_back(pair_e, *outs[1].sent, *outs[0].got)
    grad_normed, grad_unit, cross = unbranch(pair_e_late, attended, scale_out, proj_u, second.pieces)
    other_cross = swap(cross)
    pair_in_late = held_back(pair_in, grad_unit)
    grads = weight_grads((pair_in_late, pair_e), (grad_unit, gated))
    late = Scatter(send, grads)
    outs[0].move(grads[0], other_cross)
    (grad_normed,) = held_back((grad_normed,), grads[0])
    outs[2].move(grads[0])
    grad_q, grad_k, grad_v = held_back(
        attend_back(
            turn,
            decay_rates,
            scale_out,
            cross,
            other_cross,
            (query, keys, values, slope_q, slope_k, grad_normed, attended),
            width,
        ),
        *outs[0].got,
    )
    grads = weight_grads((pair_in,), (grad_q, grad_k, grad_v))
    last = Scatter(send, grads)
    (grad_q_late,) = held_back((grad_q,), grads[0], *outs[1].got, *outs[2].got)
    move_along(outs[1:], grads[0])
    last.move(grads[0])
    late.move(grads[0])
    total_own, total_other = held_back(
        input_grad((grad_q_late, grad_k, grad_v, grad_unit), first.pieces, second.pieces),
        *last.got,
        *late.got,
    )
    last.move(total_own)
    late.move(total_own, *last.sent)
    while len(outs[0].moves) > 1:
        move_along(outs, total_own, *late.sent)
    last.move(*outs[2].got)
    late.move(*last.sent, *outs[2].got)
    (y_other,) = held_back((y_other,), *outs[2].got)
    for out in (*outs, last, late):
        while out.moves:
            out.move(total_own)
    grad_in_norm = total_own + swap(total_other).astype(wide)
    tokens_grad = grad_middle + norm_back(grad_in_norm, normed_in, scale_in)
    y_sum = y_own + swap(y_other).astype(wide)
    layer_out = low(middle + y_sum)
    layer_out = low(nt(layer_out, shuffle))
    parts = []
    rest = tokens_grad
    for _ in range(3):
        part = lax.reduce_precision(rest, 8, 7)
        parts.append(low(part))
        rest = rest - part
    tokens_grad = nt(parts[0], shuffle) + (nt(parts[1], shuffle) + nt(parts[2], shuffle))
    thirds = [
        jnp.concatenate(
            [out.total[:, i * n : (i + 1) * n] for out, (_, n) in zip(outs, cuts)], axis=1
        )
        for i in range(3)
    ]
    n = w_query.shape[1]
    return (
        layer_out,
        tokens_grad,
        last.total[:, :n],
        last.total[:, n : 2 * n],
        last.total[:, 2 * n :],
        late.total[:, :n],
        late.total[:, n:].T,
        thirds[0],
        thirds[1],
        thirds[2].T,
    )


def solution(mesh):
    return jax.shard_map(
        functools.partial(shards, mesh.shape["dp"]),
        mesh=mesh,
        in_specs=(
            P(("dp", "tensor"), None),
            P("dp", "tensor"),
            P("dp", "tensor"),
            P("dp", "tensor"),
            P("dp", "tensor"),
            P("tensor", "dp"),
            P("dp", "tensor"),
            P("dp", "tensor"),
            P("tensor", "dp"),
            P("tensor"),
            P(("dp", "tensor"), None),
        ),
        out_specs=(
            P(("dp", "tensor"), None),
            P(("dp", "tensor"), None),
            P("dp", "tensor"),
            P("dp", "tensor"),
            P("dp", "tensor"),
            P("dp", "tensor"),
            P("tensor", "dp"),
            P("dp", "tensor"),
            P("dp", "tensor"),
            P("tensor", "dp"),
        ),
        check_vma=False,
    )
```

time: 436 us -> 374 us (0.86)
  waiting for transfers between devices: 171 us -> 102 us
  local copies, waits for them, and re-layouts: 15.4 us -> 30.5 us
  Pallas kernels: 106 us -> 121 us
  other arithmetic: 34.4 us -> 22.5 us
  starting transfers between devices: 89.5 us -> 79 us
    ppermute x80 -> x57, waiting for transfers between devices: 170 us -> 99.3 us  [__call__(): result = lax.ppermute(array, 'dp', pairs)]
    pallas_call x8 -> x13, Pallas kernels: 70.1 us -> 83.9 us  [the longest x3 42.5 us: ffn(): pl.pallas_call(functools.partial(ffn_kernel, chained=sums is not None, la...]
    slice x16 -> x25, local copies, waits for them, and re-layouts: 0.34 us -> 10.7 us  [the longest x10 7.38 us: far(): self.last = (self.send(side[:half], 2), self.send(up[half:], 1))]
    ppermute x80 -> x57, starting transfers between devices: 88 us -> 77.9 us  [__call__(): result = lax.ppermute(array, 'dp', pairs)]
    concatenate x15 -> x8, other arithmetic: 7.42 us -> 1.19 us  [the longest x2 1.06 us: move_along(): got = scatters[0].send(jnp.concatenate(parts, axis=1), name)]
    convert_element_type x11 -> x3, other arithmetic: 9.59 us -> 3.99 us  [low(): return value.astype(narrow)]
    unnamed x192 -> x120, local copies, waits for them, and re-layouts: 10.7 us -> 13.6 us
    add x23 -> x15, other arithmetic: 10 us -> 8.98 us  [add(): self.total = rest + sum((g.astype(wide) for g in got))]
  transfers between devices with their start and end apart: 92 -> 67, of which waited for: 36 -> 23; matrix products, arithmetic and copies ran while one was open for 13% -> 12% of each run, Pallas kernels for 25% -> 32%
where the time goes in v4:
time: 374 us; the launch traced here: 369 us
  Pallas kernels  121 us (32%)
  waiting for transfers between devices  102 us (27%)
  starting transfers between devices  79 us (21%)
  local copies, waits for them, and re-layouts  30.5 us (8%)
  other arithmetic  22.5 us (6%)
  matrix products  12 us (3%)
    ppermute x57, waiting for transfers between devices, __call__(): result = lax.ppermute(array, 'dp', pairs)  99.3 us
    ppermute x57, starting transfers between devices, __call__(): result = lax.ppermute(array, 'dp', pairs)  77.9 us
    pallas_call x3, Pallas kernels, ffn(): pl.pallas_call(functools.partial(ffn_kernel, chained=sums is not None, la...  42.5 us
    unnamed x120, local copies, waits for them, and re-layouts  13.6 us
    pallas_call x1, Pallas kernels, front(): pl.pallas_call(functools.partial(front_kernel, heads=rates.shape[0] // st...  13.4 us
    pallas_call x1, Pallas kernels, attend_back(): pl.pallas_call(functools.partial(attend_back_kernel, width=width), cost_e...  13 us
    pallas_call x2, Pallas kernels, weight_grads(): pl.pallas_call(functools.partial(weight_grad_kernel, count=count, each=le...  12.6 us
    dot_general x6, matrix products, dot(): lax.dot_general(left, right, (dims, ((), ())), preferred_element_type=wide)  12 us
  transfers between devices with their start and end apart: 67, of which 23 were waited for; matrix products, arithmetic and copies ran while one was open for 12% of the time, Pallas kernels for 32%

profile of v4, /device:TPU:0, one launch (start us, length us, event | category | flops | bytes accessed | tf_op | source)
XLA Modules:
  0.0 369.1 jit_solution(9045310098794350434)
XLA Ops:
  3.3 4.1 %collective-permute-start.2 = (bf16[64,1536]{1,0:T(8,128)(2,1)S(1)}, bf16[64,1536]{1,0:T(8,128)(2,1)S(1)}, u32[]{:S(2)}, u32[]{:S(2)}) collective-permute-start(bf16[64,1536]{1,0:T(8,128)(2,1)S(1)} %constant_dynamic-update-slice_fusion), channel_id=1, source_target_pairs={{0,16},{2,18},{4,20},{6,22},{8,24},{10,26},{12,28},{14,30},{16,0},... | collective-permute-start | bytes 589832 | tf_op jit(solution)/shard_map/ppermute | solution.py:51
  9.5 7.0 %collective-permute-done.2 = bf16[64,1536]{1,0:T(8,128)(2,1)S(1)} collective-permute-done((bf16[64,1536]{1,0:T(8,128)(2,1)S(1)}, bf16[64,1536]{1,0:T(8,128)(2,1)S(1)}, u32[]{:S(2)}, u32[]{:S(2)}) %collective-permute-start.2) | collective-permute-done | bytes 196640 | tf_op jit(solution)/shard_map/ppermute | solution.py:51
  17.7 9.2 %collective-permute-done.3 = bf16[128,1536]{1,0:T(8,128)(2,1)S(1)} collective-permute-done((bf16[128,1536]{1,0:T(8,128)(2,1)S(1)}, bf16[128,1536]{1,0:T(8,128)(2,1)S(1)}, u32[]{:S(2)}, u32[]{:S(2)}) %collective-permute-start.3) | collective-permute-done | bytes 393248 | tf_op jit(solution)/shard_map/ppermute | solution.py:51
  29.8 3.3 collective-permute-start.8
  33.2 2.3 fusion.26.refs_2_
  35.5 3.0 collective-permute-done.8
  40.6 4.3 %collective-permute-done.4.refs_1_.refs_6_.refs_11_.refs_5_.refs_10_.refs_15_ = bf16[256,1536]{1,0:T(8,128)(2,1)S(1)} collective-permute-done((bf16[256,1536]{1,0:T(8,128)(2,1)S(1)}, bf16[256,1536]{1,0:T(8,128)(2,1)S(1)}, u32[]{:S(2)}, u32[]{:S(2)}) %collective-permute-start.4) | collective-permute-done | bytes 786464 | tf_op jit(solution)/shard_map/ppermute | solution.py:51
  52.4 3.5 collective-permute-start.15
  57.1 2.6 collective-permute-done.7.refs_4_.refs_9_.refs_14_.refs_8_.refs_13_.refs_18_
  59.7 13.4 %shard_map.195 = (bf16[1024,512]{1,0:T(8,128)(2,1)}, bf16[1024,512]{1,0:T(8,128)(2,1)}, bf16[1024,512]{1,0:T(8,128)(2,1)}, bf16[1024,512]{1,0:T(8,128)(2,1)}, bf...) custom-call(s32[1]{0:T(128)} %bitcast.1.turn_ref, f32[4]{0:T(128)} %rate_ref.3, ...), custom_call_target="tpu_custom_call" | custom-call | flops 4831838208 | bytes 10485760 | tf_op jit(solution)/shard_map/pallas_call | solution.py:300
  75.2 2.4 collective-permute-start.16
  77.7 3.4 collective-permute-start.19
  81.9 3.2 collective-permute-done.19
  89.2 6.1 %collective-permute-start.20 = (bf16[128,1536]{1,0:T(8,128)(2,1)S(1)}, bf16[128,1536]{1,0:T(8,128)(2,1)S(1)}, u32[]{:S(2)}, u32[]{:S(2)}) collective-permute-start(bf16[128,1536]{1,0:T(8,128)(2,1)S(1)} %constant_dynamic-update-slice_fusion.11), channel_id=1, source_target_pairs={{0,8},{2,10},{4,12},{6,14},{8,0},{10,2},{12,4},{14,6},{16,24},{18,... | collective-permute-start | bytes 1179656 | tf_op jit(solution)/shard_map/ppermute | solution.py:51
  96.1 4.4 %shard_map.196.u_ref = f32[1024,512]{1,0:T(8,128)} custom-call(bf16[512,1024]{1,0:T(8,128)(2,1)} %copy-done.13, bf16[512,1024]{1,0:T(8,128)(2,1)} %copy-done.18, bf16[256,1024]{1,0:T(8,128)(2,1)} %copy-done.9, bf16[256,1024]{1,0:T(8,128)(2,1)} %copy-done.7, bf16[256,1024]{1,0:T(8,128)(2,1)} %copy-done.8, bf16[128,1024]{1,0:T(8,128)(2,1)} %copy-done.16, ...), custom_call_target="tpu_custom_call" | custom-call | flops 1073741824 | bytes 4194304 | tf_op jit(solution)/shard_map/pallas_call | solution.py:322
  101.1 6.0 %shard_map.197 = (bf16[1024,512]{1,0:T(8,128)(2,1)}, f32[1024,1]{1,0:T(8,128)}, f32[512,1024]{1,0:T(8,128)}, bf16[512,1024]{1,0:T(8,128)(2,1)}) custom-call(f32[8,1024]{1,0:T(8,128)} %get-tuple-element.201.sum_ref, f32[8,1024]{1,0:T(8,128)} %copy-done.45, f32[1024,512]{1,0:T(8,128)} %get-tuple-element.207.o_ref, f32[1024,512]{1,0:T(8,128)} %shard_map.196.u_ref, ...), custom_call_target="tpu_custom_call" | custom-call | flops 1073741824 | bytes 8388608 | tf_op jit(solution)/shard_map/pallas_call | solution.py:354
  110.9 2.1 multiply_reduce_fusion.1
  114.4 4.5 %collective-permute-done.25.refs_7_ = bf16[128,1536]{1,0:T(8,128)(2,1)S(1)} collective-permute-done((bf16[128,1536]{1,0:T(8,128)(2,1)S(1)}, bf16[128,1536]{1,0:T(8,128)(2,1)S(1)}, u32[]{:S(2)}, u32[]{:S(2)}) %collective-permute-start.25) | collective-permute-done | bytes 393248 | tf_op jit(solution)/shard_map/ppermute | solution.py:51
  118.9 1.9 collective-permute-done.26.refs_8_
  128.0 15.0 %shard_map.198 = (f32[512,1024]{1,0:T(8,128)}, f32[512,1024]{1,0:T(8,128)}, f32[512,1024]{1,0:T(8,128)}, f32[512,1024]{1,0:T(8,128)}, bf16[256,1536]{1,0:T(8,128...) custom-call(bf16[512,1024]{1,0:T(8,128)(2,1)} %copy-done.19, ...), custom_call_target="tpu_custom_call" | custom-call | flops 9663676416 | bytes 14680064 | tf_op jit(solution)/shard_map/pallas_call | solution.py:605
  150.3 5.5 %collective-permute-done.33.refs_5_ = bf16[256,1152]{1,0:T(8,128)(2,1)} collective-permute-done((bf16[256,1152]{1,0:T(8,128)(2,1)}, bf16[256,1152]{1,0:T(8,128)(2,1)}, u32[]{:S(2)}, u32[]{:S(2)}) %collective-permute-start.33) | collective-permute-done | bytes 589856 | tf_op jit(solution)/shard_map/ppermute | solution.py:51
  162.1 3.3 collective-permute-done.31.refs_7_
  166.9 14.6 %shard_map.199 = (f32[512,1024]{1,0:T(8,128)}, f32[512,1024]{1,0:T(8,128)}, f32[512,1024]{1,0:T(8,128)}, f32[512,1024]{1,0:T(8,128)}, bf16[256,1536]{1,0:T(8,128...) custom-call(bf16[512,1024]{1,0:T(8,128)(2,1)} %copy-done.19, ...), custom_call_target="tpu_custom_call" | custom-call | flops 9663676416 | bytes 31457280 | tf_op jit(solution)/shard_map/pallas_call | solution.py:605
  182.3 2.3 shard_map.200
  187.6 12.9 %shard_map.201 = (f32[512,1024]{1,0:T(8,128)}, bf16[512,1024]{1,0:T(8,128)(2,1)}, f32[512,1024]{1,0:T(8,128)}, bf16[512,1024]{1,0:T(8,128)(2,1)}, bf16[256,1152]...) custom-call(bf16[512,1024]{1,0:T(8,128)(2,1)} %copy-done.19, ...), custom_call_target="tpu_custom_call" | custom-call | flops 7247757312 | bytes 29884416 | tf_op jit(solution)/shard_map/pallas_call | solution.py:605
  200.6 2.9 collective-permute-done.41
  203.5 2.1 multiply_reduce_fusion
  205.6 3.6 fusion.32
  213.3 2.4 shard_map.202
  215.7 14.3 %collective-permute-done.39 = bf16[256,1536]{1,0:T(8,128)(2,1)} collective-permute-done((bf16[256,1536]{1,0:T(8,128)(2,1)}, bf16[256,1536]{1,0:T(8,128)(2,1)}, u32[]{:S(2)}, u32[]{:S(2)}) %collective-permute-start.39) | collective-permute-done | bytes 786464 | tf_op jit(solution)/shard_map/ppermute | solution.py:51
  231.1 7.2 %shard_map.203 = (f32[1024,512]{1,0:T(8,128)}, bf16[1024,512]{1,0:T(8,128)(2,1)}, f32[8,1024]{1,0:T(8,128)}) custom-call(bf16[512,1024]{1,0:T(8,128)(2,1)} %get-tuple-element.288.own_ref.refs_2_, bf16[512,1024]{1,0:T(8,128)(2,1)} %collective-permute-done.42.other_ref.refs_3_, f32[1024,512]{1,0:T(8,128)} %get-tuple-element.207.o_ref, ...), custom_call_target="tpu_custom_call" | custom-call | flops 1073741824 | bytes 8388608 | tf_op jit(solution)/shard_map/pallas_call | solution.py:385
  238.4 5.9 %shard_map.204 = (bf16[256,1024]{1,0:T(8,128)(2,1)}, bf16[256,1024]{1,0:T(8,128)(2,1)}, bf16[256,1024]{1,0:T(8,128)(2,1)}, bf16[128,1024]{1,0:T(8,128)(2,1)}, bf16[128,1024]{1,0:T(8,128)(2,1)}) custom-call(bf16[512,1024]{1,0:T(8,128)(2,1)} %copy-done.13, bf16[512,1024]{1,0:T(8,128)(2,1)} %copy-done.18, bf16[512,1024]{1,0:T(8,128)(2,1)} %get-tuple-element.288.own_ref.refs_2_, ...), custom_call_target="tpu_custom_call" | custom-call | flops 2147483648 | bytes 6291456 | tf_op jit(solution)/shard_map/pallas_call | solution.py:494
  245.0 2.1 shard_map.207
  253.8 13.0 %shard_map.205 = (bf16[1024,512]{1,0:T(8,128)(2,1)}, bf16[1024,512]{1,0:T(8,128)(2,1)}, bf16[1024,512]{1,0:T(8,128)(2,1)}) custom-call(s32[1]{0:T(128)} %bitcast.1.turn_ref, f32[4]{0:T(128)} %rate_ref.3, f32[1024,1]{1,0:T(8,128)} %get-tuple-element.290.scale_ref, f32[8,1024]{1,0:T(8,128)} %get-tuple-element.295.cross_ref, f32[8,1024]{1,0:T(8,128)} %copy-done.53, ...), custom_call_target="tpu_custom_call" | custom-call | flops 6442450944 | bytes 28311552 | tf_op jit(solution)/shard_map/pallas_call | solution.py:461
  266.9 6.7 %shard_map.206 = (bf16[256,1536]{1,0:T(8,128)(2,1)}, bf16[256,1536]{1,0:T(8,128)(2,1)}, bf16[256,1536]{1,0:T(8,128)(2,1)}, bf16[128,1536]{1,0:T(8,128)(2,1)}, bf16[128,1536]{1,0:T(8,128)(2,1)}) custom-call(bf16[512,1024]{1,0:T(8,128)(2,1)} %copy-done.13, bf16[512,1024]{1,0:T(8,128)(2,1)} %copy-done.18, bf16[1024,512]{1,0:T(8,128)(2,1)} %get-tuple-element.323.refs_2_.refs_0_, ...), custom_call_target="tpu_custom_call" | custom-call | flops 3221225472 | bytes 8388608 | tf_op jit(solution)/shard_map/pallas_call | solution.py:494
  273.6 1.9 add_add_fusion.2
  282.5 2.0 collective-permute-start.55
  284.5 10.5 %shard_map.208 = (f32[512,1024]{1,0:T(8,128)}, bf16[512,1024]{1,0:T(8,128)(2,1)}) custom-call(bf16[1024,512]{1,0:T(8,128)(2,1)} %get-tuple-element.323.refs_2_.refs_0_, bf16[1024,512]{1,0:T(8,128)(2,1)} %get-tuple-element.310.refs_3_.refs_1_, bf16[1024,512]{1,0:T(8,128)(2,1)} %get-tuple-element.311.refs_4_.refs_2_, ...), custom_call_target="tpu_custom_call" | custom-call | flops 4294967296 | bytes 12582912 | tf_op jit(solution)/shard_map/pallas_call | solution.py:521
  295.7 2.3 shard_map.209
  299.2 2.0 shard_map.210
  305.3 2.3 collective-permute-start.56
  310.5 19.2 %collective-permute-done.56 = bf16[64,4224]{1,0:T(8,128)(2,1)S(1)} collective-permute-done((bf16[64,4224]{1,0:T(8,128)(2,1)S(1)}, bf16[64,4224]{1,0:T(8,128)(2,1)S(1)}, u32[]{:S(2)}, u32[]{:S(2)}) %collective-permute-start.56) | collective-permute-done | bytes 540704 | tf_op jit(solution)/shard_map/ppermute | solution.py:51
  340.9 2.2 collective-permute-done.61
  344.4 2.8 add_add_fusion
  348.9 5.6 %collective-permute-done.62 = bf16[64,1536]{1,0:T(8,128)(2,1)S(1)} collective-permute-done((bf16[64,1536]{1,0:T(8,128)(2,1)S(1)}, bf16[64,1536]{1,0:T(8,128)(2,1)S(1)}, u32[]{:S(2)}, u32[]{:S(2)}) %collective-permute-start.62) | collective-permute-done | bytes 196640 | tf_op jit(solution)/shard_map/ppermute | solution.py:51
  354.5 4.1 %collective-permute-done.65 = bf16[128,1024]{1,0:T(8,128)(2,1)S(1)} collective-permute-done((bf16[128,1024]{1,0:T(8,128)(2,1)S(1)}, bf16[128,1024]{1,0:T(8,128)(2,1)S(1)}, u32[]{:S(2)}, u32[]{:S(2)}) %collective-permute-start.65) | collective-permute-done | bytes 262176 | tf_op jit(solution)/shard_map/ppermute | solution.py:51
  359.6 6.0 %collective-permute-done.66 = bf16[64,1024]{1,0:T(8,128)(2,1)S(1)} collective-permute-done((bf16[64,1024]{1,0:T(8,128)(2,1)S(1)}, bf16[64,1024]{1,0:T(8,128)(2,1)S(1)}, u32[]{:S(2)}, u32[]{:S(2)}) %collective-permute-start.66) | collective-permute-done | bytes 131104 | tf_op jit(solution)/shard_map/ppermute | solution.py:51
  366.3 2.4 fusion.25
  (311 shorter events, 103.2 us)
Async XLA Ops:
  3.3 13.2 %collective-permute-start.2 = (bf16[64,1536]{1,0:T(8,128)(2,1)S(1)}, bf16[64,1536]{1,0:T(8,128)(2,1)S(1)}, u32[]{:S(2)}, u32[]{:S(2)}) collective-permute-start(bf16[64,1536]{1,0:T(8,128)(2,1)S(1)} %constant_dynamic-update-slice_fusion), channel_id=1, source_target_pairs={{0,16},{2,18},{4,20},{6,22},{8,24},{10,26},{12,28},{14,30},{16,0},... | collective-permute-start | bytes 589832 | tf_op jit(solution)/shard_map/ppermute | solution.py:51
  17.6 32.0 %collective-permute-start = (bf16[512,1024]{1,0:T(8,128)(2,1)S(1)}, bf16[512,1024]{1,0:T(8,128)(2,1)S(1)}, u32[]{:S(2)}, u32[]{:S(2)}) collective-permute-start(bf16[512,1024]{1,0:T(8,128)(2,1)S(1)} %fusion.10.own_ref.refs_0_), channel_id=1, source_target_pairs={{0,1},{1,0},{2,3},{3,2},{4,5},{5,4},{6,7},{7,6},{8,9},{9,8},{10,11... | collective-permute-start | bytes 3145736 | tf_op jit(solution)/shard_map/ppermute | solution.py:653
  27.0 17.9 %collective-permute-start.4 = (bf16[256,1536]{1,0:T(8,128)(2,1)S(1)}, bf16[256,1536]{1,0:T(8,128)(2,1)S(1)}, u32[]{:S(2)}, u32[]{:S(2)}) collective-permute-start(bf16[256,1536]{1,0:T(8,128)(2,1)S(1)} %pad_maximum_fusion.refs_0_.refs_5_.refs_10_.refs_4_.refs_9_.refs_14_), channel_id=1, source_target_pairs={{0,2},{2,0},{4,6},{6,4},{8,10},{10,8},{12,14},{14,12},{16,18},{18,... | collective-permute-start | bytes 2359304 | tf_op jit(solution)/shard_map/ppermute | solution.py:51
  28.3 18.3 %collective-permute-start.5 = (bf16[256,1536]{1,0:T(8,128)(2,1)S(1)}, bf16[256,1536]{1,0:T(8,128)(2,1)S(1)}, u32[]{:S(2)}, u32[]{:S(2)}) collective-permute-start(bf16[256,1536]{1,0:T(8,128)(2,1)S(1)} %pad_maximum_fusion.refs_0_.refs_5_.refs_10_.refs_4_.refs_9_.refs_14_), channel_id=1, source_target_pairs={{0,4},{2,6},{4,0},{6,2},{8,12},{10,14},{12,8},{14,10},{16,20},{18,... | collective-permute-start | bytes 2359304 | tf_op jit(solution)/shard_map/ppermute | solution.py:51
  35.5 16.9 %collective-permute-start.1 = (bf16[512,1024]{1,0:T(8,128)(2,1)}, bf16[512,1024]{1,0:T(8,128)(2,1)}, u32[]{:S(2)}, u32[]{:S(2)}) collective-permute-start(bf16[512,1024]{1,0:T(8,128)(2,1)} %fusion.26.refs_2_), channel_id=1, source_target_pairs={{0,1},{1,0},{2,3},{3,2},{4,5},{5,4},{6,7},{7,6},{8,9},{9,8},{10,11... | collective-permute-start | bytes 3145736 | tf_op jit(solution)/shard_map/ppermute | solution.py:653
  44.9 12.2 %collective-permute-start.6 = (bf16[128,1536]{1,0:T(8,128)(2,1)S(1)}, bf16[128,1536]{1,0:T(8,128)(2,1)}, u32[]{:S(2)}, u32[]{:S(2)}) collective-permute-start(bf16[128,1536]{1,0:T(8,128)(2,1)S(1)} %slice.242), channel_id=1, source_target_pairs={{0,4},{2,6},{4,0},{6,2},{8,12},{10,14},{12,8},{14,10},{16,20},{18,... | collective-permute-start | bytes 1179656 | tf_op jit(solution)/shard_map/ppermute | solution.py:51
  47.4 12.3 %collective-permute-start.7 = (bf16[128,1536]{1,0:T(8,128)(2,1)}, bf16[128,1536]{1,0:T(8,128)(2,1)}, u32[]{:S(2)}, u32[]{:S(2)}) collective-permute-start(bf16[128,1536]{1,0:T(8,128)(2,1)} %slice.243), channel_id=1, source_target_pairs={{0,2},{2,0},{4,6},{6,4},{8,10},{10,8},{12,14},{14,12},{16,18},{18,... | collective-permute-start | bytes 1179656 | tf_op jit(solution)/shard_map/ppermute | solution.py:51
  48.6 24.5 %collective-permute-start.10 = (bf16[256,1024]{1,0:T(8,128)(2,1)S(1)}, bf16[256,1024]{1,0:T(8,128)(2,1)S(1)}, u32[]{:S(2)}, u32[]{:S(2)}) collective-permute-start(bf16[256,1024]{1,0:T(8,128)(2,1)S(1)} %constant_dynamic-update-slice_fusion.5.refs_0_.refs_19_), channel_id=1, source_target_pairs={{0,2},{2,0},{4,6},{6,4},{8,10},{10,8},{12,14},{14,12},{16,18},{18,... | collective-permute-start | bytes 1572872 | tf_op jit(solution)/shard_map/ppermute | solution.py:51
  50.5 22.6 %collective-permute-start.11 = (bf16[256,1024]{1,0:T(8,128)(2,1)S(1)}, bf16[256,1024]{1,0:T(8,128)(2,1)S(1)}, u32[]{:S(2)}, u32[]{:S(2)}) collective-permute-start(bf16[256,1024]{1,0:T(8,128)(2,1)S(1)} %constant_dynamic-update-slice_fusion.5.refs_0_.refs_19_), channel_id=1, source_target_pairs={{0,4},{2,6},{4,0},{6,2},{8,12},{10,14},{12,8},{14,10},{16,20},{18,... | collective-permute-start | bytes 1572872 | tf_op jit(solution)/shard_map/ppermute | solution.py:51
  52.4 22.8 %collective-permute-start.15 = (bf16[64,1536]{1,0:T(8,128)(2,1)S(1)}, bf16[64,1536]{1,0:T(8,128)(2,1)S(1)}, u32[]{:S(2)}, u32[]{:S(2)}) collective-permute-start(bf16[64,1536]{1,0:T(8,128)(2,1)S(1)} %pad_maximum_fusion.6), channel_id=1, source_target_pairs={{0,16},{2,18},{4,20},{6,22},{8,24},{10,26},{12,28},{14,30},{16,0},... | collective-permute-start | bytes 589832 | tf_op jit(solution)/shard_map/ppermute | solution.py:51
  73.2 11.9 %collective-permute-start.13 = (bf16[128,1024]{1,0:T(8,128)(2,1)S(1)}, bf16[128,1024]{1,0:T(8,128)(2,1)S(1)}, u32[]{:S(2)}, u32[]{:S(2)}) collective-permute-start(bf16[128,1024]{1,0:T(8,128)(2,1)S(1)} %slice.186), channel_id=1, source_target_pairs={{0,4},{2,6},{4,0},{6,2},{8,12},{10,14},{12,8},{14,10},{16,20},{18,... | collective-permute-start | bytes 786440 | tf_op jit(solution)/shard_map/ppermute | solution.py:51
  87.1 20.1 %collective-permute-start.17 = (bf16[256,1536]{1,0:T(8,128)(2,1)}, bf16[256,1536]{1,0:T(8,128)(2,1)S(1)}, u32[]{:S(2)}, u32[]{:S(2)}) collective-permute-start(bf16[256,1536]{1,0:T(8,128)(2,1)} %constant_dynamic-update-slice_fusion.9.refs_4_), channel_id=1, source_target_pairs={{0,2},{2,0},{4,6},{6,4},{8,10},{10,8},{12,14},{14,12},{16,18},{18,... | collective-permute-start | bytes 2359304 | tf_op jit(solution)/shard_map/ppermute | solution.py:51
  88.8 18.4 %collective-permute-start.18 = (bf16[256,1536]{1,0:T(8,128)(2,1)}, bf16[256,1536]{1,0:T(8,128)(2,1)}, u32[]{:S(2)}, u32[]{:S(2)}) collective-permute-start(bf16[256,1536]{1,0:T(8,128)(2,1)} %constant_dynamic-update-slice_fusion.9.refs_4_), channel_id=1, source_target_pairs={{0,4},{2,6},{4,0},{6,2},{8,12},{10,14},{12,8},{14,10},{16,20},{18,... | collective-permute-start | bytes 2359304 | tf_op jit(solution)/shard_map/ppermute | solution.py:51
  89.2 18.0 %collective-permute-start.20 = (bf16[128,1536]{1,0:T(8,128)(2,1)S(1)}, bf16[128,1536]{1,0:T(8,128)(2,1)S(1)}, u32[]{:S(2)}, u32[]{:S(2)}) collective-permute-start(bf16[128,1536]{1,0:T(8,128)(2,1)S(1)} %constant_dynamic-update-slice_fusion.11), channel_id=1, source_target_pairs={{0,8},{2,10},{4,12},{6,14},{8,0},{10,2},{12,4},{14,6},{16,24},{18,... | collective-permute-start | bytes 1179656 | tf_op jit(solution)/shard_map/ppermute | solution.py:51
  114.2 13.8 %collective-permute-start.23 = (bf16[512,1024]{1,0:T(8,128)(2,1)S(1)}, bf16[512,1024]{1,0:T(8,128)(2,1)}, u32[]{:S(2)}, u32[]{:S(2)}) collective-permute-start(bf16[512,1024]{1,0:T(8,128)(2,1)S(1)} %multiply_convert_fusion.refs_0_), channel_id=1, source_target_pairs={{0,1},{1,0},{2,3},{3,2},{4,5},{5,4},{6,7},{7,6},{8,9},{9,8},{10,11... | collective-permute-start | bytes 3145736 | tf_op jit(solution)/shard_map/ppermute | solution.py:653
  122.4 20.7 %collective-permute-start.29 = (bf16[256,1536]{1,0:T(8,128)(2,1)}, bf16[256,1536]{1,0:T(8,128)(2,1)}, u32[]{:S(2)}, u32[]{:S(2)}) collective-permute-start(bf16[256,1536]{1,0:T(8,128)(2,1)} %constant_dynamic-update-slice_fusion.15.refs_4_), channel_id=1, source_target_pairs={{0,2},{2,0},{4,6},{6,4},{8,10},{10,8},{12,14},{14,12},{16,18},{18,... | collective-permute-start | bytes 2359304 | tf_op jit(solution)/shard_map/ppermute | solution.py:51
  123.7 20.7 %collective-permute-start.30 = (bf16[256,1536]{1,0:T(8,128)(2,1)}, bf16[256,1536]{1,0:T(8,128)(2,1)}, u32[]{:S(2)}, u32[]{:S(2)}) collective-permute-start(bf16[256,1536]{1,0:T(8,128)(2,1)} %constant_dynamic-update-slice_fusion.15.refs_4_), channel_id=1, source_target_pairs={{0,4},{2,6},{4,0},{6,2},{8,12},{10,14},{12,8},{14,10},{16,20},{18,... | collective-permute-start | bytes 2359304 | tf_op jit(solution)/shard_map/ppermute | solution.py:51
  126.9 28.9 %collective-permute-start.33 = (bf16[256,1152]{1,0:T(8,128)(2,1)}, bf16[256,1152]{1,0:T(8,128)(2,1)}, u32[]{:S(2)}, u32[]{:S(2)}) collective-permute-start(bf16[256,1152]{1,0:T(8,128)(2,1)} %constant_dynamic-update-slice_fusion.17.refs_4_), channel_id=1, source_target_pairs={{0,2},{2,0},{4,6},{6,4},{8,10},{10,8},{12,14},{14,12},{16,18},{18,... | collective-permute-start | bytes 1769480 | tf_op jit(solution)/shard_map/ppermute | solution.py:51
  127.2 29.9 %collective-permute-start.34 = (bf16[256,1152]{1,0:T(8,128)(2,1)}, bf16[256,1152]{1,0:T(8,128)(2,1)}, u32[]{:S(2)}, u32[]{:S(2)}) collective-permute-start(bf16[256,1152]{1,0:T(8,128)(2,1)} %constant_dynamic-update-slice_fusion.17.refs_4_), channel_id=1, source_target_pairs={{0,4},{2,6},{4,0},{6,2},{8,12},{10,14},{12,8},{14,10},{16,20},{18,... | collective-permute-start | bytes 1769480 | tf_op jit(solution)/shard_map/ppermute | solution.py:51
  145.5 19.9 %collective-permute-start.31 = (bf16[128,1536]{1,0:T(8,128)(2,1)S(1)}, bf16[128,1536]{1,0:T(8,128)(2,1)S(1)}, u32[]{:S(2)}, u32[]{:S(2)}) collective-permute-start(bf16[128,1536]{1,0:T(8,128)(2,1)S(1)} %slice.199), channel_id=1, source_target_pairs={{0,4},{2,6},{4,0},{6,2},{8,12},{10,14},{12,8},{14,10},{16,20},{18,... | collective-permute-start | bytes 1179656 | tf_op jit(solution)/shard_map/ppermute | solution.py:51
  148.2 17.9 %collective-permute-start.32 = (bf16[128,1536]{1,0:T(8,128)(2,1)S(1)}, bf16[128,1536]{1,0:T(8,128)(2,1)S(1)}, u32[]{:S(2)}, u32[]{:S(2)}) collective-permute-start(bf16[128,1536]{1,0:T(8,128)(2,1)S(1)} %slice.200), channel_id=1, source_target_pairs={{0,2},{2,0},{4,6},{6,4},{8,10},{10,8},{12,14},{14,12},{16,18},{18,... | collective-permute-start | bytes 1179656 | tf_op jit(solution)/shard_map/ppermute | solution.py:51
  148.6 33.0 %collective-permute-start.27 = (bf16[128,1536]{1,0:T(8,128)(2,1)}, bf16[128,1536]{1,0:T(8,128)(2,1)S(1)}, u32[]{:S(2)}, u32[]{:S(2)}) collective-permute-start(bf16[128,1536]{1,0:T(8,128)(2,1)} %get-tuple-element.242), channel_id=1, source_target_pairs={{0,2},{2,0},{4,6},{6,4},{8,10},{10,8},{12,14},{14,12},{16,18},{18,... | collective-permute-start | bytes 1179656 | tf_op jit(solution)/shard_map/ppermute | solution.py:51
  155.8 25.7 %collective-permute-start.28 = (bf16[128,1536]{1,0:T(8,128)(2,1)}, bf16[128,1536]{1,0:T(8,128)(2,1)}, u32[]{:S(2)}, u32[]{:S(2)}) collective-permute-start(bf16[128,1536]{1,0:T(8,128)(2,1)} %get-tuple-element.243), channel_id=1, source_target_pairs={{0,4},{2,6},{4,0},{6,2},{8,12},{10,14},{12,8},{14,10},{16,20},{18,... | collective-permute-start | bytes 1179656 | tf_op jit(solution)/shard_map/ppermute | solution.py:51
  158.8 22.7 %collective-permute-start.35 = (bf16[128,1152]{1,0:T(8,128)(2,1)}, bf16[128,1152]{1,0:T(8,128)(2,1)}, u32[]{:S(2)}, u32[]{:S(2)}) collective-permute-start(bf16[128,1152]{1,0:T(8,128)(2,1)} %slice.201), channel_id=1, source_target_pairs={{0,4},{2,6},{4,0},{6,2},{8,12},{10,14},{12,8},{14,10},{16,20},{18,... | collective-permute-start | bytes 884744 | tf_op jit(solution)/shard_map/ppermute | solution.py:51
  165.4 16.1 %collective-permute-start.36 = (bf16[128,1152]{1,0:T(8,128)(2,1)}, bf16[128,1152]{1,0:T(8,128)(2,1)}, u32[]{:S(2)}, u32[]{:S(2)}) collective-permute-start(bf16[128,1152]{1,0:T(8,128)(2,1)} %slice.202), channel_id=1, source_target_pairs={{0,2},{2,0},{4,6},{6,4},{8,10},{10,8},{12,14},{14,12},{16,18},{18,... | collective-permute-start | bytes 884744 | tf_op jit(solution)/shard_map/ppermute | solution.py:51
  184.6 15.8 %collective-permute-start.37 = (bf16[128,1536]{1,0:T(8,128)(2,1)}, bf16[128,1536]{1,0:T(8,128)(2,1)S(1)}, u32[]{:S(2)}, u32[]{:S(2)}) collective-permute-start(bf16[128,1536]{1,0:T(8,128)(2,1)} %get-tuple-element.276), channel_id=1, source_target_pairs={{0,2},{2,0},{4,6},{6,4},{8,10},{10,8},{12,14},{14,12},{16,18},{18,... | collective-permute-start | bytes 1179656 | tf_op jit(solution)/shard_map/ppermute | solution.py:51
  185.9 14.6 %collective-permute-start.38 = (bf16[128,1536]{1,0:T(8,128)(2,1)}, bf16[128,1536]{1,0:T(8,128)(2,1)}, u32[]{:S(2)}, u32[]{:S(2)}) collective-permute-start(bf16[128,1536]{1,0:T(8,128)(2,1)} %get-tuple-element.277), channel_id=1, source_target_pairs={{0,4},{2,6},{4,0},{6,2},{8,12},{10,14},{12,8},{14,10},{16,20},{18,... | collective-permute-start | bytes 1179656 | tf_op jit(solution)/shard_map/ppermute | solution.py:51
  209.1 22.0 %collective-permute-start.42 = (bf16[512,1024]{1,0:T(8,128)(2,1)}, bf16[512,1024]{1,0:T(8,128)(2,1)}, u32[]{:S(2)}, u32[]{:S(2)}) collective-permute-start(bf16[512,1024]{1,0:T(8,128)(2,1)} %get-tuple-element.288.own_ref.refs_2_), channel_id=1, source_target_pairs={{0,1},{1,0},{2,3},{3,2},{4,5},{5,4},{6,7},{7,6},{8,9},{9,8},{10,11... | collective-permute-start | bytes 3145736 | tf_op jit(solution)/shard_map/ppermute | solution.py:653
  209.3 20.7 %collective-permute-start.39 = (bf16[256,1536]{1,0:T(8,128)(2,1)}, bf16[256,1536]{1,0:T(8,128)(2,1)}, u32[]{:S(2)}, u32[]{:S(2)}) collective-permute-start(bf16[256,1536]{1,0:T(8,128)(2,1)} %get-tuple-element.263), channel_id=1, source_target_pairs={{0,2},{2,0},{4,6},{6,4},{8,10},{10,8},{12,14},{14,12},{16,18},{18,... | collective-permute-start | bytes 2359304 | tf_op jit(solution)/shard_map/ppermute | solution.py:51
  210.0 20.7 %collective-permute-start.40 = (bf16[256,1536]{1,0:T(8,128)(2,1)}, bf16[256,1536]{1,0:T(8,128)(2,1)}, u32[]{:S(2)}, u32[]{:S(2)}) collective-permute-start(bf16[256,1536]{1,0:T(8,128)(2,1)} %get-tuple-element.262), channel_id=1, source_target_pairs={{0,4},{2,6},{4,0},{6,2},{8,12},{10,14},{12,8},{14,10},{16,20},{18,... | collective-permute-start | bytes 2359304 | tf_op jit(solution)/shard_map/ppermute | solution.py:51
  210.4 33.9 %collective-permute-start.47 = (bf16[128,1152]{1,0:T(8,128)(2,1)}, bf16[128,1152]{1,0:T(8,128)(2,1)S(1)}, u32[]{:S(2)}, u32[]{:S(2)}) collective-permute-start(bf16[128,1152]{1,0:T(8,128)(2,1)} %get-tuple-element.317), channel_id=1, source_target_pairs={{0,2},{2,0},{4,6},{6,4},{8,10},{10,8},{12,14},{14,12},{16,18},{18,... | collective-permute-start | bytes 884744 | tf_op jit(solution)/shard_map/ppermute | solution.py:51
  211.7 32.6 %collective-permute-start.48 = (bf16[128,1152]{1,0:T(8,128)(2,1)}, bf16[128,1152]{1,0:T(8,128)(2,1)}, u32[]{:S(2)}, u32[]{:S(2)}) collective-permute-start(bf16[128,1152]{1,0:T(8,128)(2,1)} %get-tuple-element.318), channel_id=1, source_target_pairs={{0,4},{2,6},{4,0},{6,2},{8,12},{10,14},{12,8},{14,10},{16,20},{18,... | collective-permute-start | bytes 884744 | tf_op jit(solution)/shard_map/ppermute | solution.py:51
  230.0 43.6 %collective-permute-start.45 = (bf16[256,1536]{1,0:T(8,128)(2,1)}, bf16[256,1536]{1,0:T(8,128)(2,1)}, u32[]{:S(2)}, u32[]{:S(2)}) collective-permute-start(bf16[256,1536]{1,0:T(8,128)(2,1)} %get-tuple-element.287), channel_id=1, source_target_pairs={{0,2},{2,0},{4,6},{6,4},{8,10},{10,8},{12,14},{14,12},{16,18},{18,... | collective-permute-start | bytes 2359304 | tf_op jit(solution)/shard_map/ppermute | solution.py:51
  230.8 42.9 %collective-permute-start.46 = (bf16[256,1536]{1,0:T(8,128)(2,1)}, bf16[256,1536]{1,0:T(8,128)(2,1)}, u32[]{:S(2)}, u32[]{:S(2)}) collective-permute-start(bf16[256,1536]{1,0:T(8,128)(2,1)} %get-tuple-element.286), channel_id=1, source_target_pairs={{0,4},{2,6},{4,0},{6,2},{8,12},{10,14},{12,8},{14,10},{16,20},{18,... | collective-permute-start | bytes 2359304 | tf_op jit(solution)/shard_map/ppermute | solution.py:51
  247.1 31.0 %collective-permute-start.49 = (bf16[256,1152]{1,0:T(8,128)(2,1)}, bf16[256,1152]{1,0:T(8,128)(2,1)}, u32[]{:S(2)}, u32[]{:S(2)}) collective-permute-start(bf16[256,1152]{1,0:T(8,128)(2,1)} %get-tuple-element.321), channel_id=1, source_target_pairs={{0,2},{2,0},{4,6},{6,4},{8,10},{10,8},{12,14},{14,12},{16,18},{18,... | collective-permute-start | bytes 1769480 | tf_op jit(solution)/shard_map/ppermute | solution.py:51
  248.4 31.4 %collective-permute-start.50 = (bf16[256,1152]{1,0:T(8,128)(2,1)}, bf16[256,1152]{1,0:T(8,128)(2,1)}, u32[]{:S(2)}, u32[]{:S(2)}) collective-permute-start(bf16[256,1152]{1,0:T(8,128)(2,1)} %get-tuple-element.322), channel_id=1, source_target_pairs={{0,4},{2,6},{4,0},{6,2},{8,12},{10,14},{12,8},{14,10},{16,20},{18,... | collective-permute-start | bytes 1769480 | tf_op jit(solution)/shard_map/ppermute | solution.py:51
  253.7 13.2 %collective-permute-start.44 = (bf16[128,1536]{1,0:T(8,128)(2,1)S(1)}, bf16[128,1536]{1,0:T(8,128)(2,1)}, u32[]{:S(2)}, u32[]{:S(2)}) collective-permute-start(bf16[128,1536]{1,0:T(8,128)(2,1)S(1)} %slice.309), channel_id=1, source_target_pairs={{0,8},{2,10},{4,12},{6,14},{8,0},{10,2},{12,4},{14,6},{16,24},{18,... | collective-permute-start | bytes 1179656 | tf_op jit(solution)/shard_map/ppermute | solution.py:51
  275.6 19.3 %collective-permute-start.51 = (bf16[128,1536]{1,0:T(8,128)(2,1)}, bf16[128,1536]{1,0:T(8,128)(2,1)S(1)}, u32[]{:S(2)}, u32[]{:S(2)}) collective-permute-start(bf16[128,1536]{1,0:T(8,128)(2,1)} %get-tuple-element.328), channel_id=1, source_target_pairs={{0,2},{2,0},{4,6},{6,4},{8,10},{10,8},{12,14},{14,12},{16,18},{18,... | collective-permute-start | bytes 1179656 | tf_op jit(solution)/shard_map/ppermute | solution.py:51
  276.5 18.5 %collective-permute-start.52 = (bf16[128,1536]{1,0:T(8,128)(2,1)}, bf16[128,1536]{1,0:T(8,128)(2,1)}, u32[]{:S(2)}, u32[]{:S(2)}) collective-permute-start(bf16[128,1536]{1,0:T(8,128)(2,1)} %get-tuple-element.329), channel_id=1, source_target_pairs={{0,4},{2,6},{4,0},{6,2},{8,12},{10,14},{12,8},{14,10},{16,20},{18,... | collective-permute-start | bytes 1179656 | tf_op jit(solution)/shard_map/ppermute | solution.py:51
  276.8 18.1 %collective-permute-start.53 = (bf16[128,1024]{1,0:T(8,128)(2,1)}, bf16[128,1024]{1,0:T(8,128)(2,1)}, u32[]{:S(2)}, u32[]{:S(2)}) collective-permute-start(bf16[128,1024]{1,0:T(8,128)(2,1)} %get-tuple-element.332), channel_id=1, source_target_pairs={{0,2},{2,0},{4,6},{6,4},{8,10},{10,8},{12,14},{14,12},{16,18},{18,... | collective-permute-start | bytes 786440 | tf_op jit(solution)/shard_map/ppermute | solution.py:51
  278.1 16.9 %collective-permute-start.54 = (bf16[128,1024]{1,0:T(8,128)(2,1)}, bf16[128,1024]{1,0:T(8,128)(2,1)}, u32[]{:S(2)}, u32[]{:S(2)}) collective-permute-start(bf16[128,1024]{1,0:T(8,128)(2,1)} %get-tuple-element.333), channel_id=1, source_target_pairs={{0,4},{2,6},{4,0},{6,2},{8,12},{10,14},{12,8},{14,10},{16,20},{18,... | collective-permute-start | bytes 786440 | tf_op jit(solution)/shard_map/ppermute | solution.py:51
  282.5 20.2 %collective-permute-start.55 = (bf16[128,2688]{1,0:T(8,128)(2,1)}, bf16[128,2688]{1,0:T(8,128)(2,1)}, u32[]{:S(2)}, u32[]{:S(2)}) collective-permute-start(bf16[128,2688]{1,0:T(8,128)(2,1)} %pad_maximum_fusion.1), channel_id=1, source_target_pairs={{0,8},{2,10},{4,12},{6,14},{8,0},{10,2},{12,4},{14,6},{16,24},{18,... | collective-permute-start | bytes 2064392 | tf_op jit(solution)/shard_map/ppermute | solution.py:51
  298.0 31.7 %collective-permute-start.59 = (bf16[256,1536]{1,0:T(8,128)(2,1)}, bf16[256,1536]{1,0:T(8,128)(2,1)}, u32[]{:S(2)}, u32[]{:S(2)}) collective-permute-start(bf16[256,1536]{1,0:T(8,128)(2,1)} %get-tuple-element.342), channel_id=1, source_target_pairs={{0,2},{2,0},{4,6},{6,4},{8,10},{10,8},{12,14},{14,12},{16,18},{18,... | collective-permute-start | bytes 2359304 | tf_op jit(solution)/shard_map/ppermute | solution.py:51
  298.8 31.5 %collective-permute-start.60 = (bf16[256,1536]{1,0:T(8,128)(2,1)}, bf16[256,1536]{1,0:T(8,128)(2,1)}, u32[]{:S(2)}, u32[]{:S(2)}) collective-permute-start(bf16[256,1536]{1,0:T(8,128)(2,1)} %get-tuple-element.341), channel_id=1, source_target_pairs={{0,4},{2,6},{4,0},{6,2},{8,12},{10,14},{12,8},{14,10},{16,20},{18,... | collective-permute-start | bytes 2359304 | tf_op jit(solution)/shard_map/ppermute | solution.py:51
  305.3 24.4 %collective-permute-start.56 = (bf16[64,4224]{1,0:T(8,128)(2,1)S(1)}, bf16[64,4224]{1,0:T(8,128)(2,1)S(1)}, u32[]{:S(2)}, u32[]{:S(2)}) collective-permute-start(bf16[64,4224]{1,0:T(8,128)(2,1)S(1)} %pad_maximum_fusion.2), channel_id=1, source_target_pairs={{0,16},{2,18},{4,20},{6,22},{8,24},{10,26},{12,28},{14,30},{16,0},... | collective-permute-start | bytes 1622024 | tf_op jit(solution)/shard_map/ppermute | solution.py:51
  307.6 24.5 %collective-permute-start.63 = (bf16[256,1024]{1,0:T(8,128)(2,1)S(1)}, bf16[256,1024]{1,0:T(8,128)(2,1)S(1)}, u32[]{:S(2)}, u32[]{:S(2)}) collective-permute-start(bf16[256,1024]{1,0:T(8,128)(2,1)S(1)} %copy-done.26), channel_id=1, source_target_pairs={{0,2},{2,0},{4,6},{6,4},{8,10},{10,8},{12,14},{14,12},{16,18},{18,... | collective-permute-start | bytes 1572872 | tf_op jit(solution)/shard_map/ppermute | solution.py:51
  308.9 23.2 %collective-permute-start.64 = (bf16[256,1024]{1,0:T(8,128)(2,1)S(1)}, bf16[256,1024]{1,0:T(8,128)(2,1)S(1)}, u32[]{:S(2)}, u32[]{:S(2)}) collective-permute-start(bf16[256,1024]{1,0:T(8,128)(2,1)S(1)} %copy-done.27), channel_id=1, source_target_pairs={{0,4},{2,6},{4,0},{6,2},{8,12},{10,14},{12,8},{14,10},{16,20},{18,... | collective-permute-start | bytes 1572872 | tf_op jit(solution)/shard_map/ppermute | solution.py:51
  329.7 36.6 %collective-permute-start.57 = (bf16[512,1024]{1,0:T(8,128)(2,1)S(1)}, bf16[512,1024]{1,0:T(8,128)(2,1)S(1)}, u32[]{:S(2)}, u32[]{:S(2)}) collective-permute-start(bf16[512,1024]{1,0:T(8,128)(2,1)S(1)} %copy-done.47), channel_id=1, source_target_pairs={{0,1},{1,0},{2,3},{3,2},{4,5},{5,4},{6,7},{7,6},{8,9},{9,8},{10,11... | collective-permute-start | bytes 3145736 | tf_op jit(solution)/shard_map/ppermute | solution.py:653
  (76 other events, 680.6 us)

commit v5 on v4

--- a/solution.py
+++ b/solution.py
@@ -729,18 +729,17 @@
     pair_mid = held_back(pair_mid, *outs[0].sent)
     sums, grads = ffn(pair_mid, pair_cot, mlp[2].pieces, sums, True)
     outs.append(Scatter(send, grads))
-    y_own, y_other, d_own, d_other = held_back(sums, *outs[1].got)
+    y_own, y_other, d_own, d_other = held_back(sums, *outs[0].got)
     outs[2].move(d_other)
 
     grad_mid_norm = d_own + swap(d_other).astype(wide)
     grad_middle = own_cot.astype(wide) + norm_back(grad_mid_norm, normed_mid, scale_mid)
     own_e = low(grad_middle)
     pair_e = (own_e, swap(own_e))
-    outs[1].move(own_e)
-    pair_e_late = held_back(pair_e, *outs[1].sent, *outs[0].got)
-    grad_normed, grad_unit, cross = unbranch(pair_e_late, attended, scale_out, proj_u, second.pieces)
+    grad_normed, grad_unit, cross = unbranch(pair_e, attended, scale_out, proj_u, second.pieces)
     other_cross = swap(cross)
-    pair_in_late = held_back(pair_in, grad_unit)
+    outs[1].move(grad_unit)
+    pair_in_late = held_back(pair_in, grad_unit, *outs[1].sent)
     grads = weight_grads((pair_in_late, pair_e), (grad_unit, gated))
     late = Scatter(send, grads)
     outs[0].move(grads[0], other_cross)
@@ -773,12 +772,13 @@
     late.move(total_own, *last.sent)
     while len(outs[0].moves) > 1:
         move_along(outs, total_own, *late.sent)
-    last.move(*outs[2].got)
-    late.move(*last.sent, *outs[2].got)
-    (y_other,) = held_back((y_other,), *outs[2].got)
+    last.move(*late.sent)
+    done = (*last.got, *outs[0].got)
+    late.move(*done)
+    (y_other,) = held_back((y_other,), *done)
     for out in (*outs, last, late):
         while out.moves:
-            out.move(total_own)
+            out.move(*done)
     grad_in_norm = total_own + swap(total_other).astype(wide)
     tokens_grad = grad_middle + norm_back(grad_in_norm, normed_in, scale_in)
     y_sum = y_own + swap(y_other).astype(wide)

time: 374 us -> 361 us (0.965)
  waiting for transfers between devices: 102 us -> 91 us
    ppermute x57, waiting for transfers between devices: 99.3 us -> 88.1 us  [__call__(): result = lax.ppermute(array, 'dp', pairs)]
    unnamed x120 -> x112, local copies, waits for them, and re-layouts: 13.6 us -> 15.1 us
  transfers between devices with their start and end apart: 67 -> 67, of which waited for: 23 -> 25; matrix products, arithmetic and copies ran while one was open for 12% -> 12% of each run, Pallas kernels for 32% -> 33%
where the time goes in v5:
time: 361 us; the launch traced here: 356 us
  Pallas kernels  121 us (34%)
  waiting for transfers between devices  91 us (25%)
  starting transfers between devices  78.3 us (22%)
  local copies, waits for them, and re-layouts  30.1 us (8%)
  other arithmetic  21.8 us (6%)
  matrix products  12.1 us (3%)
    ppermute x57, waiting for transfers between devices, __call__(): result = lax.ppermute(array, 'dp', pairs)  88.1 us
    ppermute x57, starting transfers between devices, __call__(): result = lax.ppermute(array, 'dp', pairs)  77.7 us
    pallas_call x3, Pallas kernels, ffn(): pl.pallas_call(functools.partial(ffn_kernel, chained=sums is not None, la...  42.4 us
    unnamed x112, local copies, waits for them, and re-layouts  15.1 us
    pallas_call x1, Pallas kernels, front(): pl.pallas_call(functools.partial(front_kernel, heads=rates.shape[0] // st...  13.4 us
    pallas_call x1, Pallas kernels, attend_back(): pl.pallas_call(functools.partial(attend_back_kernel, width=width), cost_e...  13 us
    pallas_call x2, Pallas kernels, weight_grads(): pl.pallas_call(functools.partial(weight_grad_kernel, count=count, each=le...  12.6 us
    dot_general x6, matrix products, dot(): lax.dot_general(left, right, (dims, ((), ())), preferred_element_type=wide)  12.1 us
  transfers between devices with their start and end apart: 67, of which 25 were waited for; matrix products, arithmetic and copies ran while one was open for 12% of the time, Pallas kernels for 33%

profile of v5, /device:TPU:0, one launch (start us, length us, event | category | flops | bytes accessed | tf_op | source)
XLA Modules:
  0.0 356.1 jit_solution(6025090902186047195)
XLA Ops:
  3.3 4.1 %collective-permute-start.2 = (bf16[64,1536]{1,0:T(8,128)(2,1)S(1)}, bf16[64,1536]{1,0:T(8,128)(2,1)S(1)}, u32[]{:S(2)}, u32[]{:S(2)}) collective-permute-start(bf16[64,1536]{1,0:T(8,128)(2,1)S(1)} %constant_dynamic-update-slice_fusion), channel_id=1, source_target_pairs={{0,16},{2,18},{4,20},{6,22},{8,24},{10,26},{12,28},{14,30},{16,0},... | collective-permute-start | bytes 589832 | tf_op jit(solution)/shard_map/ppermute | solution.py:51
  9.5 7.0 %collective-permute-done.2 = bf16[64,1536]{1,0:T(8,128)(2,1)S(1)} collective-permute-done((bf16[64,1536]{1,0:T(8,128)(2,1)S(1)}, bf16[64,1536]{1,0:T(8,128)(2,1)S(1)}, u32[]{:S(2)}, u32[]{:S(2)}) %collective-permute-start.2) | collective-permute-done | bytes 196640 | tf_op jit(solution)/shard_map/ppermute | solution.py:51
  17.7 9.2 %collective-permute-done.3 = bf16[128,1536]{1,0:T(8,128)(2,1)S(1)} collective-permute-done((bf16[128,1536]{1,0:T(8,128)(2,1)S(1)}, bf16[128,1536]{1,0:T(8,128)(2,1)S(1)}, u32[]{:S(2)}, u32[]{:S(2)}) %collective-permute-start.3) | collective-permute-done | bytes 393248 | tf_op jit(solution)/shard_map/ppermute | solution.py:51
  29.8 3.3 collective-permute-start.8
  33.2 2.3 fusion.26.refs_2_
  35.5 3.0 collective-permute-done.8
  39.4 5.5 %collective-permute-done.4.refs_1_.refs_6_.refs_11_.refs_5_.refs_10_.refs_15_ = bf16[256,1536]{1,0:T(8,128)(2,1)S(1)} collective-permute-done((bf16[256,1536]{1,0:T(8,128)(2,1)S(1)}, bf16[256,1536]{1,0:T(8,128)(2,1)S(1)}, u32[]{:S(2)}, u32[]{:S(2)}) %collective-permute-start.4) | collective-permute-done | bytes 786464 | tf_op jit(solution)/shard_map/ppermute | solution.py:51
  51.6 3.5 collective-permute-start.15
  55.1 2.0 collective-permute-done.6.refs_3_.refs_8_.refs_13_.refs_7_.refs_12_.refs_17_
  58.8 13.4 %shard_map.195 = (bf16[1024,512]{1,0:T(8,128)(2,1)}, bf16[1024,512]{1,0:T(8,128)(2,1)}, bf16[1024,512]{1,0:T(8,128)(2,1)}, bf16[1024,512]{1,0:T(8,128)(2,1)}, bf...) custom-call(s32[1]{0:T(128)} %bitcast.1.turn_ref, f32[4]{0:T(128)} %rate_ref.3, ...), custom_call_target="tpu_custom_call" | custom-call | flops 4831838208 | bytes 10485760 | tf_op jit(solution)/shard_map/pallas_call | solution.py:300
  74.3 2.4 collective-permute-start.16
  76.7 3.4 collective-permute-start.19
  80.2 4.0 %collective-permute-done.19 = bf16[64,1536]{1,0:T(8,128)(2,1)S(1)} collective-permute-done((bf16[64,1536]{1,0:T(8,128)(2,1)S(1)}, bf16[64,1536]{1,0:T(8,128)(2,1)S(1)}, u32[]{:S(2)}, u32[]{:S(2)}) %collective-permute-start.19) | collective-permute-done | bytes 196640 | tf_op jit(solution)/shard_map/ppermute | solution.py:51
  88.3 6.0 %collective-permute-start.20 = (bf16[128,1536]{1,0:T(8,128)(2,1)S(1)}, bf16[128,1536]{1,0:T(8,128)(2,1)S(1)}, u32[]{:S(2)}, u32[]{:S(2)}) collective-permute-start(bf16[128,1536]{1,0:T(8,128)(2,1)S(1)} %constant_dynamic-update-slice_fusion.11), channel_id=1, source_target_pairs={{0,8},{2,10},{4,12},{6,14},{8,0},{10,2},{12,4},{14,6},{16,24},{18,... | collective-permute-start | bytes 1179656 | tf_op jit(solution)/shard_map/ppermute | solution.py:51
  95.1 4.4 %shard_map.196.u_ref = f32[1024,512]{1,0:T(8,128)} custom-call(bf16[512,1024]{1,0:T(8,128)(2,1)} %copy-done.14, bf16[512,1024]{1,0:T(8,128)(2,1)} %copy-done.20, bf16[256,1024]{1,0:T(8,128)(2,1)} %copy-done.9, bf16[256,1024]{1,0:T(8,128)(2,1)} %copy-done.7, bf16[256,1024]{1,0:T(8,128)(2,1)} %copy-done.8, bf16[128,1024]{1,0:T(8,128)(2,1)} %copy-done.17, ...), custom_call_target="tpu_custom_call" | custom-call | flops 1073741824 | bytes 4194304 | tf_op jit(solution)/shard_map/pallas_call | solution.py:322
  100.2 6.0 %shard_map.197 = (bf16[1024,512]{1,0:T(8,128)(2,1)}, f32[1024,1]{1,0:T(8,128)}, f32[512,1024]{1,0:T(8,128)}, bf16[512,1024]{1,0:T(8,128)(2,1)}) custom-call(f32[8,1024]{1,0:T(8,128)} %get-tuple-element.199.sum_ref, f32[8,1024]{1,0:T(8,128)} %copy-done.41, f32[1024,512]{1,0:T(8,128)} %get-tuple-element.205.o_ref, f32[1024,512]{1,0:T(8,128)} %shard_map.196.u_ref, ...), custom_call_target="tpu_custom_call" | custom-call | flops 1073741824 | bytes 8388608 | tf_op jit(solution)/shard_map/pallas_call | solution.py:354
  110.9 2.1 multiply_reduce_fusion.1
  114.3 4.7 %collective-permute-done.25.refs_7_ = bf16[128,1536]{1,0:T(8,128)(2,1)S(1)} collective-permute-done((bf16[128,1536]{1,0:T(8,128)(2,1)S(1)}, bf16[128,1536]{1,0:T(8,128)(2,1)S(1)}, u32[]{:S(2)}, u32[]{:S(2)}) %collective-permute-start.25) | collective-permute-done | bytes 393248 | tf_op jit(solution)/shard_map/ppermute | solution.py:51
  119.0 2.0 collective-permute-done.26.refs_8_
  128.1 14.9 %shard_map.198 = (f32[512,1024]{1,0:T(8,128)}, f32[512,1024]{1,0:T(8,128)}, f32[512,1024]{1,0:T(8,128)}, f32[512,1024]{1,0:T(8,128)}, bf16[256,1536]{1,0:T(8,128...) custom-call(bf16[512,1024]{1,0:T(8,128)(2,1)} %copy-done.21, ...), custom_call_target="tpu_custom_call" | custom-call | flops 9663676416 | bytes 14680064 | tf_op jit(solution)/shard_map/pallas_call | solution.py:605
  150.4 5.5 %collective-permute-done.33.refs_5_ = bf16[256,1152]{1,0:T(8,128)(2,1)} collective-permute-done((bf16[256,1152]{1,0:T(8,128)(2,1)}, bf16[256,1152]{1,0:T(8,128)(2,1)}, u32[]{:S(2)}, u32[]{:S(2)}) %collective-permute-start.33) | collective-permute-done | bytes 589856 | tf_op jit(solution)/shard_map/ppermute | solution.py:51
  162.2 3.2 collective-permute-done.31.refs_7_
  167.0 14.6 %shard_map.199 = (f32[512,1024]{1,0:T(8,128)}, f32[512,1024]{1,0:T(8,128)}, f32[512,1024]{1,0:T(8,128)}, f32[512,1024]{1,0:T(8,128)}, bf16[256,1536]{1,0:T(8,128...) custom-call(bf16[512,1024]{1,0:T(8,128)(2,1)} %copy-done.21, ...), custom_call_target="tpu_custom_call" | custom-call | flops 9663676416 | bytes 31457280 | tf_op jit(solution)/shard_map/pallas_call | solution.py:605
  182.4 2.4 shard_map.200
  187.7 12.9 %shard_map.201 = (f32[512,1024]{1,0:T(8,128)}, bf16[512,1024]{1,0:T(8,128)(2,1)}, f32[512,1024]{1,0:T(8,128)}, bf16[512,1024]{1,0:T(8,128)(2,1)}, bf16[256,1152]...) custom-call(bf16[512,1024]{1,0:T(8,128)(2,1)} %copy-done.21, ...), custom_call_target="tpu_custom_call" | custom-call | flops 7247757312 | bytes 29884416 | tf_op jit(solution)/shard_map/pallas_call | solution.py:605
  201.6 2.9 collective-permute-done.39
  204.5 2.1 multiply_reduce_fusion
  206.6 3.2 fusion.32
  216.0 7.2 %shard_map.202 = (f32[1024,512]{1,0:T(8,128)}, bf16[1024,512]{1,0:T(8,128)(2,1)}, f32[8,1024]{1,0:T(8,128)}) custom-call(bf16[512,1024]{1,0:T(8,128)(2,1)} %copy-done.13, bf16[512,1024]{1,0:T(8,128)(2,1)} %copy-done.19, f32[1024,512]{1,0:T(8,128)} %get-tuple-element.205.o_ref, f32[1024,1]{1,0:T(8,128)} %get-tuple-element.274.scale_ref, ...), custom_call_target="tpu_custom_call" | custom-call | flops 1073741824 | bytes 8388608 | tf_op jit(solution)/shard_map/pallas_call | solution.py:385
  224.3 2.4 shard_map.203
  228.8 5.9 %shard_map.204 = (bf16[256,1024]{1,0:T(8,128)(2,1)}, bf16[256,1024]{1,0:T(8,128)(2,1)}, bf16[256,1024]{1,0:T(8,128)(2,1)}, bf16[128,1024]{1,0:T(8,128)(2,1)}, bf16[128,1024]{1,0:T(8,128)(2,1)}) custom-call(bf16[512,1024]{1,0:T(8,128)(2,1)} %copy-done.14, bf16[512,1024]{1,0:T(8,128)(2,1)} %copy-done.20, bf16[512,1024]{1,0:T(8,128)(2,1)} %copy-done.13, ...), custom_call_target="tpu_custom_call" | custom-call | flops 2147483648 | bytes 6291456 | tf_op jit(solution)/shard_map/pallas_call | solution.py:494
  234.7 2.1 shard_map.207
  239.3 1.9 add_add_fusion.3
  242.5 13.0 %shard_map.205 = (bf16[1024,512]{1,0:T(8,128)(2,1)}, bf16[1024,512]{1,0:T(8,128)(2,1)}, bf16[1024,512]{1,0:T(8,128)(2,1)}) custom-call(s32[1]{0:T(128)} %bitcast.1.turn_ref, f32[4]{0:T(128)} %rate_ref.3, f32[1024,1]{1,0:T(8,128)} %get-tuple-element.274.scale_ref, f32[8,1024]{1,0:T(8,128)} %get-tuple-element.277.cross_ref, f32[8,1024]{1,0:T(8,128)} %copy-done.49, ...), custom_call_target="tpu_custom_call" | custom-call | flops 6442450944 | bytes 28311552 | tf_op jit(solution)/shard_map/pallas_call | solution.py:461
  255.5 6.7 %shard_map.206 = (bf16[256,1536]{1,0:T(8,128)(2,1)}, bf16[256,1536]{1,0:T(8,128)(2,1)}, bf16[256,1536]{1,0:T(8,128)(2,1)}, bf16[128,1536]{1,0:T(8,128)(2,1)}, bf16[128,1536]{1,0:T(8,128)(2,1)}) custom-call(bf16[512,1024]{1,0:T(8,128)(2,1)} %copy-done.14, bf16[512,1024]{1,0:T(8,128)(2,1)} %copy-done.20, bf16[1024,512]{1,0:T(8,128)(2,1)} %get-tuple-element.325.refs_2_.refs_0_, ...), custom_call_target="tpu_custom_call" | custom-call | flops 3221225472 | bytes 8388608 | tf_op jit(solution)/shard_map/pallas_call | solution.py:494
  271.9 2.0 collective-permute-start.57
  273.9 10.5 %shard_map.208 = (f32[512,1024]{1,0:T(8,128)}, bf16[512,1024]{1,0:T(8,128)(2,1)}) custom-call(bf16[1024,512]{1,0:T(8,128)(2,1)} %get-tuple-element.325.refs_2_.refs_0_, bf16[1024,512]{1,0:T(8,128)(2,1)} %get-tuple-element.306.refs_3_.refs_1_, bf16[1024,512]{1,0:T(8,128)(2,1)} %get-tuple-element.307.refs_4_.refs_2_, ...), custom_call_target="tpu_custom_call" | custom-call | flops 4294967296 | bytes 12582912 | tf_op jit(solution)/shard_map/pallas_call | solution.py:521
  285.2 2.4 shard_map.209
  289.7 2.1 shard_map.210
  297.6 10.7 %collective-permute-done.55 = bf16[256,1536]{1,0:T(8,128)(2,1)} collective-permute-done((bf16[256,1536]{1,0:T(8,128)(2,1)}, bf16[256,1536]{1,0:T(8,128)(2,1)}, u32[]{:S(2)}, u32[]{:S(2)}) %collective-permute-start.55) | collective-permute-done | bytes 786464 | tf_op jit(solution)/shard_map/ppermute | solution.py:51
  308.3 2.3 collective-permute-start.59
  317.6 2.8 add_add_fusion
  320.3 10.0 %collective-permute-done.59 = bf16[64,4224]{1,0:T(8,128)(2,1)S(1)} collective-permute-done((bf16[64,4224]{1,0:T(8,128)(2,1)S(1)}, bf16[64,4224]{1,0:T(8,128)(2,1)S(1)}, u32[]{:S(2)}, u32[]{:S(2)}) %collective-permute-start.59) | collective-permute-done | bytes 540704 | tf_op jit(solution)/shard_map/ppermute | solution.py:51
  331.0 2.8 collective-permute-start.65
  336.3 6.4 %collective-permute-done.62 = bf16[64,1536]{1,0:T(8,128)(2,1)S(1)} collective-permute-done((bf16[64,1536]{1,0:T(8,128)(2,1)S(1)}, bf16[64,1536]{1,0:T(8,128)(2,1)S(1)}, u32[]{:S(2)}, u32[]{:S(2)}) %collective-permute-start.62) | collective-permute-done | bytes 196640 | tf_op jit(solution)/shard_map/ppermute | solution.py:51
  342.8 1.9 collective-permute-done.65
  345.6 7.0 %collective-permute-done.66 = bf16[64,1024]{1,0:T(8,128)(2,1)S(1)} collective-permute-done((bf16[64,1024]{1,0:T(8,128)(2,1)S(1)}, bf16[64,1024]{1,0:T(8,128)(2,1)S(1)}, u32[]{:S(2)}, u32[]{:S(2)}) %collective-permute-start.66) | collective-permute-done | bytes 131104 | tf_op jit(solution)/shard_map/ppermute | solution.py:51
  353.4 2.4 fusion.25
  (303 shorter events, 101.7 us)
Async XLA Ops:
  3.3 13.2 %collective-permute-start.2 = (bf16[64,1536]{1,0:T(8,128)(2,1)S(1)}, bf16[64,1536]{1,0:T(8,128)(2,1)S(1)}, u32[]{:S(2)}, u32[]{:S(2)}) collective-permute-start(bf16[64,1536]{1,0:T(8,128)(2,1)S(1)} %constant_dynamic-update-slice_fusion), channel_id=1, source_target_pairs={{0,16},{2,18},{4,20},{6,22},{8,24},{10,26},{12,28},{14,30},{16,0},... | collective-permute-start | bytes 589832 | tf_op jit(solution)/shard_map/ppermute | solution.py:51
  17.6 31.3 %collective-permute-start = (bf16[512,1024]{1,0:T(8,128)(2,1)S(1)}, bf16[512,1024]{1,0:T(8,128)(2,1)S(1)}, u32[]{:S(2)}, u32[]{:S(2)}) collective-permute-start(bf16[512,1024]{1,0:T(8,128)(2,1)S(1)} %fusion.10.own_ref.refs_0_), channel_id=1, source_target_pairs={{0,1},{1,0},{2,3},{3,2},{4,5},{5,4},{6,7},{7,6},{8,9},{9,8},{10,11... | collective-permute-start | bytes 3145736 | tf_op jit(solution)/shard_map/ppermute | solution.py:653
  27.0 17.9 %collective-permute-start.4 = (bf16[256,1536]{1,0:T(8,128)(2,1)S(1)}, bf16[256,1536]{1,0:T(8,128)(2,1)S(1)}, u32[]{:S(2)}, u32[]{:S(2)}) collective-permute-start(bf16[256,1536]{1,0:T(8,128)(2,1)S(1)} %pad_maximum_fusion.refs_0_.refs_5_.refs_10_.refs_4_.refs_9_.refs_14_), channel_id=1, source_target_pairs={{0,2},{2,0},{4,6},{6,4},{8,10},{10,8},{12,14},{14,12},{16,18},{18,... | collective-permute-start | bytes 2359304 | tf_op jit(solution)/shard_map/ppermute | solution.py:51
  28.3 18.3 %collective-permute-start.5 = (bf16[256,1536]{1,0:T(8,128)(2,1)S(1)}, bf16[256,1536]{1,0:T(8,128)(2,1)S(1)}, u32[]{:S(2)}, u32[]{:S(2)}) collective-permute-start(bf16[256,1536]{1,0:T(8,128)(2,1)S(1)} %pad_maximum_fusion.refs_0_.refs_5_.refs_10_.refs_4_.refs_9_.refs_14_), channel_id=1, source_target_pairs={{0,4},{2,6},{4,0},{6,2},{8,12},{10,14},{12,8},{14,10},{16,20},{18,... | collective-permute-start | bytes 2359304 | tf_op jit(solution)/shard_map/ppermute | solution.py:51
  35.5 16.1 %collective-permute-start.1 = (bf16[512,1024]{1,0:T(8,128)(2,1)}, bf16[512,1024]{1,0:T(8,128)(2,1)}, u32[]{:S(2)}, u32[]{:S(2)}) collective-permute-start(bf16[512,1024]{1,0:T(8,128)(2,1)} %fusion.26.refs_2_), channel_id=1, source_target_pairs={{0,1},{1,0},{2,3},{3,2},{4,5},{5,4},{6,7},{7,6},{8,9},{9,8},{10,11... | collective-permute-start | bytes 3145736 | tf_op jit(solution)/shard_map/ppermute | solution.py:653
  46.6 12.2 %collective-permute-start.7 = (bf16[128,1536]{1,0:T(8,128)(2,1)S(1)}, bf16[128,1536]{1,0:T(8,128)(2,1)}, u32[]{:S(2)}, u32[]{:S(2)}) collective-permute-start(bf16[128,1536]{1,0:T(8,128)(2,1)S(1)} %slice.243), channel_id=1, source_target_pairs={{0,2},{2,0},{4,6},{6,4},{8,10},{10,8},{12,14},{14,12},{16,18},{18,... | collective-permute-start | bytes 1179656 | tf_op jit(solution)/shard_map/ppermute | solution.py:51
  47.9 24.3 %collective-permute-start.10 = (bf16[256,1024]{1,0:T(8,128)(2,1)S(1)}, bf16[256,1024]{1,0:T(8,128)(2,1)S(1)}, u32[]{:S(2)}, u32[]{:S(2)}) collective-permute-start(bf16[256,1024]{1,0:T(8,128)(2,1)S(1)} %constant_dynamic-update-slice_fusion.5.refs_0_.refs_19_), channel_id=1, source_target_pairs={{0,2},{2,0},{4,6},{6,4},{8,10},{10,8},{12,14},{14,12},{16,18},{18,... | collective-permute-start | bytes 1572872 | tf_op jit(solution)/shard_map/ppermute | solution.py:51
  49.8 22.4 %collective-permute-start.11 = (bf16[256,1024]{1,0:T(8,128)(2,1)S(1)}, bf16[256,1024]{1,0:T(8,128)(2,1)S(1)}, u32[]{:S(2)}, u32[]{:S(2)}) collective-permute-start(bf16[256,1024]{1,0:T(8,128)(2,1)S(1)} %constant_dynamic-update-slice_fusion.5.refs_0_.refs_19_), channel_id=1, source_target_pairs={{0,4},{2,6},{4,0},{6,2},{8,12},{10,14},{12,8},{14,10},{16,20},{18,... | collective-permute-start | bytes 1572872 | tf_op jit(solution)/shard_map/ppermute | solution.py:51
  51.6 22.6 %collective-permute-start.15 = (bf16[64,1536]{1,0:T(8,128)(2,1)S(1)}, bf16[64,1536]{1,0:T(8,128)(2,1)S(1)}, u32[]{:S(2)}, u32[]{:S(2)}) collective-permute-start(bf16[64,1536]{1,0:T(8,128)(2,1)S(1)} %pad_maximum_fusion.6), channel_id=1, source_target_pairs={{0,16},{2,18},{4,20},{6,22},{8,24},{10,26},{12,28},{14,30},{16,0},... | collective-permute-start | bytes 589832 | tf_op jit(solution)/shard_map/ppermute | solution.py:51
  86.2 20.1 %collective-permute-start.17 = (bf16[256,1536]{1,0:T(8,128)(2,1)}, bf16[256,1536]{1,0:T(8,128)(2,1)}, u32[]{:S(2)}, u32[]{:S(2)}) collective-permute-start(bf16[256,1536]{1,0:T(8,128)(2,1)} %constant_dynamic-update-slice_fusion.9.refs_4_), channel_id=1, source_target_pairs={{0,2},{2,0},{4,6},{6,4},{8,10},{10,8},{12,14},{14,12},{16,18},{18,... | collective-permute-start | bytes 2359304 | tf_op jit(solution)/shard_map/ppermute | solution.py:51
  87.8 18.4 %collective-permute-start.18 = (bf16[256,1536]{1,0:T(8,128)(2,1)}, bf16[256,1536]{1,0:T(8,128)(2,1)}, u32[]{:S(2)}, u32[]{:S(2)}) collective-permute-start(bf16[256,1536]{1,0:T(8,128)(2,1)} %constant_dynamic-update-slice_fusion.9.refs_4_), channel_id=1, source_target_pairs={{0,4},{2,6},{4,0},{6,2},{8,12},{10,14},{12,8},{14,10},{16,20},{18,... | collective-permute-start | bytes 2359304 | tf_op jit(solution)/shard_map/ppermute | solution.py:51
  88.3 18.0 %collective-permute-start.20 = (bf16[128,1536]{1,0:T(8,128)(2,1)S(1)}, bf16[128,1536]{1,0:T(8,128)(2,1)S(1)}, u32[]{:S(2)}, u32[]{:S(2)}) collective-permute-start(bf16[128,1536]{1,0:T(8,128)(2,1)S(1)} %constant_dynamic-update-slice_fusion.11), channel_id=1, source_target_pairs={{0,8},{2,10},{4,12},{6,14},{8,0},{10,2},{12,4},{14,6},{16,24},{18,... | collective-permute-start | bytes 1179656 | tf_op jit(solution)/shard_map/ppermute | solution.py:51
  114.2 13.9 %collective-permute-start.23 = (bf16[512,1024]{1,0:T(8,128)(2,1)S(1)}, bf16[512,1024]{1,0:T(8,128)(2,1)}, u32[]{:S(2)}, u32[]{:S(2)}) collective-permute-start(bf16[512,1024]{1,0:T(8,128)(2,1)S(1)} %multiply_convert_fusion.refs_0_), channel_id=1, source_target_pairs={{0,1},{1,0},{2,3},{3,2},{4,5},{5,4},{6,7},{7,6},{8,9},{9,8},{10,11... | collective-permute-start | bytes 3145736 | tf_op jit(solution)/shard_map/ppermute | solution.py:653
  122.5 20.7 %collective-permute-start.29 = (bf16[256,1536]{1,0:T(8,128)(2,1)}, bf16[256,1536]{1,0:T(8,128)(2,1)}, u32[]{:S(2)}, u32[]{:S(2)}) collective-permute-start(bf16[256,1536]{1,0:T(8,128)(2,1)} %constant_dynamic-update-slice_fusion.15.refs_4_), channel_id=1, source_target_pairs={{0,2},{2,0},{4,6},{6,4},{8,10},{10,8},{12,14},{14,12},{16,18},{18,... | collective-permute-start | bytes 2359304 | tf_op jit(solution)/shard_map/ppermute | solution.py:51
  123.7 20.7 %collective-permute-start.30 = (bf16[256,1536]{1,0:T(8,128)(2,1)}, bf16[256,1536]{1,0:T(8,128)(2,1)}, u32[]{:S(2)}, u32[]{:S(2)}) collective-permute-start(bf16[256,1536]{1,0:T(8,128)(2,1)} %constant_dynamic-update-slice_fusion.15.refs_4_), channel_id=1, source_target_pairs={{0,4},{2,6},{4,0},{6,2},{8,12},{10,14},{12,8},{14,10},{16,20},{18,... | collective-permute-start | bytes 2359304 | tf_op jit(solution)/shard_map/ppermute | solution.py:51
  126.9 29.0 %collective-permute-start.33 = (bf16[256,1152]{1,0:T(8,128)(2,1)}, bf16[256,1152]{1,0:T(8,128)(2,1)}, u32[]{:S(2)}, u32[]{:S(2)}) collective-permute-start(bf16[256,1152]{1,0:T(8,128)(2,1)} %constant_dynamic-update-slice_fusion.17.refs_4_), channel_id=1, source_target_pairs={{0,2},{2,0},{4,6},{6,4},{8,10},{10,8},{12,14},{14,12},{16,18},{18,... | collective-permute-start | bytes 1769480 | tf_op jit(solution)/shard_map/ppermute | solution.py:51
  127.2 29.9 %collective-permute-start.34 = (bf16[256,1152]{1,0:T(8,128)(2,1)}, bf16[256,1152]{1,0:T(8,128)(2,1)}, u32[]{:S(2)}, u32[]{:S(2)}) collective-permute-start(bf16[256,1152]{1,0:T(8,128)(2,1)} %constant_dynamic-update-slice_fusion.17.refs_4_), channel_id=1, source_target_pairs={{0,4},{2,6},{4,0},{6,2},{8,12},{10,14},{12,8},{14,10},{16,20},{18,... | collective-permute-start | bytes 1769480 | tf_op jit(solution)/shard_map/ppermute | solution.py:51
  145.5 19.9 %collective-permute-start.31 = (bf16[128,1536]{1,0:T(8,128)(2,1)S(1)}, bf16[128,1536]{1,0:T(8,128)(2,1)S(1)}, u32[]{:S(2)}, u32[]{:S(2)}) collective-permute-start(bf16[128,1536]{1,0:T(8,128)(2,1)S(1)} %slice.199), channel_id=1, source_target_pairs={{0,4},{2,6},{4,0},{6,2},{8,12},{10,14},{12,8},{14,10},{16,20},{18,... | collective-permute-start | bytes 1179656 | tf_op jit(solution)/shard_map/ppermute | solution.py:51
  148.3 18.0 %collective-permute-start.32 = (bf16[128,1536]{1,0:T(8,128)(2,1)S(1)}, bf16[128,1536]{1,0:T(8,128)(2,1)S(1)}, u32[]{:S(2)}, u32[]{:S(2)}) collective-permute-start(bf16[128,1536]{1,0:T(8,128)(2,1)S(1)} %slice.200), channel_id=1, source_target_pairs={{0,2},{2,0},{4,6},{6,4},{8,10},{10,8},{12,14},{14,12},{16,18},{18,... | collective-permute-start | bytes 1179656 | tf_op jit(solution)/shard_map/ppermute | solution.py:51
  148.6 33.0 %collective-permute-start.27 = (bf16[128,1536]{1,0:T(8,128)(2,1)}, bf16[128,1536]{1,0:T(8,128)(2,1)S(1)}, u32[]{:S(2)}, u32[]{:S(2)}) collective-permute-start(bf16[128,1536]{1,0:T(8,128)(2,1)} %get-tuple-element.240), channel_id=1, source_target_pairs={{0,2},{2,0},{4,6},{6,4},{8,10},{10,8},{12,14},{14,12},{16,18},{18,... | collective-permute-start | bytes 1179656 | tf_op jit(solution)/shard_map/ppermute | solution.py:51
  155.9 25.7 %collective-permute-start.28 = (bf16[128,1536]{1,0:T(8,128)(2,1)}, bf16[128,1536]{1,0:T(8,128)(2,1)}, u32[]{:S(2)}, u32[]{:S(2)}) collective-permute-start(bf16[128,1536]{1,0:T(8,128)(2,1)} %get-tuple-element.241), channel_id=1, source_target_pairs={{0,4},{2,6},{4,0},{6,2},{8,12},{10,14},{12,8},{14,10},{16,20},{18,... | collective-permute-start | bytes 1179656 | tf_op jit(solution)/shard_map/ppermute | solution.py:51
  158.8 22.8 %collective-permute-start.35 = (bf16[128,1152]{1,0:T(8,128)(2,1)}, bf16[128,1152]{1,0:T(8,128)(2,1)}, u32[]{:S(2)}, u32[]{:S(2)}) collective-permute-start(bf16[128,1152]{1,0:T(8,128)(2,1)} %slice.201), channel_id=1, source_target_pairs={{0,4},{2,6},{4,0},{6,2},{8,12},{10,14},{12,8},{14,10},{16,20},{18,... | collective-permute-start | bytes 884744 | tf_op jit(solution)/shard_map/ppermute | solution.py:51
  165.4 16.2 %collective-permute-start.36 = (bf16[128,1152]{1,0:T(8,128)(2,1)}, bf16[128,1152]{1,0:T(8,128)(2,1)}, u32[]{:S(2)}, u32[]{:S(2)}) collective-permute-start(bf16[128,1152]{1,0:T(8,128)(2,1)} %slice.202), channel_id=1, source_target_pairs={{0,2},{2,0},{4,6},{6,4},{8,10},{10,8},{12,14},{14,12},{16,18},{18,... | collective-permute-start | bytes 884744 | tf_op jit(solution)/shard_map/ppermute | solution.py:51
  184.8 16.1 %collective-permute-start.37 = (bf16[256,1536]{1,0:T(8,128)(2,1)}, bf16[256,1536]{1,0:T(8,128)(2,1)}, u32[]{:S(2)}, u32[]{:S(2)}) collective-permute-start(bf16[256,1536]{1,0:T(8,128)(2,1)} %get-tuple-element.261), channel_id=1, source_target_pairs={{0,2},{2,0},{4,6},{6,4},{8,10},{10,8},{12,14},{14,12},{16,18},{18,... | collective-permute-start | bytes 2359304 | tf_op jit(solution)/shard_map/ppermute | solution.py:51
  186.0 15.6 %collective-permute-start.38 = (bf16[256,1536]{1,0:T(8,128)(2,1)}, bf16[256,1536]{1,0:T(8,128)(2,1)}, u32[]{:S(2)}, u32[]{:S(2)}) collective-permute-start(bf16[256,1536]{1,0:T(8,128)(2,1)} %get-tuple-element.260), channel_id=1, source_target_pairs={{0,4},{2,6},{4,0},{6,2},{8,12},{10,14},{12,8},{14,10},{16,20},{18,... | collective-permute-start | bytes 2359304 | tf_op jit(solution)/shard_map/ppermute | solution.py:51
  210.9 12.3 %collective-permute-start.42 = (bf16[128,1536]{1,0:T(8,128)(2,1)}, bf16[128,1536]{1,0:T(8,128)(2,1)S(1)}, u32[]{:S(2)}, u32[]{:S(2)}) collective-permute-start(bf16[128,1536]{1,0:T(8,128)(2,1)} %get-tuple-element.289), channel_id=1, source_target_pairs={{0,2},{2,0},{4,6},{6,4},{8,10},{10,8},{12,14},{14,12},{16,18},{18,... | collective-permute-start | bytes 1179656 | tf_op jit(solution)/shard_map/ppermute | solution.py:51
  212.0 12.3 %collective-permute-start.43 = (bf16[128,1536]{1,0:T(8,128)(2,1)}, bf16[128,1536]{1,0:T(8,128)(2,1)}, u32[]{:S(2)}, u32[]{:S(2)}) collective-permute-start(bf16[128,1536]{1,0:T(8,128)(2,1)} %get-tuple-element.290), channel_id=1, source_target_pairs={{0,4},{2,6},{4,0},{6,2},{8,12},{10,14},{12,8},{14,10},{16,20},{18,... | collective-permute-start | bytes 1179656 | tf_op jit(solution)/shard_map/ppermute | solution.py:51
  213.1 21.6 %collective-permute-start.49 = (bf16[128,1152]{1,0:T(8,128)(2,1)}, bf16[128,1152]{1,0:T(8,128)(2,1)}, u32[]{:S(2)}, u32[]{:S(2)}) collective-permute-start(bf16[128,1152]{1,0:T(8,128)(2,1)} %get-tuple-element.319), channel_id=1, source_target_pairs={{0,2},{2,0},{4,6},{6,4},{8,10},{10,8},{12,14},{14,12},{16,18},{18,... | collective-permute-start | bytes 884744 | tf_op jit(solution)/shard_map/ppermute | solution.py:51
  214.1 20.6 %collective-permute-start.50 = (bf16[128,1152]{1,0:T(8,128)(2,1)}, bf16[128,1152]{1,0:T(8,128)(2,1)}, u32[]{:S(2)}, u32[]{:S(2)}) collective-permute-start(bf16[128,1152]{1,0:T(8,128)(2,1)} %get-tuple-element.320), channel_id=1, source_target_pairs={{0,4},{2,6},{4,0},{6,2},{8,12},{10,14},{12,8},{14,10},{16,20},{18,... | collective-permute-start | bytes 884744 | tf_op jit(solution)/shard_map/ppermute | solution.py:51
  226.6 40.5 %collective-permute-start.47 = (bf16[256,1536]{1,0:T(8,128)(2,1)}, bf16[256,1536]{1,0:T(8,128)(2,1)}, u32[]{:S(2)}, u32[]{:S(2)}) collective-permute-start(bf16[256,1536]{1,0:T(8,128)(2,1)} %get-tuple-element.294), channel_id=1, source_target_pairs={{0,2},{2,0},{4,6},{6,4},{8,10},{10,8},{12,14},{14,12},{16,18},{18,... | collective-permute-start | bytes 2359304 | tf_op jit(solution)/shard_map/ppermute | solution.py:51
  227.6 40.5 %collective-permute-start.48 = (bf16[256,1536]{1,0:T(8,128)(2,1)}, bf16[256,1536]{1,0:T(8,128)(2,1)}, u32[]{:S(2)}, u32[]{:S(2)}) collective-permute-start(bf16[256,1536]{1,0:T(8,128)(2,1)} %get-tuple-element.293), channel_id=1, source_target_pairs={{0,4},{2,6},{4,0},{6,2},{8,12},{10,14},{12,8},{14,10},{16,20},{18,... | collective-permute-start | bytes 2359304 | tf_op jit(solution)/shard_map/ppermute | solution.py:51
  236.8 26.4 %collective-permute-start.51 = (bf16[256,1152]{1,0:T(8,128)(2,1)}, bf16[256,1152]{1,0:T(8,128)(2,1)}, u32[]{:S(2)}, u32[]{:S(2)}) collective-permute-start(bf16[256,1152]{1,0:T(8,128)(2,1)} %get-tuple-element.323), channel_id=1, source_target_pairs={{0,2},{2,0},{4,6},{6,4},{8,10},{10,8},{12,14},{14,12},{16,18},{18,... | collective-permute-start | bytes 1769480 | tf_op jit(solution)/shard_map/ppermute | solution.py:51
  237.9 26.6 %collective-permute-start.52 = (bf16[256,1152]{1,0:T(8,128)(2,1)}, bf16[256,1152]{1,0:T(8,128)(2,1)}, u32[]{:S(2)}, u32[]{:S(2)}) collective-permute-start(bf16[256,1152]{1,0:T(8,128)(2,1)} %get-tuple-element.324), channel_id=1, source_target_pairs={{0,4},{2,6},{4,0},{6,2},{8,12},{10,14},{12,8},{14,10},{16,20},{18,... | collective-permute-start | bytes 1769480 | tf_op jit(solution)/shard_map/ppermute | solution.py:51
  242.4 13.1 %collective-permute-start.44 = (bf16[128,1536]{1,0:T(8,128)(2,1)S(1)}, bf16[128,1536]{1,0:T(8,128)(2,1)}, u32[]{:S(2)}, u32[]{:S(2)}) collective-permute-start(bf16[128,1536]{1,0:T(8,128)(2,1)S(1)} %slice.309), channel_id=1, source_target_pairs={{0,8},{2,10},{4,12},{6,14},{8,0},{10,2},{12,4},{14,6},{16,24},{18,... | collective-permute-start | bytes 1179656 | tf_op jit(solution)/shard_map/ppermute | solution.py:51
  262.2 22.2 %collective-permute-start.45 = (bf16[128,1536]{1,0:T(8,128)(2,1)}, bf16[128,1536]{1,0:T(8,128)(2,1)S(1)}, u32[]{:S(2)}, u32[]{:S(2)}) collective-permute-start(bf16[128,1536]{1,0:T(8,128)(2,1)} %get-tuple-element.313), channel_id=1, source_target_pairs={{0,2},{2,0},{4,6},{6,4},{8,10},{10,8},{12,14},{14,12},{16,18},{18,... | collective-permute-start | bytes 1179656 | tf_op jit(solution)/shard_map/ppermute | solution.py:51
  263.2 21.2 %collective-permute-start.46 = (bf16[128,1536]{1,0:T(8,128)(2,1)}, bf16[128,1536]{1,0:T(8,128)(2,1)}, u32[]{:S(2)}, u32[]{:S(2)}) collective-permute-start(bf16[128,1536]{1,0:T(8,128)(2,1)} %get-tuple-element.314), channel_id=1, source_target_pairs={{0,4},{2,6},{4,0},{6,2},{8,12},{10,14},{12,8},{14,10},{16,20},{18,... | collective-permute-start | bytes 1179656 | tf_op jit(solution)/shard_map/ppermute | solution.py:51
  264.4 20.0 %collective-permute-start.53 = (bf16[128,1024]{1,0:T(8,128)(2,1)}, bf16[128,1024]{1,0:T(8,128)(2,1)}, u32[]{:S(2)}, u32[]{:S(2)}) collective-permute-start(bf16[128,1024]{1,0:T(8,128)(2,1)} %get-tuple-element.330), channel_id=1, source_target_pairs={{0,2},{2,0},{4,6},{6,4},{8,10},{10,8},{12,14},{14,12},{16,18},{18,... | collective-permute-start | bytes 786440 | tf_op jit(solution)/shard_map/ppermute | solution.py:51
  267.1 17.3 %collective-permute-start.54 = (bf16[128,1024]{1,0:T(8,128)(2,1)}, bf16[128,1024]{1,0:T(8,128)(2,1)}, u32[]{:S(2)}, u32[]{:S(2)}) collective-permute-start(bf16[128,1024]{1,0:T(8,128)(2,1)} %get-tuple-element.331), channel_id=1, source_target_pairs={{0,4},{2,6},{4,0},{6,2},{8,12},{10,14},{12,8},{14,10},{16,20},{18,... | collective-permute-start | bytes 786440 | tf_op jit(solution)/shard_map/ppermute | solution.py:51
  271.9 23.1 %collective-permute-start.57 = (bf16[128,2688]{1,0:T(8,128)(2,1)}, bf16[128,2688]{1,0:T(8,128)(2,1)}, u32[]{:S(2)}, u32[]{:S(2)}) collective-permute-start(bf16[128,2688]{1,0:T(8,128)(2,1)} %pad_maximum_fusion.1), channel_id=1, source_target_pairs={{0,8},{2,10},{4,12},{6,14},{8,0},{10,2},{12,4},{14,6},{16,24},{18,... | collective-permute-start | bytes 2064392 | tf_op jit(solution)/shard_map/ppermute | solution.py:51
  287.6 20.7 %collective-permute-start.55 = (bf16[256,1536]{1,0:T(8,128)(2,1)}, bf16[256,1536]{1,0:T(8,128)(2,1)}, u32[]{:S(2)}, u32[]{:S(2)}) collective-permute-start(bf16[256,1536]{1,0:T(8,128)(2,1)} %get-tuple-element.335), channel_id=1, source_target_pairs={{0,2},{2,0},{4,6},{6,4},{8,10},{10,8},{12,14},{14,12},{16,18},{18,... | collective-permute-start | bytes 2359304 | tf_op jit(solution)/shard_map/ppermute | solution.py:51
  288.6 22.0 %collective-permute-start.56 = (bf16[256,1536]{1,0:T(8,128)(2,1)}, bf16[256,1536]{1,0:T(8,128)(2,1)}, u32[]{:S(2)}, u32[]{:S(2)}) collective-permute-start(bf16[256,1536]{1,0:T(8,128)(2,1)} %get-tuple-element.336), channel_id=1, source_target_pairs={{0,4},{2,6},{4,0},{6,2},{8,12},{10,14},{12,8},{14,10},{16,20},{18,... | collective-permute-start | bytes 2359304 | tf_op jit(solution)/shard_map/ppermute | solution.py:51
  291.8 38.9 %collective-permute-start.63 = (bf16[256,1024]{1,0:T(8,128)(2,1)}, bf16[256,1024]{1,0:T(8,128)(2,1)S(1)}, u32[]{:S(2)}, u32[]{:S(2)}) collective-permute-start(bf16[256,1024]{1,0:T(8,128)(2,1)} %get-tuple-element.342), channel_id=1, source_target_pairs={{0,2},{2,0},{4,6},{6,4},{8,10},{10,8},{12,14},{14,12},{16,18},{18,... | collective-permute-start | bytes 1572872 | tf_op jit(solution)/shard_map/ppermute | solution.py:51
  292.8 37.9 %collective-permute-start.64 = (bf16[256,1024]{1,0:T(8,128)(2,1)}, bf16[256,1024]{1,0:T(8,128)(2,1)S(1)}, u32[]{:S(2)}, u32[]{:S(2)}) collective-permute-start(bf16[256,1024]{1,0:T(8,128)(2,1)} %get-tuple-element.341), channel_id=1, source_target_pairs={{0,4},{2,6},{4,0},{6,2},{8,12},{10,14},{12,8},{14,10},{16,20},{18,... | collective-permute-start | bytes 1572872 | tf_op jit(solution)/shard_map/ppermute | solution.py:51
  295.1 17.3 %collective-permute-start.61 = (bf16[512,1024]{1,0:T(8,128)(2,1)S(1)}, bf16[512,1024]{1,0:T(8,128)(2,1)S(1)}, u32[]{:S(2)}, u32[]{:S(2)}) collective-permute-start(bf16[512,1024]{1,0:T(8,128)(2,1)S(1)} %copy-done.44), channel_id=1, source_target_pairs={{0,1},{1,0},{2,3},{3,2},{4,5},{5,4},{6,7},{7,6},{8,9},{9,8},{10,11... | collective-permute-start | bytes 3145736 | tf_op jit(solution)/shard_map/ppermute | solution.py:653
  308.3 22.0 %collective-permute-start.59 = (bf16[64,4224]{1,0:T(8,128)(2,1)S(1)}, bf16[64,4224]{1,0:T(8,128)(2,1)S(1)}, u32[]{:S(2)}, u32[]{:S(2)}) collective-permute-start(bf16[64,4224]{1,0:T(8,128)(2,1)S(1)} %pad_maximum_fusion.2), channel_id=1, source_target_pairs={{0,16},{2,18},{4,20},{6,22},{8,24},{10,26},{12,28},{14,30},{16,0},... | collective-permute-start | bytes 1622024 | tf_op jit(solution)/shard_map/ppermute | solution.py:51
  312.3 18.2 %collective-permute-start.58 = (bf16[128,1536]{1,0:T(8,128)(2,1)S(1)}, bf16[128,1536]{1,0:T(8,128)(2,1)S(1)}, u32[]{:S(2)}, u32[]{:S(2)}) collective-permute-start(bf16[128,1536]{1,0:T(8,128)(2,1)S(1)} %slice.308), channel_id=1, source_target_pairs={{0,8},{2,10},{4,12},{6,14},{8,0},{10,2},{12,4},{14,6},{16,24},{18,... | collective-permute-start | bytes 1179656 | tf_op jit(solution)/shard_map/ppermute | solution.py:51
  330.5 22.9 %collective-permute-start.60 = (bf16[512,1024]{1,0:T(8,128)(2,1)S(1)}, bf16[512,1024]{1,0:T(8,128)(2,1)S(1)}, u32[]{:S(2)}, u32[]{:S(2)}) collective-permute-start(bf16[512,1024]{1,0:T(8,128)(2,1)S(1)} %copy-done.43), channel_id=1, source_target_pairs={{0,1},{1,0},{2,3},{3,2},{4,5},{5,4},{6,7},{7,6},{8,9},{9,8},{10,11... | collective-permute-start | bytes 3145736 | tf_op jit(solution)/shard_map/ppermute | solution.py:653
  331.0 13.7 %collective-permute-start.65 = (bf16[128,1024]{1,0:T(8,128)(2,1)S(1)}, bf16[128,1024]{1,0:T(8,128)(2,1)S(1)}, u32[]{:S(2)}, u32[]{:S(2)}) collective-permute-start(bf16[128,1024]{1,0:T(8,128)(2,1)S(1)} %slice.311), channel_id=1, source_target_pairs={{0,8},{2,10},{4,12},{6,14},{8,0},{10,2},{12,4},{14,6},{16,24},{18,... | collective-permute-start | bytes 786440 | tf_op jit(solution)/shard_map/ppermute | solution.py:51
  (72 other events, 599.3 us)

commit v6 on v5

--- a/solution.py
+++ b/solution.py
@@ -772,18 +772,22 @@
     late.move(total_own, *last.sent)
     while len(outs[0].moves) > 1:
         move_along(outs, total_own, *late.sent)
+    (total_other,) = held_back((total_other,), *last.got)
     last.move(*late.sent)
     done = (*last.got, *outs[0].got)
     late.move(*done)
     (y_other,) = held_back((y_other,), *done)
     for out in (*outs, last, late):
-        while out.moves:
+        while len(out.moves) > 1:
             out.move(*done)
+    for out in (*outs, last):
+        out.move(*done)
     grad_in_norm = total_own + swap(total_other).astype(wide)
     tokens_grad = grad_middle + norm_back(grad_in_norm, normed_in, scale_in)
     y_sum = y_own + swap(y_other).astype(wide)
     layer_out = low(middle + y_sum)
     layer_out = low(nt(layer_out, shuffle))
+    late.move(layer_out)
     parts = []
     rest = tokens_grad
     for _ in range(3):

time: 361 us -> 358 us (level)
  transfers between devices with their start and end apart: 67 -> 67, of which waited for: 25 -> 25; matrix products, arithmetic and copies ran while one was open for 12% -> 12% of each run, Pallas kernels for 33% -> 34%
where the time goes in v6:
time: 358 us; the launch traced here: 353 us
  Pallas kernels  121 us (34%)
  waiting for transfers between devices  89.2 us (25%)
  starting transfers between devices  77.6 us (22%)
  local copies, waits for them, and re-layouts  29.9 us (8%)
  other arithmetic  21.8 us (6%)
  matrix products  12.1 us (3%)
    ppermute x57, waiting for transfers between devices, __call__(): result = lax.ppermute(array, 'dp', pairs)  86.3 us
    ppermute x57, starting transfers between devices, __call__(): result = lax.ppermute(array, 'dp', pairs)  77 us
    pallas_call x3, Pallas kernels, ffn(): pl.pallas_call(functools.partial(ffn_kernel, chained=sums is not None, la...  42.4 us
    unnamed x112, local copies, waits for them, and re-layouts  14.8 us
    pallas_call x1, Pallas kernels, front(): pl.pallas_call(functools.partial(front_kernel, heads=rates.shape[0] // st...  13.4 us
    pallas_call x1, Pallas kernels, attend_back(): pl.pallas_call(functools.partial(attend_back_kernel, width=width), cost_e...  13 us
    pallas_call x2, Pallas kernels, weight_grads(): pl.pallas_call(functools.partial(weight_grad_kernel, count=count, each=le...  12.6 us
    dot_general x6, matrix products, dot(): lax.dot_general(left, right, (dims, ((), ())), preferred_element_type=wide)  12.1 us
  transfers between devices with their start and end apart: 67, of which 25 were waited for; matrix products, arithmetic and copies ran while one was open for 12% of the time, Pallas kernels for 34%

profile of v6, /device:TPU:0, one launch (start us, length us, event | category | flops | bytes accessed | tf_op | source)
XLA Modules:
  0.0 353.4 jit_solution(16773999416886940328)
XLA Ops:
  3.3 4.1 %collective-permute-start.2 = (bf16[64,1536]{1,0:T(8,128)(2,1)S(1)}, bf16[64,1536]{1,0:T(8,128)(2,1)S(1)}, u32[]{:S(2)}, u32[]{:S(2)}) collective-permute-start(bf16[64,1536]{1,0:T(8,128)(2,1)S(1)} %constant_dynamic-update-slice_fusion), channel_id=1, source_target_pairs={{0,16},{2,18},{4,20},{6,22},{8,24},{10,26},{12,28},{14,30},{16,0},... | collective-permute-start | bytes 589832 | tf_op jit(solution)/shard_map/ppermute | solution.py:51
  9.5 7.0 %collective-permute-done.2 = bf16[64,1536]{1,0:T(8,128)(2,1)S(1)} collective-permute-done((bf16[64,1536]{1,0:T(8,128)(2,1)S(1)}, bf16[64,1536]{1,0:T(8,128)(2,1)S(1)}, u32[]{:S(2)}, u32[]{:S(2)}) %collective-permute-start.2) | collective-permute-done | bytes 196640 | tf_op jit(solution)/shard_map/ppermute | solution.py:51
  17.7 9.2 %collective-permute-done.3 = bf16[128,1536]{1,0:T(8,128)(2,1)S(1)} collective-permute-done((bf16[128,1536]{1,0:T(8,128)(2,1)S(1)}, bf16[128,1536]{1,0:T(8,128)(2,1)S(1)}, u32[]{:S(2)}, u32[]{:S(2)}) %collective-permute-start.3) | collective-permute-done | bytes 393248 | tf_op jit(solution)/shard_map/ppermute | solution.py:51
  29.8 3.3 collective-permute-start.8
  33.2 2.3 fusion.26.refs_2_
  35.5 3.0 collective-permute-done.8
  39.4 5.5 %collective-permute-done.4.refs_1_.refs_6_.refs_11_.refs_5_.refs_10_.refs_15_ = bf16[256,1536]{1,0:T(8,128)(2,1)S(1)} collective-permute-done((bf16[256,1536]{1,0:T(8,128)(2,1)S(1)}, bf16[256,1536]{1,0:T(8,128)(2,1)S(1)}, u32[]{:S(2)}, u32[]{:S(2)}) %collective-permute-start.4) | collective-permute-done | bytes 786464 | tf_op jit(solution)/shard_map/ppermute | solution.py:51
  49.8 1.8 collective-permute-start.11
  51.6 3.5 collective-permute-start.15
  55.1 2.0 collective-permute-done.6.refs_3_.refs_8_.refs_13_.refs_7_.refs_12_.refs_17_
  58.8 13.4 %shard_map.195 = (bf16[1024,512]{1,0:T(8,128)(2,1)}, bf16[1024,512]{1,0:T(8,128)(2,1)}, bf16[1024,512]{1,0:T(8,128)(2,1)}, bf16[1024,512]{1,0:T(8,128)(2,1)}, bf...) custom-call(s32[1]{0:T(128)} %bitcast.1.turn_ref, f32[4]{0:T(128)} %rate_ref.3, ...), custom_call_target="tpu_custom_call" | custom-call | flops 4831838208 | bytes 10485760 | tf_op jit(solution)/shard_map/pallas_call | solution.py:300
  72.3 1.9 collective-permute-start.13
  74.3 2.4 collective-permute-start.16
  76.7 3.4 collective-permute-start.19
  80.2 4.0 %collective-permute-done.19 = bf16[64,1536]{1,0:T(8,128)(2,1)S(1)} collective-permute-done((bf16[64,1536]{1,0:T(8,128)(2,1)S(1)}, bf16[64,1536]{1,0:T(8,128)(2,1)S(1)}, u32[]{:S(2)}, u32[]{:S(2)}) %collective-permute-start.19) | collective-permute-done | bytes 196640 | tf_op jit(solution)/shard_map/ppermute | solution.py:51
  88.3 6.0 %collective-permute-start.20 = (bf16[128,1536]{1,0:T(8,128)(2,1)S(1)}, bf16[128,1536]{1,0:T(8,128)(2,1)S(1)}, u32[]{:S(2)}, u32[]{:S(2)}) collective-permute-start(bf16[128,1536]{1,0:T(8,128)(2,1)S(1)} %constant_dynamic-update-slice_fusion.11), channel_id=1, source_target_pairs={{0,8},{2,10},{4,12},{6,14},{8,0},{10,2},{12,4},{14,6},{16,24},{18,... | collective-permute-start | bytes 1179656 | tf_op jit(solution)/shard_map/ppermute | solution.py:51
  95.1 4.4 %shard_map.196.u_ref = f32[1024,512]{1,0:T(8,128)} custom-call(bf16[512,1024]{1,0:T(8,128)(2,1)} %copy-done.14, bf16[512,1024]{1,0:T(8,128)(2,1)} %copy-done.20, bf16[256,1024]{1,0:T(8,128)(2,1)} %copy-done.9, bf16[256,1024]{1,0:T(8,128)(2,1)} %copy-done.7, bf16[256,1024]{1,0:T(8,128)(2,1)} %copy-done.8, bf16[128,1024]{1,0:T(8,128)(2,1)} %copy-done.17, ...), custom_call_target="tpu_custom_call" | custom-call | flops 1073741824 | bytes 4194304 | tf_op jit(solution)/shard_map/pallas_call | solution.py:322
  100.2 6.0 %shard_map.197 = (bf16[1024,512]{1,0:T(8,128)(2,1)}, f32[1024,1]{1,0:T(8,128)}, f32[512,1024]{1,0:T(8,128)}, bf16[512,1024]{1,0:T(8,128)(2,1)}) custom-call(f32[8,1024]{1,0:T(8,128)} %get-tuple-element.200.sum_ref, f32[8,1024]{1,0:T(8,128)} %copy-done.41, f32[1024,512]{1,0:T(8,128)} %get-tuple-element.206.o_ref, f32[1024,512]{1,0:T(8,128)} %shard_map.196.u_ref, ...), custom_call_target="tpu_custom_call" | custom-call | flops 1073741824 | bytes 8388608 | tf_op jit(solution)/shard_map/pallas_call | solution.py:354
  110.9 2.1 multiply_reduce_fusion.1
  114.3 4.7 %collective-permute-done.25.refs_7_ = bf16[128,1536]{1,0:T(8,128)(2,1)S(1)} collective-permute-done((bf16[128,1536]{1,0:T(8,128)(2,1)S(1)}, bf16[128,1536]{1,0:T(8,128)(2,1)S(1)}, u32[]{:S(2)}, u32[]{:S(2)}) %collective-permute-start.25) | collective-permute-done | bytes 393248 | tf_op jit(solution)/shard_map/ppermute | solution.py:51
  119.0 2.0 collective-permute-done.26.refs_8_
  128.1 14.9 %shard_map.198 = (f32[512,1024]{1,0:T(8,128)}, f32[512,1024]{1,0:T(8,128)}, f32[512,1024]{1,0:T(8,128)}, f32[512,1024]{1,0:T(8,128)}, bf16[256,1536]{1,0:T(8,128...) custom-call(bf16[512,1024]{1,0:T(8,128)(2,1)} %copy-done.21, ...), custom_call_target="tpu_custom_call" | custom-call | flops 9663676416 | bytes 14680064 | tf_op jit(solution)/shard_map/pallas_call | solution.py:605
  150.4 5.5 %collective-permute-done.33.refs_5_ = bf16[256,1152]{1,0:T(8,128)(2,1)} collective-permute-done((bf16[256,1152]{1,0:T(8,128)(2,1)}, bf16[256,1152]{1,0:T(8,128)(2,1)}, u32[]{:S(2)}, u32[]{:S(2)}) %collective-permute-start.33) | collective-permute-done | bytes 589856 | tf_op jit(solution)/shard_map/ppermute | solution.py:51
  162.2 3.2 collective-permute-done.31.refs_7_
  167.0 14.6 %shard_map.199 = (f32[512,1024]{1,0:T(8,128)}, f32[512,1024]{1,0:T(8,128)}, f32[512,1024]{1,0:T(8,128)}, f32[512,1024]{1,0:T(8,128)}, bf16[256,1536]{1,0:T(8,128...) custom-call(bf16[512,1024]{1,0:T(8,128)(2,1)} %copy-done.21, ...), custom_call_target="tpu_custom_call" | custom-call | flops 9663676416 | bytes 31457280 | tf_op jit(solution)/shard_map/pallas_call | solution.py:605
  182.4 2.4 shard_map.200
  187.7 12.9 %shard_map.201 = (f32[512,1024]{1,0:T(8,128)}, bf16[512,1024]{1,0:T(8,128)(2,1)}, f32[512,1024]{1,0:T(8,128)}, bf16[512,1024]{1,0:T(8,128)(2,1)}, bf16[256,1152]...) custom-call(bf16[512,1024]{1,0:T(8,128)(2,1)} %copy-done.21, ...), custom_call_target="tpu_custom_call" | custom-call | flops 7247757312 | bytes 29884416 | tf_op jit(solution)/shard_map/pallas_call | solution.py:605
  201.6 2.9 collective-permute-done.39
  204.5 2.1 multiply_reduce_fusion
  206.6 3.2 fusion.32
  216.0 7.2 %shard_map.202 = (f32[1024,512]{1,0:T(8,128)}, bf16[1024,512]{1,0:T(8,128)(2,1)}, f32[8,1024]{1,0:T(8,128)}) custom-call(bf16[512,1024]{1,0:T(8,128)(2,1)} %copy-done.13, bf16[512,1024]{1,0:T(8,128)(2,1)} %copy-done.19, f32[1024,512]{1,0:T(8,128)} %get-tuple-element.206.o_ref, f32[1024,1]{1,0:T(8,128)} %get-tuple-element.275.scale_ref, ...), custom_call_target="tpu_custom_call" | custom-call | flops 1073741824 | bytes 8388608 | tf_op jit(solution)/shard_map/pallas_call | solution.py:385
  224.3 2.4 shard_map.203
  228.8 5.9 %shard_map.204 = (bf16[256,1024]{1,0:T(8,128)(2,1)}, bf16[256,1024]{1,0:T(8,128)(2,1)}, bf16[256,1024]{1,0:T(8,128)(2,1)}, bf16[128,1024]{1,0:T(8,128)(2,1)}, bf16[128,1024]{1,0:T(8,128)(2,1)}) custom-call(bf16[512,1024]{1,0:T(8,128)(2,1)} %copy-done.14, bf16[512,1024]{1,0:T(8,128)(2,1)} %copy-done.20, bf16[512,1024]{1,0:T(8,128)(2,1)} %copy-done.13, ...), custom_call_target="tpu_custom_call" | custom-call | flops 2147483648 | bytes 6291456 | tf_op jit(solution)/shard_map/pallas_call | solution.py:494
  234.7 2.1 shard_map.207
  239.3 1.9 add_add_fusion.3
  242.5 13.0 %shard_map.205 = (bf16[1024,512]{1,0:T(8,128)(2,1)}, bf16[1024,512]{1,0:T(8,128)(2,1)}, bf16[1024,512]{1,0:T(8,128)(2,1)}) custom-call(s32[1]{0:T(128)} %bitcast.1.turn_ref, f32[4]{0:T(128)} %rate_ref.3, f32[1024,1]{1,0:T(8,128)} %get-tuple-element.275.scale_ref, f32[8,1024]{1,0:T(8,128)} %get-tuple-element.278.cross_ref, f32[8,1024]{1,0:T(8,128)} %copy-done.49, ...), custom_call_target="tpu_custom_call" | custom-call | flops 6442450944 | bytes 28311552 | tf_op jit(solution)/shard_map/pallas_call | solution.py:461
  255.5 6.7 %shard_map.206 = (bf16[256,1536]{1,0:T(8,128)(2,1)}, bf16[256,1536]{1,0:T(8,128)(2,1)}, bf16[256,1536]{1,0:T(8,128)(2,1)}, bf16[128,1536]{1,0:T(8,128)(2,1)}, bf16[128,1536]{1,0:T(8,128)(2,1)}) custom-call(bf16[512,1024]{1,0:T(8,128)(2,1)} %copy-done.14, bf16[512,1024]{1,0:T(8,128)(2,1)} %copy-done.20, bf16[1024,512]{1,0:T(8,128)(2,1)} %get-tuple-element.326.refs_2_.refs_0_, ...), custom_call_target="tpu_custom_call" | custom-call | flops 3221225472 | bytes 8388608 | tf_op jit(solution)/shard_map/pallas_call | solution.py:494
  271.9 2.0 collective-permute-start.57
  273.9 10.5 %shard_map.208 = (f32[512,1024]{1,0:T(8,128)}, bf16[512,1024]{1,0:T(8,128)(2,1)}) custom-call(bf16[1024,512]{1,0:T(8,128)(2,1)} %get-tuple-element.326.refs_2_.refs_0_, bf16[1024,512]{1,0:T(8,128)(2,1)} %get-tuple-element.307.refs_3_.refs_1_, bf16[1024,512]{1,0:T(8,128)(2,1)} %get-tuple-element.308.refs_4_.refs_2_, ...), custom_call_target="tpu_custom_call" | custom-call | flops 4294967296 | bytes 12582912 | tf_op jit(solution)/shard_map/pallas_call | solution.py:521
  285.2 2.4 shard_map.209
  289.7 2.1 shard_map.210
  297.6 2.3 collective-permute-start.59
  299.9 8.4 %collective-permute-done.55 = bf16[256,1536]{1,0:T(8,128)(2,1)} collective-permute-done((bf16[256,1536]{1,0:T(8,128)(2,1)}, bf16[256,1536]{1,0:T(8,128)(2,1)}, u32[]{:S(2)}, u32[]{:S(2)}) %collective-permute-start.55) | collective-permute-done | bytes 786464 | tf_op jit(solution)/shard_map/ppermute | solution.py:51
  311.2 10.4 %collective-permute-done.59 = bf16[64,4224]{1,0:T(8,128)(2,1)S(1)} collective-permute-done((bf16[64,4224]{1,0:T(8,128)(2,1)S(1)}, bf16[64,4224]{1,0:T(8,128)(2,1)S(1)}, u32[]{:S(2)}, u32[]{:S(2)}) %collective-permute-start.59) | collective-permute-done | bytes 540704 | tf_op jit(solution)/shard_map/ppermute | solution.py:51
  321.6 6.7 %collective-permute-done.58 = bf16[128,1536]{1,0:T(8,128)(2,1)S(1)} collective-permute-done((bf16[128,1536]{1,0:T(8,128)(2,1)S(1)}, bf16[128,1536]{1,0:T(8,128)(2,1)S(1)}, u32[]{:S(2)}, u32[]{:S(2)}) %collective-permute-start.58) | collective-permute-done | bytes 393248 | tf_op jit(solution)/shard_map/ppermute | solution.py:51
  333.1 6.9 %collective-permute-done.62 = bf16[64,1536]{1,0:T(8,128)(2,1)S(1)} collective-permute-done((bf16[64,1536]{1,0:T(8,128)(2,1)S(1)}, bf16[64,1536]{1,0:T(8,128)(2,1)S(1)}, u32[]{:S(2)}, u32[]{:S(2)}) %collective-permute-start.62) | collective-permute-done | bytes 196640 | tf_op jit(solution)/shard_map/ppermute | solution.py:51
  347.2 2.8 add_add_fusion
  350.0 2.4 fusion.25
  (303 shorter events, 101.8 us)
Async XLA Ops:
  3.3 13.2 %collective-permute-start.2 = (bf16[64,1536]{1,0:T(8,128)(2,1)S(1)}, bf16[64,1536]{1,0:T(8,128)(2,1)S(1)}, u32[]{:S(2)}, u32[]{:S(2)}) collective-permute-start(bf16[64,1536]{1,0:T(8,128)(2,1)S(1)} %constant_dynamic-update-slice_fusion), channel_id=1, source_target_pairs={{0,16},{2,18},{4,20},{6,22},{8,24},{10,26},{12,28},{14,30},{16,0},... | collective-permute-start | bytes 589832 | tf_op jit(solution)/shard_map/ppermute | solution.py:51
  17.6 31.3 %collective-permute-start = (bf16[512,1024]{1,0:T(8,128)(2,1)S(1)}, bf16[512,1024]{1,0:T(8,128)(2,1)S(1)}, u32[]{:S(2)}, u32[]{:S(2)}) collective-permute-start(bf16[512,1024]{1,0:T(8,128)(2,1)S(1)} %fusion.10.own_ref.refs_0_), channel_id=1, source_target_pairs={{0,1},{1,0},{2,3},{3,2},{4,5},{5,4},{6,7},{7,6},{8,9},{9,8},{10,11... | collective-permute-start | bytes 3145736 | tf_op jit(solution)/shard_map/ppermute | solution.py:653
  27.0 17.9 %collective-permute-start.4 = (bf16[256,1536]{1,0:T(8,128)(2,1)S(1)}, bf16[256,1536]{1,0:T(8,128)(2,1)S(1)}, u32[]{:S(2)}, u32[]{:S(2)}) collective-permute-start(bf16[256,1536]{1,0:T(8,128)(2,1)S(1)} %pad_maximum_fusion.refs_0_.refs_5_.refs_10_.refs_4_.refs_9_.refs_14_), channel_id=1, source_target_pairs={{0,2},{2,0},{4,6},{6,4},{8,10},{10,8},{12,14},{14,12},{16,18},{18,... | collective-permute-start | bytes 2359304 | tf_op jit(solution)/shard_map/ppermute | solution.py:51
  28.3 18.3 %collective-permute-start.5 = (bf16[256,1536]{1,0:T(8,128)(2,1)S(1)}, bf16[256,1536]{1,0:T(8,128)(2,1)S(1)}, u32[]{:S(2)}, u32[]{:S(2)}) collective-permute-start(bf16[256,1536]{1,0:T(8,128)(2,1)S(1)} %pad_maximum_fusion.refs_0_.refs_5_.refs_10_.refs_4_.refs_9_.refs_14_), channel_id=1, source_target_pairs={{0,4},{2,6},{4,0},{6,2},{8,12},{10,14},{12,8},{14,10},{16,20},{18,... | collective-permute-start | bytes 2359304 | tf_op jit(solution)/shard_map/ppermute | solution.py:51
  35.5 16.1 %collective-permute-start.1 = (bf16[512,1024]{1,0:T(8,128)(2,1)}, bf16[512,1024]{1,0:T(8,128)(2,1)}, u32[]{:S(2)}, u32[]{:S(2)}) collective-permute-start(bf16[512,1024]{1,0:T(8,128)(2,1)} %fusion.26.refs_2_), channel_id=1, source_target_pairs={{0,1},{1,0},{2,3},{3,2},{4,5},{5,4},{6,7},{7,6},{8,9},{9,8},{10,11... | collective-permute-start | bytes 3145736 | tf_op jit(solution)/shard_map/ppermute | solution.py:653
  46.6 12.2 %collective-permute-start.7 = (bf16[128,1536]{1,0:T(8,128)(2,1)S(1)}, bf16[128,1536]{1,0:T(8,128)(2,1)}, u32[]{:S(2)}, u32[]{:S(2)}) collective-permute-start(bf16[128,1536]{1,0:T(8,128)(2,1)S(1)} %slice.243), channel_id=1, source_target_pairs={{0,2},{2,0},{4,6},{6,4},{8,10},{10,8},{12,14},{14,12},{16,18},{18,... | collective-permute-start | bytes 1179656 | tf_op jit(solution)/shard_map/ppermute | solution.py:51
  47.9 24.3 %collective-permute-start.10 = (bf16[256,1024]{1,0:T(8,128)(2,1)S(1)}, bf16[256,1024]{1,0:T(8,128)(2,1)S(1)}, u32[]{:S(2)}, u32[]{:S(2)}) collective-permute-start(bf16[256,1024]{1,0:T(8,128)(2,1)S(1)} %constant_dynamic-update-slice_fusion.5.refs_0_.refs_19_), channel_id=1, source_target_pairs={{0,2},{2,0},{4,6},{6,4},{8,10},{10,8},{12,14},{14,12},{16,18},{18,... | collective-permute-start | bytes 1572872 | tf_op jit(solution)/shard_map/ppermute | solution.py:51
  49.8 22.4 %collective-permute-start.11 = (bf16[256,1024]{1,0:T(8,128)(2,1)S(1)}, bf16[256,1024]{1,0:T(8,128)(2,1)S(1)}, u32[]{:S(2)}, u32[]{:S(2)}) collective-permute-start(bf16[256,1024]{1,0:T(8,128)(2,1)S(1)} %constant_dynamic-update-slice_fusion.5.refs_0_.refs_19_), channel_id=1, source_target_pairs={{0,4},{2,6},{4,0},{6,2},{8,12},{10,14},{12,8},{14,10},{16,20},{18,... | collective-permute-start | bytes 1572872 | tf_op jit(solution)/shard_map/ppermute | solution.py:51
  51.6 22.6 %collective-permute-start.15 = (bf16[64,1536]{1,0:T(8,128)(2,1)S(1)}, bf16[64,1536]{1,0:T(8,128)(2,1)S(1)}, u32[]{:S(2)}, u32[]{:S(2)}) collective-permute-start(bf16[64,1536]{1,0:T(8,128)(2,1)S(1)} %pad_maximum_fusion.6), channel_id=1, source_target_pairs={{0,16},{2,18},{4,20},{6,22},{8,24},{10,26},{12,28},{14,30},{16,0},... | collective-permute-start | bytes 589832 | tf_op jit(solution)/shard_map/ppermute | solution.py:51
  86.2 20.1 %collective-permute-start.17 = (bf16[256,1536]{1,0:T(8,128)(2,1)}, bf16[256,1536]{1,0:T(8,128)(2,1)}, u32[]{:S(2)}, u32[]{:S(2)}) collective-permute-start(bf16[256,1536]{1,0:T(8,128)(2,1)} %constant_dynamic-update-slice_fusion.9.refs_4_), channel_id=1, source_target_pairs={{0,2},{2,0},{4,6},{6,4},{8,10},{10,8},{12,14},{14,12},{16,18},{18,... | collective-permute-start | bytes 2359304 | tf_op jit(solution)/shard_map/ppermute | solution.py:51
  87.8 18.4 %collective-permute-start.18 = (bf16[256,1536]{1,0:T(8,128)(2,1)}, bf16[256,1536]{1,0:T(8,128)(2,1)}, u32[]{:S(2)}, u32[]{:S(2)}) collective-permute-start(bf16[256,1536]{1,0:T(8,128)(2,1)} %constant_dynamic-update-slice_fusion.9.refs_4_), channel_id=1, source_target_pairs={{0,4},{2,6},{4,0},{6,2},{8,12},{10,14},{12,8},{14,10},{16,20},{18,... | collective-permute-start | bytes 2359304 | tf_op jit(solution)/shard_map/ppermute | solution.py:51
  88.3 18.0 %collective-permute-start.20 = (bf16[128,1536]{1,0:T(8,128)(2,1)S(1)}, bf16[128,1536]{1,0:T(8,128)(2,1)S(1)}, u32[]{:S(2)}, u32[]{:S(2)}) collective-permute-start(bf16[128,1536]{1,0:T(8,128)(2,1)S(1)} %constant_dynamic-update-slice_fusion.11), channel_id=1, source_target_pairs={{0,8},{2,10},{4,12},{6,14},{8,0},{10,2},{12,4},{14,6},{16,24},{18,... | collective-permute-start | bytes 1179656 | tf_op jit(solution)/shard_map/ppermute | solution.py:51
  114.2 13.9 %collective-permute-start.23 = (bf16[512,1024]{1,0:T(8,128)(2,1)S(1)}, bf16[512,1024]{1,0:T(8,128)(2,1)}, u32[]{:S(2)}, u32[]{:S(2)}) collective-permute-start(bf16[512,1024]{1,0:T(8,128)(2,1)S(1)} %multiply_convert_fusion.refs_0_), channel_id=1, source_target_pairs={{0,1},{1,0},{2,3},{3,2},{4,5},{5,4},{6,7},{7,6},{8,9},{9,8},{10,11... | collective-permute-start | bytes 3145736 | tf_op jit(solution)/shard_map/ppermute | solution.py:653
  122.5 20.7 %collective-permute-start.29 = (bf16[256,1536]{1,0:T(8,128)(2,1)}, bf16[256,1536]{1,0:T(8,128)(2,1)}, u32[]{:S(2)}, u32[]{:S(2)}) collective-permute-start(bf16[256,1536]{1,0:T(8,128)(2,1)} %constant_dynamic-update-slice_fusion.15.refs_4_), channel_id=1, source_target_pairs={{0,2},{2,0},{4,6},{6,4},{8,10},{10,8},{12,14},{14,12},{16,18},{18,... | collective-permute-start | bytes 2359304 | tf_op jit(solution)/shard_map/ppermute | solution.py:51
  123.7 20.7 %collective-permute-start.30 = (bf16[256,1536]{1,0:T(8,128)(2,1)}, bf16[256,1536]{1,0:T(8,128)(2,1)}, u32[]{:S(2)}, u32[]{:S(2)}) collective-permute-start(bf16[256,1536]{1,0:T(8,128)(2,1)} %constant_dynamic-update-slice_fusion.15.refs_4_), channel_id=1, source_target_pairs={{0,4},{2,6},{4,0},{6,2},{8,12},{10,14},{12,8},{14,10},{16,20},{18,... | collective-permute-start | bytes 2359304 | tf_op jit(solution)/shard_map/ppermute | solution.py:51
  126.9 29.0 %collective-permute-start.33 = (bf16[256,1152]{1,0:T(8,128)(2,1)}, bf16[256,1152]{1,0:T(8,128)(2,1)}, u32[]{:S(2)}, u32[]{:S(2)}) collective-permute-start(bf16[256,1152]{1,0:T(8,128)(2,1)} %constant_dynamic-update-slice_fusion.17.refs_4_), channel_id=1, source_target_pairs={{0,2},{2,0},{4,6},{6,4},{8,10},{10,8},{12,14},{14,12},{16,18},{18,... | collective-permute-start | bytes 1769480 | tf_op jit(solution)/shard_map/ppermute | solution.py:51
  127.2 29.9 %collective-permute-start.34 = (bf16[256,1152]{1,0:T(8,128)(2,1)}, bf16[256,1152]{1,0:T(8,128)(2,1)}, u32[]{:S(2)}, u32[]{:S(2)}) collective-permute-start(bf16[256,1152]{1,0:T(8,128)(2,1)} %constant_dynamic-update-slice_fusion.17.refs_4_), channel_id=1, source_target_pairs={{0,4},{2,6},{4,0},{6,2},{8,12},{10,14},{12,8},{14,10},{16,20},{18,... | collective-permute-start | bytes 1769480 | tf_op jit(solution)/shard_map/ppermute | solution.py:51
  145.5 19.9 %collective-permute-start.31 = (bf16[128,1536]{1,0:T(8,128)(2,1)S(1)}, bf16[128,1536]{1,0:T(8,128)(2,1)S(1)}, u32[]{:S(2)}, u32[]{:S(2)}) collective-permute-start(bf16[128,1536]{1,0:T(8,128)(2,1)S(1)} %slice.199), channel_id=1, source_target_pairs={{0,4},{2,6},{4,0},{6,2},{8,12},{10,14},{12,8},{14,10},{16,20},{18,... | collective-permute-start | bytes 1179656 | tf_op jit(solution)/shard_map/ppermute | solution.py:51
  148.3 18.0 %collective-permute-start.32 = (bf16[128,1536]{1,0:T(8,128)(2,1)S(1)}, bf16[128,1536]{1,0:T(8,128)(2,1)S(1)}, u32[]{:S(2)}, u32[]{:S(2)}) collective-permute-start(bf16[128,1536]{1,0:T(8,128)(2,1)S(1)} %slice.200), channel_id=1, source_target_pairs={{0,2},{2,0},{4,6},{6,4},{8,10},{10,8},{12,14},{14,12},{16,18},{18,... | collective-permute-start | bytes 1179656 | tf_op jit(solution)/shard_map/ppermute | solution.py:51
  148.6 33.0 %collective-permute-start.27 = (bf16[128,1536]{1,0:T(8,128)(2,1)}, bf16[128,1536]{1,0:T(8,128)(2,1)S(1)}, u32[]{:S(2)}, u32[]{:S(2)}) collective-permute-start(bf16[128,1536]{1,0:T(8,128)(2,1)} %get-tuple-element.241), channel_id=1, source_target_pairs={{0,2},{2,0},{4,6},{6,4},{8,10},{10,8},{12,14},{14,12},{16,18},{18,... | collective-permute-start | bytes 1179656 | tf_op jit(solution)/shard_map/ppermute | solution.py:51
  155.9 25.7 %collective-permute-start.28 = (bf16[128,1536]{1,0:T(8,128)(2,1)}, bf16[128,1536]{1,0:T(8,128)(2,1)}, u32[]{:S(2)}, u32[]{:S(2)}) collective-permute-start(bf16[128,1536]{1,0:T(8,128)(2,1)} %get-tuple-element.242), channel_id=1, source_target_pairs={{0,4},{2,6},{4,0},{6,2},{8,12},{10,14},{12,8},{14,10},{16,20},{18,... | collective-permute-start | bytes 1179656 | tf_op jit(solution)/shard_map/ppermute | solution.py:51
  158.8 22.8 %collective-permute-start.35 = (bf16[128,1152]{1,0:T(8,128)(2,1)}, bf16[128,1152]{1,0:T(8,128)(2,1)}, u32[]{:S(2)}, u32[]{:S(2)}) collective-permute-start(bf16[128,1152]{1,0:T(8,128)(2,1)} %slice.201), channel_id=1, source_target_pairs={{0,4},{2,6},{4,0},{6,2},{8,12},{10,14},{12,8},{14,10},{16,20},{18,... | collective-permute-start | bytes 884744 | tf_op jit(solution)/shard_map/ppermute | solution.py:51
  165.4 16.2 %collective-permute-start.36 = (bf16[128,1152]{1,0:T(8,128)(2,1)}, bf16[128,1152]{1,0:T(8,128)(2,1)}, u32[]{:S(2)}, u32[]{:S(2)}) collective-permute-start(bf16[128,1152]{1,0:T(8,128)(2,1)} %slice.202), channel_id=1, source_target_pairs={{0,2},{2,0},{4,6},{6,4},{8,10},{10,8},{12,14},{14,12},{16,18},{18,... | collective-permute-start | bytes 884744 | tf_op jit(solution)/shard_map/ppermute | solution.py:51
  184.8 16.1 %collective-permute-start.37 = (bf16[256,1536]{1,0:T(8,128)(2,1)}, bf16[256,1536]{1,0:T(8,128)(2,1)}, u32[]{:S(2)}, u32[]{:S(2)}) collective-permute-start(bf16[256,1536]{1,0:T(8,128)(2,1)} %get-tuple-element.262), channel_id=1, source_target_pairs={{0,2},{2,0},{4,6},{6,4},{8,10},{10,8},{12,14},{14,12},{16,18},{18,... | collective-permute-start | bytes 2359304 | tf_op jit(solution)/shard_map/ppermute | solution.py:51
  186.0 15.6 %collective-permute-start.38 = (bf16[256,1536]{1,0:T(8,128)(2,1)}, bf16[256,1536]{1,0:T(8,128)(2,1)}, u32[]{:S(2)}, u32[]{:S(2)}) collective-permute-start(bf16[256,1536]{1,0:T(8,128)(2,1)} %get-tuple-element.261), channel_id=1, source_target_pairs={{0,4},{2,6},{4,0},{6,2},{8,12},{10,14},{12,8},{14,10},{16,20},{18,... | collective-permute-start | bytes 2359304 | tf_op jit(solution)/shard_map/ppermute | solution.py:51
  210.9 12.3 %collective-permute-start.42 = (bf16[128,1536]{1,0:T(8,128)(2,1)}, bf16[128,1536]{1,0:T(8,128)(2,1)S(1)}, u32[]{:S(2)}, u32[]{:S(2)}) collective-permute-start(bf16[128,1536]{1,0:T(8,128)(2,1)} %get-tuple-element.290), channel_id=1, source_target_pairs={{0,2},{2,0},{4,6},{6,4},{8,10},{10,8},{12,14},{14,12},{16,18},{18,... | collective-permute-start | bytes 1179656 | tf_op jit(solution)/shard_map/ppermute | solution.py:51
  212.0 12.3 %collective-permute-start.43 = (bf16[128,1536]{1,0:T(8,128)(2,1)}, bf16[128,1536]{1,0:T(8,128)(2,1)}, u32[]{:S(2)}, u32[]{:S(2)}) collective-permute-start(bf16[128,1536]{1,0:T(8,128)(2,1)} %get-tuple-element.291), channel_id=1, source_target_pairs={{0,4},{2,6},{4,0},{6,2},{8,12},{10,14},{12,8},{14,10},{16,20},{18,... | collective-permute-start | bytes 1179656 | tf_op jit(solution)/shard_map/ppermute | solution.py:51
  213.1 21.6 %collective-permute-start.49 = (bf16[128,1152]{1,0:T(8,128)(2,1)}, bf16[128,1152]{1,0:T(8,128)(2,1)}, u32[]{:S(2)}, u32[]{:S(2)}) collective-permute-start(bf16[128,1152]{1,0:T(8,128)(2,1)} %get-tuple-element.320), channel_id=1, source_target_pairs={{0,2},{2,0},{4,6},{6,4},{8,10},{10,8},{12,14},{14,12},{16,18},{18,... | collective-permute-start | bytes 884744 | tf_op jit(solution)/shard_map/ppermute | solution.py:51
  214.1 20.6 %collective-permute-start.50 = (bf16[128,1152]{1,0:T(8,128)(2,1)}, bf16[128,1152]{1,0:T(8,128)(2,1)}, u32[]{:S(2)}, u32[]{:S(2)}) collective-permute-start(bf16[128,1152]{1,0:T(8,128)(2,1)} %get-tuple-element.321), channel_id=1, source_target_pairs={{0,4},{2,6},{4,0},{6,2},{8,12},{10,14},{12,8},{14,10},{16,20},{18,... | collective-permute-start | bytes 884744 | tf_op jit(solution)/shard_map/ppermute | solution.py:51
  226.6 40.5 %collective-permute-start.47 = (bf16[256,1536]{1,0:T(8,128)(2,1)}, bf16[256,1536]{1,0:T(8,128)(2,1)}, u32[]{:S(2)}, u32[]{:S(2)}) collective-permute-start(bf16[256,1536]{1,0:T(8,128)(2,1)} %get-tuple-element.295), channel_id=1, source_target_pairs={{0,2},{2,0},{4,6},{6,4},{8,10},{10,8},{12,14},{14,12},{16,18},{18,... | collective-permute-start | bytes 2359304 | tf_op jit(solution)/shard_map/ppermute | solution.py:51
  227.6 40.5 %collective-permute-start.48 = (bf16[256,1536]{1,0:T(8,128)(2,1)}, bf16[256,1536]{1,0:T(8,128)(2,1)}, u32[]{:S(2)}, u32[]{:S(2)}) collective-permute-start(bf16[256,1536]{1,0:T(8,128)(2,1)} %get-tuple-element.294), channel_id=1, source_target_pairs={{0,4},{2,6},{4,0},{6,2},{8,12},{10,14},{12,8},{14,10},{16,20},{18,... | collective-permute-start | bytes 2359304 | tf_op jit(solution)/shard_map/ppermute | solution.py:51
  236.8 26.4 %collective-permute-start.51 = (bf16[256,1152]{1,0:T(8,128)(2,1)}, bf16[256,1152]{1,0:T(8,128)(2,1)}, u32[]{:S(2)}, u32[]{:S(2)}) collective-permute-start(bf16[256,1152]{1,0:T(8,128)(2,1)} %get-tuple-element.324), channel_id=1, source_target_pairs={{0,2},{2,0},{4,6},{6,4},{8,10},{10,8},{12,14},{14,12},{16,18},{18,... | collective-permute-start | bytes 1769480 | tf_op jit(solution)/shard_map/ppermute | solution.py:51
  237.9 26.6 %collective-permute-start.52 = (bf16[256,1152]{1,0:T(8,128)(2,1)}, bf16[256,1152]{1,0:T(8,128)(2,1)}, u32[]{:S(2)}, u32[]{:S(2)}) collective-permute-start(bf16[256,1152]{1,0:T(8,128)(2,1)} %get-tuple-element.325), channel_id=1, source_target_pairs={{0,4},{2,6},{4,0},{6,2},{8,12},{10,14},{12,8},{14,10},{16,20},{18,... | collective-permute-start | bytes 1769480 | tf_op jit(solution)/shard_map/ppermute | solution.py:51
  242.4 13.1 %collective-permute-start.44 = (bf16[128,1536]{1,0:T(8,128)(2,1)S(1)}, bf16[128,1536]{1,0:T(8,128)(2,1)}, u32[]{:S(2)}, u32[]{:S(2)}) collective-permute-start(bf16[128,1536]{1,0:T(8,128)(2,1)S(1)} %slice.309), channel_id=1, source_target_pairs={{0,8},{2,10},{4,12},{6,14},{8,0},{10,2},{12,4},{14,6},{16,24},{18,... | collective-permute-start | bytes 1179656 | tf_op jit(solution)/shard_map/ppermute | solution.py:51
  262.2 22.2 %collective-permute-start.45 = (bf16[128,1536]{1,0:T(8,128)(2,1)}, bf16[128,1536]{1,0:T(8,128)(2,1)S(1)}, u32[]{:S(2)}, u32[]{:S(2)}) collective-permute-start(bf16[128,1536]{1,0:T(8,128)(2,1)} %get-tuple-element.314), channel_id=1, source_target_pairs={{0,2},{2,0},{4,6},{6,4},{8,10},{10,8},{12,14},{14,12},{16,18},{18,... | collective-permute-start | bytes 1179656 | tf_op jit(solution)/shard_map/ppermute | solution.py:51
  263.2 21.2 %collective-permute-start.46 = (bf16[128,1536]{1,0:T(8,128)(2,1)}, bf16[128,1536]{1,0:T(8,128)(2,1)}, u32[]{:S(2)}, u32[]{:S(2)}) collective-permute-start(bf16[128,1536]{1,0:T(8,128)(2,1)} %get-tuple-element.315), channel_id=1, source_target_pairs={{0,4},{2,6},{4,0},{6,2},{8,12},{10,14},{12,8},{14,10},{16,20},{18,... | collective-permute-start | bytes 1179656 | tf_op jit(solution)/shard_map/ppermute | solution.py:51
  264.4 20.0 %collective-permute-start.53 = (bf16[128,1024]{1,0:T(8,128)(2,1)}, bf16[128,1024]{1,0:T(8,128)(2,1)}, u32[]{:S(2)}, u32[]{:S(2)}) collective-permute-start(bf16[128,1024]{1,0:T(8,128)(2,1)} %get-tuple-element.331), channel_id=1, source_target_pairs={{0,2},{2,0},{4,6},{6,4},{8,10},{10,8},{12,14},{14,12},{16,18},{18,... | collective-permute-start | bytes 786440 | tf_op jit(solution)/shard_map/ppermute | solution.py:51
  267.1 17.3 %collective-permute-start.54 = (bf16[128,1024]{1,0:T(8,128)(2,1)}, bf16[128,1024]{1,0:T(8,128)(2,1)}, u32[]{:S(2)}, u32[]{:S(2)}) collective-permute-start(bf16[128,1024]{1,0:T(8,128)(2,1)} %get-tuple-element.332), channel_id=1, source_target_pairs={{0,4},{2,6},{4,0},{6,2},{8,12},{10,14},{12,8},{14,10},{16,20},{18,... | collective-permute-start | bytes 786440 | tf_op jit(solution)/shard_map/ppermute | solution.py:51
  271.9 23.1 %collective-permute-start.57 = (bf16[128,2688]{1,0:T(8,128)(2,1)}, bf16[128,2688]{1,0:T(8,128)(2,1)}, u32[]{:S(2)}, u32[]{:S(2)}) collective-permute-start(bf16[128,2688]{1,0:T(8,128)(2,1)} %pad_maximum_fusion.1), channel_id=1, source_target_pairs={{0,8},{2,10},{4,12},{6,14},{8,0},{10,2},{12,4},{14,6},{16,24},{18,... | collective-permute-start | bytes 2064392 | tf_op jit(solution)/shard_map/ppermute | solution.py:51
  287.6 20.7 %collective-permute-start.55 = (bf16[256,1536]{1,0:T(8,128)(2,1)}, bf16[256,1536]{1,0:T(8,128)(2,1)}, u32[]{:S(2)}, u32[]{:S(2)}) collective-permute-start(bf16[256,1536]{1,0:T(8,128)(2,1)} %get-tuple-element.336), channel_id=1, source_target_pairs={{0,2},{2,0},{4,6},{6,4},{8,10},{10,8},{12,14},{14,12},{16,18},{18,... | collective-permute-start | bytes 2359304 | tf_op jit(solution)/shard_map/ppermute | solution.py:51
  288.6 20.7 %collective-permute-start.56 = (bf16[256,1536]{1,0:T(8,128)(2,1)}, bf16[256,1536]{1,0:T(8,128)(2,1)}, u32[]{:S(2)}, u32[]{:S(2)}) collective-permute-start(bf16[256,1536]{1,0:T(8,128)(2,1)} %get-tuple-element.337), channel_id=1, source_target_pairs={{0,4},{2,6},{4,0},{6,2},{8,12},{10,14},{12,8},{14,10},{16,20},{18,... | collective-permute-start | bytes 2359304 | tf_op jit(solution)/shard_map/ppermute | solution.py:51
  291.8 36.7 %collective-permute-start.63 = (bf16[256,1024]{1,0:T(8,128)(2,1)}, bf16[256,1024]{1,0:T(8,128)(2,1)S(1)}, u32[]{:S(2)}, u32[]{:S(2)}) collective-permute-start(bf16[256,1024]{1,0:T(8,128)(2,1)} %get-tuple-element.343), channel_id=1, source_target_pairs={{0,2},{2,0},{4,6},{6,4},{8,10},{10,8},{12,14},{14,12},{16,18},{18,... | collective-permute-start | bytes 1572872 | tf_op jit(solution)/shard_map/ppermute | solution.py:51
  292.8 35.7 %collective-permute-start.64 = (bf16[256,1024]{1,0:T(8,128)(2,1)}, bf16[256,1024]{1,0:T(8,128)(2,1)S(1)}, u32[]{:S(2)}, u32[]{:S(2)}) collective-permute-start(bf16[256,1024]{1,0:T(8,128)(2,1)} %get-tuple-element.342), channel_id=1, source_target_pairs={{0,4},{2,6},{4,0},{6,2},{8,12},{10,14},{12,8},{14,10},{16,20},{18,... | collective-permute-start | bytes 1572872 | tf_op jit(solution)/shard_map/ppermute | solution.py:51
  297.6 24.0 %collective-permute-start.59 = (bf16[64,4224]{1,0:T(8,128)(2,1)S(1)}, bf16[64,4224]{1,0:T(8,128)(2,1)S(1)}, u32[]{:S(2)}, u32[]{:S(2)}) collective-permute-start(bf16[64,4224]{1,0:T(8,128)(2,1)S(1)} %pad_maximum_fusion.2), channel_id=1, source_target_pairs={{0,16},{2,18},{4,20},{6,22},{8,24},{10,26},{12,28},{14,30},{16,0},... | collective-permute-start | bytes 1622024 | tf_op jit(solution)/shard_map/ppermute | solution.py:51
  311.0 17.3 %collective-permute-start.58 = (bf16[128,1536]{1,0:T(8,128)(2,1)S(1)}, bf16[128,1536]{1,0:T(8,128)(2,1)S(1)}, u32[]{:S(2)}, u32[]{:S(2)}) collective-permute-start(bf16[128,1536]{1,0:T(8,128)(2,1)S(1)} %slice.308), channel_id=1, source_target_pairs={{0,8},{2,10},{4,12},{6,14},{8,0},{10,2},{12,4},{14,6},{16,24},{18,... | collective-permute-start | bytes 1179656 | tf_op jit(solution)/shard_map/ppermute | solution.py:51
  311.1 31.2 %collective-permute-start.61 = (bf16[512,1024]{1,0:T(8,128)(2,1)S(1)}, bf16[512,1024]{1,0:T(8,128)(2,1)S(1)}, u32[]{:S(2)}, u32[]{:S(2)}) collective-permute-start(bf16[512,1024]{1,0:T(8,128)(2,1)S(1)} %copy-done.44), channel_id=1, source_target_pairs={{0,1},{1,0},{2,3},{3,2},{4,5},{5,4},{6,7},{7,6},{8,9},{9,8},{10,11... | collective-permute-start | bytes 3145736 | tf_op jit(solution)/shard_map/ppermute | solution.py:653
  328.3 21.7 %collective-permute-start.60 = (bf16[512,1024]{1,0:T(8,128)(2,1)S(1)}, bf16[512,1024]{1,0:T(8,128)(2,1)S(1)}, u32[]{:S(2)}, u32[]{:S(2)}) collective-permute-start(bf16[512,1024]{1,0:T(8,128)(2,1)S(1)} %copy-done.43), channel_id=1, source_target_pairs={{0,1},{1,0},{2,3},{3,2},{4,5},{5,4},{6,7},{7,6},{8,9},{9,8},{10,11... | collective-permute-start | bytes 3145736 | tf_op jit(solution)/shard_map/ppermute | solution.py:653
  328.8 13.0 %collective-permute-start.65 = (bf16[128,1024]{1,0:T(8,128)(2,1)S(1)}, bf16[128,1024]{1,0:T(8,128)(2,1)S(1)}, u32[]{:S(2)}, u32[]{:S(2)}) collective-permute-start(bf16[128,1024]{1,0:T(8,128)(2,1)S(1)} %slice.311), channel_id=1, source_target_pairs={{0,8},{2,10},{4,12},{6,14},{8,0},{10,2},{12,4},{14,6},{16,24},{18,... | collective-permute-start | bytes 786440 | tf_op jit(solution)/shard_map/ppermute | solution.py:51
  (72 other events, 617.0 us)
